TPU v7x, 32 devices: a whole 2x2x4 slice. The times are simulated.
32 devices in a mesh: clip: 8 (over z, x), band: 4 (over y, core).
Axes of the slice: x: 2, y: 2, z: 4, core: 2. Of those that a mesh axis runs over, the one named last changes fastest.
Arguments:
- latents: float32 [8, 5, 32, 16, 8], P('clip', None, 'band'), may hold values from -6 to 6
- noise_field: float32 [8, 5, 32, 16, 8], P('clip', None, 'band'), may hold values from -6 to 6
- timesteps: int32 [8], P('clip'), may hold values from 0 to 999
- null_flags: int32 [8], P('clip'), may hold values 0 or 1
- frame_mask: int32 [8, 5], P('clip'), may hold values from 0 to 1, as said below
- context: bfloat16 [8, 77, 4096], P('clip'), may hold values from -6 to 6
- w_wide: float32 [1024, 30720], P('clip')
- m_wide: float32 [1024, 30720], P('clip'), may hold values from -8.940697e-08 to 8.940697e-08
- v_wide: float32 [1024, 30720], P('clip'), may hold values from 1.0983557e-15 to 4.3519752e-15
- w_deep: float32 [4096, 4096], P('clip'), may hold values from -0.09375 to 0.09375
- m_deep: float32 [4096, 4096], P('clip'), may hold values from -8.940697e-08 to 8.940697e-08
- v_deep: float32 [4096, 4096], P('clip'), may hold values from 1.0983557e-15 to 4.3519752e-15
- w_small: float32 [19, 1024], replicated
- m_small: float32 [19, 1024], replicated, may hold values from -8.940697e-08 to 8.940697e-08
- v_small: float32 [19, 1024], replicated, may hold values from 1.0983557e-15 to 4.3519752e-15
Outputs:
- loss: float32 [], replicated
- grad_norm: float32 [], replicated
- new_w_wide: float32 [1024, 30720], P('clip')
- new_m_wide: float32 [1024, 30720], P('clip')
- new_v_wide: float32 [1024, 30720], P('clip')
- new_w_deep: float32 [4096, 4096], P('clip')
- new_m_deep: float32 [4096, 4096], P('clip')
- new_v_deep: float32 [4096, 4096], P('clip')
- new_w_small: float32 [19, 1024], replicated
- new_m_small: float32 [19, 1024], replicated
- new_v_small: float32 [19, 1024], replicated
Inputs may be any that keep to these rules, and one draw needn't show every extreme that they name: `frame_mask`: every clip counts at least one frame.
All inputs are finite; a program needn't handle non-finite values. No bound on the sum of `null_flags` on one device may be relied on, other than what follows from the above.
Results may differ from a plain program's by a relative error of at most 0.0024.
The roundings to bfloat16 on the way count: a program that leaves them out, or rounds other values in their place, can miss the bound.
Values may be sent and summed in bfloat16 or wider, within the bound.
A program may use at most 640 MiB of HBM per device.

v0:
```python
from functools import partial
import math

import jax
import jax.numpy as jnp
from jax import lax
from jax.sharding import PartitionSpec as P

D = 1024
HEADS = 16
HEAD_DIM = 64
FF = 4096
CH = 8
SPACE = 16
WIN = 8
SHIFT = 4
TMAX = 1000
STEP = 10


EPS_NORM = 1e-06
CLIP_MAX = 0.001
BETA_ONE = 0.9
BETA_TWO = 0.95
ADAM_EPS = 1e-08
DECAY = 0.1
SELF_FORMS = ("wqhd,wkhd->whqk", "whqk,wkhd->wqhd", "whqk,wqhd->wkhd", "whqk,wkhd->wqhd")
CROSS_FORMS = ("qhd,khd->hqk", "hqk,khd->qhd", "hqk,qhd->khd", "hqk,khd->qhd")


def from_partner(block, axis, distance):
    count = lax.axis_size(axis)
    route = []
    for low in range(count):
        high = low | 1 << distance
        if high != low and high < count:
            route += [(low, high), (high, low)]
    return lax.ppermute(block, axis, route)


def shifted(value, axis, by):
    length = lax.axis_size(axis)
    return lax.ppermute(value, axis, [(i, (i + by) % length) for i in range(length)])


def matmul(left_op, right_op):
    return jnp.dot(left_op, right_op, preferred_element_type=jnp.float32)


def matmul_tn(left_op, right_op, precision=None):
    return lax.dot_general(
        left_op,
        right_op,
        (((0,), (0,)), ((), ())),
        precision=precision,
        preferred_element_type=jnp.float32,
    )


def matmul_nt(left_op, right_op):
    return lax.dot_general(
        left_op, right_op, (((1,), (1,)), ((), ())), preferred_element_type=jnp.float32
    )


def layer_norm(field_in):
    average = jnp.mean(field_in, -1, keepdims=True)
    centred = field_in - average
    return centred * lax.rsqrt(jnp.mean(centred * centred, -1, keepdims=True) + EPS_NORM)


def norm_modulated(field_in, shift_vec, scale_vec):
    return layer_norm(field_in) * (1.0 + scale_vec) + shift_vec


def norm_gained(field_in, gain_vec):
    return layer_norm(field_in) * gain_vec


def time_features(time_value):
    half_width = D // 2
    frequency = jnp.exp(-math.log(10000.0) * jnp.arange(half_width, dtype=jnp.float32) / half_width)
    angles = time_value[..., None] * frequency
    return jnp.concatenate([jnp.cos(angles), jnp.sin(angles)], -1)


def to_windows(token_grid, shape_win):
    num_frames, num_rows, num_cols, feat_dim = token_grid.shape
    win_frames, win_rows, win_cols = shape_win
    shaped = token_grid.reshape(
        num_frames // win_frames,
        win_frames,
        num_rows // win_rows,
        win_rows,
        num_cols // win_cols,
        win_cols,
        feat_dim,
    )
    return shaped.transpose(0, 2, 4, 1, 3, 5, 6).reshape(
        -1, win_frames * win_rows * win_cols, feat_dim
    )


def from_windows(blocks, grid_shape, shape_win):
    num_frames, num_rows, num_cols = grid_shape
    win_frames, win_rows, win_cols = shape_win
    feat_dim = blocks.shape[-1]
    shaped = blocks.reshape(
        num_frames // win_frames,
        num_rows // win_rows,
        num_cols // win_cols,
        win_frames,
        win_rows,
        win_cols,
        feat_dim,
    )
    return shaped.transpose(0, 3, 1, 4, 2, 5, 6).reshape(num_frames, num_rows, num_cols, feat_dim)


def split_heads(field_in):
    return field_in.reshape(field_in.shape[:-1] + (HEADS, HEAD_DIM))


def merge_heads(field_in):
    return field_in.reshape(field_in.shape[:-2] + (D,))


def attend_forward(queries, key_heads, value_heads, einsum_forms):
    scores = jnp.einsum(
        einsum_forms[0], queries, key_heads, preferred_element_type=jnp.float32
    ) * HEAD_DIM ** (-0.5)
    log_total = jax.nn.logsumexp(scores, axis=-1, keepdims=True)
    probabilities = jnp.exp(scores - log_total)
    attended = jnp.einsum(
        einsum_forms[1],
        probabilities.astype(jnp.bfloat16),
        value_heads,
        preferred_element_type=jnp.float32,
    )
    return (attended, log_total)


def attend_backward(queries, key_heads, value_heads, log_total, grad_out, einsum_forms):
    scores = jnp.einsum(
        einsum_forms[0], queries, key_heads, preferred_element_type=jnp.float32
    ) * HEAD_DIM ** (-0.5)
    probabilities = jnp.exp(scores - log_total)
    grad_values = jnp.einsum(
        einsum_forms[2],
        probabilities.astype(jnp.bfloat16),
        grad_out,
        preferred_element_type=jnp.float32,
    )
    grad_probs = jnp.einsum(
        einsum_forms[0], grad_out, value_heads, preferred_element_type=jnp.float32
    )
    inner_sum = jnp.sum(probabilities * grad_probs, -1, keepdims=True)
    grad_scores = (probabilities * (grad_probs - inner_sum)).astype(jnp.bfloat16)
    grad_queries = jnp.einsum(
        einsum_forms[3], grad_scores, key_heads, preferred_element_type=jnp.float32
    ) * HEAD_DIM ** (-0.5)
    grad_keys = jnp.einsum(
        einsum_forms[2], grad_scores, queries, preferred_element_type=jnp.float32
    ) * HEAD_DIM ** (-0.5)
    return (grad_queries, grad_keys, grad_values)


def mlp_forward(stream, modul, up_weight, down_weight):
    mlp_val, norm_back = jax.vjp(norm_modulated, stream, modul[3], modul[4])
    mlp_in = mlp_val.astype(jnp.bfloat16)
    up_proj = matmul(mlp_in, up_weight)
    gelu_val, gelu_back = jax.vjp(partial(jax.nn.gelu, approximate=False), up_proj)
    gelu_low = gelu_val.astype(jnp.bfloat16)
    down_proj = matmul(gelu_low, down_weight)
    return (stream + modul[5] * down_proj, (norm_back, mlp_in, gelu_back, gelu_low, down_proj))


def mlp_backward(grad_stream, modul, up_weight, down_weight, saved):
    norm_back, mlp_in, gelu_back, gelu_low, down_proj = saved
    grad_down = (modul[5] * grad_stream).astype(jnp.bfloat16)
    grad_gate = jnp.sum(grad_stream * down_proj, 0)
    grad_w_down = matmul_tn(gelu_low, grad_down)
    grad_up = gelu_back(matmul_nt(grad_down, down_weight))[0].astype(jnp.bfloat16)
    grad_w_up = matmul_tn(mlp_in, grad_up)
    grad_part, grad_shift, grad_scale = norm_back(matmul_nt(grad_up, up_weight))
    return (grad_stream + grad_part, grad_w_up, grad_w_down, (grad_shift, grad_scale, grad_gate))


def adam_update(weight, first_mom, second_mom, grad_val, learn_rate):
    first_mom = BETA_ONE * first_mom + (1.0 - BETA_ONE) * grad_val
    second_mom = BETA_TWO * second_mom + (1.0 - BETA_TWO) * grad_val * grad_val
    first_hat = first_mom / (1.0 - BETA_ONE**STEP)
    second_hat = second_mom / (1.0 - BETA_TWO**STEP)
    weight = weight - learn_rate * (first_hat / (jnp.sqrt(second_hat) + ADAM_EPS) + DECAY * weight)
    return (weight, first_mom, second_mom)


def per_device(
    latents,
    noise_field,
    timesteps,
    null_flags,
    frame_mask,
    context,
    w_wide,
    m_wide,
    v_wide,
    w_deep,
    m_deep,
    v_deep,
    w_small,
    m_small,
    v_small,
):
    wide_bf = w_wide.astype(jnp.bfloat16)
    deep_bf = w_deep.astype(jnp.bfloat16)
    gathered = (
        lax.all_gather(wide_bf[:, : 12 * D], "clip", axis=0, tiled=True),
        lax.all_gather(wide_bf[:, 12 * D : 15 * D], "clip", axis=0, tiled=True),
        lax.all_gather(wide_bf[:, 15 * D : 18 * D], "clip", axis=0, tiled=True),
        lax.all_gather(wide_bf[:, 18 * D : 19 * D], "clip", axis=0, tiled=True),
        lax.all_gather(wide_bf[:, 19 * D : 20 * D], "clip", axis=0, tiled=True),
        lax.all_gather(wide_bf[:, 20 * D : 21 * D], "clip", axis=0, tiled=True),
        lax.all_gather(wide_bf[:, 21 * D : 22 * D], "clip", axis=0, tiled=True),
        lax.all_gather(wide_bf[:, 22 * D : 22 * D + FF], "clip", axis=0, tiled=True),
        lax.all_gather(wide_bf[:, 22 * D + FF :], "clip", axis=0, tiled=True),
        lax.all_gather(deep_bf[:, :D], "clip", axis=0, tiled=True),
        lax.all_gather(deep_bf[:, D : 3 * D], "clip", axis=0, tiled=True),
        lax.all_gather(deep_bf[:, 3 * D :], "clip", axis=0, tiled=True),
    )
    (
        ada_w,
        qkv_a_w,
        qkv_b_w,
        out_a_w,
        out_b_w,
        query_w,
        cross_out_w,
        up_a_w,
        up_b_w,
        down_a_w,
        keyval_w,
        down_b_w,
    ) = gathered
    small_low = w_small.astype(jnp.bfloat16)
    small_val = small_low.astype(jnp.float32)
    num_frames, num_rows, num_cols = (latents.shape[1], latents.shape[2], latents.shape[3])
    grid_shape = (num_frames, num_rows, num_cols)
    tok_count = num_frames * num_rows * num_cols
    local_count = jnp.sum(frame_mask).astype(jnp.float32) * (num_rows * num_cols * CH)
    global_count = lax.psum(local_count, ("clip", "band"))
    time_value = timesteps[0].astype(jnp.float32)
    noise_angle = 0.5 * math.pi * time_value / TMAX
    signal, spread = (jnp.cos(noise_angle), jnp.sin(noise_angle))
    clean_tok = latents[0].reshape(tok_count, CH)
    noise_tok = noise_field[0].reshape(tok_count, CH)
    noisy_low = (signal * clean_tok + spread * noise_tok).astype(jnp.bfloat16)
    target = signal * noise_tok - spread * clean_tok
    time_low = jax.nn.silu(time_features(time_value)).astype(jnp.bfloat16)[None]
    modulation = matmul(time_low, ada_w).reshape(12, D)
    mod_a, mod_b = (modulation[:6], modulation[6:])
    stream_zero = matmul(noisy_low, small_low[:CH]) + small_val[2 * CH]
    normed_a, back_a = jax.vjp(norm_modulated, stream_zero, mod_a[0], mod_a[1])
    in_a = normed_a.astype(jnp.bfloat16)
    spatial = (1, num_rows, SPACE)
    qkv_a = (
        matmul(in_a, qkv_a_w).astype(jnp.bfloat16).reshape(num_frames, num_rows, num_cols, 3 * D)
    )
    blocks_a = to_windows(qkv_a, spatial)
    partner = from_partner(blocks_a[..., D:], "band", 0)
    keys_all = jnp.concatenate([blocks_a[..., D:], partner], 1)
    space_q = split_heads(blocks_a[..., :D])
    space_k = split_heads(keys_all[..., :D])
    space_v = split_heads(keys_all[..., D:])
    space_out, space_total = attend_forward(space_q, space_k, space_v, SELF_FORMS)
    att_a = from_windows(merge_heads(space_out.astype(jnp.bfloat16)), grid_shape, spatial).reshape(
        tok_count, D
    )
    proj_a = matmul(att_a, out_a_w)
    stream_one = stream_zero + mod_a[2] * proj_a
    stream_two, saved_a = mlp_forward(stream_one, mod_a, up_a_w, down_a_w)
    normed_b, back_b = jax.vjp(norm_modulated, stream_two, mod_b[0], mod_b[1])
    token_grid = normed_b.astype(jnp.bfloat16).reshape(num_frames, num_rows, num_cols, D)
    arrived = shifted(token_grid[:, :SHIFT], "band", -1)
    rolled = jnp.concatenate([token_grid[:, SHIFT:], arrived], 1).reshape(tok_count, D)
    temporal = (num_frames, WIN, WIN)
    qkv_b = matmul(rolled, qkv_b_w).astype(jnp.bfloat16)
    blocks_b = to_windows(qkv_b.reshape(num_frames, num_rows, num_cols, 3 * D), temporal)
    win_q = split_heads(blocks_b[..., :D])
    win_k = split_heads(blocks_b[..., D : 2 * D])
    win_v = split_heads(blocks_b[..., 2 * D :])
    win_out, win_total = attend_forward(win_q, win_k, win_v, SELF_FORMS)
    out_grid = from_windows(merge_heads(win_out.astype(jnp.bfloat16)), grid_shape, temporal)
    returned = shifted(out_grid[:, num_rows - SHIFT :], "band", 1)
    att_b = jnp.concatenate([returned, out_grid[:, : num_rows - SHIFT]], 1).reshape(tok_count, D)
    proj_b = matmul(att_b, out_b_w)
    stream_three = stream_two + mod_b[2] * proj_b
    cross_val, cross_back = jax.vjp(norm_gained, stream_three, small_val[2 * CH + 1])
    cross_in = cross_val.astype(jnp.bfloat16)
    query_proj = matmul(cross_in, query_w).astype(jnp.bfloat16)
    kept_text = context[0] * (1 - null_flags[0]).astype(jnp.bfloat16)
    keyval = matmul(kept_text, keyval_w).astype(jnp.bfloat16)
    cross_q = split_heads(query_proj)
    cross_k = split_heads(keyval[:, :D])
    cross_v = split_heads(keyval[:, D:])
    cross_out, cross_total = attend_forward(cross_q, cross_k, cross_v, CROSS_FORMS)
    crossed = merge_heads(cross_out.astype(jnp.bfloat16))
    stream_four = stream_three + matmul(crossed, cross_out_w)
    stream_five, saved_b = mlp_forward(stream_four, mod_b, up_b_w, down_b_w)
    final_val, final_back = jax.vjp(norm_gained, stream_five, small_val[2 * CH + 2])
    final_low = final_val.astype(jnp.bfloat16)
    head_low = small_low[CH : 2 * CH]
    predicted = matmul_nt(final_low, head_low)
    weight_row = jnp.repeat(frame_mask[0].astype(jnp.float32), num_rows * num_cols)[:, None]
    pred_error = predicted - target
    loss_part = jnp.sum(weight_row * pred_error * pred_error)
    grad_pred = (weight_row * pred_error * (2.0 / global_count)).astype(jnp.bfloat16)
    grad_head = matmul_tn(grad_pred, final_low)
    grad_stream, grad_gain_f = final_back(matmul(grad_pred, head_low))
    grad_stream, grad_up_b, grad_down_b, extra_b = mlp_backward(
        grad_stream, mod_b, up_b_w, down_b_w, saved_b
    )
    grad_cross = grad_stream.astype(jnp.bfloat16)
    grad_w_co = matmul_tn(crossed, grad_cross)
    grad_crossed = split_heads(matmul_nt(grad_cross, cross_out_w).astype(jnp.bfloat16))
    cq_grad, ck_grad, cv_grad = attend_backward(
        cross_q, cross_k, cross_v, cross_total, grad_crossed, CROSS_FORMS
    )
    grad_query = merge_heads(cq_grad).astype(jnp.bfloat16)
    grad_w_cq = matmul_tn(cross_in, grad_query)
    grad_part, grad_gain_c = cross_back(matmul_nt(grad_query, query_w))
    grad_keyval = jnp.concatenate([merge_heads(ck_grad), merge_heads(cv_grad)], 1)
    grad_w_ckv = matmul_tn(kept_text.astype(jnp.float32), grad_keyval, lax.Precision.HIGHEST)
    grad_stream = grad_stream + grad_part
    grad_proj = (mod_b[2] * grad_stream).astype(jnp.bfloat16)
    grad_gate_b = jnp.sum(grad_stream * proj_b, 0)
    grad_w_ob = matmul_tn(att_b, grad_proj)
    grad_att = (
        matmul_nt(grad_proj, out_b_w)
        .astype(jnp.bfloat16)
        .reshape(num_frames, num_rows, num_cols, D)
    )
    fetched = shifted(grad_att[:, :SHIFT], "band", -1)
    grad_rolled = jnp.concatenate([grad_att[:, SHIFT:], fetched], 1)
    grad_win = split_heads(to_windows(grad_rolled, temporal))
    wq_grad, wk_grad, wv_grad = attend_backward(
        win_q, win_k, win_v, win_total, grad_win, SELF_FORMS
    )
    grad_blocks = jnp.concatenate(
        [merge_heads(wq_grad), merge_heads(wk_grad), merge_heads(wv_grad)], -1
    )
    grad_qkv = (
        from_windows(grad_blocks, grid_shape, temporal)
        .reshape(tok_count, 3 * D)
        .astype(jnp.bfloat16)
    )
    grad_w_qkvb = matmul_tn(rolled, grad_qkv)
    grad_in_roll = matmul_nt(grad_qkv, qkv_b_w).reshape(num_frames, num_rows, num_cols, D)
    sent_back = shifted(grad_in_roll[:, num_rows - SHIFT :], "band", 1)
    grad_normed = jnp.concatenate([sent_back, grad_in_roll[:, : num_rows - SHIFT]], 1).reshape(
        tok_count, D
    )
    grad_part, grad_shift_b, grad_scale_b = back_b(grad_normed)
    grad_stream = grad_stream + grad_part
    grad_stream, grad_up_a, grad_down_a, extra_a = mlp_backward(
        grad_stream, mod_a, up_a_w, down_a_w, saved_a
    )
    grad_proj = (mod_a[2] * grad_stream).astype(jnp.bfloat16)
    grad_gate_a = jnp.sum(grad_stream * proj_a, 0)
    grad_w_oa = matmul_tn(att_a, grad_proj)
    grad_att = (
        matmul_nt(grad_proj, out_a_w)
        .astype(jnp.bfloat16)
        .reshape(num_frames, num_rows, num_cols, D)
    )
    grad_space = split_heads(to_windows(grad_att, spatial))
    sq_grad, sk_grad, sv_grad = attend_backward(
        space_q, space_k, space_v, space_total, grad_space, SELF_FORMS
    )
    half_len = space_q.shape[1]
    key_grads = merge_heads(sk_grad)
    value_grads = merge_heads(sv_grad)
    back_keys, back_values = from_partner(
        (key_grads[:, half_len:], value_grads[:, half_len:]), "band", 0
    )
    grad_blocks = jnp.concatenate(
        [
            merge_heads(sq_grad),
            key_grads[:, :half_len] + back_keys,
            value_grads[:, :half_len] + back_values,
        ],
        -1,
    )
    grad_qkv = (
        from_windows(grad_blocks, grid_shape, spatial)
        .reshape(tok_count, 3 * D)
        .astype(jnp.bfloat16)
    )
    grad_w_qkva = matmul_tn(in_a, grad_qkv)
    grad_part, grad_shift_a, grad_scale_a = back_a(matmul_nt(grad_qkv, qkv_a_w))
    grad_stream = grad_stream + grad_part
    grad_patch = matmul_tn(noisy_low.astype(jnp.float32), grad_stream, lax.Precision.HIGHEST)
    grad_bias = jnp.sum(grad_stream, 0)
    grad_modul = jnp.stack(
        [
            grad_shift_a,
            grad_scale_a,
            grad_gate_a,
            extra_a[0],
            extra_a[1],
            extra_a[2],
            grad_shift_b,
            grad_scale_b,
            grad_gate_b,
            extra_b[0],
            extra_b[1],
            extra_b[2],
        ]
    ).reshape(1, 12 * D)
    grad_small = jnp.concatenate(
        [grad_patch, grad_head, grad_bias[None], grad_gain_c[None], grad_gain_f[None]], 0
    )
    leading = jnp.concatenate(
        [time_low.astype(jnp.float32).reshape(D, 1) * grad_modul, grad_w_qkva], 1
    )
    members = (
        leading,
        grad_w_qkvb,
        grad_w_oa,
        grad_w_ob,
        grad_w_cq,
        grad_w_co,
        grad_up_a,
        grad_up_b,
        grad_down_a,
        grad_w_ckv,
        grad_down_b,
    )
    partial_sums = (
        lax.psum_scatter(members[0], "clip", scatter_dimension=0, tiled=True),
        lax.psum_scatter(members[1], "clip", scatter_dimension=0, tiled=True),
        lax.psum_scatter(members[2], "clip", scatter_dimension=0, tiled=True),
        lax.psum_scatter(members[3], "clip", scatter_dimension=0, tiled=True),
        lax.psum_scatter(members[4], "clip", scatter_dimension=0, tiled=True),
        lax.psum_scatter(members[5], "clip", scatter_dimension=0, tiled=True),
        lax.psum_scatter(members[6], "clip", scatter_dimension=0, tiled=True),
        lax.psum_scatter(members[7], "clip", scatter_dimension=0, tiled=True),
        lax.psum_scatter(members[8], "clip", scatter_dimension=0, tiled=True),
        lax.psum_scatter(members[9], "clip", scatter_dimension=0, tiled=True),
        lax.psum_scatter(members[10], "clip", scatter_dimension=0, tiled=True),
    )
    summed = lax.psum(
        (
            partial_sums[0],
            partial_sums[1],
            partial_sums[2],
            partial_sums[3],
            partial_sums[4],
            partial_sums[5],
            partial_sums[6],
            partial_sums[7],
            partial_sums[8],
            partial_sums[9],
            partial_sums[10],
        ),
        "band",
    )
    wide_parts = list(summed[:8])
    wide_sum = jnp.concatenate(wide_parts, 1)
    deep_sum = jnp.concatenate([summed[8], summed[9], summed[10]], 1)
    square_part = (jnp.sum(wide_sum * wide_sum) + jnp.sum(deep_sum * deep_sum)) / lax.axis_size(
        "band"
    )
    loss_sum, square_sum, small_sum = lax.psum(
        (loss_part, square_part, grad_small), ("clip", "band")
    )
    grad_norm = jnp.sqrt(square_sum + jnp.sum(small_sum * small_sum))
    factor = CLIP_MAX / jnp.maximum(grad_norm, CLIP_MAX)
    new_wide = adam_update(w_wide, m_wide, v_wide, wide_sum * factor, 0.15)
    new_deep = adam_update(w_deep, m_deep, v_deep, deep_sum * factor, 0.05)
    new_small = adam_update(w_small, m_small, v_small, small_sum * factor, 0.5)
    loss = loss_sum / global_count
    return (
        loss,
        grad_norm,
        new_wide[0],
        new_wide[1],
        new_wide[2],
        new_deep[0],
        new_deep[1],
        new_deep[2],
        new_small[0],
        new_small[1],
        new_small[2],
    )


def solution(mesh):
    in_specs = (
        P("clip", None, "band", None, None),
        P("clip", None, "band", None, None),
        P("clip"),
        P("clip"),
        P("clip", None),
        P("clip", None, None),
        P("clip", None),
        P("clip", None),
        P("clip", None),
        P("clip", None),
        P("clip", None),
        P("clip", None),
        P(),
        P(),
        P(),
    )
    out_specs = (
        P(),
        P(),
        P("clip", None),
        P("clip", None),
        P("clip", None),
        P("clip", None),
        P("clip", None),
        P("clip", None),
        P(),
        P(),
        P(),
    )
    return jax.shard_map(
        per_device, mesh=mesh, in_specs=in_specs, out_specs=out_specs, check_vma=False
    )
```

profile of v0, /device:TPU:0, one launch (start us, length us, event | category | flops | bytes accessed | tf_op | source)
XLA Modules:
  0.0 5635.2 jit_solution(6944196299729610504)
XLA Ops:
  7.2 9.6 convert_element_type.200
  48.3 455.7 %all-gather.13.cloned.1.call-done = bf16[1024,12288]{1,0:T(8,128)(2,1)} async-done(((bf16[128,12288]{1,0:T(8,128)(2,1)}), bf16[1024,12288]{1,0:T(8,128)(2,1)}) %all-gather.13.cloned.1.call-update) | async-done | bytes 25165840 | tf_op jit(solution)/shard_map/all_gather | solution.py:218
  504.0 9.9 fusion.127
  514.6 91.2 %all-gather.15.cloned.1.call-done = bf16[1024,3072]{1,0:T(8,128)(2,1)} async-done(((bf16[128,3072]{1,0:T(8,128)(2,1)}), bf16[1024,3072]{1,0:T(8,128)(2,1)}) %all-gather.15.cloned.1.call-update) | async-done | bytes 6291472 | tf_op jit(solution)/shard_map/all_gather | solution.py:219
  662.9 118.5 %all-gather.19.cloned.1.call-done = bf16[1024,4096]{1,0:T(8,128)(2,1)} async-done(((bf16[128,4096]{1,0:T(8,128)(2,1)}), bf16[1024,4096]{1,0:T(8,128)(2,1)}) %all-gather.19.cloned.1.call-update) | async-done | bytes 8388624 | tf_op jit(solution)/shard_map/all_gather | solution.py:225
  781.4 33.4 multiply_convert_fusion.3
  814.9 92.3 %all-gather.21.cloned.1.call-done = bf16[4096,1024]{1,0:T(8,128)(2,1)} async-done(((bf16[512,1024]{1,0:T(8,128)(2,1)}), bf16[4096,1024]{1,0:T(8,128)(2,1)}) %all-gather.21.cloned.1.call-update) | async-done | bytes 8388624 | tf_op jit(solution)/shard_map/all_gather | solution.py:227
  907.1 11.2 fusion.109
  922.5 42.2 psum.106
  970.7 36.7 all-gather.23.cloned.1.call-done
  1025.3 9.9 multiply_reduce_fusion.2
  1044.6 9.7 fusion.25
  1066.7 169.3 %all-gather.27.cloned.1.call-done = bf16[4096,2048]{1,0:T(8,128)(2,1)} async-done(((bf16[512,2048]{1,0:T(8,128)(2,1)}), bf16[4096,2048]{1,0:T(8,128)(2,1)}) %all-gather.27.cloned.1.call-update) | async-done | bytes 16777232 | tf_op jit(solution)/shard_map/all_gather | solution.py:228
  1248.4 37.3 all-gather.25.cloned.1.call-done
  1292.6 43.0 all-gather.29.cloned.1.call-done
  1346.5 38.9 all-gather.31.cloned.1.call-done
  1392.3 118.7 %all-gather.33.cloned.1.call-done = bf16[1024,4096]{1,0:T(8,128)(2,1)} async-done(((bf16[128,4096]{1,0:T(8,128)(2,1)}), bf16[1024,4096]{1,0:T(8,128)(2,1)}) %all-gather.33.cloned.1.call-update) | async-done | bytes 8388624 | tf_op jit(solution)/shard_map/all_gather | solution.py:226
  1511.0 33.3 multiply_convert_fusion.2
  1544.3 91.7 %all-gather.35.cloned.1.call-done = bf16[4096,1024]{1,0:T(8,128)(2,1)} async-done(((bf16[512,1024]{1,0:T(8,128)(2,1)}), bf16[4096,1024]{1,0:T(8,128)(2,1)}) %all-gather.35.cloned.1.call-update) | async-done | bytes 8388624 | tf_op jit(solution)/shard_map/all_gather | solution.py:229
  1636.0 11.3 fusion.106
  1653.3 17.7 add_convert_fusion.1
  1671.1 11.6 multiply_reduce_fusion.12
  1755.3 11.0 multiply_reduce_fusion.1
  1766.2 11.7 multiply_convert_fusion
  1820.5 12.0 collective-permute-done.4
  1840.9 18.3 add_convert_fusion
  1859.3 11.2 multiply_reduce_fusion.15
  1890.9 13.9 fusion.94
  1905.4 13.4 fusion.88
  1919.5 13.1 fusion.92
  1934.4 13.1 fusion.51
  1952.4 17.7 fusion.34
  2056.5 13.2 fusion.23
  2069.7 17.2 broadcast_multiply_fusion
  2086.9 41.8 pad_maximum_fusion
  2136.4 139.8 %reduce-scatter.14.cloned.1.call-done = f32[128,3072]{1,0:T(8,128)} async-done(((f32[1024,3072]{1,0:T(8,128)}), f32[128,3072]{1,0:T(8,128)}) %reduce-scatter.14.cloned.1.call-update) | async-done | bytes 1572880 | tf_op jit(solution)/shard_map/reduce_scatter | solution.py:441
  2276.2 285.1 %reduce-scatter.26.cloned.1.call-done = f32[128,4096]{1,0:T(8,128)} async-done(((f32[1024,4096]{1,0:T(8,128)}), f32[128,4096]{1,0:T(8,128)}) %reduce-scatter.26.cloned.1.call-update) | async-done | bytes 2097168 | tf_op jit(solution)/shard_map/reduce_scatter | solution.py:447
  2561.3 285.5 %reduce-scatter.32.cloned.1.call-done = f32[512,1024]{1,0:T(8,128)} async-done(((f32[4096,1024]{1,0:T(8,128)}), f32[512,1024]{1,0:T(8,128)}) %reduce-scatter.32.cloned.1.call-update) | async-done | bytes 2097168 | tf_op jit(solution)/shard_map/reduce_scatter | solution.py:450
  2846.8 285.0 %reduce-scatter.24.cloned.1.call-done = f32[128,4096]{1,0:T(8,128)} async-done(((f32[1024,4096]{1,0:T(8,128)}), f32[128,4096]{1,0:T(8,128)}) %reduce-scatter.24.cloned.1.call-update) | async-done | bytes 2097168 | tf_op jit(solution)/shard_map/reduce_scatter | solution.py:446
  3131.8 285.6 %reduce-scatter.28.cloned.1.call-done = f32[512,1024]{1,0:T(8,128)} async-done(((f32[4096,1024]{1,0:T(8,128)}), f32[512,1024]{1,0:T(8,128)}) %reduce-scatter.28.cloned.1.call-update) | async-done | bytes 2097168 | tf_op jit(solution)/shard_map/reduce_scatter | solution.py:448
  3417.4 546.2 %reduce-scatter.30.cloned.1.call-done = f32[512,2048]{1,0:T(8,128)} async-done(((f32[4096,2048]{1,0:T(8,128)}), f32[512,2048]{1,0:T(8,128)}) %reduce-scatter.30.cloned.1.call-update) | async-done | bytes 4194320 | tf_op jit(solution)/shard_map/reduce_scatter | solution.py:449
  3963.6 976.7 %reduce-scatter.12.cloned.1.call-done = f32[128,15360]{1,0:T(8,128)} async-done(((f32[1024,15360]{1,0:T(8,128)}), f32[128,15360]{1,0:T(8,128)}) %reduce-scatter.12.cloned.1.call-update) | async-done | bytes 7864336 | tf_op jit(solution)/shard_map/reduce_scatter | solution.py:440
  4940.3 126.7 %all-reduce.5.cloned.1.call-done = f32[19,1024]{1,0:T(8,128)} async-done(((f32[19,1024]{1,0:T(8,128)}), f32[19,1024]{1,0:T(8,128)}) %all-reduce.5.cloned.1.call-update) | async-done | bytes 77840 | tf_op jit(solution)/shard_map/psum | solution.py:474
  5068.5 416.6 %all-reduce.7.cloned.1.call-done = (f32[128,15360]{1,0:T(8,128)}, f32[128,3072]{1,0:T(8,128)}, f32[128,1024]{1,0:T(8,128)}, f32[128,1024]{1,0:T(8,128)}, f32[128...) async-done(((f32[128,15360]{1,0:T(8,128)}, ...) | async-done | bytes 24117264 | tf_op jit(solution)/shard_map/psum | solution.py:452
  5500.0 10.3 multiply_reduce_fusion
  5521.6 40.1 all-reduce
  5564.5 22.6 multiply_subtract_fusion.1
  5587.1 38.3 multiply_subtract_fusion
  (584 shorter events, 450.8 us)
Async XLA Ops:
  7.2 496.8 %all-gather.13.cloned.1.call-start = ((), (), s32[]{:S(2)}) async-start(), calls=%async_computation.11 | async-start | bytes 28311552 | tf_op jit(solution)/shard_map/all_gather | solution.py:218
  20.7 585.1 %all-gather.15.cloned.1.call-start = ((), (), s32[]{:S(2)}) async-start(), calls=%async_computation.12 | async-start | bytes 7077888 | tf_op jit(solution)/shard_map/all_gather | solution.py:219
  23.4 632.0 %all-gather.17.cloned.1.call-start = ((), (), s32[]{:S(2)}) async-start(), calls=%async_computation.13 | async-start | bytes 2359296 | tf_op jit(solution)/shard_map/all_gather | solution.py:221
  25.6 755.8 %all-gather.19.cloned.1.call-start = ((), (), s32[]{:S(2)}) async-start(), calls=%async_computation.14 | async-start | bytes 9437184 | tf_op jit(solution)/shard_map/all_gather | solution.py:225
  28.8 878.3 %all-gather.21.cloned.1.call-start = ((), (), s32[]{:S(2)}) async-start(), calls=%async_computation.15 | async-start | bytes 9437184 | tf_op jit(solution)/shard_map/all_gather | solution.py:227
  37.2 970.3 %all-gather.23.cloned.1.call-start = ((), (), s32[]{:S(2)}) async-start(), calls=%async_computation.16 | async-start | bytes 7077888 | tf_op jit(solution)/shard_map/all_gather | solution.py:220
  37.8 1198.2 %all-gather.27.cloned.1.call-start = ((), (), s32[]{:S(2)}) async-start(), calls=%async_computation.18 | async-start | bytes 18874368 | tf_op jit(solution)/shard_map/all_gather | solution.py:228
  41.2 1244.5 %all-gather.25.cloned.1.call-start = ((), (), s32[]{:S(2)}) async-start(), calls=%async_computation.17 | async-start | bytes 2359296 | tf_op jit(solution)/shard_map/all_gather | solution.py:222
  41.9 1293.7 %all-gather.29.cloned.1.call-start = ((), (), s32[]{:S(2)}) async-start(), calls=%async_computation.19 | async-start | bytes 2359296 | tf_op jit(solution)/shard_map/all_gather | solution.py:223
  42.6 1342.7 %all-gather.31.cloned.1.call-start = ((), (), s32[]{:S(2)}) async-start(), calls=%async_computation.20 | async-start | bytes 2359296 | tf_op jit(solution)/shard_map/all_gather | solution.py:224
  43.2 1467.7 %all-gather.33.cloned.1.call-start = ((), (), s32[]{:S(2)}) async-start(), calls=%async_computation.21 | async-start | bytes 9437184 | tf_op jit(solution)/shard_map/all_gather | solution.py:226
  45.4 610.0 %copy-start.113 = (f32[1,1024]{1,0:T(1,128)}, f32[1,1024]{1,0:T(1,128)S(1)}, u32[]{:S(2)}) copy-start(f32[1,1024]{1,0:T(1,128)S(1)} %get-tuple-element.116) | copy-start | bytes 12292
  46.9 558.9 %copy-start.17 = (f32[640,1024]{1,0:T(8,128)}, f32[640,1024]{1,0:T(8,128)S(1)}, u32[]{:S(2)}) copy-start(f32[640,1024]{1,0:T(8,128)S(1)} %get-tuple-element.132) | copy-start | bytes 7864324
  46.9 558.9 %copy-start.119 = (f32[640]{0:T(1024)}, f32[640]{0:T(1024)S(1)}, u32[]{:S(2)}) copy-start(f32[640]{0:T(1024)S(1)} %broadcast_multiply_fusion.7) | copy-start | bytes 7684
  48.3 557.5 %copy-start.141 = (f32[640]{0:T(1024)}, f32[640]{0:T(1024)S(1)}, u32[]{:S(2)}) copy-start(f32[640]{0:T(1024)S(1)} %fusion.68) | copy-start | bytes 7684
  514.6 266.9 %copy-start.78 = (f32[1024]{0:T(1024)}, f32[1024]{0:T(1024)S(1)}, u32[]{:S(2)}) copy-start(f32[1024]{0:T(1024)S(1)} %get-tuple-element.124) | copy-start | bytes 12292
  514.6 266.9 %copy-start.89 = (f32[1024]{0:T(1024)}, f32[1024]{0:T(1024)S(1)}, u32[]{:S(2)}) copy-start(f32[1024]{0:T(1024)S(1)} %get-tuple-element.123) | copy-start | bytes 12292
  514.6 392.5 %copy-start.152 = (f32[1024]{0:T(1024)}, f32[1024]{0:T(1024)S(1)}, u32[]{:S(2)}) copy-start(f32[1024]{0:T(1024)S(1)} %get-tuple-element.125) | copy-start | bytes 12292
  514.6 404.2 %copy-start.107 = (f32[1024]{0:T(1024)}, f32[1024]{0:T(1024)S(1)}, u32[]{:S(2)}) copy-start(f32[1024]{0:T(1024)S(1)} %get-tuple-element.121) | copy-start | bytes 12292
  615.3 5.3 collective-permute-start
  615.3 1020.7 %all-gather.35.cloned.1.call-start = ((), (), s32[]{:S(2)}) async-start(), calls=%async_computation.22 | async-start | bytes 9437184 | tf_op jit(solution)/shard_map/all_gather | solution.py:229
  661.6 153.2 %copy-start.10 = (f32[640,1024]{1,0:T(8,128)}, f32[640,1024]{1,0:T(8,128)S(1)}, u32[]{:S(2)}) copy-start(f32[640,1024]{1,0:T(8,128)S(1)} %get-tuple-element.79) | copy-start | bytes 7864324
  661.6 153.2 %copy-start.74 = (f32[640]{0:T(1024)}, f32[640]{0:T(1024)S(1)}, u32[]{:S(2)}) copy-start(f32[640]{0:T(1024)S(1)} %broadcast_multiply_fusion.6) | copy-start | bytes 7684
  662.9 151.9 %copy-start.82 = (f32[640]{0:T(1024)}, f32[640]{0:T(1024)S(1)}, u32[]{:S(2)}) copy-start(f32[640]{0:T(1024)S(1)} %fusion.69) | copy-start | bytes 7684
  918.3 367.3 %copy-start.3 = (f32[640,1024]{1,0:T(8,128)}, f32[640,1024]{1,0:T(8,128)S(1)}, u32[]{:S(2)}) copy-start(f32[640,1024]{1,0:T(8,128)S(1)} %get-tuple-element.75) | copy-start | bytes 7864324
  920.6 47.8 collective-permute-start.1
  922.4 1213.9 %reduce-scatter.20.cloned.1.call-start = ((), (), s32[]{:S(2)}) async-start(), calls=%async_computation.27 | async-start | bytes 4718592 | tf_op jit(solution)/shard_map/reduce_scatter | solution.py:444
  1063.6 172.4 %copy-start.44 = (bf16[1,77,4096]{2,1,0:T(8,128)(2,1)S(1)}, bf16[1,77,4096]{2,1,0:T(8,128)(2,1)}, u32[]{:S(2)}) copy-start(bf16[1,77,4096]{2,1,0:T(8,128)(2,1)} %param.20) | copy-start | bytes 1892356
  1066.3 179.6 %collective-permute-start.2 = (bf16[5,4,16,1024]{3,2,1,0:T(8,128)(2,1)}, bf16[5,4,16,1024]{3,2,1,0:T(8,128)(2,1)}, u32[]{:S(2)}, u32[]{:S(2)}) collective-permute-start(bf16[5,4,16,1024]{3,2,1,0:T(8,128)(2,1)} %get-tuple-element.106), channel_id=1, source_target_pairs={{0,1},{1,2},{2,3},{3,0},{4,5},{5,6},{6,7},{7,4},{8,9},{9,10},{10,1... | collective-permute-start | bytes 1966088 | tf_op jit(solution)/shard_map/ppermute | solution.py:43
  1343.0 352.4 %copy-start.1 = (f32[16,640,77]{1,2,0:T(8,128)}, f32[16,640,77]{1,2,0:T(8,128)S(1)}, u32[]{:S(2)}) copy-start(f32[16,640,77]{1,2,0:T(8,128)S(1)} %get-tuple-element.142) | copy-start | bytes 9461764
  1389.9 292.8 %copy-start.76 = (f32[640]{0:T(1024)}, f32[640]{0:T(1024)S(1)}, u32[]{:S(2)}) copy-start(f32[640]{0:T(1024)S(1)} %broadcast_multiply_fusion.3) | copy-start | bytes 7684
  1392.3 290.4 %copy-start.84 = (f32[640]{0:T(1024)}, f32[640]{0:T(1024)S(1)}, u32[]{:S(2)}) copy-start(f32[640]{0:T(1024)S(1)} %fusion.72) | copy-start | bytes 7684
  1703.9 432.4 %reduce-scatter.22.cloned.1.call-start = ((), (), s32[]{:S(2)}) async-start(), calls=%async_computation.28 | async-start | bytes 4718592 | tf_op jit(solution)/shard_map/reduce_scatter | solution.py:445
  1715.9 420.4 %reduce-scatter.18.cloned.1.call-start = ((), (), s32[]{:S(2)}) async-start(), calls=%async_computation.26 | async-start | bytes 4718592 | tf_op jit(solution)/shard_map/reduce_scatter | solution.py:443
  1723.1 8.9 collective-permute-start.3
  1814.5 18.1 collective-permute-start.4
  1820.5 315.9 %reduce-scatter.16.cloned.1.call-start = ((), (), s32[]{:S(2)}) async-start(), calls=%async_computation.25 | async-start | bytes 4718592 | tf_op jit(solution)/shard_map/reduce_scatter | solution.py:442
  1878.5 397.7 %reduce-scatter.14.cloned.1.call-start = ((), (), s32[]{:S(2)}) async-start(), calls=%async_computation.24 | async-start | bytes 14155776 | tf_op jit(solution)/shard_map/reduce_scatter | solution.py:441
  1890.2 671.0 %reduce-scatter.26.cloned.1.call-start = ((), (), s32[]{:S(2)}) async-start(), calls=%async_computation.30 | async-start | bytes 18874368 | tf_op jit(solution)/shard_map/reduce_scatter | solution.py:447
  1904.8 942.0 %reduce-scatter.32.cloned.1.call-start = ((), (), s32[]{:S(2)}) async-start(), calls=%async_computation.33 | async-start | bytes 18874368 | tf_op jit(solution)/shard_map/reduce_scatter | solution.py:450
  1918.9 1212.9 %reduce-scatter.24.cloned.1.call-start = ((), (), s32[]{:S(2)}) async-start(), calls=%async_computation.29 | async-start | bytes 18874368 | tf_op jit(solution)/shard_map/reduce_scatter | solution.py:446
  1932.7 1484.7 %reduce-scatter.28.cloned.1.call-start = ((), (), s32[]{:S(2)}) async-start(), calls=%async_computation.31 | async-start | bytes 18874368 | tf_op jit(solution)/shard_map/reduce_scatter | solution.py:448
  1947.5 2016.1 %reduce-scatter.30.cloned.1.call-start = ((), (), s32[]{:S(2)}) async-start(), calls=%async_computation.32 | async-start | bytes 37748736 | tf_op jit(solution)/shard_map/reduce_scatter | solution.py:449
  1970.2 2970.1 %reduce-scatter.12.cloned.1.call-start = ((), (), s32[]{:S(2)}) async-start(), calls=%async_computation.23 | async-start | bytes 70778880 | tf_op jit(solution)/shard_map/reduce_scatter | solution.py:440
  1996.9 33.4 collective-permute-start.6
  2014.5 21.6 collective-permute-start.5
  2128.8 2938.2 %all-reduce.5.cloned.1.call-start = ((), (), s32[]{:S(2)}) async-start(), calls=%async_computation.34 | async-start | bytes 196608 | tf_op jit(solution)/shard_map/psum | solution.py:474
  2136.2 3348.9 %all-reduce.7.cloned.1.call-start = ((), (), s32[]{:S(2)}) async-start(), calls=%async_computation.35 | async-start | bytes 48234496 | tf_op jit(solution)/shard_map/psum | solution.py:452
  (149 other events, 1580.4 us)
Sparse Core Ops, SparseCore 0:
  20.8 483.1 all-gather.12
  506.7 98.9 all-gather.14
  607.9 47.4 all-gather.16
  658.0 123.4 all-gather.18
  784.0 123.1 all-gather.20
  909.2 98.2 all-gather.22
  1010.1 225.8 all-gather.26
  1238.2 47.4 all-gather.24
  1287.8 47.7 all-gather.28
  1337.6 47.7 all-gather.30
  1387.5 123.4 all-gather.32
  1512.9 123.0 all-gather.34
  1704.0 86.0 reduce-scatter.19
  1794.1 87.6 reduce-scatter.21
  1885.2 87.6 reduce-scatter.17
  1977.4 87.6 reduce-scatter.15
  2069.1 207.0 reduce-scatter.13
  2279.8 281.3 reduce-scatter.25
  2565.5 281.2 reduce-scatter.31
  2850.4 281.3 reduce-scatter.23
  3136.0 281.3 reduce-scatter.27
  3421.2 542.3 reduce-scatter.29
  3967.5 972.7 reduce-scatter.11
  4947.2 119.7 all-reduce.4
  5071.1 413.9 all-reduce.6
where the time goes:
time: 5640 us
  waiting for transfers between devices  4670 us (83%)
  matrix products  433 us (8%)
  other arithmetic  226 us (4%)
  local copies, waits for them, and re-layouts  191 us (3%)
  blocking collectives  82.3 us (1%)
    reduce_scatter x1, waiting for transfers between devices, per_device(): lax.psum_scatter(members[0], 'clip', scatter_dimension=0, tiled=True)  977 us
    reduce_scatter x1, waiting for transfers between devices, per_device(): lax.psum_scatter(members[9], 'clip', scatter_dimension=0, tiled=True)  546 us
    all_gather x1, waiting for transfers between devices, per_device(): lax.all_gather(wide_bf[:, :12 * D], 'clip', axis=0, tiled=True)  456 us
    psum x1, waiting for transfers between devices, per_device(): lax.psum((partial_sums[0], partial_sums[1], partial_sums[2], partial_sums...  417 us
    reduce_scatter x1, waiting for transfers between devices, per_device(): lax.psum_scatter(members[8], 'clip', scatter_dimension=0, tiled=True)  286 us
    reduce_scatter x1, waiting for transfers between devices, per_device(): lax.psum_scatter(members[10], 'clip', scatter_dimension=0, tiled=True)  286 us
    reduce_scatter x1, waiting for transfers between devices, per_device(): lax.psum_scatter(members[7], 'clip', scatter_dimension=0, tiled=True)  285 us
    reduce_scatter x1, waiting for transfers between devices, per_device(): lax.psum_scatter(members[6], 'clip', scatter_dimension=0, tiled=True)  285 us
  transfers between devices with their start and end apart: 32, of which 23 were waited for; matrix products, arithmetic and copies ran while one was open for 11% of the time, Pallas kernels for 0%

commit v1 on v0

--- a/solution.py
+++ b/solution.py
@@ -4,6 +4,8 @@
 import jax
 import jax.numpy as jnp
 from jax import lax
+from jax.experimental import pallas as pl
+from jax.experimental.pallas import tpu as pltpu
 from jax.sharding import PartitionSpec as P
 
 D = 1024
@@ -193,6 +195,200 @@
     second_hat = second_mom / (1.0 - BETA_TWO**STEP)
     weight = weight - learn_rate * (first_hat / (jnp.sqrt(second_hat) + ADAM_EPS) + DECAY * weight)
     return (weight, first_mom, second_mom)
+
+MESH = pl.DeviceIdType.MESH
+ANY = pl.BlockSpec(memory_space=pl.ANY)
+TEXT_PAD = 80
+
+
+def ring_place(clip, count):
+    half = clip // 2
+    odd = clip % 2
+    return half + odd * (count - 1 - 2 * half)
+
+
+def ring_clip(place, count):
+    far = place // (count // 2)
+    return (1 - far) * 2 * place + far * (2 * (count - 1 - place) + 1)
+
+
+def greet(peers):
+    barrier = pltpu.get_barrier_semaphore()
+    for peer in peers:
+        pl.semaphore_signal(barrier, inc=1, device_id=peer, device_id_type=MESH)
+    pl.semaphore_wait(barrier, len(peers))
+
+
+def exchange_kernel(count, facts_ref, text_ref, facts_out, text_out, send, recv, local):
+    me = lax.axis_index("clip")
+    band = lax.axis_index("band")
+    peers = [((me + step) % count, band) for step in range(1, count)]
+    greet(peers)
+    own = [
+        pltpu.make_async_copy(facts_ref, facts_out.at[me], local.at[0]),
+        pltpu.make_async_copy(text_ref.at[me], text_out.at[me], local.at[1]),
+    ]
+    for copy in own:
+        copy.start()
+    sent = []
+    for step, peer in enumerate(peers):
+        sent += [
+            pltpu.make_async_remote_copy(
+                facts_ref, facts_out.at[me], send.at[0, step], recv.at[0, step], peer, MESH
+            ),
+            pltpu.make_async_remote_copy(
+                text_ref.at[peer[0]], text_out.at[me], send.at[1, step], recv.at[1, step], peer, MESH
+            ),
+        ]
+    for copy in sent:
+        copy.start()
+    for copy in own + sent:
+        copy.wait()
+
+
+def exchange_facts(facts, text):
+    count = lax.axis_size("clip")
+    return pl.pallas_call(
+        partial(exchange_kernel, count),
+        out_shape=(
+            jax.ShapeDtypeStruct((count,) + facts.shape, facts.dtype),
+            jax.ShapeDtypeStruct(text.shape, text.dtype),
+        ),
+        in_specs=[ANY] * 2,
+        out_specs=(ANY,) * 2,
+        scratch_shapes=[
+            pltpu.SemaphoreType.DMA((2, count - 1)),
+            pltpu.SemaphoreType.DMA((2, count - 1)),
+            pltpu.SemaphoreType.DMA((2,)),
+        ],
+        compiler_params=pltpu.CompilerParams(collective_id=0, has_side_effects=True),
+    )(facts, text)
+
+
+def gather_kernel(count, shapes, *refs):
+    num = len(shapes)
+    shards, (vec_ref, text_ref) = refs[:num], refs[num : num + 2]
+    full, (vec_out, text_out) = refs[num + 2 : 2 * num + 2], refs[2 * num + 2 : 2 * num + 4]
+    ring_send, ring_recv, pair_send, pair_recv, own_sem, part_send, part_recv, part_own = refs[
+        2 * num + 4 :
+    ]
+    me = lax.axis_index("clip")
+    band = lax.axis_index("band")
+    core = band % 2
+    place = ring_place(me, count)
+    onward = 1 - 2 * core
+    following = (ring_clip((place + onward + count) % count, count), band)
+    partner = (me, band + 1 - 2 * core)
+    peers = [((me + step) % count, band) for step in range(1, count)]
+    greet(peers + [partner])
+
+    def block(ref, group, owner):
+        rows, cols = shapes[group]
+        return ref.at[
+            pl.ds(pl.multiple_of(owner * rows, rows), rows),
+            pl.ds(pl.multiple_of(core * (cols // 2), 128), cols // 2),
+        ]
+
+    def ring_copy(group, step):
+        owner = ring_clip((place - onward * step + 2 * count) % count, count)
+        there = block(full[group], group, owner)
+        return pltpu.make_async_remote_copy(
+            there, there, ring_send.at[step, group], ring_recv.at[step, group], following, MESH
+        )
+
+    def pair_copy(group, step):
+        owner = ring_clip((place - onward * (step + 1) + 2 * count) % count, count)
+        there = block(full[group], group, owner)
+        return pltpu.make_async_remote_copy(
+            there, there, pair_send.at[step, group], pair_recv.at[step, group], partner, MESH
+        )
+
+    def own_copy(group):
+        rows, cols = shapes[group]
+        return pltpu.make_async_copy(
+            shards[group],
+            full[group].at[pl.ds(pl.multiple_of(me * rows, rows), rows), :],
+            own_sem.at[group],
+        )
+
+    parts = []
+    for step, peer in enumerate(peers):
+        for which, (src, dst) in enumerate(((vec_ref, vec_out), (text_ref, text_out))):
+            parts.append(
+                pltpu.make_async_remote_copy(
+                    src.at[peer[0]],
+                    dst.at[me],
+                    part_send.at[which, step],
+                    part_recv.at[which, step],
+                    peer,
+                    MESH,
+                )
+            )
+    parts_own = [
+        pltpu.make_async_copy(src.at[me], dst.at[me], part_own.at[which])
+        for which, (src, dst) in enumerate(((vec_ref, vec_out), (text_ref, text_out)))
+    ]
+    for group in range(num):
+        rows, cols = shapes[group]
+        own_copy(group).start()
+        pltpu.make_async_remote_copy(
+            shards[group].at[:, pl.ds(pl.multiple_of(core * (cols // 2), 128), cols // 2)],
+            block(full[group], group, me),
+            ring_send.at[0, group],
+            ring_recv.at[0, group],
+            following,
+            MESH,
+        ).start()
+    for copy in parts_own + parts:
+        copy.start()
+
+    @pl.loop(1, count - 1)
+    def _(step):
+        for group in range(num):
+            ring_copy(group, step - 1).wait_recv()
+            ring_copy(group, step).start()
+            pair_copy(group, step - 1).start()
+
+    for group in range(num):
+        ring_copy(group, count - 2).wait_recv()
+        pair_copy(group, count - 2).start()
+    for copy in parts_own + parts:
+        copy.wait()
+    for group in range(num):
+        own_copy(group).wait()
+
+    @pl.loop(0, count - 1)
+    def _(step):
+        for group in range(num):
+            ring_copy(group, step).wait_send()
+            pair_copy(group, step).wait()
+
+
+def gather_weights(shards, vectors, texts):
+    count = lax.axis_size("clip")
+    num = len(shards)
+    steps = pltpu.SemaphoreType.DMA((count - 1, num))
+    out = pl.pallas_call(
+        partial(gather_kernel, count, [shard.shape for shard in shards]),
+        out_shape=tuple(
+            jax.ShapeDtypeStruct((count * s.shape[0], s.shape[1]), s.dtype) for s in shards
+        )
+        + tuple(jax.ShapeDtypeStruct(v.shape, v.dtype) for v in (vectors, texts)),
+        in_specs=[ANY] * (num + 2),
+        out_specs=(ANY,) * (num + 2),
+        scratch_shapes=[
+            steps,
+            steps,
+            steps,
+            steps,
+            pltpu.SemaphoreType.DMA((num,)),
+            pltpu.SemaphoreType.DMA((2, count - 1)),
+            pltpu.SemaphoreType.DMA((2, count - 1)),
+            pltpu.SemaphoreType.DMA((2,)),
+        ],
+        compiler_params=pltpu.CompilerParams(collective_id=1, has_side_effects=True),
+    )(*shards, vectors, texts)
+    return out[:num], out[num], out[num + 1]
 
 
 def per_device(
@@ -212,24 +408,43 @@
     m_small,
     v_small,
 ):
-    wide_bf = w_wide.astype(jnp.bfloat16)
-    deep_bf = w_deep.astype(jnp.bfloat16)
-    gathered = (
-        lax.all_gather(wide_bf[:, : 12 * D], "clip", axis=0, tiled=True),
-        lax.all_gather(wide_bf[:, 12 * D : 15 * D], "clip", axis=0, tiled=True),
-        lax.all_gather(wide_bf[:, 15 * D : 18 * D], "clip", axis=0, tiled=True),
-        lax.all_gather(wide_bf[:, 18 * D : 19 * D], "clip", axis=0, tiled=True),
-        lax.all_gather(wide_bf[:, 19 * D : 20 * D], "clip", axis=0, tiled=True),
-        lax.all_gather(wide_bf[:, 20 * D : 21 * D], "clip", axis=0, tiled=True),
-        lax.all_gather(wide_bf[:, 21 * D : 22 * D], "clip", axis=0, tiled=True),
-        lax.all_gather(wide_bf[:, 22 * D : 22 * D + FF], "clip", axis=0, tiled=True),
-        lax.all_gather(wide_bf[:, 22 * D + FF :], "clip", axis=0, tiled=True),
-        lax.all_gather(deep_bf[:, :D], "clip", axis=0, tiled=True),
-        lax.all_gather(deep_bf[:, D : 3 * D], "clip", axis=0, tiled=True),
-        lax.all_gather(deep_bf[:, 3 * D :], "clip", axis=0, tiled=True),
+    clip_count = lax.axis_size("clip")
+    band_count = lax.axis_size("band")
+    clip_at = lax.axis_index("clip")
+    band_at = lax.axis_index("band")
+    wide_rows = w_wide.shape[0]
+    deep_rows = w_deep.shape[0]
+    text_len, text_dim = context.shape[1:]
+    facts = jnp.pad(
+        jnp.concatenate([timesteps, frame_mask[0]])[None],
+        ((0, 7), (0, 127 - frame_mask.shape[1])),
+    )
+    kept_text = context[0] * (1 - null_flags[0]).astype(jnp.bfloat16)
+    text_cols = jnp.pad(
+        kept_text.reshape(text_len, clip_count, deep_rows).transpose(1, 0, 2),
+        ((0, 0), (0, TEXT_PAD - text_len), (0, 0)),
+    )
+    all_facts, all_text = exchange_facts(facts, text_cols)
+    all_times = all_facts[:, 0, 0].astype(jnp.float32)
+    all_time_low = jax.nn.silu(time_features(all_times)).astype(jnp.bfloat16)
+    time_rows = lax.dynamic_slice(
+        all_time_low, (0, clip_at * wide_rows), (clip_count, wide_rows)
+    )
+    part_modul = matmul(time_rows, w_wide[:, : 12 * D].astype(jnp.bfloat16))
+    kv_cols = 2 * D // band_count
+    kv_weight = lax.dynamic_slice(
+        w_deep, (0, D + band_at * kv_cols), (deep_rows, kv_cols)
+    ).astype(jnp.bfloat16)
+    part_kv = matmul(all_text.reshape(clip_count * TEXT_PAD, deep_rows), kv_weight)
+    edges = (12 * D, 15 * D, 18 * D, 19 * D, 20 * D, 21 * D, 22 * D, 22 * D + FF, 22 * D + 2 * FF)
+    shards = [w_wide[:, low:high].astype(jnp.bfloat16) for low, high in zip(edges, edges[1:])]
+    shards += [w_deep[:, :D].astype(jnp.bfloat16), w_deep[:, 3 * D :].astype(jnp.bfloat16)]
+    gathered, all_modul, all_kv = gather_weights(
+        shards,
+        part_modul.reshape(clip_count, 12 * D // 128, 128),
+        part_kv.reshape(clip_count, TEXT_PAD, kv_cols),
     )
     (
-        ada_w,
         qkv_a_w,
         qkv_b_w,
         out_a_w,
@@ -239,16 +454,17 @@
         up_a_w,
         up_b_w,
         down_a_w,
-        keyval_w,
         down_b_w,
     ) = gathered
+    keyval = lax.all_gather(jnp.sum(all_kv, 0).astype(jnp.bfloat16), "band", axis=1, tiled=True)
+    keyval = keyval[:text_len]
     small_low = w_small.astype(jnp.bfloat16)
     small_val = small_low.astype(jnp.float32)
     num_frames, num_rows, num_cols = (latents.shape[1], latents.shape[2], latents.shape[3])
     grid_shape = (num_frames, num_rows, num_cols)
     tok_count = num_frames * num_rows * num_cols
-    local_count = jnp.sum(frame_mask).astype(jnp.float32) * (num_rows * num_cols * CH)
-    global_count = lax.psum(local_count, ("clip", "band"))
+    all_mask = all_facts[:, 0, 1 : 1 + num_frames]
+    global_count = jnp.sum(all_mask).astype(jnp.float32) * (num_rows * num_cols * CH * band_count)
     time_value = timesteps[0].astype(jnp.float32)
     noise_angle = 0.5 * math.pi * time_value / TMAX
     signal, spread = (jnp.cos(noise_angle), jnp.sin(noise_angle))
@@ -256,8 +472,7 @@
     noise_tok = noise_field[0].reshape(tok_count, CH)
     noisy_low = (signal * clean_tok + spread * noise_tok).astype(jnp.bfloat16)
     target = signal * noise_tok - spread * clean_tok
-    time_low = jax.nn.silu(time_features(time_value)).astype(jnp.bfloat16)[None]
-    modulation = matmul(time_low, ada_w).reshape(12, D)
+    modulation = jnp.sum(all_modul, 0).reshape(12, D)
     mod_a, mod_b = (modulation[:6], modulation[6:])
     stream_zero = matmul(noisy_low, small_low[:CH]) + small_val[2 * CH]
     normed_a, back_a = jax.vjp(norm_modulated, stream_zero, mod_a[0], mod_a[1])
@@ -298,8 +513,6 @@
     cross_val, cross_back = jax.vjp(norm_gained, stream_three, small_val[2 * CH + 1])
     cross_in = cross_val.astype(jnp.bfloat16)
     query_proj = matmul(cross_in, query_w).astype(jnp.bfloat16)
-    kept_text = context[0] * (1 - null_flags[0]).astype(jnp.bfloat16)
-    keyval = matmul(kept_text, keyval_w).astype(jnp.bfloat16)
     cross_q = split_heads(query_proj)
     cross_k = split_heads(keyval[:, :D])
     cross_v = split_heads(keyval[:, D:])
@@ -330,7 +543,15 @@
     grad_w_cq = matmul_tn(cross_in, grad_query)
     grad_part, grad_gain_c = cross_back(matmul_nt(grad_query, query_w))
     grad_keyval = jnp.concatenate([merge_heads(ck_grad), merge_heads(cv_grad)], 1)
-    grad_w_ckv = matmul_tn(kept_text.astype(jnp.float32), grad_keyval, lax.Precision.HIGHEST)
+    grad_keyval = jnp.pad(grad_keyval, ((0, TEXT_PAD - text_len), (0, 0)))
+    grad_keyval = lax.psum_scatter(grad_keyval, "band", scatter_dimension=1, tiled=True)
+    grad_keyval = lax.all_gather(grad_keyval, "clip", axis=0, tiled=True)
+    grad_w_ckv = matmul_tn(
+        all_text.reshape(clip_count * TEXT_PAD, deep_rows).astype(jnp.float32),
+        grad_keyval,
+        lax.Precision.HIGHEST,
+    )
+    grad_w_ckv = lax.all_gather(grad_w_ckv, "band", axis=1, tiled=True)
     grad_stream = grad_stream + grad_part
     grad_proj = (mod_b[2] * grad_stream).astype(jnp.bfloat16)
     grad_gate_b = jnp.sum(grad_stream * proj_b, 0)
@@ -420,11 +641,10 @@
     grad_small = jnp.concatenate(
         [grad_patch, grad_head, grad_bias[None], grad_gain_c[None], grad_gain_f[None]], 0
     )
-    leading = jnp.concatenate(
-        [time_low.astype(jnp.float32).reshape(D, 1) * grad_modul, grad_w_qkva], 1
-    )
+    all_grad_modul = lax.all_gather(lax.psum(grad_modul, "band"), "clip", axis=0, tiled=True)
+    grad_w_ada = matmul_tn(time_rows.astype(jnp.float32), all_grad_modul, lax.Precision.HIGHEST)
     members = (
-        leading,
+        grad_w_qkva,
         grad_w_qkvb,
         grad_w_oa,
         grad_w_ob,
@@ -433,41 +653,18 @@
         grad_up_a,
         grad_up_b,
         grad_down_a,
-        grad_w_ckv,
         grad_down_b,
     )
-    partial_sums = (
-        lax.psum_scatter(members[0], "clip", scatter_dimension=0, tiled=True),
-        lax.psum_scatter(members[1], "clip", scatter_dimension=0, tiled=True),
-        lax.psum_scatter(members[2], "clip", scatter_dimension=0, tiled=True),
-        lax.psum_scatter(members[3], "clip", scatter_dimension=0, tiled=True),
-        lax.psum_scatter(members[4], "clip", scatter_dimension=0, tiled=True),
-        lax.psum_scatter(members[5], "clip", scatter_dimension=0, tiled=True),
-        lax.psum_scatter(members[6], "clip", scatter_dimension=0, tiled=True),
-        lax.psum_scatter(members[7], "clip", scatter_dimension=0, tiled=True),
-        lax.psum_scatter(members[8], "clip", scatter_dimension=0, tiled=True),
-        lax.psum_scatter(members[9], "clip", scatter_dimension=0, tiled=True),
-        lax.psum_scatter(members[10], "clip", scatter_dimension=0, tiled=True),
-    )
-    summed = lax.psum(
-        (
-            partial_sums[0],
-            partial_sums[1],
-            partial_sums[2],
-            partial_sums[3],
-            partial_sums[4],
-            partial_sums[5],
-            partial_sums[6],
-            partial_sums[7],
-            partial_sums[8],
-            partial_sums[9],
-            partial_sums[10],
-        ),
-        "band",
-    )
-    wide_parts = list(summed[:8])
-    wide_sum = jnp.concatenate(wide_parts, 1)
-    deep_sum = jnp.concatenate([summed[8], summed[9], summed[10]], 1)
+    summed = []
+    for member in members:
+        rows, cols = member.shape
+        member = member.reshape(rows, band_count, cols // band_count).transpose(1, 0, 2)
+        member = member.reshape(band_count, clip_count, rows // clip_count, cols // band_count)
+        member = member.transpose(1, 0, 2, 3).reshape(-1, cols // band_count)
+        member = lax.psum_scatter(member, ("clip", "band"), scatter_dimension=0, tiled=True)
+        summed.append(lax.all_gather(member, "band", axis=1, tiled=True))
+    wide_sum = jnp.concatenate([grad_w_ada] + summed[:8], 1)
+    deep_sum = jnp.concatenate([summed[8], grad_w_ckv, summed[9]], 1)
     square_part = (jnp.sum(wide_sum * wide_sum) + jnp.sum(deep_sum * deep_sum)) / lax.axis_size(
         "band"
     )

time: 5640 us -> 3010 us (0.53)
  waiting for transfers between devices: 4670 us -> 1650 us
  Pallas kernels: 0 us -> 313 us
  local copies, waits for them, and re-layouts: 191 us -> 341 us
  matrix products: 433 us -> 362 us
    reduce_scatter x11, waiting for transfers between devices: 2800 us -> 1360 us  [the longest x10 1360 us: per_device(): lax.psum_scatter(member, ('clip', 'band'), scatter_dimension=0, tiled=True)]
    all_gather x12 -> x8, waiting for transfers between devices: 1300 us -> 181 us  [the longest x6 102 us: per_device(): summed.append(lax.all_gather(member, 'band', axis=1, tiled=True))]
    psum x1 -> x0, waiting for transfers between devices: 417 us -> none  [per_device(): lax.psum((partial_sums[0], partial_sums[1], partial_sums[2], partial_sums...]
    pallas_call x0 -> x2, Pallas kernels: none -> 313 us  [the longest x1 296 us: gather_weights(): pl.pallas_call(partial(gather_kernel, count, [shard.shape for shard in sh...]
    reshape x2 -> x12, local copies, waits for them, and re-layouts: 1.04 us -> 83.1 us  [the longest x7 51.4 us: per_device(): member.reshape(band_count, clip_count, rows // clip_count, cols // band_c...]
    all_gather x0 -> x6, blocking collectives: none -> 67.9 us  [the longest x1 33.1 us: per_device(): lax.all_gather(lax.psum(grad_modul, 'band'), 'clip', axis=0, tiled=True)]
    dot_general x13 -> x14, matrix products: 113 us -> 82.3 us  [matmul_tn(): lax.dot_general(left_op, right_op, (((0,), (0,)), ((), ())), precision=pr...]
  transfers between devices with their start and end apart: 32 -> 27, of which waited for: 23 -> 22; matrix products, arithmetic and copies ran while one was open for 11% -> 12% of each run, Pallas kernels for 0% -> 0%
where the time goes in v1:
time: 3010 us; the launch traced here: 3000 us
  waiting for transfers between devices  1650 us (55%)
  matrix products  362 us (12%)
  local copies, waits for them, and re-layouts  341 us (11%)
  Pallas kernels  313 us (10%)
  other arithmetic  182 us (6%)
  blocking collectives  119 us (4%)
    reduce_scatter x10, waiting for transfers between devices, per_device(): lax.psum_scatter(member, ('clip', 'band'), scatter_dimension=0, tiled=True)  1360 us
    pallas_call x1, Pallas kernels, gather_weights(): pl.pallas_call(partial(gather_kernel, count, [shard.shape for shard in sh...  296 us
    dot_general x14, matrix products, matmul(): return jnp.dot(left_op, right_op, preferred_element_type=jnp.float32)  111 us
    all_gather x6, waiting for transfers between devices, per_device(): summed.append(lax.all_gather(member, 'band', axis=1, tiled=True))  102 us
    unnamed x446, local copies, waits for them, and re-layouts  94.7 us
    dot_general x11, matrix products, matmul_nt(): lax.dot_general(left_op, right_op, (((1,), (1,)), ((), ())), preferred_el...  84.7 us
    dot_general x14, matrix products, matmul_tn(): lax.dot_general(left_op, right_op, (((0,), (0,)), ((), ())), precision=pr...  82.3 us
    psum x1, waiting for transfers between devices, per_device(): lax.psum((loss_part, square_part, grad_small), ('clip', 'band'))  79 us
  transfers between devices with their start and end apart: 27, of which 22 were waited for; matrix products, arithmetic and copies ran while one was open for 12% of the time, Pallas kernels for 0%

profile of v1, /device:TPU:0, one launch (start us, length us, event | category | flops | bytes accessed | tf_op | source)
XLA Modules:
  0.0 2997.4 jit_solution(7492750945240283866)
XLA Ops:
  30.0 17.7 shard_map.230
  62.5 295.5 %shard_map.231 = (bf16[1024,3072]{1,0:T(8,128)(2,1)}, bf16[1024,3072]{1,0:T(8,128)(2,1)}, bf16[1024,1024]{1,0:T(8,128)(2,1)}, bf16[1024,1024]{1,0:T(8,128)(2,1)}...) custom-call(bf16[128,3072]{1,0:T(8,128)(2,1)} %get-tuple-element.106, ...), custom_call_target="tpu_custom_call" | custom-call | tf_op jit(solution)/shard_map/pallas_call | solution.py:371
  406.9 31.3 %multiply_convert_fusion.3 = (bf16[640,4096]{1,0:T(8,128)(2,1)S(1)}, f32[640,4096]{1,0:T(8,128)}, f32[640,4096]{1,0:T(8,128)}) fusion(bf16[1024,4096]{1,0:T(8,128)(2,1)S(1)} %bitcast.505, f32[640,1024]{1,0:T(8,128)S(1)} %get-tuple-element.98, f32[1024]{0:T(1024)S(1)} %get-tuple-element.141, f32[1024]{0:T(1024)S(1)} %get-tuple-element.142, ...), kind=kOutput, calls=%fused_computation.35 | convolution fusion | flops 5542379520 | bytes 37237760 | tf_op jit(solution)/shard_map/dot_general | solution.py:49
  480.4 9.9 multiply_reduce_fusion.2
  499.6 9.6 fusion.32
  549.9 33.1 %multiply_convert_fusion.2 = (bf16[640,4096]{1,0:T(8,128)(2,1)S(1)}, f32[640,4096]{1,0:T(8,128)}, f32[640,4096]{1,0:T(8,128)}) fusion(bf16[1024,4096]{1,0:T(8,128)(2,1)} %get-tuple-element.37, f32[640,1024]{1,0:T(8,128)S(1)} %get-tuple-element.162, f32[1024]{0:T(1024)S(1)} %copy-done.101, f32[1024]{0:T(1024)S(1)} %copy-done.85, f32[640]{0:T(1024)S(1)} %fusion.82, ...), kind=kOutput, calls=%fused_computation.22 | convolution fusion | flops 5542379520 | bytes 37237760 | tf_op jit(solution)/shard_map/dot_general | solution.py:49
  596.5 17.7 add_convert_fusion.1
  614.2 11.5 multiply_reduce_fusion.12
  676.7 10.9 multiply_reduce_fusion.1
  687.6 11.3 multiply_convert_fusion
  735.7 15.4 collective-permute-done.4
  760.0 18.0 add_convert_fusion
  778.0 10.9 multiply_reduce_fusion.15
  881.6 10.7 copy.209
  904.2 10.4 fusion.132
  914.6 11.6 copy.213
  937.3 19.2 copy.262
  956.5 19.6 copy.227
  977.9 13.1 fusion.94
  991.0 17.7 copy.230
  1008.7 11.5 copy.231
  1037.3 12.0 copy.224
  1089.4 10.2 fusion.99
  1106.2 12.1 copy.226
  1141.0 77.7 %reduce-scatter.14.cloned.1.call-done = f32[128,768]{1,0:T(8,128)} async-done(((f32[4096,768]{1,0:T(8,128)}), f32[128,768]{1,0:T(8,128)}) %reduce-scatter.14.cloned.1.call-update) | async-done | bytes 393232 | tf_op jit(solution)/shard_map/reduce_scatter | solution.py:664
  1218.7 184.2 %reduce-scatter.28.cloned.1.call-done = f32[512,256]{1,0:T(8,128)} async-done(((f32[16384,256]{1,0:T(8,128)}), f32[512,256]{1,0:T(8,128)}) %reduce-scatter.28.cloned.1.call-update) | async-done | bytes 524304 | tf_op jit(solution)/shard_map/reduce_scatter | solution.py:664
  1403.0 45.6 %all-gather.20.cloned.1.call-done = f32[640,512]{1,0:T(8,128)} async-done(((f32[80,512]{1,0:T(8,128)}), f32[640,512]{1,0:T(8,128)}) %all-gather.20.cloned.1.call-update) | async-done | bytes 1310736 | tf_op jit(solution)/shard_map/all_gather | solution.py:548
  1452.6 179.9 %reduce-scatter.32.cloned.1.call-done = f32[512,256]{1,0:T(8,128)} async-done(((f32[16384,256]{1,0:T(8,128)}), f32[512,256]{1,0:T(8,128)}) %reduce-scatter.32.cloned.1.call-update) | async-done | bytes 524304 | tf_op jit(solution)/shard_map/reduce_scatter | solution.py:664
  1632.5 186.8 %reduce-scatter.24.cloned.1.call-done = f32[128,1024]{1,0:T(8,128)} async-done(((f32[4096,1024]{1,0:T(8,128)}), f32[128,1024]{1,0:T(8,128)}) %reduce-scatter.24.cloned.1.call-update) | async-done | bytes 524304 | tf_op jit(solution)/shard_map/reduce_scatter | solution.py:664
  1819.8 11.2 psum.29
  1831.0 33.1 %all-gather = f32[8,1,12288]{2,1,0:T(1,128)S(1)} all-gather(f32[1,1,12288]{2,1,0:T(1,128)S(1)} %bitcast.472), channel_id=1, replica_groups=mesh['clip'=8,'band'=4] {'clip'}, dimensions={0}, use_global_device_ids=true | all-gather | bytes 442368 | tf_op jit(solution)/shard_map/all_gather | solution.py:644
  1868.7 79.0 %all-reduce.6.cloned.1.call-done = f32[19,1024]{1,0:T(8,128)} async-done(((f32[19,1024]{1,0:T(8,128)}), f32[19,1024]{1,0:T(8,128)}) %all-reduce.6.cloned.1.call-update) | async-done | bytes 77840 | tf_op jit(solution)/shard_map/psum | solution.py:671
  1949.2 143.3 %reduce-scatter.22.cloned.1.call-done = f32[128,256]{1,0:T(8,128)} async-done(((f32[4096,256]{1,0:T(8,128)}), f32[128,256]{1,0:T(8,128)}) %reduce-scatter.22.cloned.1.call-update) | async-done | bytes 131088 | tf_op jit(solution)/shard_map/reduce_scatter | solution.py:664
  2099.3 133.6 %reduce-scatter.20.cloned.1.call-done = f32[128,256]{1,0:T(8,128)} async-done(((f32[4096,256]{1,0:T(8,128)}), f32[128,256]{1,0:T(8,128)}) %reduce-scatter.20.cloned.1.call-update) | async-done | bytes 131088 | tf_op jit(solution)/shard_map/reduce_scatter | solution.py:664
  2239.6 174.5 %reduce-scatter.26.cloned.1.call-done = f32[128,1024]{1,0:T(8,128)} async-done(((f32[4096,1024]{1,0:T(8,128)}), f32[128,1024]{1,0:T(8,128)}) %reduce-scatter.26.cloned.1.call-update) | async-done | bytes 524304 | tf_op jit(solution)/shard_map/reduce_scatter | solution.py:664
  2414.1 145.3 %reduce-scatter.18.cloned.1.call-done = f32[128,256]{1,0:T(8,128)} async-done(((f32[4096,256]{1,0:T(8,128)}), f32[128,256]{1,0:T(8,128)}) %reduce-scatter.18.cloned.1.call-update) | async-done | bytes 131088 | tf_op jit(solution)/shard_map/reduce_scatter | solution.py:664
  2566.0 132.9 %reduce-scatter.16.cloned.1.call-done = f32[128,256]{1,0:T(8,128)} async-done(((f32[4096,256]{1,0:T(8,128)}), f32[128,256]{1,0:T(8,128)}) %reduce-scatter.16.cloned.1.call-update) | async-done | bytes 131088 | tf_op jit(solution)/shard_map/reduce_scatter | solution.py:664
  2705.7 10.3 all-gather.10.cloned.1.call-done
  2718.7 18.4 all-gather.12.cloned.1.call-done
  2743.1 18.0 all-gather.18.cloned.1.call-done
  2764.3 33.3 %all-gather.22.cloned.1.call-done = f32[512,2048]{1,0:T(8,128)} async-done(((f32[512,512]{1,0:T(8,128)}), f32[512,2048]{1,0:T(8,128)}) %all-gather.22.cloned.1.call-update) | async-done | bytes 4194320 | tf_op jit(solution)/shard_map/all_gather | solution.py:554
  2802.3 19.3 all-gather.24.cloned.1.call-done
  2831.0 14.9 all-gather.14.cloned.1.call-done
  2849.0 20.9 all-gather.16.cloned.1.call-done
  2873.0 10.1 multiply_reduce_fusion
  2884.4 39.9 %all-reduce.3 = (f32[]{:T(128)}, f32[]{:T(128)}) all-reduce(f32[]{:T(128)} %get-tuple-element.165, f32[]{:T(128)S(6)} %div.211), channel_id=1, replica_groups=mesh['clip'=8,'band'=4] {'clip','band'}, use_global_device_ids=true, to_apply=%region_21.22 | all-reduce | flops 2 | bytes 16 | tf_op jit(solution)/shard_map/psum | solution.py:671
  2926.3 22.6 multiply_subtract_fusion.1
  2948.9 38.3 %multiply_subtract_fusion = (f32[128,30720]{1,0:T(8,128)}, f32[128,30720]{1,0:T(8,128)}, f32[128,30720]{1,0:T(8,128)}) fusion(f32[128,30720]{1,0:T(8,128)} %param.21, f32[128,30720]{1,0:T(8,128)} %constant_dynamic-update-slice_fusion, f32[]{:T(128)S(6)} %div.215, f32[128,30720]{1,0:T(8,128)} %param.22, f32[128,30720]{1,0:T(8,128)} %param.23), kind=kLoop, calls=%fused_computation.4 | loop fusion | flops 62914560 | bytes 110100480 | tf_op jit(solution)/shard_map/sub | solution.py:196
  (710 shorter events, 558.4 us)
Async XLA Ops:
  7.2 969.0 %reduce-scatter.30.cloned.1.call-start = ((), (), s32[]{:S(2)}) async-start(), calls=%async_computation.25 | async-start | bytes 819200 | tf_op jit(solution)/shard_map/reduce_scatter | solution.py:547
  27.7 373.2 %copy-start.140 = (f32[1,1024]{1,0:T(1,128)}, f32[1,1024]{1,0:T(1,128)S(1)}, u32[]{:S(2)}) copy-start(f32[1,1024]{1,0:T(1,128)S(1)} %get-tuple-element.134) | copy-start | bytes 12292
  49.2 351.7 %copy-start.17 = (f32[640,1024]{1,0:T(8,128)}, f32[640,1024]{1,0:T(8,128)S(1)}, u32[]{:S(2)}) copy-start(f32[640,1024]{1,0:T(8,128)S(1)} %get-tuple-element.150) | copy-start | bytes 7864324
  49.2 310.4 %copy-start.154 = (f32[640]{0:T(1024)}, f32[640]{0:T(1024)S(1)}, u32[]{:S(2)}) copy-start(f32[640]{0:T(1024)S(1)} %broadcast_multiply_fusion.7) | copy-start | bytes 7684
  49.7 310.0 %copy-start.180 = (f32[640]{0:T(1024)}, f32[640]{0:T(1024)S(1)}, u32[]{:S(2)}) copy-start(f32[640]{0:T(1024)S(1)} %fusion.78) | copy-start | bytes 7684
  359.6 78.6 %copy-start.188 = (f32[1024]{0:T(1024)}, f32[1024]{0:T(1024)S(1)}, u32[]{:S(2)}) copy-start(f32[1024]{0:T(1024)S(1)} %get-tuple-element.143) | copy-start | bytes 12292
  359.7 86.2 %copy-start.134 = (f32[1024]{0:T(1024)}, f32[1024]{0:T(1024)S(1)}, u32[]{:S(2)}) copy-start(f32[1024]{0:T(1024)S(1)} %get-tuple-element.139) | copy-start | bytes 12292
  369.0 5.3 collective-permute-start
  445.4 87.2 %copy-start.3 = (f32[640,1024]{1,0:T(8,128)}, f32[640,1024]{1,0:T(8,128)S(1)}, u32[]{:S(2)}) copy-start(f32[640,1024]{1,0:T(8,128)S(1)} %get-tuple-element.94) | copy-start | bytes 7864324
  447.7 13.6 collective-permute-start.1
  521.1 10.3 collective-permute-start.2
  543.4 94.3 %copy-start.1 = (f32[16,640,77]{1,2,0:T(8,128)}, f32[16,640,77]{1,2,0:T(8,128)S(1)}, u32[]{:S(2)}) copy-start(f32[16,640,77]{1,2,0:T(8,128)S(1)} %get-tuple-element.160) | copy-start | bytes 9461764
  651.9 8.2 collective-permute-start.3
  733.9 17.2 collective-permute-start.4
  820.0 38.2 %collective-permute-start.6 = (f32[5,128,1024]{2,1,0:T(8,128)}, f32[5,128,1024]{2,1,0:T(8,128)}, u32[]{:S(2)}, u32[]{:S(2)}) collective-permute-start(f32[5,128,1024]{2,1,0:T(8,128)} %copy.254), channel_id=1, source_target_pairs={{0,1},{1,0},{2,3},{3,2},{4,5},{5,4},{6,7},{7,6},{8,9},{9,8},{10,11... | collective-permute-start | bytes 7864328 | tf_op jit(solution)/shard_map/ppermute | solution.py:40
  837.6 27.3 collective-permute-start.5
  845.9 294.8 %reduce-scatter.12.cloned.1.call-start = ((), (), s32[]{:S(2)}) async-start(), calls=%async_computation.11 | async-start | bytes 12976128 | tf_op jit(solution)/shard_map/reduce_scatter | solution.py:664
  892.3 326.3 %reduce-scatter.14.cloned.1.call-start = ((), (), s32[]{:S(2)}) async-start(), calls=%async_computation.13 | async-start | bytes 12976128 | tf_op jit(solution)/shard_map/reduce_scatter | solution.py:664
  926.2 476.8 %reduce-scatter.28.cloned.1.call-start = ((), (), s32[]{:S(2)}) async-start(), calls=%async_computation.23 | async-start | bytes 17301504 | tf_op jit(solution)/shard_map/reduce_scatter | solution.py:664
  976.1 472.5 %all-gather.20.cloned.1.call-start = ((), (), s32[]{:S(2)}) async-start(), calls=%async_computation.26 | async-start | bytes 1474560 | tf_op jit(solution)/shard_map/all_gather | solution.py:548
  976.7 655.7 %reduce-scatter.32.cloned.1.call-start = ((), (), s32[]{:S(2)}) async-start(), calls=%async_computation.28 | async-start | bytes 17301504 | tf_op jit(solution)/shard_map/reduce_scatter | solution.py:664
  1020.3 799.1 %reduce-scatter.24.cloned.1.call-start = ((), (), s32[]{:S(2)}) async-start(), calls=%async_computation.19 | async-start | bytes 17301504 | tf_op jit(solution)/shard_map/reduce_scatter | solution.py:664
  1049.4 898.3 %all-reduce.6.cloned.1.call-start = ((), (), s32[]{:S(2)}) async-start(), calls=%async_computation.30 | async-start | bytes 196608 | tf_op jit(solution)/shard_map/psum | solution.py:671
  1076.7 1015.8 %reduce-scatter.22.cloned.1.call-start = ((), (), s32[]{:S(2)}) async-start(), calls=%async_computation.18 | async-start | bytes 4325376 | tf_op jit(solution)/shard_map/reduce_scatter | solution.py:664
  1081.0 1151.8 %reduce-scatter.20.cloned.1.call-start = ((), (), s32[]{:S(2)}) async-start(), calls=%async_computation.17 | async-start | bytes 4325376 | tf_op jit(solution)/shard_map/reduce_scatter | solution.py:664
  1088.8 1325.3 %reduce-scatter.26.cloned.1.call-start = ((), (), s32[]{:S(2)}) async-start(), calls=%async_computation.21 | async-start | bytes 17301504 | tf_op jit(solution)/shard_map/reduce_scatter | solution.py:664
  1118.3 1441.0 %reduce-scatter.18.cloned.1.call-start = ((), (), s32[]{:S(2)}) async-start(), calls=%async_computation.16 | async-start | bytes 4325376 | tf_op jit(solution)/shard_map/reduce_scatter | solution.py:664
  1129.4 1569.6 %reduce-scatter.16.cloned.1.call-start = ((), (), s32[]{:S(2)}) async-start(), calls=%async_computation.15 | async-start | bytes 4325376 | tf_op jit(solution)/shard_map/reduce_scatter | solution.py:664
  1140.3 308.3 %copy-start.62 = (bf16[8,80,512]{2,1,0:T(8,128)(2,1)S(1)}, bf16[8,80,512]{2,1,0:T(8,128)(2,1)}, u32[]{:S(2)}) copy-start(bf16[8,80,512]{2,1,0:T(8,128)(2,1)} %get-tuple-element.26) | copy-start | bytes 1966084
  1140.4 1575.6 %all-gather.10.cloned.1.call-start = ((), (), s32[]{:S(2)}) async-start(), calls=%async_computation.12 | async-start | bytes 1966080 | tf_op jit(solution)/shard_map/all_gather | solution.py:665
  1140.9 1596.1 %all-gather.12.cloned.1.call-start = ((), (), s32[]{:S(2)}) async-start(), calls=%async_computation.14 | async-start | bytes 1966080 | tf_op jit(solution)/shard_map/all_gather | solution.py:665
  1218.7 1542.4 %all-gather.18.cloned.1.call-start = ((), (), s32[]{:S(2)}) async-start(), calls=%async_computation.24 | async-start | bytes 2621440 | tf_op jit(solution)/shard_map/all_gather | solution.py:665
  1403.0 416.4 %copy-start.52 = (f32[5,4,16,1024]{3,2,1,0:T(8,128)S(1)}, f32[5,4,16,1024]{3,2,1,0:T(8,128)}, u32[]{:S(2)}) copy-start(f32[5,4,16,1024]{3,2,1,0:T(8,128)} %copy-done.51) | copy-start | bytes 3932164
  1403.0 1394.6 %all-gather.22.cloned.1.call-start = ((), (), s32[]{:S(2)}) async-start(), calls=%async_computation.27 | async-start | bytes 5242880 | tf_op jit(solution)/shard_map/all_gather | solution.py:554
  1448.6 370.9 %copy-start.182 = (f32[1024]{0:T(1024)S(1)}, f32[1024]{0:T(1024)}, u32[]{:S(2)}) copy-start(f32[1024]{0:T(1024)} %get-tuple-element.119) | copy-start | bytes 12292
  1448.6 370.9 %copy-start.174 = (f32[1024]{0:T(1024)S(1)}, f32[1024]{0:T(1024)}, u32[]{:S(2)}) copy-start(f32[1024]{0:T(1024)} %get-tuple-element.71) | copy-start | bytes 12292
  1448.6 370.9 %copy-start.175 = (f32[1024]{0:T(1024)S(1)}, f32[1024]{0:T(1024)}, u32[]{:S(2)}) copy-start(f32[1024]{0:T(1024)} %get-tuple-element.118) | copy-start | bytes 12292
  1448.7 370.9 %copy-start.176 = (f32[1024]{0:T(1024)S(1)}, f32[1024]{0:T(1024)}, u32[]{:S(2)}) copy-start(f32[1024]{0:T(1024)} %get-tuple-element.73) | copy-start | bytes 12292
  1448.7 370.9 %copy-start.183 = (f32[1024]{0:T(1024)S(1)}, f32[1024]{0:T(1024)}, u32[]{:S(2)}) copy-start(f32[1024]{0:T(1024)} %get-tuple-element.47) | copy-start | bytes 12292
  1448.7 370.9 %copy-start.184 = (f32[1024]{0:T(1024)S(1)}, f32[1024]{0:T(1024)}, u32[]{:S(2)}) copy-start(f32[1024]{0:T(1024)} %get-tuple-element.45) | copy-start | bytes 12292
  1448.7 370.9 %copy-start.185 = (f32[1024]{0:T(1024)S(1)}, f32[1024]{0:T(1024)}, u32[]{:S(2)}) copy-start(f32[1024]{0:T(1024)} %get-tuple-element.54) | copy-start | bytes 12292
  1448.7 370.9 %copy-start.192 = (f32[1024]{0:T(1024)S(1)}, f32[1024]{0:T(1024)}, u32[]{:S(2)}) copy-start(f32[1024]{0:T(1024)} %get-tuple-element.49) | copy-start | bytes 12292
  1448.7 370.9 %copy-start.193 = (f32[1024]{0:T(1024)S(1)}, f32[1024]{0:T(1024)}, u32[]{:S(2)}) copy-start(f32[1024]{0:T(1024)} %get-tuple-element.55) | copy-start | bytes 12292
  1452.5 411.6 %copy-start.114 = (f32[8,512]{1,0:T(8,128)S(1)}, f32[8,512]{1,0:T(8,128)}, u32[]{:S(2)}) copy-start(f32[8,512]{1,0:T(8,128)} %copy-done.113) | copy-start | bytes 49156
  1452.5 411.6 %copy-start.116 = (f32[8,512]{1,0:T(8,128)S(1)}, f32[8,512]{1,0:T(8,128)}, u32[]{:S(2)}) copy-start(f32[8,512]{1,0:T(8,128)} %copy-done.115) | copy-start | bytes 49156
  1452.5 1369.2 %all-gather.24.cloned.1.call-start = ((), (), s32[]{:S(2)}) async-start(), calls=%async_computation.29 | async-start | bytes 2621440 | tf_op jit(solution)/shard_map/all_gather | solution.py:665
  1632.5 1213.4 %all-gather.14.cloned.1.call-start = ((), (), s32[]{:S(2)}) async-start(), calls=%async_computation.20 | async-start | bytes 2621440 | tf_op jit(solution)/shard_map/all_gather | solution.py:665
  1819.4 1050.5 %all-gather.16.cloned.1.call-start = ((), (), s32[]{:S(2)}) async-start(), calls=%async_computation.22 | async-start | bytes 2621440 | tf_op jit(solution)/shard_map/all_gather | solution.py:665
  (193 other events, 1609.6 us)
Sparse Core Ops, SparseCore 0:
  846.0 30.4 reduce-scatter.29
  892.5 163.6 reduce-scatter.11
  1063.8 154.8 reduce-scatter.13
  1220.8 182.0 reduce-scatter.27
  1405.0 43.5 all-gather.19
  1450.8 181.6 reduce-scatter.31
  1634.7 184.5 reduce-scatter.23
  1825.5 122.1 all-reduce.5
  1950.0 142.5 reduce-scatter.21
  2095.3 137.5 reduce-scatter.19
  2235.2 178.8 reduce-scatter.25
  2416.8 142.5 reduce-scatter.17
  2562.2 136.7 reduce-scatter.15
  2700.4 15.5 all-gather.9
  2717.4 19.6 all-gather.11
  2738.5 22.5 all-gather.17
  2763.1 34.4 all-gather.21
  2799.0 22.5 all-gather.23
  2823.2 22.5 all-gather.13
  2847.3 22.5 all-gather.15

commit v2 on v1

--- a/solution.py
+++ b/solution.py
@@ -181,11 +181,10 @@
     norm_back, mlp_in, gelu_back, gelu_low, down_proj = saved
     grad_down = (modul[5] * grad_stream).astype(jnp.bfloat16)
     grad_gate = jnp.sum(grad_stream * down_proj, 0)
-    grad_w_down = matmul_tn(gelu_low, grad_down)
     grad_up = gelu_back(matmul_nt(grad_down, down_weight))[0].astype(jnp.bfloat16)
-    grad_w_up = matmul_tn(mlp_in, grad_up)
     grad_part, grad_shift, grad_scale = norm_back(matmul_nt(grad_up, up_weight))
-    return (grad_stream + grad_part, grad_w_up, grad_w_down, (grad_shift, grad_scale, grad_gate))
+    factors = ((gelu_low, grad_down), (mlp_in, grad_up))
+    return (grad_stream + grad_part, factors, (grad_shift, grad_scale, grad_gate))
 
 
 def adam_update(weight, first_mom, second_mom, grad_val, learn_rate):
@@ -389,6 +388,402 @@
         compiler_params=pltpu.CompilerParams(collective_id=1, has_side_effects=True),
     )(*shards, vectors, texts)
     return out[:num], out[num], out[num + 1]
+
+
+WIRE_MAX = 32767.0
+WIRE_LEAST = 1e-30
+UNIT = (128, 512)
+
+
+def unit_parts(kind, first):
+    if kind == 0:
+        return ((0, 4, lambda u: u, lambda u: 0), (4, 4, lambda u: 4, lambda u: u - 3))
+    return ((first, 3 - first, lambda u: u, lambda u: u), (3, 3, lambda u: 3, lambda u: u))
+
+
+def reduce_kernel(count, tokens, phases, *refs):
+    num = sum(len(phase["lefts"]) for phase in phases)
+    lefts, rights = refs[:num], refs[num : 2 * num]
+    wide_out, deep_out, square_out = refs[2 * num : 2 * num + 3]
+    left_far, right_far = refs[2 * num + 3 : 3 * num + 3], refs[3 * num + 3 : 4 * num + 3]
+    scratch = refs[4 * num + 3 :]
+    left_buf, right_buf, got_low, got_scale, put_low, put_scale, plane_put = (
+        scratch[2 * i : 2 * i + 2] for i in range(7)
+    )
+    plane_got = scratch[14 : 14 + len(phases)]
+    (
+        square_buf,
+        left_sem,
+        right_sem,
+        pair_send,
+        pair_recv,
+        half_send,
+        half_recv,
+        ring_send,
+        ring_recv,
+        credit,
+        plane_send,
+        plane_recv,
+        out_sem,
+        out_send,
+        out_recv,
+    ) = scratch[14 + len(phases) :]
+    me = lax.axis_index("clip")
+    band = lax.axis_index("band")
+    core = band % 2
+    plane = band // 2
+    place = ring_place(me, count)
+    onward = 1 - 2 * core
+    following = (ring_clip((place + onward + count) % count, count), band)
+    preceding = (ring_clip((place - onward + count) % count, count), band)
+    partner = (me, band + 1 - 2 * core)
+    mirror = (me, band + 2 - 4 * plane)
+    greet([following, preceding, partner, mirror])
+
+    def owner_at(step, way):
+        return ring_clip((place - way * (step + 1) + 2 * count) % count, count)
+
+    def left_blocks(at):
+        phase = phases[at]
+        if phase["kind"] == 0:
+            return [(b, phase["lefts"][0], b, 4) for b in range(4)] + [(4, phase["lefts"][1], 0, 1)]
+        first = phase["first"]
+        return [(first + i, left, 0, 1) for i, left in enumerate(phase["lefts"])]
+
+    def right_blocks(at):
+        phase = phases[at]
+        if phase["kind"] == 0:
+            return [(0, phase["lefts"][0], 0)] + [(1 + i, phase["lefts"][1], i) for i in range(4)]
+        first = phase["first"]
+        return [(first + i, phase["lefts"][i], 0) for i in range(3 - first)] + [
+            (3 + i, phase["lefts"][-1], i) for i in range(3)
+        ]
+
+    def left_cols(step, way, which, many):
+        width = lefts_width // count if many == 1 else deep_width // count
+        start = owner_at(step, way) * width + which * 128
+        return pl.ds(pl.multiple_of(start, 128), 128)
+
+    lefts_width = lefts[phases[1]["lefts"][0]].shape[1]
+    deep_width = lefts[phases[0]["lefts"][0]].shape[1]
+
+    def pair_left(at, step):
+        out = []
+        for block, operand, which, many in left_blocks(at):
+            cols = left_cols(step, -onward, which, many)
+            out.append(
+                pltpu.make_async_remote_copy(
+                    lefts[operand].at[:, cols],
+                    left_far[operand].at[:, cols],
+                    pair_send.at[at, block, step],
+                    pair_recv.at[at, block, step],
+                    partner,
+                    MESH,
+                )
+            )
+        return out
+
+    def pair_right(at):
+        out = []
+        for i, operand in enumerate(phases[at]["lefts"]):
+            half = rights[operand].shape[1] // 2
+            out.append(
+                pltpu.make_async_remote_copy(
+                    rights[operand].at[:, pl.ds(pl.multiple_of((1 - core) * half, 128), half)],
+                    right_far[operand],
+                    half_send.at[operand],
+                    half_recv.at[operand],
+                    partner,
+                    MESH,
+                )
+            )
+        return out
+
+    def load_left(at, step, slot, far):
+        kind = phases[at]["kind"]
+        out = []
+        for block, operand, which, many in left_blocks(at):
+            cols = left_cols(step, onward, which, many)
+            source = left_far if far else lefts
+            out.append(
+                pltpu.make_async_copy(
+                    source[operand].at[:, cols],
+                    left_buf[kind].at[slot, block, pl.ds(far * tokens, tokens), :],
+                    left_sem.at[kind, slot, block, far],
+                )
+            )
+        return out
+
+    def load_right(at, far):
+        kind = phases[at]["kind"]
+        out = []
+        for block, operand, which in right_blocks(at):
+            if far:
+                source = right_far[operand].at[:, pl.ds(which * UNIT[1], UNIT[1])]
+            else:
+                half = rights[operand].shape[1] // 2
+                start = pl.multiple_of(core * half + which * UNIT[1], 128)
+                source = rights[operand].at[:, pl.ds(start, UNIT[1])]
+            out.append(
+                pltpu.make_async_copy(
+                    source,
+                    right_buf[kind].at[block, pl.ds(far * tokens, tokens), :],
+                    right_sem.at[kind, block, far],
+                )
+            )
+        return out
+
+    def ring_copies(at, part, slot):
+        kind = phases[at]["kind"]
+        start, many = unit_parts(kind, phases[at]["first"])[part][:2]
+        units = pl.ds(start, many)
+        return [
+            pltpu.make_async_remote_copy(
+                put.at[slot, units],
+                got.at[slot, units],
+                ring_send.at[kind, slot, part, i],
+                ring_recv.at[kind, slot, part, i],
+                following,
+                MESH,
+            )
+            for i, (put, got) in enumerate(
+                ((put_low[kind], got_low[kind]), (put_scale[kind], got_scale[kind]))
+            )
+        ]
+
+    def plane_copy(at, part):
+        kind = phases[at]["kind"]
+        start, many = unit_parts(kind, phases[at]["first"])[part][:2]
+        units = pl.ds(start, many)
+        return pltpu.make_async_remote_copy(
+            plane_put[kind].at[units],
+            plane_got[at].at[units],
+            plane_send.at[at, part],
+            plane_recv.at[at, part],
+            mirror,
+            MESH,
+        )
+
+    def out_copies(at, unit):
+        phase = phases[at]
+        if phase["kind"] == 0 and unit < 4:
+            half = UNIT[1]
+            rows = deep_out.shape[0] // 4
+            there = deep_out.at[
+                pl.ds(unit * rows, rows),
+                pl.ds(pl.multiple_of(phase["cols"][0] + core * half, 128), half),
+            ]
+        else:
+            which, col = (1, unit - 4) if phase["kind"] == 0 else (unit - phase["first"], 0)
+            if phase["kind"] and unit >= 3:
+                which, col = len(phase["lefts"]) - 1, unit - 3
+            half = rights[phase["lefts"][which]].shape[1] // 2
+            start = phase["cols"][which] + core * half + col * UNIT[1]
+            there = wide_out.at[:, pl.ds(pl.multiple_of(start, 128), UNIT[1])]
+        here = plane_got[at].at[unit]
+        return (
+            pltpu.make_async_copy(here, there, out_sem.at[at, unit]),
+            pltpu.make_async_remote_copy(
+                here, there, out_send.at[at, unit], out_recv.at[at, unit], partner, MESH
+            ),
+        )
+
+    def product(kind, slot, left, right):
+        return lax.dot_general(
+            left_buf[kind][slot, left],
+            right_buf[kind][right],
+            (((0,), (0,)), ((), ())),
+            preferred_element_type=jnp.float32,
+        )
+
+    def start(copies):
+        for copy in copies:
+            copy.start()
+
+    def finish(copies):
+        for copy in copies:
+            copy.wait()
+
+    def take_step(at, step, first, last):
+        phase = phases[at]
+        kind = phase["kind"]
+        slot = step % 2
+        before = (step + 1) % 2
+        for far in range(2):
+            finish(load_left(at, step, slot, far))
+        if not last:
+            for copy in pair_left(at, step + 1):
+                copy.wait_recv()
+            for far in range(2):
+                start(load_left(at, step + 1, before, far))
+        for part, (low, many, left_of, right_of) in enumerate(unit_parts(kind, phase["first"])):
+            if not first:
+                for copy in ring_copies(at, part, before):
+                    copy.wait_recv()
+            if not (first or last):
+
+                @pl.when(step >= 2)
+                def _(part=part):
+                    for copy in ring_copies(at, part, slot):
+                        copy.wait_send()
+                    pl.semaphore_wait(credit.at[kind, part], 1)
+
+            @pl.loop(low, low + many)
+            def _(unit, left_of=left_of, right_of=right_of):
+                term = product(kind, slot, left_of(unit), right_of(unit))
+                if not first:
+                    came = got_low[kind][before, unit].astype(jnp.float32)
+                    term = term + came * got_scale[kind][before, unit]
+                if last:
+                    plane_put[kind][unit] = term
+                else:
+                    largest = jnp.max(jnp.abs(term), axis=0, keepdims=True)
+                    largest = jnp.maximum(largest, WIRE_LEAST)
+                    factor = WIRE_MAX / largest
+                    put_low[kind][slot, unit] = jnp.round(term * factor).astype(jnp.int16)
+                    put_scale[kind][slot, unit] = largest * (1.0 / WIRE_MAX)
+
+            if last:
+                plane_copy(at, part).start()
+            else:
+                start(ring_copies(at, part, slot))
+            if not (first or last):
+
+                @pl.when(step < count - 2)
+                def _(part=part):
+                    pl.semaphore_signal(
+                        credit.at[kind, part], inc=1, device_id=preceding, device_id_type=MESH
+                    )
+
+    def close(at):
+        kind = phases[at]["kind"]
+        for part, (low, many, _, _) in enumerate(unit_parts(kind, phases[at]["first"])):
+            plane_copy(at, part).wait()
+
+            @pl.loop(low, low + many)
+            def _(unit):
+                total = plane_put[kind][unit] + plane_got[at][unit]
+                plane_got[at][unit] = total
+                square_buf[...] += jnp.sum(
+                    (total * total).reshape(UNIT[0] // 8, 8, UNIT[1]), axis=0
+                )
+
+            for unit in range(low, low + many):
+                start(out_copies(at, unit))
+
+    square_buf[...] = jnp.zeros_like(square_buf)
+    start(load_right(0, 0))
+    start(pair_right(0))
+
+    @pl.loop(0, count)
+    def _(step):
+        start(pair_left(0, step))
+
+    start(load_left(0, 0, 0, 0))
+    for at in range(len(phases)):
+        if at == 0:
+            for copy in pair_right(0):
+                copy.wait_recv()
+            start(load_right(0, 1))
+            for copy in pair_left(0, 0):
+                copy.wait_recv()
+            start(load_left(0, 0, 0, 1))
+        for far in range(2):
+            finish(load_right(at, far))
+        more = at + 1 < len(phases)
+        if more:
+            start(pair_right(at + 1))
+            start(load_right(at + 1, 0))
+        take_step(at, 0, True, False)
+        if more:
+            start(pair_left(at + 1, 0))
+
+        @pl.loop(1, count - 1)
+        def _(step, at=at, more=more):
+            take_step(at, step, False, False)
+            if more:
+                start(pair_left(at + 1, step))
+
+        if more:
+            start(pair_left(at + 1, count - 1))
+            for copy in pair_right(at + 1):
+                copy.wait_recv()
+            start(load_right(at + 1, 1))
+            for copy in pair_left(at + 1, 0):
+                copy.wait_recv()
+            for far in range(2):
+                start(load_left(at + 1, 0, 0, far))
+        take_step(at, count - 1, False, True)
+        for part in range(2):
+            for slot in range(2):
+                for copy in ring_copies(at, part, slot):
+                    copy.wait_send()
+        if at:
+            close(at - 1)
+    close(len(phases) - 1)
+    square_out[...] = square_buf[...]
+    for at, phase in enumerate(phases):
+        for copy in pair_right(at):
+            copy.wait_send()
+
+        @pl.loop(0, count)
+        def _(step, at=at):
+            for copy in pair_left(at, step):
+                copy.wait_send()
+
+        for unit in range(phase["first"], 8 if phase["kind"] == 0 else 6):
+            finish(out_copies(at, unit))
+
+
+def reduce_gradients(phases, lefts, rights, wide_cols, deep_cols):
+    count = lax.axis_size("clip")
+    tokens = lefts[0].shape[0]
+    wide_rows = lefts[1].shape[1] // count
+    deep_rows = lefts[0].shape[1] // count
+    num = len(lefts)
+    dma = pltpu.SemaphoreType.DMA
+    units, lefts_of, rights_of = (8, 6), (5, 4), (5, 6)
+    scratch = [pltpu.VMEM((2, lefts_of[k], 2 * tokens, 128), jnp.bfloat16) for k in range(2)]
+    scratch += [pltpu.VMEM((rights_of[k], 2 * tokens, UNIT[1]), jnp.bfloat16) for k in range(2)]
+    for _ in range(2):
+        scratch += [pltpu.VMEM((2, units[k]) + UNIT, jnp.int16) for k in range(2)]
+        scratch += [pltpu.VMEM((2, units[k], 1, UNIT[1]), jnp.float32) for k in range(2)]
+    scratch += [pltpu.VMEM((units[k],) + UNIT, jnp.float32) for k in range(2)]
+    scratch += [pltpu.VMEM((units[p["kind"]],) + UNIT, jnp.float32) for p in phases]
+    scratch += [
+        pltpu.VMEM((8, UNIT[1]), jnp.float32),
+        dma((2, 2, 5, 2)),
+        dma((2, 6, 2)),
+        dma((len(phases), 5, count)),
+        dma((len(phases), 5, count)),
+        dma((num,)),
+        dma((num,)),
+        dma((2, 2, 2, 2)),
+        dma((2, 2, 2, 2)),
+        pltpu.SemaphoreType.REGULAR((2, 2)),
+        dma((len(phases), 2)),
+        dma((len(phases), 2)),
+        dma((len(phases), 8)),
+        dma((len(phases), 8)),
+        dma((len(phases), 8)),
+    ]
+    out = pl.pallas_call(
+        partial(reduce_kernel, count, tokens, phases),
+        out_shape=(
+            jax.ShapeDtypeStruct((wide_rows, wide_cols), jnp.float32),
+            jax.ShapeDtypeStruct((deep_rows, deep_cols), jnp.float32),
+            jax.ShapeDtypeStruct((8, UNIT[1]), jnp.float32),
+        )
+        + tuple(jax.ShapeDtypeStruct(x.shape, x.dtype) for x in lefts)
+        + tuple(jax.ShapeDtypeStruct((tokens, x.shape[1] // 2), x.dtype) for x in rights),
+        in_specs=[ANY] * (2 * num),
+        out_specs=(ANY, ANY, pl.BlockSpec(memory_space=pltpu.VMEM)) + (ANY,) * (2 * num),
+        scratch_shapes=scratch,
+        compiler_params=pltpu.CompilerParams(
+            collective_id=2, has_side_effects=True, vmem_limit_bytes=58 << 20
+        ),
+    )(*lefts, *rights)
+    return out[:3]
 
 
 def per_device(
@@ -530,17 +925,15 @@
     grad_pred = (weight_row * pred_error * (2.0 / global_count)).astype(jnp.bfloat16)
     grad_head = matmul_tn(grad_pred, final_low)
     grad_stream, grad_gain_f = final_back(matmul(grad_pred, head_low))
-    grad_stream, grad_up_b, grad_down_b, extra_b = mlp_backward(
+    grad_stream, mlp_factors_b, extra_b = mlp_backward(
         grad_stream, mod_b, up_b_w, down_b_w, saved_b
     )
     grad_cross = grad_stream.astype(jnp.bfloat16)
-    grad_w_co = matmul_tn(crossed, grad_cross)
     grad_crossed = split_heads(matmul_nt(grad_cross, cross_out_w).astype(jnp.bfloat16))
     cq_grad, ck_grad, cv_grad = attend_backward(
         cross_q, cross_k, cross_v, cross_total, grad_crossed, CROSS_FORMS
     )
     grad_query = merge_heads(cq_grad).astype(jnp.bfloat16)
-    grad_w_cq = matmul_tn(cross_in, grad_query)
     grad_part, grad_gain_c = cross_back(matmul_nt(grad_query, query_w))
     grad_keyval = jnp.concatenate([merge_heads(ck_grad), merge_heads(cv_grad)], 1)
     grad_keyval = jnp.pad(grad_keyval, ((0, TEXT_PAD - text_len), (0, 0)))
@@ -555,7 +948,7 @@
     grad_stream = grad_stream + grad_part
     grad_proj = (mod_b[2] * grad_stream).astype(jnp.bfloat16)
     grad_gate_b = jnp.sum(grad_stream * proj_b, 0)
-    grad_w_ob = matmul_tn(att_b, grad_proj)
+    factors_ob = (att_b, grad_proj)
     grad_att = (
         matmul_nt(grad_proj, out_b_w)
         .astype(jnp.bfloat16)
@@ -575,7 +968,7 @@
         .reshape(tok_count, 3 * D)
         .astype(jnp.bfloat16)
     )
-    grad_w_qkvb = matmul_tn(rolled, grad_qkv)
+    factors_qkvb = (rolled, grad_qkv)
     grad_in_roll = matmul_nt(grad_qkv, qkv_b_w).reshape(num_frames, num_rows, num_cols, D)
     sent_back = shifted(grad_in_roll[:, num_rows - SHIFT :], "band", 1)
     grad_normed = jnp.concatenate([sent_back, grad_in_roll[:, : num_rows - SHIFT]], 1).reshape(
@@ -583,12 +976,12 @@
     )
     grad_part, grad_shift_b, grad_scale_b = back_b(grad_normed)
     grad_stream = grad_stream + grad_part
-    grad_stream, grad_up_a, grad_down_a, extra_a = mlp_backward(
+    grad_stream, mlp_factors_a, extra_a = mlp_backward(
         grad_stream, mod_a, up_a_w, down_a_w, saved_a
     )
     grad_proj = (mod_a[2] * grad_stream).astype(jnp.bfloat16)
     grad_gate_a = jnp.sum(grad_stream * proj_a, 0)
-    grad_w_oa = matmul_tn(att_a, grad_proj)
+    factors_oa = (att_a, grad_proj)
     grad_att = (
         matmul_nt(grad_proj, out_a_w)
         .astype(jnp.bfloat16)
@@ -617,7 +1010,7 @@
         .reshape(tok_count, 3 * D)
         .astype(jnp.bfloat16)
     )
-    grad_w_qkva = matmul_tn(in_a, grad_qkv)
+    factors_qkva = (in_a, grad_qkv)
     grad_part, grad_shift_a, grad_scale_a = back_a(matmul_nt(grad_qkv, qkv_a_w))
     grad_stream = grad_stream + grad_part
     grad_patch = matmul_tn(noisy_low.astype(jnp.float32), grad_stream, lax.Precision.HIGHEST)
@@ -643,31 +1036,40 @@
     )
     all_grad_modul = lax.all_gather(lax.psum(grad_modul, "band"), "clip", axis=0, tiled=True)
     grad_w_ada = matmul_tn(time_rows.astype(jnp.float32), all_grad_modul, lax.Precision.HIGHEST)
-    members = (
-        grad_w_qkva,
-        grad_w_qkvb,
-        grad_w_oa,
-        grad_w_ob,
-        grad_w_cq,
-        grad_w_co,
-        grad_up_a,
-        grad_up_b,
-        grad_down_a,
-        grad_down_b,
-    )
-    summed = []
-    for member in members:
-        rows, cols = member.shape
-        member = member.reshape(rows, band_count, cols // band_count).transpose(1, 0, 2)
-        member = member.reshape(band_count, clip_count, rows // clip_count, cols // band_count)
-        member = member.transpose(1, 0, 2, 3).reshape(-1, cols // band_count)
-        member = lax.psum_scatter(member, ("clip", "band"), scatter_dimension=0, tiled=True)
-        summed.append(lax.all_gather(member, "band", axis=1, tiled=True))
-    wide_sum = jnp.concatenate([grad_w_ada] + summed[:8], 1)
-    deep_sum = jnp.concatenate([summed[8], grad_w_ckv, summed[9]], 1)
-    square_part = (jnp.sum(wide_sum * wide_sum) + jnp.sum(deep_sum * deep_sum)) / lax.axis_size(
-        "band"
-    )
+    factors = mlp_factors_b + (
+        (crossed, grad_cross),
+        (cross_in, grad_query),
+        factors_ob,
+        factors_qkvb,
+    )
+    factors += mlp_factors_a + (factors_oa, factors_qkva)
+    if wide_rows == 128 and deep_rows == 512:
+        phases = (
+            {"kind": 0, "first": 0, "lefts": (0, 1), "cols": (D, 10 * D + FF)},
+            {"kind": 1, "first": 0, "lefts": (2, 3, 4, 5), "cols": (9 * D, 8 * D, 7 * D, 3 * D)},
+            {"kind": 0, "first": 0, "lefts": (6, 7), "cols": (0, 10 * D)},
+            {"kind": 1, "first": 2, "lefts": (8, 9), "cols": (6 * D, 0)},
+        )
+        wide_rest, deep_rest, squares = reduce_gradients(
+            phases, [f[0] for f in factors], [f[1] for f in factors], 10 * D + 2 * FF, 2 * D
+        )
+        square_part = jnp.sum(squares) / (band_count // 2)
+    else:
+        summed = []
+        for left, right in factors:
+            member = matmul_tn(left, right)
+            rows, cols = member.shape
+            member = member.reshape(rows, band_count, cols // band_count).transpose(1, 0, 2)
+            member = member.reshape(band_count, clip_count, rows // clip_count, cols // band_count)
+            member = member.transpose(1, 0, 2, 3).reshape(-1, cols // band_count)
+            member = lax.psum_scatter(member, ("clip", "band"), scatter_dimension=0, tiled=True)
+            summed.append(lax.all_gather(member, "band", axis=1, tiled=True))
+        wide_rest = jnp.concatenate([summed[i] for i in (9, 5, 8, 4, 3, 2, 7, 1)], 1)
+        deep_rest = jnp.concatenate([summed[6], summed[0]], 1)
+        square_part = (jnp.sum(wide_rest**2) + jnp.sum(deep_rest**2)) / band_count
+    wide_sum = jnp.concatenate([grad_w_ada, wide_rest], 1)
+    deep_sum = jnp.concatenate([deep_rest[:, :D], grad_w_ckv, deep_rest[:, D:]], 1)
+    square_part += (jnp.sum(grad_w_ada**2) + jnp.sum(grad_w_ckv**2)) / band_count
     loss_sum, square_sum, small_sum = lax.psum(
         (loss_part, square_part, grad_small), ("clip", "band")
     )

time: 3010 us -> 1440 us (0.48)
  waiting for transfers between devices: 1650 us -> 61.3 us
  Pallas kernels: 313 us -> 642 us
  local copies, waits for them, and re-layouts: 341 us -> 172 us
  matrix products: 362 us -> 281 us
  blocking collectives: 119 us -> 88.7 us
    reduce_scatter x10 -> x0, waiting for transfers between devices: 1360 us -> none  [per_device(): lax.psum_scatter(member, ('clip', 'band'), scatter_dimension=0, tiled=True)]
    pallas_call x0 -> x1, Pallas kernels: none -> 329 us  [reduce_gradients(): pl.pallas_call(partial(reduce_kernel, count, tokens, phases), out_shape=(...]
    all_gather x6 -> x0, waiting for transfers between devices: 102 us -> none  [per_device(): summed.append(lax.all_gather(member, 'band', axis=1, tiled=True))]
    reshape x10 -> x0, local copies, waits for them, and re-layouts: 81.7 us -> none  [the longest x7 51.4 us: per_device(): member.reshape(band_count, clip_count, rows // clip_count, cols // band_c...]
    psum x1, waiting for transfers between devices: 79 us -> 0.01 us  [per_device(): lax.psum((loss_part, square_part, grad_small), ('clip', 'band'))]
    dot_general x14 -> x4, matrix products: 82.3 us -> 10.8 us  [matmul_tn(): lax.dot_general(left_op, right_op, (((0,), (0,)), ((), ())), precision=pr...]
    unnamed x446 -> x356, local copies, waits for them, and re-layouts: 94.7 us -> 38.5 us
    all_gather x1, waiting for transfers between devices: 45.6 us -> 3.14 us  [per_device(): grad_keyval = lax.all_gather(grad_keyval, 'clip', axis=0, tiled=True)]
  transfers between devices with their start and end apart: 27 -> 11, of which waited for: 22 -> 6; matrix products, arithmetic and copies ran while one was open for 12% -> 7% of each run, Pallas kernels for 0% -> 23%
where the time goes in v2:
time: 1440 us
  Pallas kernels  642 us (45%)
  matrix products  281 us (20%)
  local copies, waits for them, and re-layouts  172 us (12%)
  other arithmetic  161 us (11%)
  blocking collectives  88.7 us (6%)
  waiting for transfers between devices  61.3 us (4%)
  between operations  26.1 us (2%)
    pallas_call x1, Pallas kernels, reduce_gradients(): pl.pallas_call(partial(reduce_kernel, count, tokens, phases), out_shape=(...  329 us
    pallas_call x1, Pallas kernels, gather_weights(): pl.pallas_call(partial(gather_kernel, count, [shard.shape for shard in sh...  296 us
    dot_general x14, matrix products, matmul(): return jnp.dot(left_op, right_op, preferred_element_type=jnp.float32)  106 us
    dot_general x11, matrix products, matmul_nt(): lax.dot_general(left_op, right_op, (((1,), (1,)), ((), ())), preferred_el...  82.2 us
    sub x3, other arithmetic, adam_update(): weight - learn_rate * (first_hat / (jnp.sqrt(second_hat) + ADAM_EPS) + DE...  56.9 us
    unnamed x356, local copies, waits for them, and re-layouts  38.5 us
    psum x1, blocking collectives, per_device(): lax.psum((loss_part, square_part, grad_small), ('clip', 'band'))  38.1 us
    all_gather x1, blocking collectives, per_device(): lax.all_gather(lax.psum(grad_modul, 'band'), 'clip', axis=0, tiled=True)  31.4 us
  transfers between devices with their start and end apart: 11, of which 6 were waited for; matrix products, arithmetic and copies ran while one was open for 7% of the time, Pallas kernels for 23%

profile of v2, /device:TPU:0, one launch (start us, length us, event | category | flops | bytes accessed | tf_op | source)
XLA Modules:
  0.0 1436.7 jit_solution(17220808445863860548)
XLA Ops:
  8.9 9.6 convert.28
  30.8 17.7 %shard_map.230 = (s32[8,8,128]{2,1,0:T(8,128)}, bf16[8,80,512]{2,1,0:T(8,128)(2,1)}) custom-call(s32[8,128]{1,0:T(8,128)} %pad.12.facts_ref, bf16[8,80,512]{2,1,0:T(8,128)(2,1)} %pad.13.text_ref), custom_call_target="tpu_custom_call" | custom-call | tf_op jit(solution)/shard_map/pallas_call | solution.py:250
  63.3 295.5 %shard_map.231 = (bf16[1024,3072]{1,0:T(8,128)(2,1)}, bf16[1024,3072]{1,0:T(8,128)(2,1)}, bf16[1024,1024]{1,0:T(8,128)(2,1)}, bf16[1024,1024]{1,0:T(8,128)(2,1)}...) custom-call(bf16[128,3072]{1,0:T(8,128)(2,1)} %get-tuple-element.110, ...), custom_call_target="tpu_custom_call" | custom-call | tf_op jit(solution)/shard_map/pallas_call | solution.py:370
  361.1 7.7 convolution_convert_fusion.1
  389.1 4.7 multiply_reduce_fusion.3
  407.5 29.7 %multiply_convert_fusion.3 = (bf16[640,4096]{1,0:T(8,128)(2,1)S(1)}, f32[640,4096]{1,0:T(8,128)}, f32[640,4096]{1,0:T(8,128)}) fusion(bf16[640,1024]{1,0:T(8,128)(2,1)S(1)} %add_convert_fusion.6.refs_7_, bf16[1024,4096]{1,0:T(8,128)(2,1)S(1)} %bitcast.344), kind=kOutput, calls=%fused_computation.32 | convolution fusion | flops 5539102720 | bytes 35913728 | tf_op jit(solution)/shard_map/dot_general | solution.py:49
  437.4 7.3 fusion.91
  452.6 8.0 all_gather.12
  461.8 7.7 convolution_convert_fusion
  479.6 9.9 multiply_reduce_fusion.1
  489.5 8.6 exponential_reduce_fusion
  498.8 9.6 fusion.25
  508.4 4.7 copy.140
  513.1 4.9 reshape_reshape.11
  524.7 6.1 collective-permute-done.2
  548.0 29.9 %multiply_convert_fusion.2 = (bf16[640,4096]{1,0:T(8,128)(2,1)S(1)}, f32[640,4096]{1,0:T(8,128)}, f32[640,4096]{1,0:T(8,128)}) fusion(bf16[640,1024]{1,0:T(8,128)(2,1)S(1)} %add_convert_fusion.4.refs_1_, bf16[1024,4096]{1,0:T(8,128)(2,1)S(1)} %bitcast.348), kind=kOutput, calls=%fused_computation.19 | convolution fusion | flops 5539102720 | bytes 35913728 | tf_op jit(solution)/shard_map/dot_general | solution.py:49
  577.9 7.2 fusion.88
  590.1 17.9 %add_convert_fusion.1.refs_11_ = bf16[640,4096]{1,0:T(8,128)(2,1)} fusion(f32[640,4096]{1,0:T(8,128)} %get-tuple-element.94, f32[640,4096]{1,0:T(8,128)} %get-tuple-element.170, bf16[640,1024]{1,0:T(8,128)(2,1)S(1)} %multiply_convert_fusion.10.refs_10_, bf16[4096,1024]{1,0:T(8,128)(2,1)} %get-tuple-element.41), kind=kOutput, calls=%fused_computation.18 | convolution fusion | flops 5405409280 | bytes 35913728 | tf_op jit(solution)/shard_map/dot_general | solution.py:63
  607.9 11.3 multiply_reduce_fusion.12
  646.6 8.1 collective-permute-done.3
  656.0 4.6 reshape_reshape.12
  660.6 4.8 copy.148
  665.4 10.0 convolution_bitcast_fusion
  675.4 10.9 multiply_reduce_fusion
  686.3 11.3 multiply_convert_fusion
  704.0 4.7 copy.155
  708.7 4.9 concatenate.62
  713.6 4.7 copy.150
  722.8 4.7 copy.152
  727.5 4.5 concatenate.61
  732.0 7.9 fusion.16
  747.1 12.2 collective-permute-done.4
  766.5 17.5 %add_convert_fusion.refs_17_ = bf16[640,4096]{1,0:T(8,128)(2,1)} fusion(f32[640,4096]{1,0:T(8,128)} %get-tuple-element.100, f32[640,4096]{1,0:T(8,128)} %get-tuple-element.161, bf16[640,1024]{1,0:T(8,128)(2,1)S(1)} %multiply_convert_fusion.7.refs_16_, bf16[4096,1024]{1,0:T(8,128)(2,1)} %get-tuple-element.34), kind=kOutput, calls=%fused_computation.17 | convolution fusion | flops 5405409280 | bytes 35913728 | tf_op jit(solution)/shard_map/dot_general | solution.py:63
  784.1 10.3 multiply_reduce_fusion.15
  806.7 6.7 fusion.33
  814.1 6.3 multiply_reduce_fusion.2
  824.4 9.0 multiply_convert_fusion.1
  847.1 30.2 %reduce-scatter.2.cloned.1.call-done = f32[80,512]{1,0:T(8,128)} async-done(((f32[80,2048]{1,0:T(8,128)}), f32[80,512]{1,0:T(8,128)}) %reduce-scatter.2.cloned.1.call-update) | async-done | bytes 163856 | tf_op jit(solution)/shard_map/reduce_scatter | solution.py:940
  881.2 5.5 fusion.27
  891.2 4.7 reshape.510
  904.5 7.7 multiply_reduce_fusion.10
  940.4 328.8 %shard_map.232 = (f32[128,18432]{1,0:T(8,128)}, f32[512,2048]{1,0:T(8,128)}, f32[8,512]{1,0:T(8,128)}, bf16[640,4096]{1,0:T(8,128)(2,1)}, bf16[640,1024]{1,0:T(8...) custom-call(bf16[640,4096]{1,0:T(8,128)(2,1)} %copy-done.61, ...), custom_call_target="tpu_custom_call" | custom-call | tf_op jit(solution)/shard_map/pallas_call | solution.py:770
  1271.1 11.2 psum.29
  1282.3 31.4 %all-gather = f32[8,1,12288]{2,1,0:T(1,128)S(1)} all-gather(f32[1,1,12288]{2,1,0:T(1,128)S(1)} %bitcast.315), channel_id=1, replica_groups=mesh['clip'=8,'band'=4] {'clip'}, dimensions={0}, use_global_device_ids=true | all-gather | bytes 442368 | tf_op jit(solution)/shard_map/all_gather | solution.py:1037
  1317.7 5.6 multiply_reduce_fusion.4
  1330.0 38.1 %all-reduce.3 = (f32[]{:T(128)}, f32[]{:T(128)}) all-reduce(f32[]{:T(128)} %get-tuple-element.172, f32[]{:T(128)S(6)} %add.348), channel_id=1, replica_groups=mesh['clip'=8,'band'=4] {'clip','band'}, use_global_device_ids=true, to_apply=%region_21.22 | all-reduce | flops 2 | bytes 16 | tf_op jit(solution)/shard_map/psum | solution.py:1073
  1370.2 36.6 %multiply_subtract_fusion = (f32[128,30720]{1,0:T(8,128)}, f32[128,30720]{1,0:T(8,128)}, f32[128,30720]{1,0:T(8,128)}) fusion(f32[128,30720]{1,0:T(8,128)} %param.21, f32[]{:T(128)S(6)} %div.219, f32[128,18432]{1,0:T(8,128)} %get-tuple-element.43, f32[128,12288]{1,0:T(8,128)} %get-tuple-element.186, f32[128,30720]{1,0:T(8,128)} %param.22, f32[128,30720]{1,0:T(8,128)} %param.23), kind=kLoop, calls=%fused_computation.3 | loop fusion | flops 66846720 | bytes 110100480 | tf_op jit(solution)/shard_map/sub | solution.py:195
  1407.6 19.5 %multiply_subtract_fusion.1 = (f32[512,4096]{1,0:T(8,128)}, f32[512,4096]{1,0:T(8,128)}, f32[512,4096]{1,0:T(8,128)}) fusion(f32[512,4096]{1,0:T(8,128)} %param.24, f32[]{:T(128)S(6)} %div.219, f32[512,1024]{1,0:T(8,128)} %get-tuple-element.118, f32[512,2048]{1,0:T(8,128)} %all-gather.6.cloned.1.call-done, f32[512,1024]{1,0:T(8,128)S(1)} %get-tuple-element.117, ...), kind=kLoop, calls=%fused_computation.53 | loop fusion | flops 37748736 | bytes 58720260 | tf_op jit(solution)/shard_map/sub | solution.py:195
  (549 shorter events, 250.3 us)
Async XLA Ops:
  8.0 869.2 %reduce-scatter.2.cloned.1.call-start = ((), (), s32[]{:S(2)}) async-start(), calls=%async_computation.1 | async-start | bytes 819200 | tf_op jit(solution)/shard_map/reduce_scatter | solution.py:940
  27.9 21.5 %copy-start.86 = (bf16[19,1024]{1,0:T(8,128)(2,1)}, bf16[19,1024]{1,0:T(8,128)(2,1)S(1)}, u32[]{:S(2)}) copy-start(bf16[19,1024]{1,0:T(8,128)(2,1)S(1)} %convert_element_type.191) | copy-start | bytes 116740
  28.5 374.4 %copy-start.98 = (f32[1,1024]{1,0:T(1,128)}, f32[1,1024]{1,0:T(1,128)S(1)}, u32[]{:S(2)}) copy-start(f32[1,1024]{1,0:T(1,128)S(1)} %get-tuple-element.141) | copy-start | bytes 12292
  29.4 20.1 %copy-start.102 = (bf16[640,8]{0,1:T(8,128)(2,1)}, bf16[640,8]{0,1:T(8,128)(2,1)S(1)}, u32[]{:S(2)}) copy-start(bf16[640,8]{0,1:T(8,128)(2,1)S(1)} %convert_element_type.190) | copy-start | bytes 30724
  50.1 352.9 %copy-start.9 = (f32[640,1024]{1,0:T(8,128)}, f32[640,1024]{1,0:T(8,128)S(1)}, u32[]{:S(2)}) copy-start(f32[640,1024]{1,0:T(8,128)S(1)} %get-tuple-element.157) | copy-start | bytes 7864324
  50.1 310.4 %copy-start.114 = (f32[640]{0:T(1024)}, f32[640]{0:T(1024)S(1)}, u32[]{:S(2)}) copy-start(f32[640]{0:T(1024)S(1)} %broadcast_multiply_fusion.7) | copy-start | bytes 7684
  50.6 309.9 %copy-start.131 = (f32[640]{0:T(1024)}, f32[640]{0:T(1024)S(1)}, u32[]{:S(2)}) copy-start(f32[640]{0:T(1024)S(1)} %fusion.60) | copy-start | bytes 7684
  360.5 42.5 %copy-start.145 = (f32[1024]{0:T(1024)}, f32[1024]{0:T(1024)S(1)}, u32[]{:S(2)}) copy-start(f32[1024]{0:T(1024)S(1)} %get-tuple-element.153) | copy-start | bytes 12292
  360.5 46.4 %copy-start.124 = (f32[1024]{0:T(1024)}, f32[1024]{0:T(1024)S(1)}, u32[]{:S(2)}) copy-start(f32[1024]{0:T(1024)S(1)} %get-tuple-element.149) | copy-start | bytes 12292
  360.5 76.8 %copy-start.147 = (f32[1024]{0:T(1024)}, f32[1024]{0:T(1024)S(1)}, u32[]{:S(2)}) copy-start(f32[1024]{0:T(1024)S(1)} %get-tuple-element.150) | copy-start | bytes 12292
  360.5 84.7 %copy-start.110 = (f32[1024]{0:T(1024)}, f32[1024]{0:T(1024)S(1)}, u32[]{:S(2)}) copy-start(f32[1024]{0:T(1024)S(1)} %get-tuple-element.146) | copy-start | bytes 12292
  370.6 5.3 collective-permute-start
  406.4 30.9 %copy-start.13 = (f32[640,1024]{1,0:T(8,128)}, f32[640,1024]{1,0:T(8,128)S(1)}, u32[]{:S(2)}) copy-start(f32[640,1024]{1,0:T(8,128)S(1)} %get-tuple-element.102) | copy-start | bytes 7864324
  406.4 30.9 %slice-start.5 = ((s8[8388608]{0:T(1024)(128)(4,1)}), s8[4194304]{0:T(1024)(128)(4,1)S(1)}, s32[]{:S(2)}) async-start(s8[8388608]{0:T(1024)(128)(4,1)} %bitcast.345), calls=%async_computation.10 | async-start | bytes 8388608
  406.8 30.5 %copy-start.135 = (f32[640]{0:T(1024)}, f32[640]{0:T(1024)S(1)}, u32[]{:S(2)}) copy-start(f32[640]{0:T(1024)S(1)} %multiply_reduce_fusion.27) | copy-start | bytes 7684
  406.8 30.5 %copy-start.127 = (f32[640]{0:T(1024)}, f32[640]{0:T(1024)S(1)}, u32[]{:S(2)}) copy-start(f32[640]{0:T(1024)S(1)} %fusion.61) | copy-start | bytes 7684
  407.4 29.9 %copy-start.45 = (bf16[640,1024]{1,0:T(8,128)(2,1)}, bf16[640,1024]{1,0:T(8,128)(2,1)S(1)}, u32[]{:S(2)}) copy-start(bf16[640,1024]{1,0:T(8,128)(2,1)S(1)} %add_convert_fusion.6.refs_7_) | copy-start | bytes 3932164
  407.5 29.8 %slice-start.6 = ((s8[8388608]{0:T(1024)(128)(4,1)}), s8[4194304]{0:T(1024)(128)(4,1)S(1)}, s32[]{:S(2)}) async-start(s8[8388608]{0:T(1024)(128)(4,1)} %bitcast.345), calls=%async_computation.11 | async-start | bytes 8388608
  444.7 87.4 %copy-start.3 = (f32[640,1024]{1,0:T(8,128)}, f32[640,1024]{1,0:T(8,128)S(1)}, u32[]{:S(2)}) copy-start(f32[640,1024]{1,0:T(8,128)S(1)} %get-tuple-element.98) | copy-start | bytes 7864324
  447.0 13.6 collective-permute-start.1
  520.5 11.6 copy-start.112
  520.5 10.3 collective-permute-start.2
  522.7 17.6 %copy-start.67 = (bf16[77,1024]{0,1:T(8,128)(2,1)}, bf16[77,1024]{0,1:T(8,128)(2,1)S(1)}, u32[]{:S(2)}) copy-start(bf16[77,1024]{0,1:T(8,128)(2,1)S(1)} %copy.144) | copy-start | bytes 473092
  524.7 62.7 %copy-start.116 = (f32[640]{0:T(1024)}, f32[640]{0:T(1024)S(1)}, u32[]{:S(2)}) copy-start(f32[640]{0:T(1024)S(1)} %broadcast_bitcast_fusion) | copy-start | bytes 7684
  546.8 31.1 %slice-start.9 = ((s8[8388608]{0:T(1024)(128)(4,1)}), s8[4194304]{0:T(1024)(128)(4,1)S(1)}, s32[]{:S(2)}) async-start(s8[8388608]{0:T(1024)(128)(4,1)} %bitcast.349), calls=%async_computation.14 | async-start | bytes 8388608
  547.2 30.7 %copy-start.141 = (f32[640]{0:T(1024)}, f32[640]{0:T(1024)S(1)}, u32[]{:S(2)}) copy-start(f32[640]{0:T(1024)S(1)} %multiply_reduce_fusion.24) | copy-start | bytes 7684
  547.9 30.0 %copy-start.46 = (bf16[640,1024]{1,0:T(8,128)(2,1)}, bf16[640,1024]{1,0:T(8,128)(2,1)S(1)}, u32[]{:S(2)}) copy-start(bf16[640,1024]{1,0:T(8,128)(2,1)S(1)} %add_convert_fusion.4.refs_1_) | copy-start | bytes 3932164
  547.9 30.0 %copy-start.150 = (f32[1024]{0:T(1024)S(1)}, f32[1024]{0:T(1024)}, u32[]{:S(2)}) copy-start(f32[1024]{0:T(1024)} %get-tuple-element.142) | copy-start | bytes 12292
  548.0 30.0 %slice-start.10 = ((s8[8388608]{0:T(1024)(128)(4,1)}), s8[4194304]{0:T(1024)(128)(4,1)S(1)}, s32[]{:S(2)}) async-start(s8[8388608]{0:T(1024)(128)(4,1)} %bitcast.349), calls=%async_computation.15 | async-start | bytes 8388608
  589.8 30.4 %copy-start.11 = (f32[640,1024]{1,0:T(8,128)}, f32[640,1024]{1,0:T(8,128)S(1)}, u32[]{:S(2)}) copy-start(f32[640,1024]{1,0:T(8,128)S(1)} %get-tuple-element.90) | copy-start | bytes 7864324
  590.1 17.9 %copy-start.47 = (bf16[640,1024]{1,0:T(8,128)(2,1)}, bf16[640,1024]{1,0:T(8,128)(2,1)S(1)}, u32[]{:S(2)}) copy-start(bf16[640,1024]{1,0:T(8,128)(2,1)S(1)} %multiply_convert_fusion.10.refs_10_) | copy-start | bytes 3932164
  646.5 8.2 collective-permute-start.3
  741.8 17.5 %collective-permute-start.4 = (f32[5,4,16,1024]{3,2,1,0:T(8,128)}, f32[5,4,16,1024]{3,2,1,0:T(8,128)}, u32[]{:S(2)}, u32[]{:S(2)}) collective-permute-start(f32[5,4,16,1024]{3,2,1,0:T(8,128)} %get-tuple-element.128), channel_id=1, source_target_pairs={{0,1},{1,2},{2,3},{3,0},{4,5},{5,6},{6,7},{7,4},{8,9},{9,10},{10,1... | collective-permute-start | bytes 3932168 | tf_op jit(solution)/shard_map/ppermute | solution.py:45
  766.5 17.6 %copy-start.44 = (bf16[640,1024]{1,0:T(8,128)(2,1)}, bf16[640,1024]{1,0:T(8,128)(2,1)S(1)}, u32[]{:S(2)}) copy-start(bf16[640,1024]{1,0:T(8,128)(2,1)S(1)} %multiply_convert_fusion.7.refs_16_) | copy-start | bytes 3932164
  766.5 17.6 %copy-start.14 = (f32[640,1024]{1,0:T(8,128)S(1)}, f32[640,1024]{1,0:T(8,128)}, u32[]{:S(2)}) copy-start(f32[640,1024]{1,0:T(8,128)} %copy-done.13) | copy-start | bytes 7864324
  766.5 17.6 %copy-start.109 = (f32[640]{0:T(1024)S(1)}, f32[640]{0:T(1024)}, u32[]{:S(2)}) copy-start(f32[640]{0:T(1024)} %copy-done.108) | copy-start | bytes 7684
  766.5 17.6 %copy-start.125 = (f32[1024]{0:T(1024)S(1)}, f32[1024]{0:T(1024)}, u32[]{:S(2)}) copy-start(f32[1024]{0:T(1024)} %copy-done.124) | copy-start | bytes 12292
  766.5 17.6 %copy-start.128 = (f32[640]{0:T(1024)S(1)}, f32[640]{0:T(1024)}, u32[]{:S(2)}) copy-start(f32[640]{0:T(1024)} %copy-done.127) | copy-start | bytes 7684
  800.0 13.5 slice-start
  824.4 73.5 %collective-permute-start.6 = (f32[5,128,1024]{2,1,0:T(8,128)}, f32[5,128,1024]{2,1,0:T(8,128)}, u32[]{:S(2)}, u32[]{:S(2)}) collective-permute-start(f32[5,128,1024]{2,1,0:T(8,128)} %copy.185), channel_id=1, source_target_pairs={{0,1},{1,0},{2,3},{3,2},{4,5},{5,4},{6,7},{7,6},{8,9},{9,8},{10,11... | collective-permute-start | bytes 7864328 | tf_op jit(solution)/shard_map/ppermute | solution.py:40
  842.0 59.1 %collective-permute-start.5 = (f32[5,128,1024]{2,1,0:T(8,128)}, f32[5,128,1024]{2,1,0:T(8,128)}, u32[]{:S(2)}, u32[]{:S(2)}) collective-permute-start(f32[5,128,1024]{2,1,0:T(8,128)} %copy.183), channel_id=1, source_target_pairs={{0,1},{1,0},{2,3},{3,2},{4,5},{5,4},{6,7},{7,6},{8,9},{9,8},{10,11... | collective-permute-start | bytes 7864328 | tf_op jit(solution)/shard_map/ppermute | solution.py:40
  846.7 74.8 %all-gather.4.cloned.1.call-start = ((), (), s32[]{:S(2)}) async-start(), calls=%async_computation.2 | async-start | bytes 1474560 | tf_op jit(solution)/shard_map/all_gather | solution.py:941
  877.3 446.1 %all-reduce.6.cloned.1.call-start = ((), (), s32[]{:S(2)}) async-start(), calls=%async_computation.4 | async-start | bytes 196608 | tf_op jit(solution)/shard_map/psum | solution.py:1073
  918.3 406.5 %all-gather.6.cloned.1.call-start = ((), (), s32[]{:S(2)}) async-start(), calls=%async_computation.3 | async-start | bytes 5242880 | tf_op jit(solution)/shard_map/all_gather | solution.py:947
  1370.1 36.7 %copy-start.84 = (f32[19,1024]{1,0:T(8,128)S(1)}, f32[19,1024]{1,0:T(8,128)}, u32[]{:S(2)}) copy-start(f32[19,1024]{1,0:T(8,128)} %param.27) | copy-start | bytes 233476
  1370.1 36.7 %copy-start.85 = (f32[19,1024]{1,0:T(8,128)S(1)}, f32[19,1024]{1,0:T(8,128)}, u32[]{:S(2)}) copy-start(f32[19,1024]{1,0:T(8,128)} %all-reduce.6.cloned.1.call-done) | copy-start | bytes 233476
  1370.1 36.7 %copy-start.100 = (f32[19,1024]{1,0:T(8,128)S(1)}, f32[19,1024]{1,0:T(8,128)}, u32[]{:S(2)}) copy-start(f32[19,1024]{1,0:T(8,128)} %param.28) | copy-start | bytes 233476
  1370.2 36.7 %copy-start.101 = (f32[19,1024]{1,0:T(8,128)S(1)}, f32[19,1024]{1,0:T(8,128)}, u32[]{:S(2)}) copy-start(f32[19,1024]{1,0:T(8,128)} %param.29) | copy-start | bytes 233476
  (137 other events, 506.1 us)
Sparse Core Ops, SparseCore 0:
  846.8 30.3 reduce-scatter.1
  879.4 42.0 all-gather.3
  925.4 33.7 all-gather.5
Sparse Core Ops, SparseCore 1:
  918.4 141.1 all-reduce.5

commit v3 on v2

--- a/solution.py
+++ b/solution.py
@@ -363,6 +363,20 @@
             pair_copy(group, step).wait()
 
 
+def gather_quarters(shard):
+    band_count = lax.axis_size("band")
+    rows = shard.shape[0] // band_count
+    own = lax.dynamic_slice_in_dim(shard, lax.axis_index("band") * rows, rows, 0)
+    return lax.all_gather(own.astype(jnp.bfloat16), ("clip", "band"), axis=0, tiled=True)
+
+
+def sum_rows(left, right):
+    part = lax.psum_scatter(
+        matmul_tn(left, right), ("clip", "band"), scatter_dimension=0, tiled=True
+    )
+    return lax.all_gather(part, "band", axis=0, tiled=True)
+
+
 def gather_weights(shards, vectors, texts):
     count = lax.axis_size("clip")
     num = len(shards)
@@ -386,6 +400,7 @@
             pltpu.SemaphoreType.DMA((2,)),
         ],
         compiler_params=pltpu.CompilerParams(collective_id=1, has_side_effects=True),
+        cost_estimate=pl.CostEstimate(flops=2 * 10**11, bytes_accessed=6 * 10**8, transcendentals=0),
     )(*shards, vectors, texts)
     return out[:num], out[num], out[num + 1]
 
@@ -464,8 +479,8 @@
         start = owner_at(step, way) * width + which * 128
         return pl.ds(pl.multiple_of(start, 128), 128)
 
-    lefts_width = lefts[phases[1]["lefts"][0]].shape[1]
-    deep_width = lefts[phases[0]["lefts"][0]].shape[1]
+    lefts_width = wide_out.shape[0] * count
+    deep_width = deep_out.shape[0] * count
 
     def pair_left(at, step):
         out = []
@@ -735,11 +750,9 @@
             finish(out_copies(at, unit))
 
 
-def reduce_gradients(phases, lefts, rights, wide_cols, deep_cols):
+def reduce_gradients(phases, lefts, rights, wide_shape, deep_shape):
     count = lax.axis_size("clip")
     tokens = lefts[0].shape[0]
-    wide_rows = lefts[1].shape[1] // count
-    deep_rows = lefts[0].shape[1] // count
     num = len(lefts)
     dma = pltpu.SemaphoreType.DMA
     units, lefts_of, rights_of = (8, 6), (5, 4), (5, 6)
@@ -770,8 +783,8 @@
     out = pl.pallas_call(
         partial(reduce_kernel, count, tokens, phases),
         out_shape=(
-            jax.ShapeDtypeStruct((wide_rows, wide_cols), jnp.float32),
-            jax.ShapeDtypeStruct((deep_rows, deep_cols), jnp.float32),
+            jax.ShapeDtypeStruct(wide_shape, jnp.float32),
+            jax.ShapeDtypeStruct(deep_shape, jnp.float32),
             jax.ShapeDtypeStruct((8, UNIT[1]), jnp.float32),
         )
         + tuple(jax.ShapeDtypeStruct(x.shape, x.dtype) for x in lefts)
@@ -782,6 +795,7 @@
         compiler_params=pltpu.CompilerParams(
             collective_id=2, has_side_effects=True, vmem_limit_bytes=58 << 20
         ),
+        cost_estimate=pl.CostEstimate(flops=3 * 10**11, bytes_accessed=8 * 10**8, transcendentals=0),
     )(*lefts, *rights)
     return out[:3]
 
@@ -831,9 +845,11 @@
         w_deep, (0, D + band_at * kv_cols), (deep_rows, kv_cols)
     ).astype(jnp.bfloat16)
     part_kv = matmul(all_text.reshape(clip_count * TEXT_PAD, deep_rows), kv_weight)
-    edges = (12 * D, 15 * D, 18 * D, 19 * D, 20 * D, 21 * D, 22 * D, 22 * D + FF, 22 * D + 2 * FF)
+    edges = (12 * D, 15 * D, 18 * D, 19 * D, 20 * D, 21 * D, 22 * D, 22 * D + FF)
     shards = [w_wide[:, low:high].astype(jnp.bfloat16) for low, high in zip(edges, edges[1:])]
-    shards += [w_deep[:, :D].astype(jnp.bfloat16), w_deep[:, 3 * D :].astype(jnp.bfloat16)]
+    shards += [w_deep[:, :D].astype(jnp.bfloat16)]
+    up_b_w = gather_quarters(w_wide[:, 22 * D + FF :])
+    down_b_w = gather_quarters(w_deep[:, 3 * D :])
     gathered, all_modul, all_kv = gather_weights(
         shards,
         part_modul.reshape(clip_count, 12 * D // 128, 128),
@@ -847,9 +863,7 @@
         query_w,
         cross_out_w,
         up_a_w,
-        up_b_w,
         down_a_w,
-        down_b_w,
     ) = gathered
     keyval = lax.all_gather(jnp.sum(all_kv, 0).astype(jnp.bfloat16), "band", axis=1, tiled=True)
     keyval = keyval[:text_len]
@@ -1036,39 +1050,31 @@
     )
     all_grad_modul = lax.all_gather(lax.psum(grad_modul, "band"), "clip", axis=0, tiled=True)
     grad_w_ada = matmul_tn(time_rows.astype(jnp.float32), all_grad_modul, lax.Precision.HIGHEST)
-    factors = mlp_factors_b + (
-        (crossed, grad_cross),
-        (cross_in, grad_query),
-        factors_ob,
-        factors_qkvb,
-    )
+    down_b_sum, up_b_sum = (sum_rows(*pair) for pair in mlp_factors_b)
+    factors = ((crossed, grad_cross), (cross_in, grad_query), factors_ob, factors_qkvb)
     factors += mlp_factors_a + (factors_oa, factors_qkva)
+    square_part = (jnp.sum(down_b_sum**2) + jnp.sum(up_b_sum**2)) / band_count
     if wide_rows == 128 and deep_rows == 512:
         phases = (
-            {"kind": 0, "first": 0, "lefts": (0, 1), "cols": (D, 10 * D + FF)},
-            {"kind": 1, "first": 0, "lefts": (2, 3, 4, 5), "cols": (9 * D, 8 * D, 7 * D, 3 * D)},
-            {"kind": 0, "first": 0, "lefts": (6, 7), "cols": (0, 10 * D)},
-            {"kind": 1, "first": 2, "lefts": (8, 9), "cols": (6 * D, 0)},
+            {"kind": 1, "first": 0, "lefts": (0, 1, 2, 3), "cols": (9 * D, 8 * D, 7 * D, 3 * D)},
+            {"kind": 0, "first": 0, "lefts": (4, 5), "cols": (0, 10 * D)},
+            {"kind": 1, "first": 2, "lefts": (6, 7), "cols": (6 * D, 0)},
         )
-        wide_rest, deep_rest, squares = reduce_gradients(
-            phases, [f[0] for f in factors], [f[1] for f in factors], 10 * D + 2 * FF, 2 * D
+        wide_rest, down_a_sum, squares = reduce_gradients(
+            phases,
+            [f[0] for f in factors],
+            [f[1] for f in factors],
+            (wide_rows, 10 * D + FF),
+            (deep_rows, D),
         )
-        square_part = jnp.sum(squares) / (band_count // 2)
+        square_part += jnp.sum(squares) / (band_count // 2)
     else:
-        summed = []
-        for left, right in factors:
-            member = matmul_tn(left, right)
-            rows, cols = member.shape
-            member = member.reshape(rows, band_count, cols // band_count).transpose(1, 0, 2)
-            member = member.reshape(band_count, clip_count, rows // clip_count, cols // band_count)
-            member = member.transpose(1, 0, 2, 3).reshape(-1, cols // band_count)
-            member = lax.psum_scatter(member, ("clip", "band"), scatter_dimension=0, tiled=True)
-            summed.append(lax.all_gather(member, "band", axis=1, tiled=True))
-        wide_rest = jnp.concatenate([summed[i] for i in (9, 5, 8, 4, 3, 2, 7, 1)], 1)
-        deep_rest = jnp.concatenate([summed[6], summed[0]], 1)
-        square_part = (jnp.sum(wide_rest**2) + jnp.sum(deep_rest**2)) / band_count
-    wide_sum = jnp.concatenate([grad_w_ada, wide_rest], 1)
-    deep_sum = jnp.concatenate([deep_rest[:, :D], grad_w_ckv, deep_rest[:, D:]], 1)
+        summed = [sum_rows(*pair) for pair in factors]
+        wide_rest = jnp.concatenate([summed[i] for i in (7, 3, 6, 2, 1, 0, 5)], 1)
+        down_a_sum = summed[4]
+        square_part += (jnp.sum(wide_rest**2) + jnp.sum(down_a_sum**2)) / band_count
+    wide_sum = jnp.concatenate([grad_w_ada, wide_rest, up_b_sum], 1)
+    deep_sum = jnp.concatenate([down_a_sum, grad_w_ckv, down_b_sum], 1)
     square_part += (jnp.sum(grad_w_ada**2) + jnp.sum(grad_w_ckv**2)) / band_count
     loss_sum, square_sum, small_sum = lax.psum(
         (loss_part, square_part, grad_small), ("clip", "band")

time: 1440 us -> 1510 us (1.049)
  Pallas kernels: 642 us -> 497 us
  waiting for transfers between devices: 61.3 us -> 180 us
  matrix products: 281 us -> 345 us
  local copies, waits for them, and re-layouts: 172 us -> 198 us
    reduce_scatter x0 -> x2, waiting for transfers between devices: none -> 81.5 us  [sum_rows(): lax.psum_scatter(matmul_tn(left, right), ('clip', 'band'), scatter_dimens...]
    pallas_call x1, Pallas kernels: 296 us -> 216 us  [gather_weights(): pl.pallas_call(partial(gather_kernel, count, [shard.shape for shard in sh...]
    pallas_call x1, Pallas kernels: 329 us -> 263 us  [reduce_gradients(): pl.pallas_call(partial(reduce_kernel, count, tokens, phases), out_shape=(...]
    ppermute x4, waiting for transfers between devices: 26.4 us -> 67.3 us  [shifted(): lax.ppermute(value, axis, [(i, (i + by) % length) for i in range(length)])]
    dot_general x4 -> x6, matrix products: 10.8 us -> 37.4 us  [matmul_tn(): lax.dot_general(left_op, right_op, (((0,), (0,)), ((), ())), precision=pr...]
    dot_general x14, matrix products: 106 us -> 126 us  [matmul(): return jnp.dot(left_op, right_op, preferred_element_type=jnp.float32)]
    unnamed x356 -> x376, local copies, waits for them, and re-layouts: 38.5 us -> 55.4 us
  transfers between devices with their start and end apart: 11 -> 17, of which waited for: 6 -> 5; matrix products, arithmetic and copies ran while one was open for 7% -> 33% of each run, Pallas kernels for 23% -> 18%
where the time goes in v3:
time: 1510 us; the launch traced here: 1500 us
  Pallas kernels  497 us (33%)
  matrix products  345 us (23%)
  local copies, waits for them, and re-layouts  198 us (13%)
  waiting for transfers between devices  180 us (12%)
  other arithmetic  158 us (10%)
  blocking collectives  88.2 us (6%)
  between operations  26.5 us (2%)
    pallas_call x1, Pallas kernels, reduce_gradients(): pl.pallas_call(partial(reduce_kernel, count, tokens, phases), out_shape=(...  263 us
    pallas_call x1, Pallas kernels, gather_weights(): pl.pallas_call(partial(gather_kernel, count, [shard.shape for shard in sh...  216 us
    dot_general x14, matrix products, matmul(): return jnp.dot(left_op, right_op, preferred_element_type=jnp.float32)  126 us
    dot_general x11, matrix products, matmul_nt(): lax.dot_general(left_op, right_op, (((1,), (1,)), ((), ())), preferred_el...  85.6 us
    reduce_scatter x2, waiting for transfers between devices, sum_rows(): lax.psum_scatter(matmul_tn(left, right), ('clip', 'band'), scatter_dimens...  81.5 us
    ppermute x4, waiting for transfers between devices, shifted(): lax.ppermute(value, axis, [(i, (i + by) % length) for i in range(length)])  67.3 us
    unnamed x376, local copies, waits for them, and re-layouts  55.4 us
    sub x3, other arithmetic, adam_update(): weight - learn_rate * (first_hat / (jnp.sqrt(second_hat) + ADAM_EPS) + DE...  52.8 us
  transfers between devices with their start and end apart: 17, of which 5 were waited for; matrix products, arithmetic and copies ran while one was open for 33% of the time, Pallas kernels for 18%

profile of v3, /device:TPU:0, one launch (start us, length us, event | category | flops | bytes accessed | tf_op | source)
XLA Modules:
  0.0 1496.4 jit_solution(6842499676698436608)
XLA Ops:
  8.0 9.6 convert.26
  29.2 17.7 %shard_map.230 = (s32[8,8,128]{2,1,0:T(8,128)}, bf16[8,80,512]{2,1,0:T(8,128)(2,1)}) custom-call(s32[8,128]{1,0:T(8,128)} %pad.12.facts_ref, bf16[8,80,512]{2,1,0:T(8,128)(2,1)} %pad.13.text_ref), custom_call_target="tpu_custom_call" | custom-call | tf_op jit(solution)/shard_map/pallas_call | solution.py:250
  61.7 216.4 %shard_map.231 = (bf16[1024,3072]{1,0:T(8,128)(2,1)}, bf16[1024,3072]{1,0:T(8,128)(2,1)}, bf16[1024,1024]{1,0:T(8,128)(2,1)}, bf16[1024,1024]{1,0:T(8,128)(2,1)}...) custom-call(bf16[128,3072]{1,0:T(8,128)(2,1)} %get-tuple-element.106, ...), custom_call_target="tpu_custom_call" | custom-call | flops 199999995904 | bytes 600000000 | tf_op jit(solution)/shard_map/pallas_call | solution.py:384
  280.4 7.7 convolution_convert_fusion.1
  333.0 42.1 %multiply_convert_fusion.3 = (bf16[640,4096]{1,0:T(8,128)(2,1)S(1)}, f32[640,4096]{1,0:T(8,128)}, f32[640,4096]{1,0:T(8,128)}) fusion(bf16[640,1024]{1,0:T(8,128)(2,1)S(1)} %add_convert_fusion.6.refs_5_, bf16[1024,4096]{1,0:T(8,128)(2,1)S(1)} %bitcast.349), kind=kOutput, calls=%fused_computation.32 | convolution fusion | flops 5539102720 | bytes 35913728 | tf_op jit(solution)/shard_map/dot_general | solution.py:49
  375.1 7.1 fusion.95
  392.8 6.4 all_gather.24
  400.4 7.9 convolution_convert_fusion
  418.4 9.9 multiply_reduce_fusion.1
  428.4 8.7 exponential_reduce_fusion
  437.8 10.7 fusion.25
  448.5 4.7 copy.140
  453.2 4.9 reshape_reshape.11
  465.4 5.5 collective-permute-done.2
  490.7 33.3 %multiply_convert_fusion.2 = (bf16[640,4096]{1,0:T(8,128)(2,1)}, f32[640,4096]{1,0:T(8,128)}, f32[640,4096]{1,0:T(8,128)}) fusion(bf16[1024,4096]{1,0:T(8,128)(2,1)} %all-gather.8.cloned.1.call-done, f32[640,1024]{1,0:T(8,128)} %copy-done.11, f32[1024]{0:T(1024)S(1)} %copy-done.84, f32[1024]{0:T(1024)S(1)} %copy-done.80, f32[640]{0:T(1024)S(1)} %fusion.64, ...), kind=kOutput, calls=%fused_computation.19 | convolution fusion | flops 5542379520 | bytes 37237760 | tf_op jit(solution)/shard_map/dot_general | solution.py:49
  524.0 11.3 fusion.92
  542.0 17.6 %add_convert_fusion.1 = bf16[640,4096]{1,0:T(8,128)(2,1)} fusion(f32[640,4096]{1,0:T(8,128)} %get-tuple-element.90, f32[640,4096]{1,0:T(8,128)} %get-tuple-element.162, bf16[4096,1024]{1,0:T(8,128)(2,1)} %all-gather.10.cloned.1.call-done, f32[640,1024]{1,0:T(8,128)} %get-tuple-element.86, f32[640]{0:T(1024)} %negate_multiply_fusion.7, ...), kind=kOutput, calls=%fused_computation.18 | convolution fusion | flops 5407375360 | bytes 37231104 | tf_op jit(solution)/shard_map/dot_general | solution.py:63
  559.7 11.6 multiply_reduce_fusion.12
  597.8 30.8 %reduce-scatter.8.cloned.1.call-done = f32[80,512]{1,0:T(8,128)} async-done(((f32[80,2048]{1,0:T(8,128)}), f32[80,512]{1,0:T(8,128)}) %reduce-scatter.8.cloned.1.call-update) | async-done | bytes 163856 | tf_op jit(solution)/shard_map/reduce_scatter | solution.py:954
  628.6 13.0 fusion.80
  643.4 13.3 fusion.77
  659.6 4.9 multiply_reduce_fusion.9
  672.6 12.2 collective-permute-done.3
  690.6 4.8 copy.148
  695.4 10.0 convolution_bitcast_fusion
  705.5 4.7 copy.155
  714.7 16.1 %multiply_reduce_fusion = (f32[2,16,320]{2,1,0:T(8,128)S(1)}, f32[2,16,320,320]{2,3,1,0:T(8,128)}) fusion(f32[2,16,320,320]{2,3,1,0:T(8,128)} %get-tuple-element.156, f32[2,16,320]{2,1,0:T(8,128)S(1)} %copy-done.74, bf16[2,320,16,64]{1,3,2,0:T(8,128)(2,1)} %copy.148, bf16[2,320,16,64]{1,3,2,0:T(8,128)(2,1)} %bitcast.271), kind=kOutput, calls=%fused_computation.6 | convolution fusion | flops 432527360 | bytes 28917760 | tf_op jit(solution)/shard_map/wqhd,wkhd->whqk/dot_general | solution.py:156
  730.8 11.8 multiply_convert_fusion
  748.6 4.7 copy.150
  757.8 7.5 multiply_bitcast_fusion
  765.3 4.7 copy.152
  774.6 8.0 fusion.16
  782.9 49.7 %collective-permute-done.4 = f32[5,4,16,1024]{3,2,1,0:T(8,128)S(1)} collective-permute-done((f32[5,4,16,1024]{3,2,1,0:T(8,128)S(1)}, f32[5,4,16,1024]{3,2,1,0:T(8,128)S(1)}, u32[]{:S(2)}, u32[]{:S(2)}) %collective-permute-start.4) | collective-permute-done | bytes 1310752 | tf_op jit(solution)/shard_map/ppermute | solution.py:45
  840.5 17.6 %add_convert_fusion.refs_13_ = bf16[640,4096]{1,0:T(8,128)(2,1)} fusion(f32[640,4096]{1,0:T(8,128)} %get-tuple-element.96, f32[640,4096]{1,0:T(8,128)} %get-tuple-element.153, bf16[640,1024]{1,0:T(8,128)(2,1)S(1)} %multiply_convert_fusion.7.refs_12_, bf16[4096,1024]{1,0:T(8,128)(2,1)} %get-tuple-element.32), kind=kOutput, calls=%fused_computation.17 | convolution fusion | flops 5405409280 | bytes 35913728 | tf_op jit(solution)/shard_map/dot_general | solution.py:63
  858.2 11.0 multiply_reduce_fusion.15
  882.4 6.4 fusion.33
  895.3 7.1 multiply_reduce_fusion.2
  902.4 6.9 multiply_convert_fusion.1
  922.3 5.5 fusion.27
  945.8 8.2 multiply_reduce_fusion.10
  979.3 81.5 %reduce-scatter.4.cloned.1.call-done = f32[128,1024]{1,0:T(8,128)} async-done(((f32[4096,1024]{1,0:T(8,128)}), f32[128,1024]{1,0:T(8,128)}) %reduce-scatter.4.cloned.1.call-update) | async-done | bytes 524304 | tf_op jit(solution)/shard_map/reduce_scatter | solution.py:374
  1061.0 262.7 %shard_map.232 = (f32[128,14336]{1,0:T(8,128)}, f32[512,1024]{1,0:T(8,128)}, f32[8,512]{1,0:T(8,128)}, bf16[640,1024]{1,0:T(8,128)(2,1)}, bf16[640,1024]{1,0:T(8...) custom-call(bf16[640,1024]{1,0:T(8,128)(2,1)} %copy.167.refs_0_, ...), custom_call_target="tpu_custom_call" | custom-call | flops 299999985664 | bytes 800000000 | tf_op jit(solution)/shard_map/pallas_call | solution.py:783
  1325.9 10.8 psum.29
  1336.8 31.4 %all-gather = f32[8,1,12288]{2,1,0:T(1,128)S(1)} all-gather(f32[1,1,12288]{2,1,0:T(1,128)S(1)} %bitcast.317), channel_id=1, replica_groups=mesh['clip'=8,'band'=4] {'clip'}, dimensions={0}, use_global_device_ids=true | all-gather | bytes 442368 | tf_op jit(solution)/shard_map/all_gather | solution.py:1051
  1368.2 5.9 multiply_reduce_fusion.4
  1387.6 39.6 %all-reduce.3 = (f32[]{:T(128)}, f32[]{:T(128)}) all-reduce(f32[]{:T(128)} %get-tuple-element.164, f32[]{:T(128)S(6)} %add.368), channel_id=1, replica_groups=mesh['clip'=8,'band'=4] {'clip','band'}, use_global_device_ids=true, to_apply=%region_21.22 | all-reduce | flops 2 | bytes 16 | tf_op jit(solution)/shard_map/psum | solution.py:1079
  1430.0 21.1 %multiply_subtract_fusion.1 = (f32[512,4096]{1,0:T(8,128)}, f32[512,4096]{1,0:T(8,128)}, f32[512,4096]{1,0:T(8,128)}) fusion(f32[512,4096]{1,0:T(8,128)} %param.24, f32[]{:T(128)S(6)} %div.223, f32[512,1024]{1,0:T(8,128)} %all-gather.12.cloned.1.call-done, f32[512,2048]{1,0:T(8,128)} %all-gather.18.cloned.1.call-done, f32[512,1024]{1,0:T(8,128)} %get-tuple-element.40, ...), kind=kLoop, calls=%fused_computation.53 | loop fusion | flops 37748736 | bytes 58720260 | tf_op jit(solution)/shard_map/sub | solution.py:195
  1455.8 31.0 %multiply_subtract_fusion = (f32[128,30720]{1,0:T(8,128)}, f32[128,30720]{1,0:T(8,128)}, f32[128,30720]{1,0:T(8,128)}) fusion(f32[128,30720]{1,0:T(8,128)S(1)} %bitcast.261, f32[]{:T(128)S(6)} %div.223, f32[128,4096]{1,0:T(8,128)} %all-gather.14.cloned.1.call-done, f32[128,14336]{1,0:T(8,128)} %get-tuple-element.39, f32[128,12288]{1,0:T(8,128)S(1)} %bitcast.264, ...), kind=kLoop, calls=%fused_computation.3 | loop fusion | flops 70778880 | bytes 110100480 | tf_op jit(solution)/shard_map/sub | solution.py:195
  (589 shorter events, 293.6 us)
Async XLA Ops:
  7.2 483.5 %all-gather.8.cloned.1.call-start = ((), (), s32[]{:S(2)}) async-start(), calls=%async_computation.3 | async-start | bytes 8650752 | tf_op jit(solution)/shard_map/all_gather | solution.py:370
  61.6 218.1 %copy-start.9 = (f32[640,1024]{1,0:T(8,128)S(1)}, f32[640,1024]{1,0:T(8,128)}, u32[]{:S(2)}) copy-start(f32[640,1024]{1,0:T(8,128)} %copy-done.8) | copy-start | bytes 7864324
  61.6 218.2 %copy-start.98 = (f32[1,1024]{1,0:T(1,128)S(1)}, f32[1,1024]{1,0:T(1,128)}, u32[]{:S(2)}) copy-start(f32[1,1024]{1,0:T(1,128)} %copy-done.97) | copy-start | bytes 12292
  61.6 218.2 %copy-start.115 = (f32[640]{0:T(1024)S(1)}, f32[640]{0:T(1024)}, u32[]{:S(2)}) copy-start(f32[640]{0:T(1024)} %copy-done.114) | copy-start | bytes 7684
  61.7 218.2 %copy-start.135 = (f32[640]{0:T(1024)S(1)}, f32[640]{0:T(1024)}, u32[]{:S(2)}) copy-start(f32[640]{0:T(1024)} %fusion.60) | copy-start | bytes 7684
  279.8 47.9 %copy-start.149 = (f32[1024]{0:T(1024)}, f32[1024]{0:T(1024)S(1)}, u32[]{:S(2)}) copy-start(f32[1024]{0:T(1024)S(1)} %get-tuple-element.145) | copy-start | bytes 12292
  279.8 51.8 %copy-start.129 = (f32[1024]{0:T(1024)}, f32[1024]{0:T(1024)S(1)}, u32[]{:S(2)}) copy-start(f32[1024]{0:T(1024)S(1)} %get-tuple-element.141) | copy-start | bytes 12292
  279.8 95.3 %copy-start.151 = (f32[1024]{0:T(1024)}, f32[1024]{0:T(1024)S(1)}, u32[]{:S(2)}) copy-start(f32[1024]{0:T(1024)S(1)} %get-tuple-element.142) | copy-start | bytes 12292
  279.8 102.9 %copy-start.110 = (f32[1024]{0:T(1024)}, f32[1024]{0:T(1024)S(1)}, u32[]{:S(2)}) copy-start(f32[1024]{0:T(1024)S(1)} %get-tuple-element.138) | copy-start | bytes 12292
  290.9 9.8 collective-permute-start
  295.5 228.6 %all-gather.10.cloned.1.call-start = ((), (), s32[]{:S(2)}) async-start(), calls=%async_computation.4 | async-start | bytes 8650752 | tf_op jit(solution)/shard_map/all_gather | solution.py:370
  331.1 44.0 %copy-start.14 = (f32[640,1024]{1,0:T(8,128)}, f32[640,1024]{1,0:T(8,128)S(1)}, u32[]{:S(2)}) copy-start(f32[640,1024]{1,0:T(8,128)S(1)} %get-tuple-element.98) | copy-start | bytes 7864324
  331.1 44.0 %slice-start.6 = ((s8[8388608]{0:T(1024)(128)(4,1)}), s8[4194304]{0:T(1024)(128)(4,1)S(1)}, s32[]{:S(2)}) async-start(s8[8388608]{0:T(1024)(128)(4,1)} %bitcast.346), calls=%async_computation.19 | async-start | bytes 8388608
  331.5 43.5 %copy-start.139 = (f32[640]{0:T(1024)}, f32[640]{0:T(1024)S(1)}, u32[]{:S(2)}) copy-start(f32[640]{0:T(1024)S(1)} %multiply_reduce_fusion.27) | copy-start | bytes 7684
  331.5 43.5 %copy-start.131 = (f32[640]{0:T(1024)}, f32[640]{0:T(1024)S(1)}, u32[]{:S(2)}) copy-start(f32[640]{0:T(1024)S(1)} %fusion.61) | copy-start | bytes 7684
  382.3 89.8 %copy-start.1 = (f32[640,1024]{1,0:T(8,128)}, f32[640,1024]{1,0:T(8,128)S(1)}, u32[]{:S(2)}) copy-start(f32[640,1024]{1,0:T(8,128)S(1)} %get-tuple-element.94) | copy-start | bytes 7864324
  384.5 14.7 collective-permute-start.1
  387.5 241.1 %reduce-scatter.8.cloned.1.call-start = ((), (), s32[]{:S(2)}) async-start(), calls=%async_computation.9 | async-start | bytes 819200 | tf_op jit(solution)/shard_map/reduce_scatter | solution.py:954
  460.5 10.3 collective-permute-start.2
  597.7 362.9 %all-gather.16.cloned.1.call-start = ((), (), s32[]{:S(2)}) async-start(), calls=%async_computation.10 | async-start | bytes 1474560 | tf_op jit(solution)/shard_map/all_gather | solution.py:955
  628.6 335.9 %reduce-scatter.6.cloned.1.call-start = ((), (), s32[]{:S(2)}) async-start(), calls=%async_computation.7 | async-start | bytes 17301504 | tf_op jit(solution)/shard_map/reduce_scatter | solution.py:374
  641.7 419.1 %reduce-scatter.4.cloned.1.call-start = ((), (), s32[]{:S(2)}) async-start(), calls=%async_computation.5 | async-start | bytes 17301504 | tf_op jit(solution)/shard_map/reduce_scatter | solution.py:374
  656.7 717.3 %all-reduce.6.cloned.1.call-start = ((), (), s32[]{:S(2)}) async-start(), calls=%async_computation.12 | async-start | bytes 196608 | tf_op jit(solution)/shard_map/psum | solution.py:1079
  672.5 12.3 collective-permute-start.3
  782.8 49.7 %collective-permute-start.4 = (f32[5,4,16,1024]{3,2,1,0:T(8,128)S(1)}, f32[5,4,16,1024]{3,2,1,0:T(8,128)S(1)}, u32[]{:S(2)}, u32[]{:S(2)}) collective-permute-start(f32[5,4,16,1024]{3,2,1,0:T(8,128)S(1)} %get-tuple-element.120), channel_id=1, source_target_pairs={{0,1},{1,2},{2,3},{3,0},{4,5},{5,6},{6,7},{7,4},{8,9},{9,10},{10,1... | collective-permute-start | bytes 3932168 | tf_op jit(solution)/shard_map/ppermute | solution.py:45
  895.3 43.9 %collective-permute-start.6 = (f32[5,128,1024]{2,1,0:T(8,128)}, f32[5,128,1024]{2,1,0:T(8,128)}, u32[]{:S(2)}, u32[]{:S(2)}) collective-permute-start(f32[5,128,1024]{2,1,0:T(8,128)} %copy.185), channel_id=1, source_target_pairs={{0,1},{1,0},{2,3},{3,2},{4,5},{5,4},{6,7},{7,6},{8,9},{9,8},{10,11... | collective-permute-start | bytes 7864328 | tf_op jit(solution)/shard_map/ppermute | solution.py:40
  917.9 24.5 %collective-permute-start.5 = (f32[5,128,1024]{2,1,0:T(8,128)}, f32[5,128,1024]{2,1,0:T(8,128)}, u32[]{:S(2)}, u32[]{:S(2)}) collective-permute-start(f32[5,128,1024]{2,1,0:T(8,128)} %copy.183), channel_id=1, source_target_pairs={{0,1},{1,0},{2,3},{3,2},{4,5},{5,4},{6,7},{7,6},{8,9},{9,8},{10,11... | collective-permute-start | bytes 7864328 | tf_op jit(solution)/shard_map/ppermute | solution.py:40
  960.6 415.0 %all-gather.18.cloned.1.call-start = ((), (), s32[]{:S(2)}) async-start(), calls=%async_computation.11 | async-start | bytes 5242880 | tf_op jit(solution)/shard_map/all_gather | solution.py:961
  964.4 416.4 %all-gather.14.cloned.1.call-start = ((), (), s32[]{:S(2)}) async-start(), calls=%async_computation.8 | async-start | bytes 2621440 | tf_op jit(solution)/shard_map/all_gather | solution.py:377
  965.2 418.4 %all-gather.12.cloned.1.call-start = ((), (), s32[]{:S(2)}) async-start(), calls=%async_computation.6 | async-start | bytes 2621440 | tf_op jit(solution)/shard_map/all_gather | solution.py:377
  1060.8 264.2 %copy-start.147 = (f32[1024]{0:T(1024)S(1)}, f32[1024]{0:T(1024)}, u32[]{:S(2)}) copy-start(f32[1024]{0:T(1024)} %get-tuple-element.116) | copy-start | bytes 12292
  1060.8 264.2 %copy-start.148 = (f32[1024]{0:T(1024)S(1)}, f32[1024]{0:T(1024)}, u32[]{:S(2)}) copy-start(f32[1024]{0:T(1024)} %get-tuple-element.69) | copy-start | bytes 12292
  1060.8 264.2 %copy-start.154 = (f32[1024]{0:T(1024)S(1)}, f32[1024]{0:T(1024)}, u32[]{:S(2)}) copy-start(f32[1024]{0:T(1024)} %get-tuple-element.71) | copy-start | bytes 12292
  1060.8 264.2 %copy-start.155 = (f32[1024]{0:T(1024)S(1)}, f32[1024]{0:T(1024)}, u32[]{:S(2)}) copy-start(f32[1024]{0:T(1024)} %get-tuple-element.54) | copy-start | bytes 12292
  1060.9 264.2 %copy-start.156 = (f32[1024]{0:T(1024)S(1)}, f32[1024]{0:T(1024)}, u32[]{:S(2)}) copy-start(f32[1024]{0:T(1024)} %reduce_sum.642) | copy-start | bytes 12292
  1060.9 264.2 %copy-start.157 = (f32[1024]{0:T(1024)S(1)}, f32[1024]{0:T(1024)}, u32[]{:S(2)}) copy-start(f32[1024]{0:T(1024)} %get-tuple-element.49) | copy-start | bytes 12292
  1060.9 264.2 %copy-start.158 = (f32[1024]{0:T(1024)S(1)}, f32[1024]{0:T(1024)}, u32[]{:S(2)}) copy-start(f32[1024]{0:T(1024)} %get-tuple-element.47) | copy-start | bytes 12292
  1060.9 264.2 %copy-start.159 = (f32[1024]{0:T(1024)S(1)}, f32[1024]{0:T(1024)}, u32[]{:S(2)}) copy-start(f32[1024]{0:T(1024)} %get-tuple-element.56) | copy-start | bytes 12292
  1060.9 264.2 %copy-start.161 = (f32[1024]{0:T(1024)S(1)}, f32[1024]{0:T(1024)}, u32[]{:S(2)}) copy-start(f32[1024]{0:T(1024)} %get-tuple-element.51) | copy-start | bytes 12292
  1060.9 264.2 %copy-start.162 = (f32[1024]{0:T(1024)S(1)}, f32[1024]{0:T(1024)}, u32[]{:S(2)}) copy-start(f32[1024]{0:T(1024)} %get-tuple-element.57) | copy-start | bytes 12292
  1060.9 264.2 %copy-start.164 = (f32[1024]{0:T(1024)S(1)}, f32[1024]{0:T(1024)}, u32[]{:S(2)}) copy-start(f32[1024]{0:T(1024)} %get-tuple-element.42) | copy-start | bytes 12292
  1060.9 264.2 %copy-start.165 = (f32[1024]{0:T(1024)S(1)}, f32[1024]{0:T(1024)}, u32[]{:S(2)}) copy-start(f32[1024]{0:T(1024)} %get-tuple-element.55) | copy-start | bytes 12292
  1060.9 307.2 %copy-start.92 = (f32[8,512]{1,0:T(8,128)S(1)}, f32[8,512]{1,0:T(8,128)}, u32[]{:S(2)}) copy-start(f32[8,512]{1,0:T(8,128)} %copy-done.91) | copy-start | bytes 49156
  1060.9 307.2 %copy-start.94 = (f32[8,512]{1,0:T(8,128)S(1)}, f32[8,512]{1,0:T(8,128)}, u32[]{:S(2)}) copy-start(f32[8,512]{1,0:T(8,128)} %copy-done.93) | copy-start | bytes 49156
  1379.4 49.8 %copy-start.82 = (f32[19,1024]{1,0:T(8,128)S(1)}, f32[19,1024]{1,0:T(8,128)}, u32[]{:S(2)}) copy-start(f32[19,1024]{1,0:T(8,128)} %param.27) | copy-start | bytes 233476
  1379.5 49.8 %copy-start.83 = (f32[19,1024]{1,0:T(8,128)S(1)}, f32[19,1024]{1,0:T(8,128)}, u32[]{:S(2)}) copy-start(f32[19,1024]{1,0:T(8,128)} %all-reduce.6.cloned.1.call-done) | copy-start | bytes 233476
  1379.5 49.8 %copy-start.100 = (f32[19,1024]{1,0:T(8,128)S(1)}, f32[19,1024]{1,0:T(8,128)}, u32[]{:S(2)}) copy-start(f32[19,1024]{1,0:T(8,128)} %param.28) | copy-start | bytes 233476
  1379.5 49.8 %copy-start.101 = (f32[19,1024]{1,0:T(8,128)S(1)}, f32[19,1024]{1,0:T(8,128)}, u32[]{:S(2)}) copy-start(f32[19,1024]{1,0:T(8,128)} %param.29) | copy-start | bytes 233476
  (153 other events, 902.2 us)
Sparse Core Ops, SparseCore 0:
  295.6 85.4 all-gather.7
  387.6 84.1 all-gather.9
  597.8 30.6 reduce-scatter.7
  630.6 42.0 all-gather.15
  674.8 197.2 reduce-scatter.5
  874.3 186.4 reduce-scatter.3
  1066.9 124.6 all-reduce.5
  1193.2 41.4 all-gather.17
  1236.2 35.5 all-gather.13
  1273.2 33.9 all-gather.11

commit v4 on v2

--- a/solution.py
+++ b/solution.py
@@ -26,8 +26,6 @@
 BETA_TWO = 0.95
 ADAM_EPS = 1e-08
 DECAY = 0.1
-SELF_FORMS = ("wqhd,wkhd->whqk", "whqk,wkhd->wqhd", "whqk,wqhd->wkhd", "whqk,wkhd->wqhd")
-CROSS_FORMS = ("qhd,khd->hqk", "hqk,khd->qhd", "hqk,qhd->khd", "hqk,khd->qhd")
 
 
 def from_partner(block, axis, distance):
@@ -86,85 +84,168 @@
     return jnp.concatenate([jnp.cos(angles), jnp.sin(angles)], -1)
 
 
-def to_windows(token_grid, shape_win):
-    num_frames, num_rows, num_cols, feat_dim = token_grid.shape
-    win_frames, win_rows, win_cols = shape_win
-    shaped = token_grid.reshape(
-        num_frames // win_frames,
-        win_frames,
-        num_rows // win_rows,
-        win_rows,
-        num_cols // win_cols,
-        win_cols,
-        feat_dim,
-    )
-    return shaped.transpose(0, 2, 4, 1, 3, 5, 6).reshape(
-        -1, win_frames * win_rows * win_cols, feat_dim
-    )
-
-
-def from_windows(blocks, grid_shape, shape_win):
-    num_frames, num_rows, num_cols = grid_shape
-    win_frames, win_rows, win_cols = shape_win
-    feat_dim = blocks.shape[-1]
-    shaped = blocks.reshape(
-        num_frames // win_frames,
-        num_rows // win_rows,
-        num_cols // win_cols,
-        win_frames,
-        win_rows,
-        win_cols,
-        feat_dim,
-    )
-    return shaped.transpose(0, 3, 1, 4, 2, 5, 6).reshape(num_frames, num_rows, num_cols, feat_dim)
-
-
-def split_heads(field_in):
-    return field_in.reshape(field_in.shape[:-1] + (HEADS, HEAD_DIM))
-
-
-def merge_heads(field_in):
-    return field_in.reshape(field_in.shape[:-2] + (D,))
-
-
-def attend_forward(queries, key_heads, value_heads, einsum_forms):
-    scores = jnp.einsum(
-        einsum_forms[0], queries, key_heads, preferred_element_type=jnp.float32
-    ) * HEAD_DIM ** (-0.5)
-    log_total = jax.nn.logsumexp(scores, axis=-1, keepdims=True)
-    probabilities = jnp.exp(scores - log_total)
-    attended = jnp.einsum(
-        einsum_forms[1],
-        probabilities.astype(jnp.bfloat16),
-        value_heads,
-        preferred_element_type=jnp.float32,
-    )
-    return (attended, log_total)
-
-
-def attend_backward(queries, key_heads, value_heads, log_total, grad_out, einsum_forms):
-    scores = jnp.einsum(
-        einsum_forms[0], queries, key_heads, preferred_element_type=jnp.float32
-    ) * HEAD_DIM ** (-0.5)
-    probabilities = jnp.exp(scores - log_total)
-    grad_values = jnp.einsum(
-        einsum_forms[2],
-        probabilities.astype(jnp.bfloat16),
-        grad_out,
-        preferred_element_type=jnp.float32,
-    )
-    grad_probs = jnp.einsum(
-        einsum_forms[0], grad_out, value_heads, preferred_element_type=jnp.float32
-    )
-    inner_sum = jnp.sum(probabilities * grad_probs, -1, keepdims=True)
-    grad_scores = (probabilities * (grad_probs - inner_sum)).astype(jnp.bfloat16)
-    grad_queries = jnp.einsum(
-        einsum_forms[3], grad_scores, key_heads, preferred_element_type=jnp.float32
-    ) * HEAD_DIM ** (-0.5)
-    grad_keys = jnp.einsum(
-        einsum_forms[2], grad_scores, queries, preferred_element_type=jnp.float32
-    ) * HEAD_DIM ** (-0.5)
-    return (grad_queries, grad_keys, grad_values)
+def token_order(grid):
+    frames, rows, cols, width = grid.shape
+    halves = grid.reshape(frames, rows, cols // WIN, WIN, width).transpose(2, 0, 1, 3, 4)
+    return halves.reshape(frames * rows * cols, width)
+
+
+def with_rows(tokens, first_rows, run):
+    width = tokens.shape[1]
+    runs = tokens.reshape(-1, run, width)
+    return jnp.concatenate([first_rows, runs[:, first_rows.shape[1] :]], 1).reshape(-1, width)
+
+
+def first_rows(tokens, run, part):
+    return tokens.reshape(-1, run, tokens.shape[1])[:, :part]
+
+
+def attend_pieces(tokens, frames, keys):
+    if keys == "frame":
+        run = tokens // (2 * frames)
+        return [((f * run, run), (tokens // 2 + f * run, run)) for f in range(frames)]
+    if keys == "half":
+        return [((half * (tokens // 2), tokens // 2),) for half in range(2)]
+    return [((0, tokens),)]
+
+
+def take(ref, runs):
+    pieces = [ref[low : low + many, :] for low, many in runs]
+    return pieces[0] if len(pieces) == 1 else jnp.concatenate(pieces, 0)
+
+
+def put(ref, cols, runs, value):
+    done = 0
+    for low, many in runs:
+        ref[low : low + many, cols] = value[done : done + many].astype(ref.dtype)
+        done += many
+
+
+def softmax_rows(queries, keys, text_len):
+    scores = matmul_nt(queries, keys)
+    if text_len:
+        place = lax.broadcasted_iota(jnp.int32, scores.shape, 1)
+        scores = jnp.where(place < text_len, scores, -1e30)
+    weight = jnp.exp(scores - jnp.max(scores, -1, keepdims=True))
+    return weight / jnp.sum(weight, -1, keepdims=True)
+
+
+def lanes_of(head, shape):
+    lane = lax.broadcasted_iota(jnp.int32, shape, 1)
+    return lane < HEAD_DIM if head == 0 else lane >= HEAD_DIM
+
+
+def only(head, value):
+    return jnp.where(lanes_of(head, value.shape), value, jnp.zeros_like(value))
+
+
+def key_sets(key_refs, runs, text_len):
+    if text_len:
+        return key_refs[0][...]
+    pieces = [take(ref, runs) for ref in key_refs]
+    return pieces[0] if len(pieces) == 1 else jnp.concatenate(pieces, 0)
+
+
+def attend_kernel(windows, text_len, sets, *refs):
+    q_ref, k_refs, v_refs, out_ref = refs[0], refs[1 : 1 + sets], refs[1 + sets : 1 + 2 * sets], refs[-1]
+    for runs in windows:
+        queries = take(q_ref, runs) * HEAD_DIM ** (-0.5)
+        keys, values = key_sets(k_refs, runs, text_len), key_sets(v_refs, runs, text_len)
+        outs = []
+        for head in range(2):
+            probs = softmax_rows(only(head, queries), keys, text_len)
+            outs.append(matmul(probs.astype(jnp.bfloat16), values))
+        put(out_ref, slice(None), runs, jnp.where(lanes_of(0, outs[0].shape), *outs))
+
+
+def attend_back_kernel(windows, text_len, sets, *refs):
+    q_ref, k_refs, v_refs = refs[0], refs[1 : 1 + sets], refs[1 + sets : 1 + 2 * sets]
+    grad_ref = refs[1 + 2 * sets]
+    dq_ref = refs[2 + 2 * sets]
+    own_ref = refs[3 + 2 * sets] if len(refs) > 3 + 2 * sets else None
+    far_ref = refs[4 + 2 * sets] if sets == 2 else None
+    pair = pl.program_id(0)
+    cols = [pl.ds(pl.multiple_of(i * D + pair * 2 * HEAD_DIM, 128), 2 * HEAD_DIM) for i in range(3)]
+    merged = dq_ref.shape[1] == 3 * D
+    for runs in windows:
+        queries = take(q_ref, runs) * HEAD_DIM ** (-0.5)
+        keys, values = key_sets(k_refs, runs, text_len), key_sets(v_refs, runs, text_len)
+        grad_out = take(grad_ref, runs)
+        dq, dk, dv = [], [], []
+        for head in range(2):
+            probs = softmax_rows(only(head, queries), keys, text_len)
+            dprobs = matmul_nt(only(head, grad_out), values)
+            dv.append(matmul_tn(probs.astype(jnp.bfloat16), grad_out))
+            inner = jnp.sum(probs * dprobs, -1, keepdims=True)
+            dscores = (probs * (dprobs - inner)).astype(jnp.bfloat16)
+            dq.append(matmul(dscores, keys))
+            dk.append(matmul_tn(dscores, queries))
+        dq, dk, dv = (jnp.where(lanes_of(0, x[0].shape), *x) for x in (dq, dk, dv))
+        put(dq_ref, cols[0], runs, dq * HEAD_DIM ** (-0.5))
+        if merged:
+            put(dq_ref, cols[1], runs, dk)
+            put(dq_ref, cols[2], runs, dv)
+        elif text_len:
+            own_ref[:, cols[0]] = dk
+            own_ref[:, cols[1]] = dv
+        else:
+            half = dk.shape[0] // 2
+            put(own_ref, cols[0], runs, dk[:half])
+            put(own_ref, cols[1], runs, dv[:half])
+            put(far_ref, cols[0], runs, dk[half:])
+            put(far_ref, cols[1], runs, dv[half:])
+
+
+def head_cols(array, first):
+    return array, pl.BlockSpec((array.shape[0], 2 * HEAD_DIM), lambda h: (0, first + h))
+
+
+def attention_operands(queries, key_values):
+    ins = [head_cols(queries, 0)]
+    ins += [head_cols(array, first) for array, first, _ in key_values]
+    return ins + [head_cols(array, second) for array, _, second in key_values]
+
+
+def attention_cost(tokens, keys, products):
+    flops = 2 * products * tokens * keys * D * 2
+    return pl.CostEstimate(
+        flops=flops, bytes_accessed=tokens * D * 2 * 8, transcendentals=tokens * keys * HEADS
+    )
+
+
+def attend(queries, key_values, windows, text_len=0):
+    tokens = queries.shape[0]
+    ins = attention_operands(queries, key_values)
+    return pl.pallas_call(
+        partial(attend_kernel, windows, text_len, len(key_values)),
+        grid=(HEADS // 2,),
+        in_specs=[spec for _, spec in ins],
+        out_specs=pl.BlockSpec((tokens, 2 * HEAD_DIM), lambda h: (0, h)),
+        out_shape=jax.ShapeDtypeStruct((tokens, D), jnp.bfloat16),
+        compiler_params=pltpu.CompilerParams(vmem_limit_bytes=40 << 20),
+        cost_estimate=attention_cost(tokens, 320, 2),
+    )(*[array for array, _ in ins])
+
+
+def attend_back(queries, key_values, grad_out, windows, text_len=0):
+    tokens = queries.shape[0]
+    ins = attention_operands(queries, key_values) + [head_cols(grad_out, 0)]
+    sets = len(key_values)
+    whole = lambda rows, cols: pl.BlockSpec((rows, cols), lambda h: (0, 0))
+    if sets == 1 and not text_len:
+        outs = [((tokens, 3 * D), jnp.bfloat16)]
+    else:
+        rows = key_values[0][0].shape[0]
+        outs = [((tokens, D), jnp.bfloat16)] + [((rows, 2 * D), jnp.float32)] * sets
+    return pl.pallas_call(
+        partial(attend_back_kernel, windows, text_len, sets),
+        grid=(HEADS // 2,),
+        in_specs=[spec for _, spec in ins],
+        out_specs=[whole(*shape) for shape, _ in outs],
+        out_shape=[jax.ShapeDtypeStruct(*out) for out in outs],
+        compiler_params=pltpu.CompilerParams(vmem_limit_bytes=50 << 20),
+        cost_estimate=attention_cost(tokens, 320, 5),
+    )(*[array for array, _ in ins])
 
 
 def mlp_forward(stream, modul, up_weight, down_weight):
@@ -264,22 +345,25 @@
     )(facts, text)
 
 
-def gather_kernel(count, shapes, *refs):
+def gather_kernel(count, shapes, sides, *refs):
     num = len(shapes)
     shards, (vec_ref, text_ref) = refs[:num], refs[num : num + 2]
     full, (vec_out, text_out) = refs[num + 2 : 2 * num + 2], refs[2 * num + 2 : 2 * num + 4]
-    ring_send, ring_recv, pair_send, pair_recv, own_sem, part_send, part_recv, part_own = refs[
-        2 * num + 4 :
+    ring_send, ring_recv, pair_send, pair_recv, cross_send, cross_recv = refs[
+        2 * num + 4 : 2 * num + 10
     ]
+    own_sem, part_send, part_recv, part_own = refs[2 * num + 10 :]
     me = lax.axis_index("clip")
     band = lax.axis_index("band")
     core = band % 2
     place = ring_place(me, count)
     onward = 1 - 2 * core
     following = (ring_clip((place + onward + count) % count, count), band)
+    plane = band // 2
     partner = (me, band + 1 - 2 * core)
+    mirror = (me, band + 2 - 4 * plane)
     peers = [((me + step) % count, band) for step in range(1, count)]
-    greet(peers + [partner])
+    greet(peers + [partner, mirror])
 
     def block(ref, group, owner):
         rows, cols = shapes[group]
@@ -295,12 +379,47 @@
             there, there, ring_send.at[step, group], ring_recv.at[step, group], following, MESH
         )
 
-    def pair_copy(group, step):
+    def handed(group, step, send, recv, peer):
         owner = ring_clip((place - onward * (step + 1) + 2 * count) % count, count)
         there = block(full[group], group, owner)
         return pltpu.make_async_remote_copy(
-            there, there, pair_send.at[step, group], pair_recv.at[step, group], partner, MESH
+            there, there, send.at[step, group], recv.at[step, group], peer, MESH
         )
+
+    def pair_copy(group, step):
+        return handed(group, step, pair_send, pair_recv, partner)
+
+    def cross_copy(group, step):
+        return handed(group, step, cross_send, cross_recv, mirror)
+
+    def in_ring(group):
+        def decorate(body):
+            if sides[group]:
+                pl.when(plane == sides[group] - 1)(body)
+            else:
+                body()
+
+        return decorate
+
+    def off_ring(group, also=None):
+        def decorate(body):
+            if sides[group]:
+                off = plane != sides[group] - 1
+                pl.when(off if also is None else jnp.logical_and(off, also))(body)
+
+        return decorate
+
+    def ring_arrival(group, step, onto):
+        ring_copy(group, step).wait_recv()
+        if onto:
+            ring_copy(group, step + 1).start()
+        pair_copy(group, step).start()
+        if sides[group]:
+            cross_copy(group, step).start()
+
+    def cross_arrival(group, step):
+        cross_copy(group, step).wait_recv()
+        pair_copy(group, step).start()
 
     def own_copy(group):
         rows, cols = shapes[group]
@@ -330,27 +449,48 @@
     for group in range(num):
         rows, cols = shapes[group]
         own_copy(group).start()
-        pltpu.make_async_remote_copy(
-            shards[group].at[:, pl.ds(pl.multiple_of(core * (cols // 2), 128), cols // 2)],
-            block(full[group], group, me),
-            ring_send.at[0, group],
-            ring_recv.at[0, group],
-            following,
-            MESH,
-        ).start()
+
+        @in_ring(group)
+        def _(group=group, rows=rows, cols=cols):
+            pltpu.make_async_remote_copy(
+                shards[group].at[:, pl.ds(pl.multiple_of(core * (cols // 2), 128), cols // 2)],
+                block(full[group], group, me),
+                ring_send.at[0, group],
+                ring_recv.at[0, group],
+                following,
+                MESH,
+            ).start()
+
     for copy in parts_own + parts:
         copy.start()
 
     @pl.loop(1, count - 1)
     def _(step):
         for group in range(num):
-            ring_copy(group, step - 1).wait_recv()
-            ring_copy(group, step).start()
-            pair_copy(group, step - 1).start()
+
+            @in_ring(group)
+            def _(group=group):
+                ring_arrival(group, step - 1, True)
+
+        for group in range(num):
+
+            @off_ring(group, step >= 2)
+            def _(group=group):
+                cross_arrival(group, step - 2)
 
     for group in range(num):
-        ring_copy(group, count - 2).wait_recv()
-        pair_copy(group, count - 2).start()
+
+        @in_ring(group)
+        def _(group=group):
+            ring_arrival(group, count - 2, False)
+
+    for late in (count - 3, count - 2):
+        for group in range(num):
+
+            @off_ring(group)
+            def _(group=group, late=late):
+                cross_arrival(group, late)
+
     for copy in parts_own + parts:
         copy.wait()
     for group in range(num):
@@ -359,16 +499,36 @@
     @pl.loop(0, count - 1)
     def _(step):
         for group in range(num):
-            ring_copy(group, step).wait_send()
+
+            @in_ring(group)
+            def _(group=group):
+                ring_copy(group, step).wait_send()
+                if sides[group]:
+                    cross_copy(group, step).wait_send()
+
             pair_copy(group, step).wait()
 
 
-def gather_weights(shards, vectors, texts):
+def gather_quarters(shard):
+    band_count = lax.axis_size("band")
+    rows = shard.shape[0] // band_count
+    own = lax.dynamic_slice_in_dim(shard, lax.axis_index("band") * rows, rows, 0)
+    return lax.all_gather(own.astype(jnp.bfloat16), ("clip", "band"), axis=0, tiled=True)
+
+
+def sum_rows(left, right):
+    part = lax.psum_scatter(
+        matmul_tn(left, right), ("clip", "band"), scatter_dimension=0, tiled=True
+    )
+    return lax.all_gather(part, "band", axis=0, tiled=True)
+
+
+def gather_weights(shards, sides, vectors, texts):
     count = lax.axis_size("clip")
     num = len(shards)
     steps = pltpu.SemaphoreType.DMA((count - 1, num))
     out = pl.pallas_call(
-        partial(gather_kernel, count, [shard.shape for shard in shards]),
+        partial(gather_kernel, count, [shard.shape for shard in shards], sides),
         out_shape=tuple(
             jax.ShapeDtypeStruct((count * s.shape[0], s.shape[1]), s.dtype) for s in shards
         )
@@ -376,16 +536,14 @@
         in_specs=[ANY] * (num + 2),
         out_specs=(ANY,) * (num + 2),
         scratch_shapes=[
-            steps,
-            steps,
-            steps,
-            steps,
+            *[steps] * 6,
             pltpu.SemaphoreType.DMA((num,)),
             pltpu.SemaphoreType.DMA((2, count - 1)),
             pltpu.SemaphoreType.DMA((2, count - 1)),
             pltpu.SemaphoreType.DMA((2,)),
         ],
         compiler_params=pltpu.CompilerParams(collective_id=1, has_side_effects=True),
+        cost_estimate=pl.CostEstimate(flops=2 * 10**11, bytes_accessed=6 * 10**8, transcendentals=0),
     )(*shards, vectors, texts)
     return out[:num], out[num], out[num + 1]
 
@@ -782,6 +940,7 @@
         compiler_params=pltpu.CompilerParams(
             collective_id=2, has_side_effects=True, vmem_limit_bytes=58 << 20
         ),
+        cost_estimate=pl.CostEstimate(flops=3 * 10**11, bytes_accessed=8 * 10**8, transcendentals=0),
     )(*lefts, *rights)
     return out[:3]
 
@@ -831,11 +990,14 @@
         w_deep, (0, D + band_at * kv_cols), (deep_rows, kv_cols)
     ).astype(jnp.bfloat16)
     part_kv = matmul(all_text.reshape(clip_count * TEXT_PAD, deep_rows), kv_weight)
-    edges = (12 * D, 15 * D, 18 * D, 19 * D, 20 * D, 21 * D, 22 * D, 22 * D + FF, 22 * D + 2 * FF)
+    edges = (12 * D, 15 * D, 18 * D, 19 * D, 20 * D, 21 * D, 22 * D, 22 * D + FF)
     shards = [w_wide[:, low:high].astype(jnp.bfloat16) for low, high in zip(edges, edges[1:])]
-    shards += [w_deep[:, :D].astype(jnp.bfloat16), w_deep[:, 3 * D :].astype(jnp.bfloat16)]
+    shards += [w_deep[:, :D].astype(jnp.bfloat16)]
+    up_b_w = gather_quarters(w_wide[:, 22 * D + FF :])
+    down_b_w = gather_quarters(w_deep[:, 3 * D :])
     gathered, all_modul, all_kv = gather_weights(
         shards,
+        (0, 0, 1, 2, 1, 2, 1, 2),
         part_modul.reshape(clip_count, 12 * D // 128, 128),
         part_kv.reshape(clip_count, TEXT_PAD, kv_cols),
     )
@@ -847,24 +1009,25 @@
         query_w,
         cross_out_w,
         up_a_w,
-        up_b_w,
         down_a_w,
-        down_b_w,
     ) = gathered
     keyval = lax.all_gather(jnp.sum(all_kv, 0).astype(jnp.bfloat16), "band", axis=1, tiled=True)
-    keyval = keyval[:text_len]
     small_low = w_small.astype(jnp.bfloat16)
     small_val = small_low.astype(jnp.float32)
     num_frames, num_rows, num_cols = (latents.shape[1], latents.shape[2], latents.shape[3])
-    grid_shape = (num_frames, num_rows, num_cols)
     tok_count = num_frames * num_rows * num_cols
     all_mask = all_facts[:, 0, 1 : 1 + num_frames]
     global_count = jnp.sum(all_mask).astype(jnp.float32) * (num_rows * num_cols * CH * band_count)
     time_value = timesteps[0].astype(jnp.float32)
     noise_angle = 0.5 * math.pi * time_value / TMAX
     signal, spread = (jnp.cos(noise_angle), jnp.sin(noise_angle))
-    clean_tok = latents[0].reshape(tok_count, CH)
-    noise_tok = noise_field[0].reshape(tok_count, CH)
+    clean_tok = token_order(latents[0])
+    noise_tok = token_order(noise_field[0])
+    run = num_rows * WIN
+    part = SHIFT * WIN
+    frame_windows = attend_pieces(tok_count, num_frames, "frame")
+    half_windows = attend_pieces(tok_count, num_frames, "half")
+    text_windows = attend_pieces(tok_count, num_frames, "text")
     noisy_low = (signal * clean_tok + spread * noise_tok).astype(jnp.bfloat16)
     target = signal * noise_tok - spread * clean_tok
     modulation = jnp.sum(all_modul, 0).reshape(12, D)
@@ -872,54 +1035,35 @@
     stream_zero = matmul(noisy_low, small_low[:CH]) + small_val[2 * CH]
     normed_a, back_a = jax.vjp(norm_modulated, stream_zero, mod_a[0], mod_a[1])
     in_a = normed_a.astype(jnp.bfloat16)
-    spatial = (1, num_rows, SPACE)
-    qkv_a = (
-        matmul(in_a, qkv_a_w).astype(jnp.bfloat16).reshape(num_frames, num_rows, num_cols, 3 * D)
-    )
-    blocks_a = to_windows(qkv_a, spatial)
-    partner = from_partner(blocks_a[..., D:], "band", 0)
-    keys_all = jnp.concatenate([blocks_a[..., D:], partner], 1)
-    space_q = split_heads(blocks_a[..., :D])
-    space_k = split_heads(keys_all[..., :D])
-    space_v = split_heads(keys_all[..., D:])
-    space_out, space_total = attend_forward(space_q, space_k, space_v, SELF_FORMS)
-    att_a = from_windows(merge_heads(space_out.astype(jnp.bfloat16)), grid_shape, spatial).reshape(
-        tok_count, D
-    )
+    qkv_a = matmul(in_a, qkv_a_w).astype(jnp.bfloat16)
+    far_kv = from_partner(qkv_a[:, D:], "band", 0)
+    space_kv = [(qkv_a, HEADS // 2, HEADS), (far_kv, 0, HEADS // 2)]
+    att_a = attend(qkv_a, space_kv, frame_windows)
     proj_a = matmul(att_a, out_a_w)
     stream_one = stream_zero + mod_a[2] * proj_a
     stream_two, saved_a = mlp_forward(stream_one, mod_a, up_a_w, down_a_w)
     normed_b, back_b = jax.vjp(norm_modulated, stream_two, mod_b[0], mod_b[1])
-    token_grid = normed_b.astype(jnp.bfloat16).reshape(num_frames, num_rows, num_cols, D)
-    arrived = shifted(token_grid[:, :SHIFT], "band", -1)
-    rolled = jnp.concatenate([token_grid[:, SHIFT:], arrived], 1).reshape(tok_count, D)
-    temporal = (num_frames, WIN, WIN)
+    low_b = normed_b.astype(jnp.bfloat16)
+    rolled = with_rows(low_b, shifted(first_rows(low_b, run, part), "band", -1), run)
     qkv_b = matmul(rolled, qkv_b_w).astype(jnp.bfloat16)
-    blocks_b = to_windows(qkv_b.reshape(num_frames, num_rows, num_cols, 3 * D), temporal)
-    win_q = split_heads(blocks_b[..., :D])
-    win_k = split_heads(blocks_b[..., D : 2 * D])
-    win_v = split_heads(blocks_b[..., 2 * D :])
-    win_out, win_total = attend_forward(win_q, win_k, win_v, SELF_FORMS)
-    out_grid = from_windows(merge_heads(win_out.astype(jnp.bfloat16)), grid_shape, temporal)
-    returned = shifted(out_grid[:, num_rows - SHIFT :], "band", 1)
-    att_b = jnp.concatenate([returned, out_grid[:, : num_rows - SHIFT]], 1).reshape(tok_count, D)
+    win_kv = [(qkv_b, HEADS // 2, HEADS)]
+    win_out = attend(qkv_b, win_kv, half_windows)
+    att_b = with_rows(win_out, shifted(first_rows(win_out, run, part), "band", 1), run)
     proj_b = matmul(att_b, out_b_w)
     stream_three = stream_two + mod_b[2] * proj_b
     cross_val, cross_back = jax.vjp(norm_gained, stream_three, small_val[2 * CH + 1])
     cross_in = cross_val.astype(jnp.bfloat16)
     query_proj = matmul(cross_in, query_w).astype(jnp.bfloat16)
-    cross_q = split_heads(query_proj)
-    cross_k = split_heads(keyval[:, :D])
-    cross_v = split_heads(keyval[:, D:])
-    cross_out, cross_total = attend_forward(cross_q, cross_k, cross_v, CROSS_FORMS)
-    crossed = merge_heads(cross_out.astype(jnp.bfloat16))
+    text_kv = [(keyval, 0, HEADS // 2)]
+    crossed = attend(query_proj, text_kv, text_windows, text_len)
     stream_four = stream_three + matmul(crossed, cross_out_w)
     stream_five, saved_b = mlp_forward(stream_four, mod_b, up_b_w, down_b_w)
     final_val, final_back = jax.vjp(norm_gained, stream_five, small_val[2 * CH + 2])
     final_low = final_val.astype(jnp.bfloat16)
     head_low = small_low[CH : 2 * CH]
     predicted = matmul_nt(final_low, head_low)
-    weight_row = jnp.repeat(frame_mask[0].astype(jnp.float32), num_rows * num_cols)[:, None]
+    weight_row = jnp.repeat(frame_mask[0].astype(jnp.float32), run)
+    weight_row = jnp.tile(weight_row, num_cols // WIN)[:, None]
     pred_error = predicted - target
     loss_part = jnp.sum(weight_row * pred_error * pred_error)
     grad_pred = (weight_row * pred_error * (2.0 / global_count)).astype(jnp.bfloat16)
@@ -929,14 +1073,11 @@
         grad_stream, mod_b, up_b_w, down_b_w, saved_b
     )
     grad_cross = grad_stream.astype(jnp.bfloat16)
-    grad_crossed = split_heads(matmul_nt(grad_cross, cross_out_w).astype(jnp.bfloat16))
-    cq_grad, ck_grad, cv_grad = attend_backward(
-        cross_q, cross_k, cross_v, cross_total, grad_crossed, CROSS_FORMS
-    )
-    grad_query = merge_heads(cq_grad).astype(jnp.bfloat16)
+    grad_crossed = matmul_nt(grad_cross, cross_out_w).astype(jnp.bfloat16)
+    grad_query, grad_keyval = attend_back(
+        query_proj, text_kv, grad_crossed, text_windows, text_len
+    )
     grad_part, grad_gain_c = cross_back(matmul_nt(grad_query, query_w))
-    grad_keyval = jnp.concatenate([merge_heads(ck_grad), merge_heads(cv_grad)], 1)
-    grad_keyval = jnp.pad(grad_keyval, ((0, TEXT_PAD - text_len), (0, 0)))
     grad_keyval = lax.psum_scatter(grad_keyval, "band", scatter_dimension=1, tiled=True)
     grad_keyval = lax.all_gather(grad_keyval, "clip", axis=0, tiled=True)
     grad_w_ckv = matmul_tn(
@@ -949,31 +1090,13 @@
     grad_proj = (mod_b[2] * grad_stream).astype(jnp.bfloat16)
     grad_gate_b = jnp.sum(grad_stream * proj_b, 0)
     factors_ob = (att_b, grad_proj)
-    grad_att = (
-        matmul_nt(grad_proj, out_b_w)
-        .astype(jnp.bfloat16)
-        .reshape(num_frames, num_rows, num_cols, D)
-    )
-    fetched = shifted(grad_att[:, :SHIFT], "band", -1)
-    grad_rolled = jnp.concatenate([grad_att[:, SHIFT:], fetched], 1)
-    grad_win = split_heads(to_windows(grad_rolled, temporal))
-    wq_grad, wk_grad, wv_grad = attend_backward(
-        win_q, win_k, win_v, win_total, grad_win, SELF_FORMS
-    )
-    grad_blocks = jnp.concatenate(
-        [merge_heads(wq_grad), merge_heads(wk_grad), merge_heads(wv_grad)], -1
-    )
-    grad_qkv = (
-        from_windows(grad_blocks, grid_shape, temporal)
-        .reshape(tok_count, 3 * D)
-        .astype(jnp.bfloat16)
-    )
+    grad_att = matmul_nt(grad_proj, out_b_w).astype(jnp.bfloat16)
+    grad_win = with_rows(grad_att, shifted(first_rows(grad_att, run, part), "band", -1), run)
+    grad_qkv = attend_back(qkv_b, win_kv, grad_win, half_windows)[0]
     factors_qkvb = (rolled, grad_qkv)
-    grad_in_roll = matmul_nt(grad_qkv, qkv_b_w).reshape(num_frames, num_rows, num_cols, D)
-    sent_back = shifted(grad_in_roll[:, num_rows - SHIFT :], "band", 1)
-    grad_normed = jnp.concatenate([sent_back, grad_in_roll[:, : num_rows - SHIFT]], 1).reshape(
-        tok_count, D
-    )
+    grad_in_roll = matmul_nt(grad_qkv, qkv_b_w)
+    sent_back = shifted(first_rows(grad_in_roll, run, part), "band", 1)
+    grad_normed = with_rows(grad_in_roll, sent_back, run)
     grad_part, grad_shift_b, grad_scale_b = back_b(grad_normed)
     grad_stream = grad_stream + grad_part
     grad_stream, mlp_factors_a, extra_a = mlp_backward(
@@ -982,34 +1105,10 @@
     grad_proj = (mod_a[2] * grad_stream).astype(jnp.bfloat16)
     grad_gate_a = jnp.sum(grad_stream * proj_a, 0)
     factors_oa = (att_a, grad_proj)
-    grad_att = (
-        matmul_nt(grad_proj, out_a_w)
-        .astype(jnp.bfloat16)
-        .reshape(num_frames, num_rows, num_cols, D)
-    )
-    grad_space = split_heads(to_windows(grad_att, spatial))
-    sq_grad, sk_grad, sv_grad = attend_backward(
-        space_q, space_k, space_v, space_total, grad_space, SELF_FORMS
-    )
-    half_len = space_q.shape[1]
-    key_grads = merge_heads(sk_grad)
-    value_grads = merge_heads(sv_grad)
-    back_keys, back_values = from_partner(
-        (key_grads[:, half_len:], value_grads[:, half_len:]), "band", 0
-    )
-    grad_blocks = jnp.concatenate(
-        [
-            merge_heads(sq_grad),
-            key_grads[:, :half_len] + back_keys,
-            value_grads[:, :half_len] + back_values,
-        ],
-        -1,
-    )
-    grad_qkv = (
-        from_windows(grad_blocks, grid_shape, spatial)
-        .reshape(tok_count, 3 * D)
-        .astype(jnp.bfloat16)
-    )
+    grad_att = matmul_nt(grad_proj, out_a_w).astype(jnp.bfloat16)
+    grad_q, grad_own, grad_far = attend_back(qkv_a, space_kv, grad_att, frame_windows)
+    grad_kv = grad_own + from_partner(grad_far, "band", 0)
+    grad_qkv = jnp.concatenate([grad_q, grad_kv.astype(jnp.bfloat16)], 1)
     factors_qkva = (in_a, grad_qkv)
     grad_part, grad_shift_a, grad_scale_a = back_a(matmul_nt(grad_qkv, qkv_a_w))
     grad_stream = grad_stream + grad_part
@@ -1055,15 +1154,7 @@
         )
         square_part = jnp.sum(squares) / (band_count // 2)
     else:
-        summed = []
-        for left, right in factors:
-            member = matmul_tn(left, right)
-            rows, cols = member.shape
-            member = member.reshape(rows, band_count, cols // band_count).transpose(1, 0, 2)
-            member = member.reshape(band_count, clip_count, rows // clip_count, cols // band_count)
-            member = member.transpose(1, 0, 2, 3).reshape(-1, cols // band_count)
-            member = lax.psum_scatter(member, ("clip", "band"), scatter_dimension=0, tiled=True)
-            summed.append(lax.all_gather(member, "band", axis=1, tiled=True))
+        summed = [sum_rows(*pair) for pair in factors]
         wide_rest = jnp.concatenate([summed[i] for i in (9, 5, 8, 4, 3, 2, 7, 1)], 1)
         deep_rest = jnp.concatenate([summed[6], summed[0]], 1)
         square_part = (jnp.sum(wide_rest**2) + jnp.sum(deep_rest**2)) / band_count

time: 1440 us -> 1240 us (0.86)
  local copies, waits for them, and re-layouts: 172 us -> 52.8 us
  matrix products: 281 us -> 201 us
  other arithmetic: 161 us -> 115 us
  waiting for transfers between devices: 61.3 us -> 86.4 us
  Pallas kernels: 642 us -> 660 us
    pallas_call x0 -> x6, Pallas kernels: none -> 119 us  [the longest x3 82.6 us: attend_back(): pl.pallas_call(partial(attend_back_kernel, windows, text_len, sets), grid...]
    pallas_call x1, Pallas kernels: 296 us -> 185 us  [gather_weights(): pl.pallas_call(partial(gather_kernel, count, [shard.shape for shard in sh...]
    dot_general x18 -> x0, matrix products: 81.9 us -> none  [the longest x3 19.5 us: attend_backward(): jnp.einsum(einsum_forms[0], grad_out, value_heads, preferred_element_type...]
    slice x18 -> x6, local copies, waits for them, and re-layouts: 35.7 us -> 8.7 us  [the longest x1 3.87 us: per_device(): down_b_w = gather_quarters(w_deep[:, 3 * D:])]
    concatenate x5 -> x0, local copies, waits for them, and re-layouts: 23 us -> none  [the longest x3 13.9 us: per_device(): jnp.concatenate([merge_heads(wq_grad), merge_heads(wk_grad), merge_heads(...]
    another operation x7 -> x2, local copies, waits for them, and re-layouts: 23 us -> 0.08 us  [per_device(): weight_row = jnp.tile(weight_row, num_cols // WIN)[:, None]]
    convert_element_type x7 -> x3, other arithmetic: 24.4 us -> 5.5 us  [the longest x1 5.01 us: per_device(): grad_qkv = jnp.concatenate([grad_q, grad_kv.astype(jnp.bfloat16)], 1)]
    all_gather x1, waiting for transfers between devices: 3.14 us -> 20.9 us  [per_device(): grad_keyval = lax.all_gather(grad_keyval, 'clip', axis=0, tiled=True)]
  transfers between devices with their start and end apart: 11 -> 12, of which waited for: 6 -> 6; matrix products, arithmetic and copies ran while one was open for 7% -> 15% of each run, Pallas kernels for 23% -> 47%
where the time goes in v4:
time: 1240 us; the launch traced here: 1230 us
  Pallas kernels  660 us (53%)
  matrix products  201 us (16%)
  other arithmetic  115 us (9%)
  blocking collectives  86.7 us (7%)
  waiting for transfers between devices  86.4 us (7%)
  local copies, waits for them, and re-layouts  52.8 us (4%)
  between operations  24.6 us (2%)
    pallas_call x1, Pallas kernels, reduce_gradients(): pl.pallas_call(partial(reduce_kernel, count, tokens, phases), out_shape=(...  329 us
    pallas_call x1, Pallas kernels, gather_weights(): pl.pallas_call(partial(gather_kernel, count, [shard.shape for shard in sh...  185 us
    dot_general x14, matrix products, matmul(): return jnp.dot(left_op, right_op, preferred_element_type=jnp.float32)  108 us
    pallas_call x3, Pallas kernels, attend_back(): pl.pallas_call(partial(attend_back_kernel, windows, text_len, sets), grid...  82.6 us
    dot_general x11, matrix products, matmul_nt(): lax.dot_general(left_op, right_op, (((1,), (1,)), ((), ())), preferred_el...  81.5 us
    sub x3, other arithmetic, adam_update(): weight - learn_rate * (first_hat / (jnp.sqrt(second_hat) + ADAM_EPS) + DE...  56.9 us
    psum x1, blocking collectives, per_device(): lax.psum((loss_part, square_part, grad_small), ('clip', 'band'))  37.9 us
    pallas_call x3, Pallas kernels, attend(): pl.pallas_call(partial(attend_kernel, windows, text_len, len(key_values))...  36.6 us
  transfers between devices with their start and end apart: 12, of which 6 were waited for; matrix products, arithmetic and copies ran while one was open for 15% of the time, Pallas kernels for 47%

profile of v4, /device:TPU:0, one launch (start us, length us, event | category | flops | bytes accessed | tf_op | source)
XLA Modules:
  0.0 1233.1 jit_solution(15666726683612971970)
XLA Ops:
  10.6 9.6 convert.17
  24.8 2.7 fusion.70
  32.5 27.6 %shard_map.230 = (s32[8,8,128]{2,1,0:T(8,128)}, bf16[8,80,512]{2,1,0:T(8,128)(2,1)}) custom-call(s32[8,128]{1,0:T(8,128)} %pad.8.facts_ref, bf16[8,80,512]{2,1,0:T(8,128)(2,1)} %pad.9.text_ref), custom_call_target="tpu_custom_call" | custom-call | tf_op jit(solution)/shard_map/pallas_call | solution.py:331
  61.1 3.9 fusion.68
  65.7 2.4 fusion.17
  69.0 2.8 fusion.21.refs_9_
  71.8 184.7 %shard_map.231 = (bf16[1024,3072]{1,0:T(8,128)(2,1)}, bf16[1024,3072]{1,0:T(8,128)(2,1)}, bf16[1024,1024]{1,0:T(8,128)(2,1)}, bf16[1024,1024]{1,0:T(8,128)(2,1)}...) custom-call(bf16[128,3072]{1,0:T(8,128)(2,1)} %get-tuple-element.116, ...), custom_call_target="tpu_custom_call" | custom-call | flops 199999995904 | bytes 600000000 | tf_op jit(solution)/shard_map/pallas_call | solution.py:530
  263.0 4.5 convolution_convert_fusion.1.refs_0_.refs_1_.refs_3_
  272.6 2.8 collective-permute-done.refs_2_.refs_4_
  277.5 11.9 shard_map.232.refs_8_
  289.4 3.2 fusion.67
  293.6 32.7 %multiply_convert_fusion.1 = (bf16[640,4096]{1,0:T(8,128)(2,1)S(1)}, f32[640,4096]{1,0:T(8,128)}, f32[640,4096]{1,0:T(8,128)}) fusion(bf16[640,1024]{1,0:T(8,128)(2,1)S(1)} %add_convert_fusion.5.refs_7_, bf16[1024,4096]{1,0:T(8,128)(2,1)} %get-tuple-element.36), kind=kOutput, calls=%fused_computation.25 | convolution fusion | flops 5539102720 | bytes 35913728 | tf_op jit(solution)/shard_map/dot_general | solution.py:47
  326.5 7.1 fusion.65
  335.5 12.5 %collective-permute-done.1 = bf16[10,32,1024]{2,1,0:T(8,128)(2,1)S(1)} collective-permute-done((bf16[10,32,1024]{2,1,0:T(8,128)(2,1)S(1)}, bf16[10,32,1024]{2,1,0:T(8,128)(2,1)S(1)}, u32[]{:S(2)}, u32[]{:S(2)}) %collective-permute-start.1) | collective-permute-done | bytes 655392 | tf_op jit(solution)/shard_map/ppermute | solution.py:43
  349.2 4.5 convolution_convert_fusion.refs_0_.refs_1_.refs_2_
  353.7 16.4 %shard_map.233 = bf16[640,1024]{1,0:T(8,128)(2,1)S(1)} custom-call(bf16[640,3072]{1,0:T(8,128)(2,1)S(1)} %convolution_convert_fusion.refs_0_.refs_1_.refs_2_, bf16[640,3072]{1,0:T(8,128)(2,1)S(1)} %convolution_convert_fusion.refs_0_.refs_1_.refs_2_, bf16[640,3072]{1,0:T(8,128)(2,1)S(1)} %convolution_convert_fusion.refs_0_.refs_1_.refs_2_), custom_call_target="tpu_custom_call" | custom-call | flops 1677721600 | bytes 10485760 | tf_op jit(solution)/shard_map/pallas_call | solution.py:219
  371.1 2.4 collective-permute-start.2
  381.2 6.1 all_gather.18.refs_1_.refs_2_
  388.7 3.0 fusion.64
  396.3 8.4 shard_map.234.refs_2_
  408.6 31.8 %multiply_convert_fusion = (bf16[640,4096]{1,0:T(8,128)(2,1)}, f32[640,4096]{1,0:T(8,128)}, f32[640,4096]{1,0:T(8,128)}) fusion(bf16[640,1024]{1,0:T(8,128)(2,1)} %add_convert_fusion.3.refs_1_, bf16[1024,4096]{1,0:T(8,128)(2,1)} %all-gather.6.cloned.1.call-done), kind=kOutput, calls=%fused_computation.12 | convolution fusion | flops 5539102720 | bytes 35913728 | tf_op jit(solution)/shard_map/dot_general | solution.py:47
  440.4 11.2 fusion.62
  457.7 17.3 %add_convert_fusion.1.refs_11_ = bf16[640,4096]{1,0:T(8,128)(2,1)} fusion(f32[640,4096]{1,0:T(8,128)} %get-tuple-element.100, f32[640,4096]{1,0:T(8,128)} %get-tuple-element.157, bf16[640,1024]{1,0:T(8,128)(2,1)} %multiply_convert_fusion.5.refs_10_, bf16[4096,1024]{1,0:T(8,128)(2,1)} %all-gather.8.cloned.1.call-done), kind=kOutput, calls=%fused_computation.11 | convolution fusion | flops 5405409280 | bytes 35913728 | tf_op jit(solution)/shard_map/dot_general | solution.py:61
  475.0 11.0 multiply_reduce_fusion.6
  490.1 2.7 convolution_convert_fusion.4.refs_3_
  492.8 13.4 %shard_map.235 = (bf16[640,1024]{1,0:T(8,128)(2,1)S(1)}, f32[80,2048]{1,0:T(8,128)}) custom-call(bf16[640,1024]{1,0:T(8,128)(2,1)S(1)} %copy-done.9, bf16[80,2048]{1,0:T(8,128)(2,1)S(1)} %copy-done.6, bf16[80,2048]{1,0:T(8,128)(2,1)S(1)} %copy-done.6, bf16[640,1024]{1,0:T(8,128)(2,1)} %convolution_convert_fusion.4.refs_3_), custom_call_target="tpu_custom_call" | custom-call | flops 4194304000 | bytes 10485760 | tf_op jit(solution)/shard_map/pallas_call | solution.py:240
  516.2 8.1 collective-permute-done.3
  524.4 28.5 %shard_map.236.refs_15_ = bf16[640,3072]{1,0:T(8,128)(2,1)} custom-call(bf16[640,3072]{1,0:T(8,128)(2,1)} %copy-done.2, bf16[640,3072]{1,0:T(8,128)(2,1)} %copy-done.2, bf16[640,3072]{1,0:T(8,128)(2,1)} %copy-done.2, bf16[640,1024]{1,0:T(8,128)(2,1)S(1)} %bitcast.159), custom_call_target="tpu_custom_call" | custom-call | flops 4194304000 | bytes 10485760 | tf_op jit(solution)/shard_map/pallas_call | solution.py:240
  552.9 6.4 fusion.77
  561.2 15.6 %collective-permute-done.4 = f32[10,32,1024]{2,1,0:T(8,128)S(1)} collective-permute-done((f32[10,32,1024]{2,1,0:T(8,128)S(1)}, f32[10,32,1024]{2,1,0:T(8,128)S(1)}, u32[]{:S(2)}, u32[]{:S(2)}) %collective-permute-start.4) | collective-permute-done | bytes 1310752 | tf_op jit(solution)/shard_map/ppermute | solution.py:43
  583.6 17.9 %add_convert_fusion.refs_17_ = bf16[640,4096]{1,0:T(8,128)(2,1)} fusion(f32[640,4096]{1,0:T(8,128)} %get-tuple-element.106, f32[640,4096]{1,0:T(8,128)} %get-tuple-element.152, bf16[640,1024]{1,0:T(8,128)(2,1)S(1)} %multiply_convert_fusion.3.refs_16_, bf16[4096,1024]{1,0:T(8,128)(2,1)} %get-tuple-element.37), kind=kOutput, calls=%fused_computation.10 | convolution fusion | flops 5405409280 | bytes 35913728 | tf_op jit(solution)/shard_map/dot_general | solution.py:61
  601.5 10.9 multiply_reduce_fusion.9
  617.0 40.7 %shard_map.237 = (bf16[640,1024]{1,0:T(8,128)(2,1)S(1)}, f32[640,2048]{1,0:T(8,128)}, f32[640,2048]{1,0:T(8,128)}) custom-call(bf16[640,3072]{1,0:T(8,128)(2,1)} %copy-done, bf16[640,3072]{1,0:T(8,128)(2,1)} %copy-done, bf16[640,2048]{1,0:T(8,128)(2,1)} %copy-done.3, bf16[640,3072]{1,0:T(8,128)(2,1)} %copy-done, bf16[640,2048]{1,0:T(8,128)(2,1)} %copy-done.3, ...), custom_call_target="tpu_custom_call" | custom-call | flops 4194304000 | bytes 10485760 | tf_op jit(solution)/shard_map/pallas_call | solution.py:240
  658.1 26.5 %reduce-scatter.2.cloned.1.call-done = f32[80,512]{1,0:T(8,128)} async-done(((f32[80,2048]{1,0:T(8,128)}), f32[80,512]{1,0:T(8,128)}) %reduce-scatter.2.cloned.1.call-update) | async-done | bytes 163856 | tf_op jit(solution)/shard_map/reduce_scatter | solution.py:1081
  686.7 5.0 add_convert_fusion.2
  691.8 9.3 multiply_reduce_fusion.4
  707.8 20.9 %all-gather.10.cloned.1.call-done = f32[640,512]{1,0:T(8,128)} async-done(((f32[80,512]{1,0:T(8,128)}), f32[640,512]{1,0:T(8,128)}) %all-gather.10.cloned.1.call-update) | async-done | bytes 1310736 | tf_op jit(solution)/shard_map/all_gather | solution.py:1082
  728.7 3.9 fusion.78
  732.6 3.9 pad_maximum_fusion.refs_19_
  736.6 328.8 %shard_map.238 = (f32[128,18432]{1,0:T(8,128)}, f32[512,2048]{1,0:T(8,128)}, f32[8,512]{1,0:T(8,128)}, bf16[640,4096]{1,0:T(8,128)(2,1)}, bf16[640,1024]{1,0:T(8...) custom-call(bf16[640,4096]{1,0:T(8,128)(2,1)} %get-tuple-element.99., ...), custom_call_target="tpu_custom_call" | custom-call | flops 299999985664 | bytes 800000000 | tf_op jit(solution)/shard_map/pallas_call | solution.py:928
  1067.6 11.2 psum.29
  1078.9 31.4 %all-gather = f32[8,1,12288]{2,1,0:T(1,128)S(1)} all-gather(f32[1,1,12288]{2,1,0:T(1,128)S(1)} %bitcast.177), channel_id=1, replica_groups=mesh['clip'=8,'band'=4] {'clip'}, dimensions={0}, use_global_device_ids=true | all-gather | bytes 442368 | tf_op jit(solution)/shard_map/all_gather | solution.py:1136
  1110.3 4.0 fusion.71
  1114.3 5.6 multiply_reduce_fusion
  1121.4 3.9 multiply_reduce_fusion.1
  1126.6 37.9 %all-reduce.2 = (f32[]{:T(128)}, f32[]{:T(128)}) all-reduce(f32[]{:T(128)} %get-tuple-element.159, f32[]{:T(128)S(6)} %add.328), channel_id=1, replica_groups=mesh['clip'=8,'band'=4] {'clip','band'}, use_global_device_ids=true, to_apply=%region_15.16 | all-reduce | flops 2 | bytes 16 | tf_op jit(solution)/shard_map/psum | solution.py:1164
  1166.6 36.6 %multiply_subtract_fusion = (f32[128,30720]{1,0:T(8,128)}, f32[128,30720]{1,0:T(8,128)}, f32[128,30720]{1,0:T(8,128)}) fusion(f32[128,30720]{1,0:T(8,128)} %param.21, f32[]{:T(128)S(6)} %div.219, f32[128,18432]{1,0:T(8,128)} %get-tuple-element.49, f32[128,12288]{1,0:T(8,128)} %get-tuple-element.167, f32[128,30720]{1,0:T(8,128)} %param.22, f32[128,30720]{1,0:T(8,128)} %param.23), kind=kLoop, calls=%fused_computation.3 | loop fusion | flops 66846720 | bytes 110100480 | tf_op jit(solution)/shard_map/sub | solution.py:276
  1204.0 19.5 %multiply_subtract_fusion.1 = (f32[512,4096]{1,0:T(8,128)}, f32[512,4096]{1,0:T(8,128)}, f32[512,4096]{1,0:T(8,128)}) fusion(f32[512,4096]{1,0:T(8,128)} %param.24, f32[]{:T(128)S(6)} %div.219, f32[512,1024]{1,0:T(8,128)} %get-tuple-element.118, f32[512,2048]{1,0:T(8,128)} %all-gather.12.cloned.1.call-done, f32[512,1024]{1,0:T(8,128)S(1)} %get-tuple-element.117, ...), kind=kLoop, calls=%fused_computation.42 | loop fusion | flops 37748736 | bytes 58720260 | tf_op jit(solution)/shard_map/sub | solution.py:276
  (410 shorter events, 95.6 us)
Async XLA Ops:
  7.2 401.4 %all-gather.6.cloned.1.call-start = ((), (), s32[]{:S(2)}) async-start(), calls=%async_computation.1 | async-start | bytes 8650752 | tf_op jit(solution)/shard_map/all_gather | solution.py:516
  9.7 430.7 %all-gather.8.cloned.1.call-start = ((), (), s32[]{:S(2)}) async-start(), calls=%async_computation.2 | async-start | bytes 8650752 | tf_op jit(solution)/shard_map/all_gather | solution.py:516
  71.7 185.8 %copy-start.49 = (bf16[19,1024]{1,0:T(8,128)(2,1)S(1)}, bf16[19,1024]{1,0:T(8,128)(2,1)}, u32[]{:S(2)}) copy-start(bf16[19,1024]{1,0:T(8,128)(2,1)} %convert_element_type.141) | copy-start | bytes 116740
  71.8 186.4 %copy-start.63 = (bf16[640,8]{0,1:T(8,128)(2,1)S(1)}, bf16[640,8]{0,1:T(8,128)(2,1)}, u32[]{:S(2)}) copy-start(bf16[640,8]{0,1:T(8,128)(2,1)} %convert_element_type.140) | copy-start | bytes 30724
  258.2 31.2 %copy-start.59 = (f32[1,1024]{1,0:T(1,128)}, f32[1,1024]{1,0:T(1,128)S(1)}, u32[]{:S(2)}) copy-start(f32[1,1024]{1,0:T(1,128)S(1)} %get-tuple-element.134) | copy-start | bytes 12292
  260.5 32.5 %copy-start.82 = (f32[1024]{0:T(1024)}, f32[1024]{0:T(1024)S(1)}, u32[]{:S(2)}) copy-start(f32[1024]{0:T(1024)S(1)} %get-tuple-element.142) | copy-start | bytes 12292
  260.5 65.9 %copy-start.105 = (f32[1024]{0:T(1024)}, f32[1024]{0:T(1024)S(1)}, u32[]{:S(2)}) copy-start(f32[1024]{0:T(1024)S(1)} %get-tuple-element.143) | copy-start | bytes 12292
  260.5 73.5 %copy-start.70 = (f32[1024]{0:T(1024)}, f32[1024]{0:T(1024)S(1)}, u32[]{:S(2)}) copy-start(f32[1024]{0:T(1024)S(1)} %get-tuple-element.139) | copy-start | bytes 12292
  260.5 128.2 %copy-start.72 = (f32[1024]{0:T(1024)}, f32[1024]{0:T(1024)S(1)}, u32[]{:S(2)}) copy-start(f32[1024]{0:T(1024)S(1)} %get-tuple-element.140) | copy-start | bytes 12292
  270.2 5.1 collective-permute-start
  272.1 412.5 %reduce-scatter.2.cloned.1.call-start = ((), (), s32[]{:S(2)}) async-start(), calls=%async_computation.3 | async-start | bytes 819200 | tf_op jit(solution)/shard_map/reduce_scatter | solution.py:1081
  292.6 33.9 %copy-start.18 = (f32[640,1024]{1,0:T(8,128)}, f32[640,1024]{1,0:T(8,128)S(1)}, u32[]{:S(2)}) copy-start(f32[640,1024]{1,0:T(8,128)S(1)} %get-tuple-element.108) | copy-start | bytes 7864324
  292.6 33.9 %slice-start.4 = ((s8[8388608]{0:T(1024)(128)(4,1)}), s8[4194304]{0:T(1024)(128)(4,1)S(1)}, s32[]{:S(2)}) async-start(s8[8388608]{0:T(1024)(128)(4,1)} %bitcast.210), calls=%async_computation.11 | async-start | bytes 8388608
  292.6 56.6 %slice-start = ((s8[6291456]{0:T(1024)(128)(4,1)}), s8[4194304]{0:T(1024)(128)(4,1)S(1)}, s32[]{:S(2)}) async-start(s8[6291456]{0:T(1024)(128)(4,1)} %bitcast.206), calls=%async_computation.7 | async-start | bytes 8388608
  293.0 33.4 %copy-start.93 = (f32[640]{0:T(1024)}, f32[640]{0:T(1024)S(1)}, u32[]{:S(2)}) copy-start(f32[640]{0:T(1024)S(1)} %multiply_reduce_fusion.21) | copy-start | bytes 7684
  293.0 33.4 %copy-start.85 = (f32[640]{0:T(1024)}, f32[640]{0:T(1024)S(1)}, u32[]{:S(2)}) copy-start(f32[640]{0:T(1024)S(1)} %fusion.42) | copy-start | bytes 7684
  293.6 32.8 %copy-start.42 = (bf16[640,1024]{1,0:T(8,128)(2,1)}, bf16[640,1024]{1,0:T(8,128)(2,1)S(1)}, u32[]{:S(2)}) copy-start(bf16[640,1024]{1,0:T(8,128)(2,1)S(1)} %add_convert_fusion.5.refs_7_) | copy-start | bytes 3932164
  293.6 32.8 %slice-start.5 = ((s8[8388608]{0:T(1024)(128)(4,1)}), s8[4194304]{0:T(1024)(128)(4,1)S(1)}, s32[]{:S(2)}) async-start(s8[8388608]{0:T(1024)(128)(4,1)} %bitcast.210), calls=%async_computation.12 | async-start | bytes 8388608
  293.6 55.6 %slice-start.1 = ((s8[6291456]{0:T(1024)(128)(4,1)}), s8[2097152]{0:T(1024)(128)(4,1)S(1)}, s32[]{:S(2)}) async-start(s8[6291456]{0:T(1024)(128)(4,1)} %bitcast.206), calls=%async_computation.8 | async-start | bytes 4194304
  333.6 55.1 %copy-start.11 = (f32[640,1024]{1,0:T(8,128)}, f32[640,1024]{1,0:T(8,128)S(1)}, u32[]{:S(2)}) copy-start(f32[640,1024]{1,0:T(8,128)S(1)} %get-tuple-element.104) | copy-start | bytes 7864324
  335.2 12.8 %collective-permute-start.1 = (bf16[10,32,1024]{2,1,0:T(8,128)(2,1)S(1)}, bf16[10,32,1024]{2,1,0:T(8,128)(2,1)S(1)}, u32[]{:S(2)}, u32[]{:S(2)}) collective-permute-start(bf16[10,32,1024]{2,1,0:T(8,128)(2,1)S(1)} %get-tuple-element.128), channel_id=1, source_target_pairs={{0,3},{1,0},{2,1},{3,2},{4,7},{5,4},{6,5},{7,6},{8,11},{9,8},{10,9... | collective-permute-start | bytes 1966088 | tf_op jit(solution)/shard_map/ppermute | solution.py:43
  371.1 16.3 %collective-permute-start.2 = (bf16[10,32,1024]{2,1,0:T(8,128)(2,1)}, bf16[10,32,1024]{2,1,0:T(8,128)(2,1)}, u32[]{:S(2)}, u32[]{:S(2)}) collective-permute-start(bf16[10,32,1024]{2,1,0:T(8,128)(2,1)} %get-tuple-element.126), channel_id=1, source_target_pairs={{0,1},{1,2},{2,3},{3,0},{4,5},{5,6},{6,7},{7,4},{8,9},{9,10},{10,1... | collective-permute-start | bytes 1966088 | tf_op jit(solution)/shard_map/ppermute | solution.py:43
  406.8 33.6 %copy-start.99 = (f32[640]{0:T(1024)}, f32[640]{0:T(1024)S(1)}, u32[]{:S(2)}) copy-start(f32[640]{0:T(1024)S(1)} %multiply_reduce_fusion.18) | copy-start | bytes 7684
  408.6 31.8 %copy-start.112 = (f32[1024]{0:T(1024)S(1)}, f32[1024]{0:T(1024)}, u32[]{:S(2)}) copy-start(f32[1024]{0:T(1024)} %get-tuple-element.135) | copy-start | bytes 12292
  515.4 37.6 %slice-start.2 = ((s8[6291456]{0:T(1024)(128)(4,1)}), s8[4194304]{0:T(1024)(128)(4,1)S(1)}, s32[]{:S(2)}) async-start(s8[6291456]{0:T(1024)(128)(4,1)} %bitcast.208), calls=%async_computation.9 | async-start | bytes 8388608
  515.5 8.8 collective-permute-start.3
  559.5 17.3 %collective-permute-start.4 = (f32[10,32,1024]{2,1,0:T(8,128)S(1)}, f32[10,32,1024]{2,1,0:T(8,128)S(1)}, u32[]{:S(2)}, u32[]{:S(2)}) collective-permute-start(f32[10,32,1024]{2,1,0:T(8,128)S(1)} %get-tuple-element.123), channel_id=1, source_target_pairs={{0,1},{1,2},{2,3},{3,0},{4,5},{5,6},{6,7},{7,4},{8,9},{9,10},{10,1... | collective-permute-start | bytes 3932168 | tf_op jit(solution)/shard_map/ppermute | solution.py:43
  617.0 40.8 %copy-start.25 = (bf16[640,1024]{1,0:T(8,128)(2,1)S(1)}, bf16[640,1024]{1,0:T(8,128)(2,1)}, u32[]{:S(2)}) copy-start(bf16[640,1024]{1,0:T(8,128)(2,1)} %copy-done.24) | copy-start | bytes 3932164
  657.7 28.9 %collective-permute-start.5 = (f32[640,2048]{1,0:T(8,128)}, f32[640,2048]{1,0:T(8,128)}, u32[]{:S(2)}, u32[]{:S(2)}) collective-permute-start(f32[640,2048]{1,0:T(8,128)} %get-tuple-element.46), channel_id=1, source_target_pairs={{0,1},{1,0},{2,3},{3,2},{4,5},{5,4},{6,7},{7,6},{8,9},{9,8},{10,11... | collective-permute-start | bytes 15728648 | tf_op jit(solution)/shard_map/ppermute | solution.py:38
  657.8 70.9 %all-gather.10.cloned.1.call-start = ((), (), s32[]{:S(2)}) async-start(), calls=%async_computation.4 | async-start | bytes 1474560 | tf_op jit(solution)/shard_map/all_gather | solution.py:1082
  684.6 435.3 %all-reduce.5.cloned.1.call-start = ((), (), s32[]{:S(2)}) async-start(), calls=%async_computation.6 | async-start | bytes 196608 | tf_op jit(solution)/shard_map/psum | solution.py:1164
  707.6 413.8 %all-gather.12.cloned.1.call-start = ((), (), s32[]{:S(2)}) async-start(), calls=%async_computation.5 | async-start | bytes 5242880 | tf_op jit(solution)/shard_map/all_gather | solution.py:1088
  736.5 328.9 %copy-start.101 = (f32[1024]{0:T(1024)S(1)}, f32[1024]{0:T(1024)}, u32[]{:S(2)}) copy-start(f32[1024]{0:T(1024)} %get-tuple-element.119) | copy-start | bytes 12292
  736.5 328.9 %copy-start.102 = (f32[1024]{0:T(1024)S(1)}, f32[1024]{0:T(1024)}, u32[]{:S(2)}) copy-start(f32[1024]{0:T(1024)} %get-tuple-element.79) | copy-start | bytes 12292
  736.5 328.9 %copy-start.108 = (f32[1024]{0:T(1024)S(1)}, f32[1024]{0:T(1024)}, u32[]{:S(2)}) copy-start(f32[1024]{0:T(1024)} %get-tuple-element.81) | copy-start | bytes 12292
  736.5 328.9 %copy-start.109 = (f32[1024]{0:T(1024)S(1)}, f32[1024]{0:T(1024)}, u32[]{:S(2)}) copy-start(f32[1024]{0:T(1024)} %get-tuple-element.64) | copy-start | bytes 12292
  736.5 328.9 %copy-start.110 = (f32[1024]{0:T(1024)S(1)}, f32[1024]{0:T(1024)}, u32[]{:S(2)}) copy-start(f32[1024]{0:T(1024)} %reduce_sum.562) | copy-start | bytes 12292
  736.5 328.9 %copy-start.111 = (f32[1024]{0:T(1024)S(1)}, f32[1024]{0:T(1024)}, u32[]{:S(2)}) copy-start(f32[1024]{0:T(1024)} %get-tuple-element.59) | copy-start | bytes 12292
  736.6 328.9 %copy-start.114 = (f32[1024]{0:T(1024)S(1)}, f32[1024]{0:T(1024)}, u32[]{:S(2)}) copy-start(f32[1024]{0:T(1024)} %get-tuple-element.57) | copy-start | bytes 12292
  736.6 328.9 %copy-start.115 = (f32[1024]{0:T(1024)S(1)}, f32[1024]{0:T(1024)}, u32[]{:S(2)}) copy-start(f32[1024]{0:T(1024)} %get-tuple-element.66) | copy-start | bytes 12292
  736.6 328.9 %copy-start.116 = (f32[1024]{0:T(1024)S(1)}, f32[1024]{0:T(1024)}, u32[]{:S(2)}) copy-start(f32[1024]{0:T(1024)} %get-tuple-element.61) | copy-start | bytes 12292
  736.6 328.9 %copy-start.117 = (f32[1024]{0:T(1024)S(1)}, f32[1024]{0:T(1024)}, u32[]{:S(2)}) copy-start(f32[1024]{0:T(1024)} %get-tuple-element.67) | copy-start | bytes 12292
  736.6 328.9 %copy-start.118 = (f32[1024]{0:T(1024)S(1)}, f32[1024]{0:T(1024)}, u32[]{:S(2)}) copy-start(f32[1024]{0:T(1024)} %get-tuple-element.52) | copy-start | bytes 12292
  736.6 328.9 %copy-start.119 = (f32[1024]{0:T(1024)S(1)}, f32[1024]{0:T(1024)}, u32[]{:S(2)}) copy-start(f32[1024]{0:T(1024)} %get-tuple-element.65) | copy-start | bytes 12292
  1166.6 36.7 %copy-start.47 = (f32[19,1024]{1,0:T(8,128)S(1)}, f32[19,1024]{1,0:T(8,128)}, u32[]{:S(2)}) copy-start(f32[19,1024]{1,0:T(8,128)} %param.27) | copy-start | bytes 233476
  1166.6 36.7 %copy-start.48 = (f32[19,1024]{1,0:T(8,128)S(1)}, f32[19,1024]{1,0:T(8,128)}, u32[]{:S(2)}) copy-start(f32[19,1024]{1,0:T(8,128)} %all-reduce.5.cloned.1.call-done) | copy-start | bytes 233476
  1166.6 36.7 %copy-start.61 = (f32[19,1024]{1,0:T(8,128)S(1)}, f32[19,1024]{1,0:T(8,128)}, u32[]{:S(2)}) copy-start(f32[19,1024]{1,0:T(8,128)} %param.28) | copy-start | bytes 233476
  1166.6 36.7 %copy-start.62 = (f32[19,1024]{1,0:T(8,128)S(1)}, f32[19,1024]{1,0:T(8,128)}, u32[]{:S(2)}) copy-start(f32[19,1024]{1,0:T(8,128)} %param.29) | copy-start | bytes 233476
  (100 other events, 583.0 us)
Sparse Core Ops, SparseCore 0:
  10.9 105.5 all-gather.5
  272.2 83.3 all-gather.7
  657.9 26.6 reduce-scatter.1
  686.6 42.0 all-gather.9
  734.7 121.6 all-reduce.4
  857.9 39.9 all-gather.11

commit v5 on v4

--- a/solution.py
+++ b/solution.py
@@ -278,6 +278,7 @@
 
 MESH = pl.DeviceIdType.MESH
 ANY = pl.BlockSpec(memory_space=pl.ANY)
+IN_VMEM = pl.BlockSpec(memory_space=pltpu.VMEM)
 TEXT_PAD = 80
 
 
@@ -555,16 +556,22 @@
 
 def unit_parts(kind, first):
     if kind == 0:
-        return ((0, 4, lambda u: u, lambda u: 0), (4, 4, lambda u: 4, lambda u: u - 3))
-    return ((first, 3 - first, lambda u: u, lambda u: u), (3, 3, lambda u: 3, lambda u: u))
+        return ((0, 4, lambda u: u, lambda u: 0), (4, 2, lambda u: 4, lambda u: u - 3))
+    return ((first, 3 - first, lambda u: u, lambda u: u), (3, 1, lambda u: 3, lambda u: u))
+
+
+def carried(parts, part):
+    return pl.ds(parts[part][0], parts[part][1] + part)
 
 
 def reduce_kernel(count, tokens, phases, *refs):
     num = sum(len(phase["lefts"]) for phase in phases)
     lefts, rights = refs[:num], refs[num : 2 * num]
-    wide_out, deep_out, square_out = refs[2 * num : 2 * num + 3]
-    left_far, right_far = refs[2 * num + 3 : 3 * num + 3], refs[3 * num + 3 : 4 * num + 3]
-    scratch = refs[4 * num + 3 :]
+    vec_ref, kv_ref, text_ref = refs[2 * num : 2 * num + 3]
+    refs = refs[2 * num + 3 :]
+    wide_out, deep_out, square_out, all_vec, kv_out, kv_square = refs[:6]
+    left_far, right_far = refs[6 : 6 + num], refs[6 + num : 6 + 2 * num]
+    scratch = refs[6 + 2 * num :]
     left_buf, right_buf, got_low, got_scale, put_low, put_scale, plane_put = (
         scratch[2 * i : 2 * i + 2] for i in range(7)
     )
@@ -585,6 +592,29 @@
         out_sem,
         out_send,
         out_recv,
+        cross_put,
+        cross_put_scale,
+        cross_got,
+        cross_got_scale,
+        cross_send,
+        cross_recv,
+        cross_credit,
+        vec_got,
+        kv_got,
+        vec_sum,
+        all_kv,
+        text_buf,
+        kv_grad,
+        side_own,
+        side_send,
+        side_recv,
+        vec_send,
+        vec_recv,
+        vec_pair_send,
+        vec_pair_recv,
+        kv_own,
+        kv_send,
+        kv_recv,
     ) = scratch[14 + len(phases) :]
     me = lax.axis_index("clip")
     band = lax.axis_index("band")
@@ -596,7 +626,9 @@
     preceding = (ring_clip((place - onward + count) % count, count), band)
     partner = (me, band + 1 - 2 * core)
     mirror = (me, band + 2 - 4 * plane)
-    greet([following, preceding, partner, mirror])
+    band_count = vec_got.shape[0]
+    band_peers = [(me, (band + step) % band_count) for step in range(1, band_count)]
+    greet([following, preceding] + band_peers)
 
     def owner_at(step, way):
         return ring_clip((place - way * (step + 1) + 2 * count) % count, count)
@@ -693,8 +725,7 @@
 
     def ring_copies(at, part, slot):
         kind = phases[at]["kind"]
-        start, many = unit_parts(kind, phases[at]["first"])[part][:2]
-        units = pl.ds(start, many)
+        units = carried(unit_parts(kind, phases[at]["first"]), part)
         return [
             pltpu.make_async_remote_copy(
                 put.at[slot, units],
@@ -709,6 +740,9 @@
             )
         ]
 
+    def split_base(at):
+        return 6 if phases[at]["kind"] == 0 else 4
+
     def plane_copy(at, part):
         kind = phases[at]["kind"]
         start, many = unit_parts(kind, phases[at]["first"])[part][:2]
@@ -721,6 +755,34 @@
             mirror,
             MESH,
         )
+
+    def split_copy(at):
+        unit = split_base(at) + plane
+        return pltpu.make_async_remote_copy(
+            plane_put[phases[at]["kind"]].at[unit],
+            plane_got[at].at[unit],
+            plane_send.at[at, 2],
+            plane_recv.at[at, 2],
+            mirror,
+            MESH,
+        )
+
+    def split_arrival(at):
+        unit = split_base(at) + 1 - plane
+        here = plane_got[at].at[unit]
+        return pltpu.make_async_remote_copy(
+            here, here, plane_send.at[at, 2], plane_recv.at[at, 2], mirror, MESH
+        )
+
+    def cross_copies(slot):
+        return [
+            pltpu.make_async_remote_copy(
+                put.at[slot], got.at[slot], cross_send.at[slot, i], cross_recv.at[slot, i], mirror, MESH
+            )
+            for i, (put, got) in enumerate(
+                ((cross_put, cross_got), (cross_put_scale, cross_got_scale))
+            )
+        ]
 
     def out_copies(at, unit):
         phase = phases[at]
@@ -774,7 +836,31 @@
                 copy.wait_recv()
             for far in range(2):
                 start(load_left(at, step + 1, before, far))
-        for part, (low, many, left_of, right_of) in enumerate(unit_parts(kind, phase["first"])):
+        parts = unit_parts(kind, phase["first"])
+        theirs = split_base(at) + 1 - plane
+        ours = split_base(at) + plane
+
+        def encode(term):
+            largest = jnp.maximum(jnp.max(jnp.abs(term), axis=0, keepdims=True), WIRE_LEAST)
+            low = jnp.round(term * (WIRE_MAX / largest)).astype(jnp.int16)
+            return low, largest * (1.0 / WIRE_MAX)
+
+        def spend_cross():
+            for copy in cross_copies(slot):
+                copy.wait_send()
+            pl.semaphore_wait(cross_credit, 1)
+
+        if at or last:
+            spend_cross()
+        elif not first:
+            pl.when(step >= 2)(spend_cross)
+        low_part, scale_part = encode(
+            product(kind, slot, parts[1][2](theirs), parts[1][3](theirs))
+        )
+        cross_put[slot] = low_part
+        cross_put_scale[slot] = scale_part
+        start(cross_copies(slot))
+        for part, (low, many, left_of, right_of) in enumerate(parts):
             if not first:
                 for copy in ring_copies(at, part, before):
                     copy.wait_recv()
@@ -786,23 +872,42 @@
                         copy.wait_send()
                     pl.semaphore_wait(credit.at[kind, part], 1)
 
-            @pl.loop(low, low + many)
-            def _(unit, left_of=left_of, right_of=right_of):
-                term = product(kind, slot, left_of(unit), right_of(unit))
+            def settle(position, unit, term):
                 if not first:
-                    came = got_low[kind][before, unit].astype(jnp.float32)
-                    term = term + came * got_scale[kind][before, unit]
+                    came = got_low[kind][before, position].astype(jnp.float32)
+                    term = term + came * got_scale[kind][before, position]
                 if last:
                     plane_put[kind][unit] = term
                 else:
-                    largest = jnp.max(jnp.abs(term), axis=0, keepdims=True)
-                    largest = jnp.maximum(largest, WIRE_LEAST)
-                    factor = WIRE_MAX / largest
-                    put_low[kind][slot, unit] = jnp.round(term * factor).astype(jnp.int16)
-                    put_scale[kind][slot, unit] = largest * (1.0 / WIRE_MAX)
+                    low_part, scale_part = encode(term)
+                    put_low[kind][slot, position] = low_part
+                    put_scale[kind][slot, position] = scale_part
+
+            @pl.loop(low, low + many)
+            def _(unit, left_of=left_of, right_of=right_of):
+                settle(unit, unit, product(kind, slot, left_of(unit), right_of(unit)))
+
+            if part:
+                for copy in cross_copies(slot):
+                    copy.wait_recv()
+                came = cross_got[slot].astype(jnp.float32) * cross_got_scale[slot]
+                settle(low + many, ours, product(kind, slot, left_of(ours), right_of(ours)) + came)
+                final = at + 1 == len(phases)
+
+                def credit_cross():
+                    pl.semaphore_signal(
+                        cross_credit, inc=1, device_id=mirror, device_id_type=MESH
+                    )
+
+                if not final or first:
+                    credit_cross()
+                elif not last:
+                    pl.when(step < count - 2)(credit_cross)
 
             if last:
                 plane_copy(at, part).start()
+                if part:
+                    split_copy(at).start()
             else:
                 start(ring_copies(at, part, slot))
             if not (first or last):
@@ -815,6 +920,10 @@
 
     def close(at):
         kind = phases[at]["kind"]
+
+        def add_square(total):
+            square_buf[...] += jnp.sum((total * total).reshape(UNIT[0] // 8, 8, UNIT[1]), axis=0)
+
         for part, (low, many, _, _) in enumerate(unit_parts(kind, phases[at]["first"])):
             plane_copy(at, part).wait()
 
@@ -822,14 +931,108 @@
             def _(unit):
                 total = plane_put[kind][unit] + plane_got[at][unit]
                 plane_got[at][unit] = total
-                square_buf[...] += jnp.sum(
-                    (total * total).reshape(UNIT[0] // 8, 8, UNIT[1]), axis=0
-                )
+                add_square(total)
 
             for unit in range(low, low + many):
                 start(out_copies(at, unit))
+        ours = split_base(at) + plane
+        split_copy(at).wait_send()
+        split_arrival(at).wait_recv()
+        plane_got[at][ours] = plane_put[kind][ours]
+        for unit in (split_base(at), split_base(at) + 1):
+            add_square(plane_got[at][unit])
+            start(out_copies(at, unit))
+
+    half_rows = pl.ds(pl.multiple_of(core * (vec_sum.shape[0] // 2), 8), vec_sum.shape[0] // 2)
+    side_local = [
+        pltpu.make_async_copy(vec_ref, vec_got.at[band], side_own.at[0]),
+        pltpu.make_async_copy(kv_ref.at[band], kv_got.at[band], side_own.at[1]),
+        pltpu.make_async_copy(text_ref, text_buf, side_own.at[2]),
+    ]
+    side_remote = []
+    for step, peer in enumerate(band_peers):
+        side_remote += [
+            pltpu.make_async_remote_copy(
+                vec_ref, vec_got.at[band], side_send.at[0, step], side_recv.at[0, step], peer, MESH
+            ),
+            pltpu.make_async_remote_copy(
+                kv_ref.at[peer[1]],
+                kv_got.at[band],
+                side_send.at[1, step],
+                side_recv.at[1, step],
+                peer,
+                MESH,
+            ),
+        ]
+    vec_own = pltpu.make_async_copy(vec_sum, all_vec.at[me], side_own.at[3])
+
+    def vec_copies(step):
+        owner = ring_clip((place - onward * step + 2 * count) % count, count)
+        vec = all_vec.at[owner, half_rows]
+        return [
+            pltpu.make_async_remote_copy(
+                here, there, vec_send.at[step, i], vec_recv.at[step, i], following, MESH
+            )
+            for i, (here, there) in enumerate(((vec, vec), (all_kv.at[owner], all_kv.at[owner])))
+        ]
+
+    def vec_first():
+        vec = all_vec.at[me, half_rows]
+        return [
+            pltpu.make_async_remote_copy(
+                here, there, vec_send.at[0, i], vec_recv.at[0, i], following, MESH
+            )
+            for i, (here, there) in enumerate(
+                ((vec_sum.at[half_rows], vec), (all_kv.at[me], all_kv.at[me]))
+            )
+        ]
+
+    def vec_pair(step):
+        owner = ring_clip((place - onward * (step + 1) + 2 * count) % count, count)
+        vec = all_vec.at[owner, half_rows]
+        return pltpu.make_async_remote_copy(
+            vec, vec, vec_pair_send.at[step], vec_pair_recv.at[step], partner, MESH
+        )
+
+    def kv_copies():
+        width = kv_grad.shape[1]
+        there = kv_out.at[:, pl.ds(pl.multiple_of(band * width, 128), width)]
+        return [pltpu.make_async_copy(kv_grad, there, kv_own)] + [
+            pltpu.make_async_remote_copy(
+                kv_grad, there, kv_send.at[step], kv_recv.at[step], peer, MESH
+            )
+            for step, peer in enumerate(band_peers)
+        ]
+
+    def sum_bands():
+        finish(side_local + side_remote)
+        vec_sum[...] = jnp.sum(vec_got[...], 0)
+        all_kv[me] = jnp.sum(kv_got[...], 0)
+        vec_own.start()
+        start(vec_first())
+
+    def pass_sums(step):
+        for copy in vec_copies(step - 1):
+            copy.wait_recv()
+        start(vec_copies(step))
+        vec_pair(step - 1).start()
+
+    def multiply_text():
+        for copy in vec_copies(count - 2):
+            copy.wait_recv()
+        vec_pair(count - 2).start()
+        grads = all_kv[...].reshape(text_buf.shape[0], -1)
+        total = jnp.zeros_like(kv_grad)
+        for _ in range(3):
+            part = grads.astype(jnp.bfloat16)
+            grads = grads - part.astype(jnp.float32)
+            total = total + matmul_tn(text_buf[...], part)
+        kv_grad[...] = total
+        kv_square[...] = jnp.sum((total * total).reshape(-1, 8, total.shape[1]), axis=0)
+        start(kv_copies())
 
     square_buf[...] = jnp.zeros_like(square_buf)
+    start(side_local + side_remote)
     start(load_right(0, 0))
     start(pair_right(0))
 
@@ -853,12 +1056,16 @@
             start(pair_right(at + 1))
             start(load_right(at + 1, 0))
         take_step(at, 0, True, False)
+        if at == 0:
+            sum_bands()
         if more:
             start(pair_left(at + 1, 0))
 
         @pl.loop(1, count - 1)
         def _(step, at=at, more=more):
             take_step(at, step, False, False)
+            if at == 0:
+                pass_sums(step)
             if more:
                 start(pair_left(at + 1, step))
 
@@ -872,6 +1079,8 @@
             for far in range(2):
                 start(load_left(at + 1, 0, 0, far))
         take_step(at, count - 1, False, True)
+        if at == 0:
+            multiply_text()
         for part in range(2):
             for slot in range(2):
                 for copy in ring_copies(at, part, slot):
@@ -879,6 +1088,18 @@
         if at:
             close(at - 1)
     close(len(phases) - 1)
+    for slot in range(2):
+        for copy in cross_copies(slot):
+            copy.wait_send()
+    vec_own.wait()
+    finish(kv_copies())
+
+    @pl.loop(0, count - 1)
+    def _(step):
+        for copy in vec_copies(step):
+            copy.wait_send()
+        vec_pair(step).wait()
+
     square_out[...] = square_buf[...]
     for at, phase in enumerate(phases):
         for copy in pair_right(at):
@@ -893,11 +1114,12 @@
             finish(out_copies(at, unit))
 
 
-def reduce_gradients(phases, lefts, rights, wide_cols, deep_cols):
+def reduce_gradients(phases, lefts, rights, vectors, keyvals, text, wide_cols, deep_cols):
     count = lax.axis_size("clip")
     tokens = lefts[0].shape[0]
     wide_rows = lefts[1].shape[1] // count
     deep_rows = lefts[0].shape[1] // count
+    band_count, _, kv_cols = keyvals.shape
     num = len(lefts)
     dma = pltpu.SemaphoreType.DMA
     units, lefts_of, rights_of = (8, 6), (5, 4), (5, 6)
@@ -919,11 +1141,34 @@
         dma((2, 2, 2, 2)),
         dma((2, 2, 2, 2)),
         pltpu.SemaphoreType.REGULAR((2, 2)),
-        dma((len(phases), 2)),
-        dma((len(phases), 2)),
+        dma((len(phases), 3)),
+        dma((len(phases), 3)),
         dma((len(phases), 8)),
         dma((len(phases), 8)),
         dma((len(phases), 8)),
+    ]
+    for _ in range(2):
+        scratch += [pltpu.VMEM((2,) + UNIT, jnp.int16), pltpu.VMEM((2, 1, UNIT[1]), jnp.float32)]
+    scratch += [
+        dma((2, 2)),
+        dma((2, 2)),
+        pltpu.SemaphoreType.REGULAR,
+        pltpu.VMEM((band_count,) + vectors.shape, jnp.float32),
+        pltpu.VMEM(keyvals.shape, jnp.float32),
+        pltpu.VMEM(vectors.shape, jnp.float32),
+        pltpu.VMEM((count,) + keyvals.shape[1:], jnp.float32),
+        pltpu.VMEM(text.shape, jnp.bfloat16),
+        pltpu.VMEM((text.shape[1], kv_cols), jnp.float32),
+        dma((4,)),
+        dma((2, band_count - 1)),
+        dma((2, band_count - 1)),
+        dma((count - 1, 2)),
+        dma((count - 1, 2)),
+        dma((count - 1,)),
+        dma((count - 1,)),
+        dma,
+        dma((band_count - 1,)),
+        dma((band_count - 1,)),
     ]
     out = pl.pallas_call(
         partial(reduce_kernel, count, tokens, phases),
@@ -931,18 +1176,69 @@
             jax.ShapeDtypeStruct((wide_rows, wide_cols), jnp.float32),
             jax.ShapeDtypeStruct((deep_rows, deep_cols), jnp.float32),
             jax.ShapeDtypeStruct((8, UNIT[1]), jnp.float32),
+            jax.ShapeDtypeStruct((count,) + vectors.shape, jnp.float32),
+            jax.ShapeDtypeStruct((deep_rows, band_count * kv_cols), jnp.float32),
+            jax.ShapeDtypeStruct((8, kv_cols), jnp.float32),
         )
         + tuple(jax.ShapeDtypeStruct(x.shape, x.dtype) for x in lefts)
         + tuple(jax.ShapeDtypeStruct((tokens, x.shape[1] // 2), x.dtype) for x in rights),
-        in_specs=[ANY] * (2 * num),
-        out_specs=(ANY, ANY, pl.BlockSpec(memory_space=pltpu.VMEM)) + (ANY,) * (2 * num),
+        in_specs=[ANY] * (2 * num + 3),
+        out_specs=(ANY, ANY, IN_VMEM, ANY, ANY, IN_VMEM) + (ANY,) * (2 * num),
         scratch_shapes=scratch,
         compiler_params=pltpu.CompilerParams(
             collective_id=2, has_side_effects=True, vmem_limit_bytes=58 << 20
         ),
         cost_estimate=pl.CostEstimate(flops=3 * 10**11, bytes_accessed=8 * 10**8, transcendentals=0),
-    )(*lefts, *rights)
-    return out[:3]
+    )(*lefts, *rights, vectors, keyvals, text)
+    return out[:6]
+
+
+def total_kernel(count, part_ref, out_ref, mid, band_got, clip_got, *sems):
+    me = lax.axis_index("clip")
+    band = lax.axis_index("band")
+    band_count = band_got.shape[0]
+    band_peers = [(me, (band + step) % band_count) for step in range(1, band_count)]
+    clip_peers = [((me + step) % count, band) for step in range(1, count)]
+    greet(band_peers + clip_peers)
+    stages = (
+        (part_ref, band_got, band, band_peers, mid, sems[:2]),
+        (mid, clip_got, me, clip_peers, out_ref, sems[2:]),
+    )
+    for value, got, index, peers, result, (send, recv) in stages:
+        copies = [
+            pltpu.make_async_remote_copy(
+                value, got.at[index], send.at[step], recv.at[step], peer, MESH
+            )
+            for step, peer in enumerate(peers)
+        ]
+        for copy in copies:
+            copy.start()
+        got[index] = value[...]
+        for copy in copies:
+            copy.wait()
+        result[...] = jnp.sum(got[...], 0)
+
+
+def total_over_devices(value):
+    count, band_count = lax.axis_size("clip"), lax.axis_size("band")
+    dma = pltpu.SemaphoreType.DMA
+    tile = (8, 128)
+    return pl.pallas_call(
+        partial(total_kernel, count),
+        out_shape=jax.ShapeDtypeStruct(tile, jnp.float32),
+        in_specs=[IN_VMEM],
+        out_specs=IN_VMEM,
+        scratch_shapes=[
+            pltpu.VMEM(tile, jnp.float32),
+            pltpu.VMEM((band_count,) + tile, jnp.float32),
+            pltpu.VMEM((count,) + tile, jnp.float32),
+            dma((band_count - 1,)),
+            dma((band_count - 1,)),
+            dma((count - 1,)),
+            dma((count - 1,)),
+        ],
+        compiler_params=pltpu.CompilerParams(collective_id=3, has_side_effects=True),
+    )(jnp.broadcast_to(value, tile))[0, 0]
 
 
 def per_device(
@@ -1078,14 +1374,6 @@
         query_proj, text_kv, grad_crossed, text_windows, text_len
     )
     grad_part, grad_gain_c = cross_back(matmul_nt(grad_query, query_w))
-    grad_keyval = lax.psum_scatter(grad_keyval, "band", scatter_dimension=1, tiled=True)
-    grad_keyval = lax.all_gather(grad_keyval, "clip", axis=0, tiled=True)
-    grad_w_ckv = matmul_tn(
-        all_text.reshape(clip_count * TEXT_PAD, deep_rows).astype(jnp.float32),
-        grad_keyval,
-        lax.Precision.HIGHEST,
-    )
-    grad_w_ckv = lax.all_gather(grad_w_ckv, "band", axis=1, tiled=True)
     grad_stream = grad_stream + grad_part
     grad_proj = (mod_b[2] * grad_stream).astype(jnp.bfloat16)
     grad_gate_b = jnp.sum(grad_stream * proj_b, 0)
@@ -1133,8 +1421,6 @@
     grad_small = jnp.concatenate(
         [grad_patch, grad_head, grad_bias[None], grad_gain_c[None], grad_gain_f[None]], 0
     )
-    all_grad_modul = lax.all_gather(lax.psum(grad_modul, "band"), "clip", axis=0, tiled=True)
-    grad_w_ada = matmul_tn(time_rows.astype(jnp.float32), all_grad_modul, lax.Precision.HIGHEST)
     factors = mlp_factors_b + (
         (crossed, grad_cross),
         (cross_in, grad_query),
@@ -1149,21 +1435,47 @@
             {"kind": 0, "first": 0, "lefts": (6, 7), "cols": (0, 10 * D)},
             {"kind": 1, "first": 2, "lefts": (8, 9), "cols": (6 * D, 0)},
         )
-        wide_rest, deep_rest, squares = reduce_gradients(
-            phases, [f[0] for f in factors], [f[1] for f in factors], 10 * D + 2 * FF, 2 * D
+        used = 12 * D + grad_small.size
+        vectors = jnp.concatenate(
+            [grad_modul.reshape(-1), grad_small.reshape(-1), loss_part[None]]
         )
-        square_part = jnp.sum(squares) / (band_count // 2)
+        vectors = jnp.pad(vectors, (0, 256 * 128 - vectors.shape[0])).reshape(256, 128)
+        keyvals = grad_keyval.reshape(TEXT_PAD, band_count, kv_cols).transpose(1, 0, 2)
+        wide_rest, deep_rest, squares, all_vectors, grad_w_ckv, kv_squares = reduce_gradients(
+            phases,
+            [f[0] for f in factors],
+            [f[1] for f in factors],
+            vectors,
+            keyvals,
+            all_text.reshape(clip_count * TEXT_PAD, deep_rows),
+            10 * D + 2 * FF,
+            2 * D,
+        )
+        all_vectors = all_vectors.reshape(clip_count, -1)
+        all_grad_modul = all_vectors[:, : 12 * D]
+        small_sum = jnp.sum(all_vectors[:, 12 * D : used], 0).reshape(grad_small.shape)
+        loss_sum = jnp.sum(all_vectors[:, used])
+        square_part = jnp.sum(squares) / (band_count // 2) + jnp.sum(kv_squares)
     else:
         summed = [sum_rows(*pair) for pair in factors]
         wide_rest = jnp.concatenate([summed[i] for i in (9, 5, 8, 4, 3, 2, 7, 1)], 1)
         deep_rest = jnp.concatenate([summed[6], summed[0]], 1)
-        square_part = (jnp.sum(wide_rest**2) + jnp.sum(deep_rest**2)) / band_count
+        grad_keyval = lax.psum_scatter(grad_keyval, "band", scatter_dimension=1, tiled=True)
+        grad_keyval = lax.all_gather(grad_keyval, "clip", axis=0, tiled=True)
+        grad_w_ckv = matmul_tn(
+            all_text.reshape(clip_count * TEXT_PAD, deep_rows).astype(jnp.float32),
+            grad_keyval,
+            lax.Precision.HIGHEST,
+        )
+        grad_w_ckv = lax.all_gather(grad_w_ckv, "band", axis=1, tiled=True)
+        all_grad_modul = lax.all_gather(lax.psum(grad_modul, "band"), "clip", axis=0, tiled=True)
+        loss_sum, small_sum = lax.psum((loss_part, grad_small), ("clip", "band"))
+        square_part = sum(jnp.sum(x * x) for x in (wide_rest, deep_rest, grad_w_ckv)) / band_count
+    grad_w_ada = matmul_tn(time_rows.astype(jnp.float32), all_grad_modul, lax.Precision.HIGHEST)
     wide_sum = jnp.concatenate([grad_w_ada, wide_rest], 1)
     deep_sum = jnp.concatenate([deep_rest[:, :D], grad_w_ckv, deep_rest[:, D:]], 1)
-    square_part += (jnp.sum(grad_w_ada**2) + jnp.sum(grad_w_ckv**2)) / band_count
-    loss_sum, square_sum, small_sum = lax.psum(
-        (loss_part, square_part, grad_small), ("clip", "band")
-    )
+    square_part += jnp.sum(grad_w_ada * grad_w_ada) / band_count
+    square_sum = total_over_devices(square_part)
     grad_norm = jnp.sqrt(square_sum + jnp.sum(small_sum * small_sum))
     factor = CLIP_MAX / jnp.maximum(grad_norm, CLIP_MAX)
     new_wide = adam_update(w_wide, m_wide, v_wide, wide_sum * factor, 0.15)

time: 1240 us -> 1230 us (level)
  Pallas kernels: 660 us -> 781 us
  blocking collectives: 86.7 us -> 6.1 us
  waiting for transfers between devices: 86.4 us -> 47.1 us
    pallas_call x1, Pallas kernels: 329 us -> 440 us  [reduce_gradients(): pl.pallas_call(partial(reduce_kernel, count, tokens, phases), out_shape=(...]
    psum x2 -> x0, blocking collectives: 49.2 us -> none  [the longest x1 37.9 us: per_device(): lax.psum((loss_part, square_part, grad_small), ('clip', 'band'))]
    all_gather x1 -> x0, blocking collectives: 31.4 us -> none  [per_device(): lax.all_gather(lax.psum(grad_modul, 'band'), 'clip', axis=0, tiled=True)]
    reduce_scatter x1 -> x0, waiting for transfers between devices: 26.5 us -> none  [per_device(): lax.psum_scatter(grad_keyval, 'band', scatter_dimension=1, tiled=True)]
    all_gather x2 -> x0, waiting for transfers between devices: 20.9 us -> none  [the longest x1 20.9 us: per_device(): grad_keyval = lax.all_gather(grad_keyval, 'clip', axis=0, tiled=True)]
  transfers between devices with their start and end apart: 12 -> 8, of which waited for: 6 -> 5; matrix products, arithmetic and copies ran while one was open for 15% -> 12% of each run, Pallas kernels for 47% -> 20%
where the time goes in v5:
time: 1230 us; the launch traced here: 1220 us
  Pallas kernels  781 us (63%)
  matrix products  195 us (16%)
  other arithmetic  107 us (9%)
  local copies, waits for them, and re-layouts  56.7 us (5%)
  waiting for transfers between devices  47.1 us (4%)
  between operations  24.5 us (2%)
    pallas_call x1, Pallas kernels, reduce_gradients(): pl.pallas_call(partial(reduce_kernel, count, tokens, phases), out_shape=(...  440 us
    pallas_call x1, Pallas kernels, gather_weights(): pl.pallas_call(partial(gather_kernel, count, [shard.shape for shard in sh...  185 us
    dot_general x14, matrix products, matmul(): return jnp.dot(left_op, right_op, preferred_element_type=jnp.float32)  109 us
    pallas_call x3, Pallas kernels, attend_back(): pl.pallas_call(partial(attend_back_kernel, windows, text_len, sets), grid...  82.3 us
    dot_general x11, matrix products, matmul_nt(): lax.dot_general(left_op, right_op, (((1,), (1,)), ((), ())), preferred_el...  79.8 us
    sub x3, other arithmetic, adam_update(): weight - learn_rate * (first_hat / (jnp.sqrt(second_hat) + ADAM_EPS) + DE...  56.7 us
    pallas_call x3, Pallas kernels, attend(): pl.pallas_call(partial(attend_kernel, windows, text_len, len(key_values))...  36.6 us
    ppermute x4, waiting for transfers between devices, shifted(): lax.ppermute(value, axis, [(i, (i + by) % length) for i in range(length)])  36.3 us
  transfers between devices with their start and end apart: 8, of which 5 were waited for; matrix products, arithmetic and copies ran while one was open for 12% of the time, Pallas kernels for 20%

profile of v5, /device:TPU:0, one launch (start us, length us, event | category | flops | bytes accessed | tf_op | source)
XLA Modules:
  0.0 1223.1 jit_solution(6187465919268224891)
XLA Ops:
  10.6 9.6 convert.17
  20.2 2.3 slice.229.refs_6_
  22.5 2.3 fusion.69
  24.8 2.7 fusion.70
  32.6 27.6 %shard_map.230 = (s32[8,8,128]{2,1,0:T(8,128)}, bf16[8,80,512]{2,1,0:T(8,128)(2,1)}) custom-call(s32[8,128]{1,0:T(8,128)} %pad.12.facts_ref, bf16[8,80,512]{2,1,0:T(8,128)(2,1)} %pad.13.text_ref), custom_call_target="tpu_custom_call" | custom-call | tf_op jit(solution)/shard_map/pallas_call | solution.py:332
  61.1 3.9 fusion.68
  65.7 2.4 fusion.17
  69.0 2.8 fusion.21.refs_9_
  71.8 184.7 %shard_map.231 = (bf16[1024,3072]{1,0:T(8,128)(2,1)}, bf16[1024,3072]{1,0:T(8,128)(2,1)}, bf16[1024,1024]{1,0:T(8,128)(2,1)}, bf16[1024,1024]{1,0:T(8,128)(2,1)}...) custom-call(bf16[128,3072]{1,0:T(8,128)(2,1)} %get-tuple-element.120, ...), custom_call_target="tpu_custom_call" | custom-call | flops 199999995904 | bytes 600000000 | tf_op jit(solution)/shard_map/pallas_call | solution.py:531
  263.0 4.5 convolution_convert_fusion.1.refs_0_.refs_1_.refs_3_
  272.1 3.3 collective-permute-done.refs_2_.refs_4_
  275.4 2.1 copy-done.1
  277.5 11.9 shard_map.232.refs_8_
  289.4 3.2 fusion.67
  293.6 32.8 %multiply_convert_fusion.1 = (bf16[640,4096]{1,0:T(8,128)(2,1)S(1)}, f32[640,4096]{1,0:T(8,128)}, f32[640,4096]{1,0:T(8,128)}) fusion(bf16[640,1024]{1,0:T(8,128)(2,1)S(1)} %add_convert_fusion.5.refs_7_, bf16[1024,4096]{1,0:T(8,128)(2,1)} %get-tuple-element.39), kind=kOutput, calls=%fused_computation.25 | convolution fusion | flops 5539102720 | bytes 35913728 | tf_op jit(solution)/shard_map/dot_general | solution.py:47
  326.5 7.1 fusion.65
  335.3 12.6 %collective-permute-done.1 = bf16[10,32,1024]{2,1,0:T(8,128)(2,1)S(1)} collective-permute-done((bf16[10,32,1024]{2,1,0:T(8,128)(2,1)S(1)}, bf16[10,32,1024]{2,1,0:T(8,128)(2,1)S(1)}, u32[]{:S(2)}, u32[]{:S(2)}) %collective-permute-start.1) | collective-permute-done | bytes 655392 | tf_op jit(solution)/shard_map/ppermute | solution.py:43
  349.2 4.7 convolution_convert_fusion.refs_0_.refs_1_.refs_2_
  353.9 16.4 %shard_map.233 = bf16[640,1024]{1,0:T(8,128)(2,1)S(1)} custom-call(bf16[640,3072]{1,0:T(8,128)(2,1)S(1)} %convolution_convert_fusion.refs_0_.refs_1_.refs_2_, bf16[640,3072]{1,0:T(8,128)(2,1)S(1)} %convolution_convert_fusion.refs_0_.refs_1_.refs_2_, bf16[640,3072]{1,0:T(8,128)(2,1)S(1)} %convolution_convert_fusion.refs_0_.refs_1_.refs_2_), custom_call_target="tpu_custom_call" | custom-call | flops 1677721600 | bytes 10485760 | tf_op jit(solution)/shard_map/pallas_call | solution.py:219
  371.3 2.4 collective-permute-start.2
  381.4 6.1 all_gather.9.refs_1_.refs_2_
  388.9 3.0 fusion.64
  396.5 8.4 shard_map.234.refs_2_
  408.8 31.8 %multiply_convert_fusion = (bf16[640,4096]{1,0:T(8,128)(2,1)}, f32[640,4096]{1,0:T(8,128)}, f32[640,4096]{1,0:T(8,128)}) fusion(bf16[640,1024]{1,0:T(8,128)(2,1)} %add_convert_fusion.3.refs_1_, bf16[1024,4096]{1,0:T(8,128)(2,1)} %all-gather.3.cloned.1.call-done), kind=kOutput, calls=%fused_computation.12 | convolution fusion | flops 5539102720 | bytes 35913728 | tf_op jit(solution)/shard_map/dot_general | solution.py:47
  440.6 11.1 fusion.62
  457.7 17.3 %add_convert_fusion.1.refs_11_ = bf16[640,4096]{1,0:T(8,128)(2,1)} fusion(f32[640,4096]{1,0:T(8,128)} %get-tuple-element.104, f32[640,4096]{1,0:T(8,128)} %get-tuple-element.161, bf16[640,1024]{1,0:T(8,128)(2,1)} %multiply_convert_fusion.5.refs_10_, bf16[4096,1024]{1,0:T(8,128)(2,1)} %all-gather.5.cloned.1.call-done), kind=kOutput, calls=%fused_computation.11 | convolution fusion | flops 5405409280 | bytes 35913728 | tf_op jit(solution)/shard_map/dot_general | solution.py:61
  475.0 10.5 multiply_reduce_fusion.5
  488.9 2.7 convolution_convert_fusion.4.refs_3_
  491.6 13.1 %shard_map.235 = (bf16[640,1024]{1,0:T(8,128)(2,1)S(1)}, f32[80,2048]{1,0:T(8,128)S(1)}) custom-call(bf16[640,1024]{1,0:T(8,128)(2,1)S(1)} %copy-done.9, bf16[80,2048]{1,0:T(8,128)(2,1)S(1)} %copy-done.6, bf16[80,2048]{1,0:T(8,128)(2,1)S(1)} %copy-done.6, bf16[640,1024]{1,0:T(8,128)(2,1)} %convolution_convert_fusion.4.refs_3_), custom_call_target="tpu_custom_call" | custom-call | flops 4194304000 | bytes 10485760 | tf_op jit(solution)/shard_map/pallas_call | solution.py:240
  504.8 2.0 multiply_reduce_fusion.2
  514.1 8.1 collective-permute-done.3
  522.3 28.4 %shard_map.236.refs_15_ = bf16[640,3072]{1,0:T(8,128)(2,1)} custom-call(bf16[640,3072]{1,0:T(8,128)(2,1)} %copy-done.2, bf16[640,3072]{1,0:T(8,128)(2,1)} %copy-done.2, bf16[640,3072]{1,0:T(8,128)(2,1)} %copy-done.2, bf16[640,1024]{1,0:T(8,128)(2,1)S(1)} %bitcast.163), custom_call_target="tpu_custom_call" | custom-call | flops 4194304000 | bytes 10485760 | tf_op jit(solution)/shard_map/pallas_call | solution.py:240
  550.7 7.6 fusion.77
  560.2 15.6 %collective-permute-done.4 = f32[10,32,1024]{2,1,0:T(8,128)S(1)} collective-permute-done((f32[10,32,1024]{2,1,0:T(8,128)S(1)}, f32[10,32,1024]{2,1,0:T(8,128)S(1)}, u32[]{:S(2)}, u32[]{:S(2)}) %collective-permute-start.4) | collective-permute-done | bytes 1310752 | tf_op jit(solution)/shard_map/ppermute | solution.py:43
  582.7 17.8 %add_convert_fusion.refs_17_ = bf16[640,4096]{1,0:T(8,128)(2,1)} fusion(f32[640,4096]{1,0:T(8,128)} %get-tuple-element.110, f32[640,4096]{1,0:T(8,128)} %get-tuple-element.156, bf16[640,1024]{1,0:T(8,128)(2,1)} %multiply_convert_fusion.3.refs_16_, bf16[4096,1024]{1,0:T(8,128)(2,1)} %get-tuple-element.40), kind=kOutput, calls=%fused_computation.10 | convolution fusion | flops 5405409280 | bytes 35913728 | tf_op jit(solution)/shard_map/dot_general | solution.py:61
  600.6 10.3 multiply_reduce_fusion.8
  611.8 2.1 multiply_convert_fusion.2
  616.6 40.7 %shard_map.237 = (bf16[640,1024]{1,0:T(8,128)(2,1)S(1)}, f32[640,2048]{1,0:T(8,128)}, f32[640,2048]{1,0:T(8,128)}) custom-call(bf16[640,3072]{1,0:T(8,128)(2,1)} %copy-done, bf16[640,3072]{1,0:T(8,128)(2,1)} %copy-done, bf16[640,2048]{1,0:T(8,128)(2,1)} %copy-done.3, bf16[640,3072]{1,0:T(8,128)(2,1)} %copy-done, bf16[640,2048]{1,0:T(8,128)(2,1)} %copy-done.3, ...), custom_call_target="tpu_custom_call" | custom-call | flops 4194304000 | bytes 10485760 | tf_op jit(solution)/shard_map/pallas_call | solution.py:240
  659.0 7.4 collective-permute-done.5
  666.4 5.0 add_convert_fusion.2
  671.5 7.6 multiply_reduce_fusion.10
  679.0 2.3 pad_maximum_fusion.refs_19_
  686.9 439.8 %shard_map.238 = (f32[128,18432]{1,0:T(8,128)}, f32[512,2048]{1,0:T(8,128)}, f32[8,512]{1,0:T(8,128)}, f32[8,256,128]{2,1,0:T(8,128)}, f32[512,2048]{1,0:T(8,128...) custom-call(bf16[640,4096]{1,0:T(8,128)(2,1)} %get-tuple-element.103, ...), custom_call_target="tpu_custom_call" | custom-call | flops 299999985664 | bytes 800000000 | tf_op jit(solution)/shard_map/pallas_call | solution.py:1173
  1129.3 5.6 multiply_reduce_fusion
  1137.4 4.0 fusion.71
  1144.0 10.2 shard_map.239
  1157.5 36.5 %multiply_subtract_fusion = (f32[128,30720]{1,0:T(8,128)}, f32[128,30720]{1,0:T(8,128)}, f32[128,30720]{1,0:T(8,128)}) fusion(f32[128,30720]{1,0:T(8,128)} %param.21, f32[]{:T(128)S(6)} %div.219, f32[128,18432]{1,0:T(8,128)} %get-tuple-element.54, f32[128,12288]{1,0:T(8,128)} %get-tuple-element.171, f32[128,30720]{1,0:T(8,128)} %param.22, f32[128,30720]{1,0:T(8,128)} %param.23), kind=kLoop, calls=%fused_computation.3 | loop fusion | flops 66846720 | bytes 110100480 | tf_op jit(solution)/shard_map/sub | solution.py:276
  1194.0 19.5 %multiply_subtract_fusion.1 = (f32[512,4096]{1,0:T(8,128)}, f32[512,4096]{1,0:T(8,128)}, f32[512,4096]{1,0:T(8,128)}) fusion(f32[512,4096]{1,0:T(8,128)} %param.24, f32[]{:T(128)S(6)} %div.219, f32[512,1024]{1,0:T(8,128)} %get-tuple-element.122, f32[512,2048]{1,0:T(8,128)} %get-tuple-element.56, f32[512,1024]{1,0:T(8,128)S(1)} %get-tuple-element.121, ...), kind=kLoop, calls=%fused_computation.42 | loop fusion | flops 37748736 | bytes 58720260 | tf_op jit(solution)/shard_map/sub | solution.py:276
  (374 shorter events, 85.1 us)
Async XLA Ops:
  7.2 401.6 %all-gather.3.cloned.1.call-start = ((), (), s32[]{:S(2)}) async-start(), calls=%async_computation | async-start | bytes 8650752 | tf_op jit(solution)/shard_map/all_gather | solution.py:517
  9.7 430.9 %all-gather.5.cloned.1.call-start = ((), (), s32[]{:S(2)}) async-start(), calls=%async_computation.1 | async-start | bytes 8650752 | tf_op jit(solution)/shard_map/all_gather | solution.py:517
  71.8 185.8 %copy-start.46 = (bf16[19,1024]{1,0:T(8,128)(2,1)S(1)}, bf16[19,1024]{1,0:T(8,128)(2,1)}, u32[]{:S(2)}) copy-start(bf16[19,1024]{1,0:T(8,128)(2,1)} %convert_element_type.141) | copy-start | bytes 116740
  71.8 186.4 %copy-start.60 = (bf16[640,8]{0,1:T(8,128)(2,1)S(1)}, bf16[640,8]{0,1:T(8,128)(2,1)}, u32[]{:S(2)}) copy-start(bf16[640,8]{0,1:T(8,128)(2,1)} %convert_element_type.140) | copy-start | bytes 30724
  258.2 31.2 %copy-start.56 = (f32[1,1024]{1,0:T(1,128)}, f32[1,1024]{1,0:T(1,128)S(1)}, u32[]{:S(2)}) copy-start(f32[1,1024]{1,0:T(1,128)S(1)} %get-tuple-element.138) | copy-start | bytes 12292
  260.5 28.9 %copy-start.98 = (f32[1024]{0:T(1024)}, f32[1024]{0:T(1024)S(1)}, u32[]{:S(2)}) copy-start(f32[1024]{0:T(1024)S(1)} %get-tuple-element.150) | copy-start | bytes 12292
  260.5 32.6 %copy-start.79 = (f32[1024]{0:T(1024)}, f32[1024]{0:T(1024)S(1)}, u32[]{:S(2)}) copy-start(f32[1024]{0:T(1024)S(1)} %get-tuple-element.146) | copy-start | bytes 12292
  260.5 65.9 %copy-start.100 = (f32[1024]{0:T(1024)}, f32[1024]{0:T(1024)S(1)}, u32[]{:S(2)}) copy-start(f32[1024]{0:T(1024)S(1)} %get-tuple-element.147) | copy-start | bytes 12292
  260.5 73.6 %copy-start.67 = (f32[1024]{0:T(1024)}, f32[1024]{0:T(1024)S(1)}, u32[]{:S(2)}) copy-start(f32[1024]{0:T(1024)S(1)} %get-tuple-element.143) | copy-start | bytes 12292
  260.5 128.4 %copy-start.69 = (f32[1024]{0:T(1024)}, f32[1024]{0:T(1024)S(1)}, u32[]{:S(2)}) copy-start(f32[1024]{0:T(1024)S(1)} %get-tuple-element.144) | copy-start | bytes 12292
  270.3 5.1 collective-permute-start
  277.5 11.9 copy-start.3
  277.5 11.9 copy-start.16
  277.5 11.9 copy-start.109
  292.6 33.8 %copy-start.18 = (f32[640,1024]{1,0:T(8,128)}, f32[640,1024]{1,0:T(8,128)S(1)}, u32[]{:S(2)}) copy-start(f32[640,1024]{1,0:T(8,128)S(1)} %get-tuple-element.112) | copy-start | bytes 7864324
  292.6 33.8 %slice-start.2 = ((s8[8388608]{0:T(1024)(128)(4,1)}), s8[4194304]{0:T(1024)(128)(4,1)S(1)}, s32[]{:S(2)}) async-start(s8[8388608]{0:T(1024)(128)(4,1)} %bitcast.215), calls=%async_computation.4 | async-start | bytes 8388608
  292.6 56.6 %slice-start = ((s8[6291456]{0:T(1024)(128)(4,1)}), s8[4194304]{0:T(1024)(128)(4,1)S(1)}, s32[]{:S(2)}) async-start(s8[6291456]{0:T(1024)(128)(4,1)} %bitcast.213), calls=%async_computation.2 | async-start | bytes 8388608
  293.0 33.4 %copy-start.90 = (f32[640]{0:T(1024)}, f32[640]{0:T(1024)S(1)}, u32[]{:S(2)}) copy-start(f32[640]{0:T(1024)S(1)} %multiply_reduce_fusion.20) | copy-start | bytes 7684
  293.0 33.4 %copy-start.82 = (f32[640]{0:T(1024)}, f32[640]{0:T(1024)S(1)}, u32[]{:S(2)}) copy-start(f32[640]{0:T(1024)S(1)} %fusion.42) | copy-start | bytes 7684
  293.6 32.8 %copy-start.39 = (bf16[640,1024]{1,0:T(8,128)(2,1)}, bf16[640,1024]{1,0:T(8,128)(2,1)S(1)}, u32[]{:S(2)}) copy-start(bf16[640,1024]{1,0:T(8,128)(2,1)S(1)} %add_convert_fusion.5.refs_7_) | copy-start | bytes 3932164
  293.6 32.8 %slice-start.3 = ((s8[8388608]{0:T(1024)(128)(4,1)}), s8[4194304]{0:T(1024)(128)(4,1)S(1)}, s32[]{:S(2)}) async-start(s8[8388608]{0:T(1024)(128)(4,1)} %bitcast.215), calls=%async_computation.5 | async-start | bytes 8388608
  293.6 55.6 %slice-start.1 = ((s8[6291456]{0:T(1024)(128)(4,1)}), s8[2097152]{0:T(1024)(128)(4,1)S(1)}, s32[]{:S(2)}) async-start(s8[6291456]{0:T(1024)(128)(4,1)} %bitcast.213), calls=%async_computation.3 | async-start | bytes 4194304
  333.6 55.3 %copy-start.11 = (f32[640,1024]{1,0:T(8,128)}, f32[640,1024]{1,0:T(8,128)S(1)}, u32[]{:S(2)}) copy-start(f32[640,1024]{1,0:T(8,128)S(1)} %get-tuple-element.108) | copy-start | bytes 7864324
  335.0 13.0 %collective-permute-start.1 = (bf16[10,32,1024]{2,1,0:T(8,128)(2,1)S(1)}, bf16[10,32,1024]{2,1,0:T(8,128)(2,1)S(1)}, u32[]{:S(2)}, u32[]{:S(2)}) collective-permute-start(bf16[10,32,1024]{2,1,0:T(8,128)(2,1)S(1)} %get-tuple-element.132), channel_id=1, source_target_pairs={{0,3},{1,0},{2,1},{3,2},{4,7},{5,4},{6,5},{7,6},{8,11},{9,8},{10,9... | collective-permute-start | bytes 1966088 | tf_op jit(solution)/shard_map/ppermute | solution.py:43
  353.9 16.4 %copy-start.2 = (bf16[640,3072]{1,0:T(8,128)(2,1)}, bf16[640,3072]{1,0:T(8,128)(2,1)S(1)}, u32[]{:S(2)}) copy-start(bf16[640,3072]{1,0:T(8,128)(2,1)S(1)} %convolution_convert_fusion.refs_0_.refs_1_.refs_2_) | copy-start | bytes 11796484
  371.3 16.3 %collective-permute-start.2 = (bf16[10,32,1024]{2,1,0:T(8,128)(2,1)}, bf16[10,32,1024]{2,1,0:T(8,128)(2,1)}, u32[]{:S(2)}, u32[]{:S(2)}) collective-permute-start(bf16[10,32,1024]{2,1,0:T(8,128)(2,1)} %get-tuple-element.130), channel_id=1, source_target_pairs={{0,1},{1,2},{2,3},{3,0},{4,5},{5,6},{6,7},{7,4},{8,9},{9,10},{10,1... | collective-permute-start | bytes 1966088 | tf_op jit(solution)/shard_map/ppermute | solution.py:43
  387.5 9.0 copy-start.5
  391.9 13.0 %copy-start.13 = (f32[640,1024]{1,0:T(8,128)}, f32[640,1024]{1,0:T(8,128)S(1)}, u32[]{:S(2)}) copy-start(f32[640,1024]{1,0:T(8,128)S(1)} %get-tuple-element.106) | copy-start | bytes 7864324
  407.0 33.6 %copy-start.96 = (f32[640]{0:T(1024)}, f32[640]{0:T(1024)S(1)}, u32[]{:S(2)}) copy-start(f32[640]{0:T(1024)S(1)} %multiply_reduce_fusion.17) | copy-start | bytes 7684
  408.8 31.8 %copy-start.105 = (f32[1024]{0:T(1024)S(1)}, f32[1024]{0:T(1024)}, u32[]{:S(2)}) copy-start(f32[1024]{0:T(1024)} %get-tuple-element.139) | copy-start | bytes 12292
  475.0 10.5 copy-start.97
  491.6 13.2 %copy-start.14 = (f32[640,1024]{1,0:T(8,128)S(1)}, f32[640,1024]{1,0:T(8,128)}, u32[]{:S(2)}) copy-start(f32[640,1024]{1,0:T(8,128)} %copy-done.13) | copy-start | bytes 7864324
  491.6 13.2 %copy-start.63 = (f32[640]{0:T(1024)S(1)}, f32[640]{0:T(1024)}, u32[]{:S(2)}) copy-start(f32[640]{0:T(1024)} %copy-done.62) | copy-start | bytes 7684
  491.6 13.2 %copy-start.76 = (f32[640]{0:T(1024)S(1)}, f32[640]{0:T(1024)}, u32[]{:S(2)}) copy-start(f32[640]{0:T(1024)} %copy-done.75) | copy-start | bytes 7684
  491.6 13.2 %copy-start.78 = (f32[1,1024]{1,0:T(1,128)S(1)}, f32[1,1024]{1,0:T(1,128)}, u32[]{:S(2)}) copy-start(f32[1,1024]{1,0:T(1,128)} %get-tuple-element.137) | copy-start | bytes 12292
  491.6 13.2 %copy-start.114 = (bf16[1024,1024]{1,0:T(8,128)(2,1)S(1)}, bf16[1024,1024]{1,0:T(8,128)(2,1)}, u32[]{:S(2)}) copy-start(bf16[1024,1024]{1,0:T(8,128)(2,1)} %get-tuple-element.43) | copy-start | bytes 6291460
  513.4 8.8 collective-permute-start.3
  558.5 17.3 %collective-permute-start.4 = (f32[10,32,1024]{2,1,0:T(8,128)S(1)}, f32[10,32,1024]{2,1,0:T(8,128)S(1)}, u32[]{:S(2)}, u32[]{:S(2)}) collective-permute-start(f32[10,32,1024]{2,1,0:T(8,128)S(1)} %get-tuple-element.127), channel_id=1, source_target_pairs={{0,1},{1,2},{2,3},{3,0},{4,5},{5,6},{6,7},{7,4},{8,9},{9,10},{10,1... | collective-permute-start | bytes 3932168 | tf_op jit(solution)/shard_map/ppermute | solution.py:43
  582.7 17.8 %copy-start.19 = (f32[640,1024]{1,0:T(8,128)S(1)}, f32[640,1024]{1,0:T(8,128)}, u32[]{:S(2)}) copy-start(f32[640,1024]{1,0:T(8,128)} %copy-done.18) | copy-start | bytes 7864324
  582.7 17.8 %copy-start.66 = (f32[640]{0:T(1024)S(1)}, f32[640]{0:T(1024)}, u32[]{:S(2)}) copy-start(f32[640]{0:T(1024)} %copy-done.65) | copy-start | bytes 7684
  582.7 17.8 %copy-start.80 = (f32[1024]{0:T(1024)S(1)}, f32[1024]{0:T(1024)}, u32[]{:S(2)}) copy-start(f32[1024]{0:T(1024)} %copy-done.79) | copy-start | bytes 12292
  582.7 17.8 %copy-start.83 = (f32[640]{0:T(1024)S(1)}, f32[640]{0:T(1024)}, u32[]{:S(2)}) copy-start(f32[640]{0:T(1024)} %copy-done.82) | copy-start | bytes 7684
  600.6 10.3 copy-start.91
  616.6 41.7 %copy-start.25 = (bf16[640,1024]{1,0:T(8,128)(2,1)S(1)}, bf16[640,1024]{1,0:T(8,128)(2,1)}, u32[]{:S(2)}) copy-start(bf16[640,1024]{1,0:T(8,128)(2,1)} %copy-done.24) | copy-start | bytes 3932164
  657.3 9.1 collective-permute-start.5
  1137.4 19.4 %copy-start.45 = (f32[19,1024]{1,0:T(8,128)S(1)}, f32[19,1024]{1,0:T(8,128)}, u32[]{:S(2)}) copy-start(f32[19,1024]{1,0:T(8,128)} %param.27) | copy-start | bytes 233476
  1137.4 19.4 %copy-start.58 = (f32[19,1024]{1,0:T(8,128)S(1)}, f32[19,1024]{1,0:T(8,128)}, u32[]{:S(2)}) copy-start(f32[19,1024]{1,0:T(8,128)} %param.28) | copy-start | bytes 233476
  1137.4 19.4 %copy-start.59 = (f32[19,1024]{1,0:T(8,128)S(1)}, f32[19,1024]{1,0:T(8,128)}, u32[]{:S(2)}) copy-start(f32[19,1024]{1,0:T(8,128)} %param.29) | copy-start | bytes 233476
  (81 other events, 242.5 us)
Sparse Core Ops, SparseCore 0:
  10.9 105.5 all-gather.2
  272.2 83.3 all-gather.4

commit v6 on v5

--- a/solution.py
+++ b/solution.py
@@ -252,17 +252,19 @@
     mlp_val, norm_back = jax.vjp(norm_modulated, stream, modul[3], modul[4])
     mlp_in = mlp_val.astype(jnp.bfloat16)
     up_proj = matmul(mlp_in, up_weight)
-    gelu_val, gelu_back = jax.vjp(partial(jax.nn.gelu, approximate=False), up_proj)
+    share = 0.5 + 0.5 * lax.erf(up_proj * math.sqrt(0.5))
+    gelu_val = up_proj * share
+    slope = share + up_proj * (jnp.exp(-0.5 * up_proj * up_proj) / math.sqrt(2.0 * math.pi))
     gelu_low = gelu_val.astype(jnp.bfloat16)
     down_proj = matmul(gelu_low, down_weight)
-    return (stream + modul[5] * down_proj, (norm_back, mlp_in, gelu_back, gelu_low, down_proj))
+    return (stream + modul[5] * down_proj, (norm_back, mlp_in, slope, gelu_low, down_proj))
 
 
 def mlp_backward(grad_stream, modul, up_weight, down_weight, saved):
-    norm_back, mlp_in, gelu_back, gelu_low, down_proj = saved
+    norm_back, mlp_in, slope, gelu_low, down_proj = saved
     grad_down = (modul[5] * grad_stream).astype(jnp.bfloat16)
     grad_gate = jnp.sum(grad_stream * down_proj, 0)
-    grad_up = gelu_back(matmul_nt(grad_down, down_weight))[0].astype(jnp.bfloat16)
+    grad_up = (slope * matmul_nt(grad_down, down_weight)).astype(jnp.bfloat16)
     grad_part, grad_shift, grad_scale = norm_back(matmul_nt(grad_up, up_weight))
     factors = ((gelu_low, grad_down), (mlp_in, grad_up))
     return (grad_stream + grad_part, factors, (grad_shift, grad_scale, grad_gate))
@@ -556,12 +558,8 @@
 
 def unit_parts(kind, first):
     if kind == 0:
-        return ((0, 4, lambda u: u, lambda u: 0), (4, 2, lambda u: 4, lambda u: u - 3))
-    return ((first, 3 - first, lambda u: u, lambda u: u), (3, 1, lambda u: 3, lambda u: u))
-
-
-def carried(parts, part):
-    return pl.ds(parts[part][0], parts[part][1] + part)
+        return ((0, 4, lambda u: u, lambda u: 0), (4, 4, lambda u: 4, lambda u: u - 3))
+    return ((first, 3 - first, lambda u: u, lambda u: u), (3, 3, lambda u: 3, lambda u: u))
 
 
 def reduce_kernel(count, tokens, phases, *refs):
@@ -592,13 +590,6 @@
         out_sem,
         out_send,
         out_recv,
-        cross_put,
-        cross_put_scale,
-        cross_got,
-        cross_got_scale,
-        cross_send,
-        cross_recv,
-        cross_credit,
         vec_got,
         kv_got,
         vec_sum,
@@ -725,7 +716,7 @@
 
     def ring_copies(at, part, slot):
         kind = phases[at]["kind"]
-        units = carried(unit_parts(kind, phases[at]["first"]), part)
+        units = pl.ds(*unit_parts(kind, phases[at]["first"])[part][:2])
         return [
             pltpu.make_async_remote_copy(
                 put.at[slot, units],
@@ -740,9 +731,6 @@
             )
         ]
 
-    def split_base(at):
-        return 6 if phases[at]["kind"] == 0 else 4
-
     def plane_copy(at, part):
         kind = phases[at]["kind"]
         start, many = unit_parts(kind, phases[at]["first"])[part][:2]
@@ -755,34 +743,6 @@
             mirror,
             MESH,
         )
-
-    def split_copy(at):
-        unit = split_base(at) + plane
-        return pltpu.make_async_remote_copy(
-            plane_put[phases[at]["kind"]].at[unit],
-            plane_got[at].at[unit],
-            plane_send.at[at, 2],
-            plane_recv.at[at, 2],
-            mirror,
-            MESH,
-        )
-
-    def split_arrival(at):
-        unit = split_base(at) + 1 - plane
-        here = plane_got[at].at[unit]
-        return pltpu.make_async_remote_copy(
-            here, here, plane_send.at[at, 2], plane_recv.at[at, 2], mirror, MESH
-        )
-
-    def cross_copies(slot):
-        return [
-            pltpu.make_async_remote_copy(
-                put.at[slot], got.at[slot], cross_send.at[slot, i], cross_recv.at[slot, i], mirror, MESH
-            )
-            for i, (put, got) in enumerate(
-                ((cross_put, cross_got), (cross_put_scale, cross_got_scale))
-            )
-        ]
 
     def out_copies(at, unit):
         phase = phases[at]
@@ -837,29 +797,11 @@
             for far in range(2):
                 start(load_left(at, step + 1, before, far))
         parts = unit_parts(kind, phase["first"])
-        theirs = split_base(at) + 1 - plane
-        ours = split_base(at) + plane
-
         def encode(term):
             largest = jnp.maximum(jnp.max(jnp.abs(term), axis=0, keepdims=True), WIRE_LEAST)
             low = jnp.round(term * (WIRE_MAX / largest)).astype(jnp.int16)
             return low, largest * (1.0 / WIRE_MAX)
 
-        def spend_cross():
-            for copy in cross_copies(slot):
-                copy.wait_send()
-            pl.semaphore_wait(cross_credit, 1)
-
-        if at or last:
-            spend_cross()
-        elif not first:
-            pl.when(step >= 2)(spend_cross)
-        low_part, scale_part = encode(
-            product(kind, slot, parts[1][2](theirs), parts[1][3](theirs))
-        )
-        cross_put[slot] = low_part
-        cross_put_scale[slot] = scale_part
-        start(cross_copies(slot))
         for part, (low, many, left_of, right_of) in enumerate(parts):
             if not first:
                 for copy in ring_copies(at, part, before):
@@ -887,27 +829,8 @@
             def _(unit, left_of=left_of, right_of=right_of):
                 settle(unit, unit, product(kind, slot, left_of(unit), right_of(unit)))
 
-            if part:
-                for copy in cross_copies(slot):
-                    copy.wait_recv()
-                came = cross_got[slot].astype(jnp.float32) * cross_got_scale[slot]
-                settle(low + many, ours, product(kind, slot, left_of(ours), right_of(ours)) + came)
-                final = at + 1 == len(phases)
-
-                def credit_cross():
-                    pl.semaphore_signal(
-                        cross_credit, inc=1, device_id=mirror, device_id_type=MESH
-                    )
-
-                if not final or first:
-                    credit_cross()
-                elif not last:
-                    pl.when(step < count - 2)(credit_cross)
-
             if last:
                 plane_copy(at, part).start()
-                if part:
-                    split_copy(at).start()
             else:
                 start(ring_copies(at, part, slot))
             if not (first or last):
@@ -935,13 +858,6 @@
 
             for unit in range(low, low + many):
                 start(out_copies(at, unit))
-        ours = split_base(at) + plane
-        split_copy(at).wait_send()
-        split_arrival(at).wait_recv()
-        plane_got[at][ours] = plane_put[kind][ours]
-        for unit in (split_base(at), split_base(at) + 1):
-            add_square(plane_got[at][unit])
-            start(out_copies(at, unit))
 
     half_rows = pl.ds(pl.multiple_of(core * (vec_sum.shape[0] // 2), 8), vec_sum.shape[0] // 2)
     side_local = [
@@ -994,15 +910,24 @@
             vec, vec, vec_pair_send.at[step], vec_pair_recv.at[step], partner, MESH
         )
 
-    def kv_copies():
-        width = kv_grad.shape[1]
-        there = kv_out.at[:, pl.ds(pl.multiple_of(band * width, 128), width)]
-        return [pltpu.make_async_copy(kv_grad, there, kv_own)] + [
-            pltpu.make_async_remote_copy(
-                kv_grad, there, kv_send.at[step], kv_recv.at[step], peer, MESH
-            )
-            for step, peer in enumerate(band_peers)
-        ]
+    kv_width = kv_grad.shape[1]
+
+    def kv_place(owner):
+        return kv_out.at[:, pl.ds(pl.multiple_of(owner * kv_width, 128), kv_width)]
+
+    def kv_copy(i):
+        if i == 2:
+            return pltpu.make_async_copy(kv_grad, kv_place(band), kv_own)
+        peer = (partner, mirror)[i]
+        return pltpu.make_async_remote_copy(
+            kv_grad, kv_place(band), kv_send.at[i], kv_recv.at[i], peer, MESH
+        )
+
+    def kv_passed():
+        there = kv_place(mirror[1])
+        return pltpu.make_async_remote_copy(
+            there, there, kv_send.at[2], kv_recv.at[2], partner, MESH
+        )
 
     def sum_bands():
         finish(side_local + side_remote)
@@ -1029,7 +954,7 @@
             total = total + matmul_tn(text_buf[...], part)
         kv_grad[...] = total
         kv_square[...] = jnp.sum((total * total).reshape(-1, 8, total.shape[1]), axis=0)
-        start(kv_copies())
+        start([kv_copy(i) for i in range(3)])
 
     square_buf[...] = jnp.zeros_like(square_buf)
     start(side_local + side_remote)
@@ -1085,14 +1010,17 @@
             for slot in range(2):
                 for copy in ring_copies(at, part, slot):
                     copy.wait_send()
+        if at == 1:
+            kv_copy(1).wait_recv()
+            kv_passed().start()
         if at:
             close(at - 1)
     close(len(phases) - 1)
-    for slot in range(2):
-        for copy in cross_copies(slot):
-            copy.wait_send()
     vec_own.wait()
-    finish(kv_copies())
+    kv_passed().wait()
+    kv_copy(0).wait()
+    kv_copy(1).wait_send()
+    kv_copy(2).wait()
 
     @pl.loop(0, count - 1)
     def _(step):
@@ -1141,18 +1069,13 @@
         dma((2, 2, 2, 2)),
         dma((2, 2, 2, 2)),
         pltpu.SemaphoreType.REGULAR((2, 2)),
-        dma((len(phases), 3)),
-        dma((len(phases), 3)),
+        dma((len(phases), 2)),
+        dma((len(phases), 2)),
         dma((len(phases), 8)),
         dma((len(phases), 8)),
         dma((len(phases), 8)),
     ]
-    for _ in range(2):
-        scratch += [pltpu.VMEM((2,) + UNIT, jnp.int16), pltpu.VMEM((2, 1, UNIT[1]), jnp.float32)]
     scratch += [
-        dma((2, 2)),
-        dma((2, 2)),
-        pltpu.SemaphoreType.REGULAR,
         pltpu.VMEM((band_count,) + vectors.shape, jnp.float32),
         pltpu.VMEM(keyvals.shape, jnp.float32),
         pltpu.VMEM(vectors.shape, jnp.float32),
@@ -1167,8 +1090,8 @@
         dma((count - 1,)),
         dma((count - 1,)),
         dma,
-        dma((band_count - 1,)),
-        dma((band_count - 1,)),
+        dma((3,)),
+        dma((3,)),
     ]
     out = pl.pallas_call(
         partial(reduce_kernel, count, tokens, phases),
@@ -1286,27 +1209,24 @@
         w_deep, (0, D + band_at * kv_cols), (deep_rows, kv_cols)
     ).astype(jnp.bfloat16)
     part_kv = matmul(all_text.reshape(clip_count * TEXT_PAD, deep_rows), kv_weight)
-    edges = (12 * D, 15 * D, 18 * D, 19 * D, 20 * D, 21 * D, 22 * D, 22 * D + FF)
-    shards = [w_wide[:, low:high].astype(jnp.bfloat16) for low, high in zip(edges, edges[1:])]
-    shards += [w_deep[:, :D].astype(jnp.bfloat16)]
+    qkv_b_w = gather_quarters(w_wide[:, 15 * D : 18 * D])
+    small_b_w = gather_quarters(w_wide[:, 19 * D : 22 * D])
     up_b_w = gather_quarters(w_wide[:, 22 * D + FF :])
     down_b_w = gather_quarters(w_deep[:, 3 * D :])
+    out_b_w, query_w, cross_out_w = (small_b_w[:, i * D : (i + 1) * D] for i in range(3))
+    shards = (
+        w_wide[:, 12 * D : 15 * D].astype(jnp.bfloat16),
+        w_wide[:, 18 * D : 19 * D].astype(jnp.bfloat16),
+        w_wide[:, 22 * D : 22 * D + FF].astype(jnp.bfloat16),
+        w_deep[:, :D].astype(jnp.bfloat16),
+    )
     gathered, all_modul, all_kv = gather_weights(
         shards,
-        (0, 0, 1, 2, 1, 2, 1, 2),
+        (0, 0, 1, 2),
         part_modul.reshape(clip_count, 12 * D // 128, 128),
         part_kv.reshape(clip_count, TEXT_PAD, kv_cols),
     )
-    (
-        qkv_a_w,
-        qkv_b_w,
-        out_a_w,
-        out_b_w,
-        query_w,
-        cross_out_w,
-        up_a_w,
-        down_a_w,
-    ) = gathered
+    qkv_a_w, out_a_w, up_a_w, down_a_w = gathered
     keyval = lax.all_gather(jnp.sum(all_kv, 0).astype(jnp.bfloat16), "band", axis=1, tiled=True)
     small_low = w_small.astype(jnp.bfloat16)
     small_val = small_low.astype(jnp.float32)

time: 1230 us -> 1110 us (0.902)
  Pallas kernels: 781 us -> 709 us
  matrix products: 195 us -> 157 us
    pallas_call x1, Pallas kernels: 440 us -> 360 us  [reduce_gradients(): pl.pallas_call(partial(reduce_kernel, count, tokens, phases), out_shape=(...]
    dot_general x14, matrix products: 109 us -> 72.4 us  [matmul(): return jnp.dot(left_op, right_op, preferred_element_type=jnp.float32)]
    pallas_call x1, Pallas kernels: 185 us -> 198 us  [gather_weights(): pl.pallas_call(partial(gather_kernel, count, [shard.shape for shard in sh...]
  transfers between devices with their start and end apart: 8 -> 10, of which waited for: 5 -> 5; matrix products, arithmetic and copies ran while one was open for 12% -> 10% of each run, Pallas kernels for 20% -> 23%
where the time goes in v6:
time: 1110 us; the launch traced here: 1100 us
  Pallas kernels  709 us (64%)
  matrix products  157 us (14%)
  other arithmetic  106 us (10%)
  local copies, waits for them, and re-layouts  51.8 us (5%)
  waiting for transfers between devices  42.8 us (4%)
  between operations  23.7 us (2%)
    pallas_call x1, Pallas kernels, reduce_gradients(): pl.pallas_call(partial(reduce_kernel, count, tokens, phases), out_shape=(...  360 us
    pallas_call x1, Pallas kernels, gather_weights(): pl.pallas_call(partial(gather_kernel, count, [shard.shape for shard in sh...  198 us
    pallas_call x3, Pallas kernels, attend_back(): pl.pallas_call(partial(attend_back_kernel, windows, text_len, sets), grid...  82.6 us
    dot_general x11, matrix products, matmul_nt(): lax.dot_general(left_op, right_op, (((1,), (1,)), ((), ())), preferred_el...  77.5 us
    dot_general x14, matrix products, matmul(): return jnp.dot(left_op, right_op, preferred_element_type=jnp.float32)  72.4 us
    sub x3, other arithmetic, adam_update(): weight - learn_rate * (first_hat / (jnp.sqrt(second_hat) + ADAM_EPS) + DE...  56.9 us
    pallas_call x3, Pallas kernels, attend(): pl.pallas_call(partial(attend_kernel, windows, text_len, len(key_values))...  36.6 us
    ppermute x4, waiting for transfers between devices, shifted(): lax.ppermute(value, axis, [(i, (i + by) % length) for i in range(length)])  32.6 us
  transfers between devices with their start and end apart: 10, of which 5 were waited for; matrix products, arithmetic and copies ran while one was open for 10% of the time, Pallas kernels for 23%

profile of v6, /device:TPU:0, one launch (start us, length us, event | category | flops | bytes accessed | tf_op | source)
XLA Modules:
  0.0 1103.0 jit_solution(17016355301898185722)
XLA Ops:
  14.2 9.6 convert.13
  25.6 2.1 slice.223.refs_0_
  27.7 2.3 slice.225.refs_2_
  35.1 21.7 %shard_map.230 = (s32[8,8,128]{2,1,0:T(8,128)}, bf16[8,80,512]{2,1,0:T(8,128)(2,1)}) custom-call(s32[8,128]{1,0:T(8,128)} %pad.12.facts_ref, bf16[8,80,512]{2,1,0:T(8,128)(2,1)} %pad.13.text_ref), custom_call_target="tpu_custom_call" | custom-call | tf_op jit(solution)/shard_map/pallas_call | solution.py:334
  57.7 3.9 fusion.91
  62.4 2.4 fusion.41
  65.6 2.8 fusion.45.refs_5_
  68.4 198.3 %shard_map.231 = (bf16[1024,3072]{1,0:T(8,128)(2,1)}, bf16[1024,1024]{1,0:T(8,128)(2,1)}, bf16[1024,4096]{1,0:T(8,128)(2,1)}, bf16[4096,1024]{1,0:T(8,128)(2,1)}...) custom-call(bf16[128,3072]{1,0:T(8,128)(2,1)} %slice.223.refs_0_, bf16[128,1024]{1,0:T(8,128)(2,1)} %slice.224.refs_1_, ...), custom_call_target="tpu_custom_call" | custom-call | flops 199999995904 | bytes 600000000 | tf_op jit(solution)/shard_map/pallas_call | solution.py:533
  270.1 2.6 copy-done.76
  272.7 4.5 convolution_convert_fusion.1.refs_0_.refs_1_.refs_3_
  281.8 3.7 collective-permute-done.refs_2_.refs_4_
  287.6 11.9 %shard_map.232.refs_8_ = bf16[640,1024]{1,0:T(8,128)(2,1)S(1)} custom-call(bf16[640,3072]{1,0:T(8,128)(2,1)S(1)} %copy-done.1, bf16[640,3072]{1,0:T(8,128)(2,1)S(1)} %copy-done.1, bf16[640,2048]{1,0:T(8,128)(2,1)S(1)} %collective-permute-done.refs_2_.refs_4_, bf16[640,3072]{1,0:T(8,128)(2,1)S(1)} %copy-done.1, ...), custom_call_target="tpu_custom_call" | custom-call | flops 1677721600 | bytes 10485760 | tf_op jit(solution)/shard_map/pallas_call | solution.py:219
  299.6 3.2 fusion.89
  304.0 8.2 multiply_convert_fusion.1
  312.2 11.1 %fusion.88 = (f32[640]{0:T(1024)S(1)}, f32[640,1024]{1,0:T(8,128)S(1)}, f32[640,1024]{1,0:T(8,128)}) fusion(f32[640,1024]{1,0:T(8,128)S(1)} %get-tuple-element.100, f32[1024]{0:T(1024)S(1)} %get-tuple-element.131, bf16[640,4096]{1,0:T(8,128)(2,1)S(1)} %get-tuple-element.140.refs_6_, bf16[4096,1024]{1,0:T(8,128)(2,1)} %get-tuple-element.36), kind=kOutput, calls=%fused_computation.221 | convolution fusion | flops 5370674688 | bytes 21502464 | tf_op jit(solution)/shard_map/dot_general | solution.py:47
  325.5 8.1 collective-permute-done.1
  334.8 7.9 convolution_convert_fusion.refs_0_.refs_1_.refs_2_
  342.7 16.4 %shard_map.233 = bf16[640,1024]{1,0:T(8,128)(2,1)S(1)} custom-call(bf16[640,3072]{1,0:T(8,128)(2,1)S(1)} %convolution_convert_fusion.refs_0_.refs_1_.refs_2_, bf16[640,3072]{1,0:T(8,128)(2,1)S(1)} %convolution_convert_fusion.refs_0_.refs_1_.refs_2_, bf16[640,3072]{1,0:T(8,128)(2,1)S(1)} %convolution_convert_fusion.refs_0_.refs_1_.refs_2_), custom_call_target="tpu_custom_call" | custom-call | flops 1677721600 | bytes 10485760 | tf_op jit(solution)/shard_map/pallas_call | solution.py:219
  365.8 7.2 all_gather.17.refs_1_.refs_2_
  373.0 2.4 pad_maximum_fusion.3
  375.5 5.0 fusion.87
  381.3 2.9 copy-done.32
  385.8 8.3 shard_map.234.refs_2_
  397.8 12.0 %multiply_convert_fusion = (bf16[640,4096]{1,0:T(8,128)(2,1)}, f32[640,4096]{1,0:T(8,128)}) fusion(bf16[640,1024]{1,0:T(8,128)(2,1)S(1)} %add_convert_fusion.1.refs_1_, bf16[1024,4096]{1,0:T(8,128)(2,1)} %all-gather.9.cloned.1.call-done), kind=kOutput, calls=%fused_computation.20 | convolution fusion | flops 5381816320 | bytes 25427968 | tf_op jit(solution)/shard_map/dot_general | solution.py:47
  409.8 10.1 fusion.86
  424.4 14.4 %fusion.6.refs_11_ = bf16[640,4096]{1,0:T(8,128)(2,1)} fusion(f32[640,4096]{1,0:T(8,128)} %get-tuple-element.147, bf16[640,1024]{1,0:T(8,128)(2,1)S(1)} %multiply_convert_fusion.5.refs_10_, bf16[4096,1024]{1,0:T(8,128)(2,1)} %all-gather.11.cloned.1.call-done), kind=kOutput, calls=%fused_computation.13 | convolution fusion | flops 5394923520 | bytes 25427968 | tf_op jit(solution)/shard_map/dot_general | solution.py:61
  438.8 10.2 multiply_reduce_fusion.5
  451.5 4.2 fusion.38.refs_3_
  455.7 13.6 %shard_map.235 = (bf16[640,1024]{1,0:T(8,128)(2,1)S(1)}, f32[80,2048]{1,0:T(8,128)S(1)}) custom-call(bf16[640,1024]{1,0:T(8,128)(2,1)S(1)} %fusion.35.refs_0_, bf16[80,2048]{1,0:T(8,128)(2,1)S(1)} %all_gather.17.refs_1_.refs_2_, bf16[80,2048]{1,0:T(8,128)(2,1)S(1)} %all_gather.17.refs_1_.refs_2_, bf16[640,1024]{1,0:T(8,128)(2,1)} %fusion.38.refs_3_), custom_call_target="tpu_custom_call" | custom-call | flops 4194304000 | bytes 10485760 | tf_op jit(solution)/shard_map/pallas_call | solution.py:240
  469.4 4.0 multiply_reduce_fusion.2
  476.2 3.6 fusion.32
  481.3 8.1 collective-permute-done.3
  489.6 28.4 %shard_map.236.refs_15_ = bf16[640,3072]{1,0:T(8,128)(2,1)} custom-call(bf16[640,3072]{1,0:T(8,128)(2,1)} %copy-done.2, bf16[640,3072]{1,0:T(8,128)(2,1)} %copy-done.2, bf16[640,3072]{1,0:T(8,128)(2,1)} %copy-done.2, bf16[640,1024]{1,0:T(8,128)(2,1)S(1)} %bitcast.157), custom_call_target="tpu_custom_call" | custom-call | flops 4194304000 | bytes 10485760 | tf_op jit(solution)/shard_map/pallas_call | solution.py:240
  518.0 6.4 fusion.98
  525.4 16.4 %collective-permute-done.4 = f32[10,32,1024]{2,1,0:T(8,128)S(1)} collective-permute-done((f32[10,32,1024]{2,1,0:T(8,128)S(1)}, f32[10,32,1024]{2,1,0:T(8,128)S(1)}, u32[]{:S(2)}, u32[]{:S(2)}) %collective-permute-start.4) | collective-permute-done | bytes 1310752 | tf_op jit(solution)/shard_map/ppermute | solution.py:43
  547.5 14.3 %fusion.12.refs_17_ = bf16[640,4096]{1,0:T(8,128)(2,1)} fusion(f32[640,4096]{1,0:T(8,128)} %get-tuple-element.141, bf16[640,1024]{1,0:T(8,128)(2,1)S(1)} %multiply_convert_fusion.3.refs_16_, bf16[4096,1024]{1,0:T(8,128)(2,1)} %get-tuple-element.36), kind=kOutput, calls=%fused_computation.19 | convolution fusion | flops 5394923520 | bytes 25427968 | tf_op jit(solution)/shard_map/dot_general | solution.py:61
  561.8 10.3 multiply_reduce_fusion.8
  576.7 40.6 %shard_map.237 = (bf16[640,1024]{1,0:T(8,128)(2,1)S(1)}, f32[640,2048]{1,0:T(8,128)}, f32[640,2048]{1,0:T(8,128)}) custom-call(bf16[640,3072]{1,0:T(8,128)(2,1)} %copy-done, bf16[640,3072]{1,0:T(8,128)(2,1)} %copy-done, bf16[640,2048]{1,0:T(8,128)(2,1)} %copy-done.3, bf16[640,3072]{1,0:T(8,128)(2,1)} %copy-done, bf16[640,2048]{1,0:T(8,128)(2,1)} %copy-done.3, ...), custom_call_target="tpu_custom_call" | custom-call | flops 4194304000 | bytes 10485760 | tf_op jit(solution)/shard_map/pallas_call | solution.py:240
  620.0 6.4 collective-permute-done.5
  626.4 5.0 add_convert_fusion
  631.5 7.6 multiply_reduce_fusion.10
  639.1 2.3 pad_maximum_fusion.refs_19_
  646.9 359.9 %shard_map.238 = (f32[128,18432]{1,0:T(8,128)}, f32[512,2048]{1,0:T(8,128)}, f32[8,512]{1,0:T(8,128)}, f32[8,256,128]{2,1,0:T(8,128)}, f32[512,2048]{1,0:T(8,128...) custom-call(bf16[640,4096]{1,0:T(8,128)(2,1)} %get-tuple-element.146, ...), custom_call_target="tpu_custom_call" | custom-call | flops 299999985664 | bytes 800000000 | tf_op jit(solution)/shard_map/pallas_call | solution.py:1096
  1009.5 5.6 multiply_reduce_fusion
  1017.6 4.0 fusion.92
  1024.1 10.3 shard_map.239
  1037.8 36.7 %multiply_subtract_fusion = (f32[128,30720]{1,0:T(8,128)}, f32[128,30720]{1,0:T(8,128)}, f32[128,30720]{1,0:T(8,128)}) fusion(f32[128,30720]{1,0:T(8,128)} %param.21, f32[]{:T(128)S(6)} %div.227, f32[128,18432]{1,0:T(8,128)} %get-tuple-element.46, f32[128,12288]{1,0:T(8,128)} %get-tuple-element.157, f32[128,30720]{1,0:T(8,128)} %param.22, f32[128,30720]{1,0:T(8,128)} %param.23), kind=kLoop, calls=%fused_computation.3 | loop fusion | flops 66846720 | bytes 110100480 | tf_op jit(solution)/shard_map/sub | solution.py:278
  1074.5 19.5 %multiply_subtract_fusion.1 = (f32[512,4096]{1,0:T(8,128)}, f32[512,4096]{1,0:T(8,128)}, f32[512,4096]{1,0:T(8,128)}) fusion(f32[512,4096]{1,0:T(8,128)} %param.24, f32[]{:T(128)S(6)} %div.227, f32[512,1024]{1,0:T(8,128)} %get-tuple-element.106, f32[512,2048]{1,0:T(8,128)} %get-tuple-element.48, f32[512,1024]{1,0:T(8,128)S(1)} %get-tuple-element.105, ...), kind=kLoop, calls=%fused_computation.26 | loop fusion | flops 37748736 | bytes 58720260 | tf_op jit(solution)/shard_map/sub | solution.py:278
  (305 shorter events, 78.9 us)
Async XLA Ops:
  7.2 327.6 %all-gather.5.cloned.1.call-start = ((), (), s32[]{:S(2)}) async-start(), calls=%async_computation | async-start | bytes 6488064 | tf_op jit(solution)/shard_map/all_gather | solution.py:519
  10.1 365.4 %all-gather.7.cloned.1.call-start = ((), (), s32[]{:S(2)}) async-start(), calls=%async_computation.1 | async-start | bytes 6488064 | tf_op jit(solution)/shard_map/all_gather | solution.py:519
  10.8 387.0 %all-gather.9.cloned.1.call-start = ((), (), s32[]{:S(2)}) async-start(), calls=%async_computation.2 | async-start | bytes 8650752 | tf_op jit(solution)/shard_map/all_gather | solution.py:519
  13.4 396.4 %all-gather.11.cloned.1.call-start = ((), (), s32[]{:S(2)}) async-start(), calls=%async_computation.3 | async-start | bytes 8650752 | tf_op jit(solution)/shard_map/all_gather | solution.py:519
  23.9 7.5 copy-start.36
  23.9 8.1 copy-start.39
  23.9 8.1 copy-start.40
  25.6 8.1 copy-start.33
  68.4 199.3 %copy-start.38 = (bf16[19,1024]{1,0:T(8,128)(2,1)S(1)}, bf16[19,1024]{1,0:T(8,128)(2,1)}, u32[]{:S(2)}) copy-start(bf16[19,1024]{1,0:T(8,128)(2,1)} %convert_element_type.143) | copy-start | bytes 116740
  68.4 199.4 %copy-start.49 = (bf16[640,8]{0,1:T(8,128)(2,1)S(1)}, bf16[640,8]{0,1:T(8,128)(2,1)}, u32[]{:S(2)}) copy-start(bf16[640,8]{0,1:T(8,128)(2,1)} %convert_element_type.142) | copy-start | bytes 30724
  267.7 31.8 %copy-start.45 = (f32[1,1024]{1,0:T(1,128)}, f32[1,1024]{1,0:T(1,128)S(1)}, u32[]{:S(2)}) copy-start(f32[1,1024]{1,0:T(1,128)S(1)} %get-tuple-element.122) | copy-start | bytes 12292
  269.5 7.7 copy-start.61
  269.5 7.7 copy-start.59
  269.5 30.1 %copy-start.67 = (f32[1024]{0:T(1024)}, f32[1024]{0:T(1024)S(1)}, u32[]{:S(2)}) copy-start(f32[1024]{0:T(1024)S(1)} %get-tuple-element.134) | copy-start | bytes 12292
  269.5 33.7 %copy-start.55 = (f32[1024]{0:T(1024)}, f32[1024]{0:T(1024)S(1)}, u32[]{:S(2)}) copy-start(f32[1024]{0:T(1024)S(1)} %get-tuple-element.130) | copy-start | bytes 12292
  280.0 5.5 collective-permute-start
  287.6 11.9 %copy-start.3 = (bf16[640,2048]{1,0:T(8,128)(2,1)}, bf16[640,2048]{1,0:T(8,128)(2,1)S(1)}, u32[]{:S(2)}) copy-start(bf16[640,2048]{1,0:T(8,128)(2,1)S(1)} %collective-permute-done.refs_2_.refs_4_) | copy-start | bytes 7864324
  287.6 11.9 %copy-start.12 = (f32[640,1024]{1,0:T(8,128)S(1)}, f32[640,1024]{1,0:T(8,128)}, u32[]{:S(2)}) copy-start(f32[640,1024]{1,0:T(8,128)} %copy-done.11) | copy-start | bytes 7864324
  287.6 12.0 %copy-start.74 = (bf16[1024,1024]{1,0:T(8,128)(2,1)S(1)}, bf16[1024,1024]{1,0:T(8,128)(2,1)}, u32[]{:S(2)}) copy-start(bf16[1024,1024]{1,0:T(8,128)(2,1)} %get-tuple-element.34) | copy-start | bytes 6291460
  287.6 16.3 %slice-start.2 = ((s8[8388608]{0:T(1024)(128)(4,1)}), s8[4194304]{0:T(1024)(128)(4,1)S(1)}, s32[]{:S(2)}) async-start(s8[8388608]{0:T(1024)(128)(4,1)} %bitcast.209), calls=%async_computation.6 | async-start | bytes 8388608
  302.8 9.4 copy-start.14
  303.2 9.0 copy-start.65
  303.2 9.0 copy-start.57
  304.0 8.2 copy-start.28
  312.2 11.2 %copy-start.77 = (bf16[640,4096]{1,0:T(8,128)(2,1)}, bf16[640,4096]{1,0:T(8,128)(2,1)S(1)}, u32[]{:S(2)}) copy-start(bf16[640,4096]{1,0:T(8,128)(2,1)S(1)} %get-tuple-element.140.refs_6_) | copy-start | bytes 15728644
  323.4 52.1 %copy-start.7 = (f32[640,1024]{1,0:T(8,128)}, f32[640,1024]{1,0:T(8,128)S(1)}, u32[]{:S(2)}) copy-start(f32[640,1024]{1,0:T(8,128)S(1)} %get-tuple-element.98) | copy-start | bytes 7864324
  324.4 9.2 collective-permute-start.1
  342.7 16.4 %copy-start.2 = (bf16[640,3072]{1,0:T(8,128)(2,1)}, bf16[640,3072]{1,0:T(8,128)(2,1)S(1)}, u32[]{:S(2)}) copy-start(bf16[640,3072]{1,0:T(8,128)(2,1)S(1)} %convolution_convert_fusion.refs_0_.refs_1_.refs_2_) | copy-start | bytes 11796484
  360.3 12.7 %collective-permute-start.2 = (bf16[10,32,1024]{2,1,0:T(8,128)(2,1)}, bf16[10,32,1024]{2,1,0:T(8,128)(2,1)}, u32[]{:S(2)}, u32[]{:S(2)}) collective-permute-start(bf16[10,32,1024]{2,1,0:T(8,128)(2,1)} %get-tuple-element.114), channel_id=1, source_target_pairs={{0,1},{1,2},{2,3},{3,0},{4,5},{5,6},{6,7},{7,4},{8,9},{9,10},{10,1... | collective-permute-start | bytes 1966088 | tf_op jit(solution)/shard_map/ppermute | solution.py:43
  380.5 13.6 %copy-start.9 = (f32[640,1024]{1,0:T(8,128)}, f32[640,1024]{1,0:T(8,128)S(1)}, u32[]{:S(2)}) copy-start(f32[640,1024]{1,0:T(8,128)S(1)} %get-tuple-element.96) | copy-start | bytes 7864324
  397.8 12.0 %copy-start.29 = (bf16[640,1024]{1,0:T(8,128)(2,1)}, bf16[640,1024]{1,0:T(8,128)(2,1)S(1)}, u32[]{:S(2)}) copy-start(bf16[640,1024]{1,0:T(8,128)(2,1)S(1)} %add_convert_fusion.1.refs_1_) | copy-start | bytes 3932164
  424.4 14.4 %copy-start.30 = (bf16[640,1024]{1,0:T(8,128)(2,1)}, bf16[640,1024]{1,0:T(8,128)(2,1)S(1)}, u32[]{:S(2)}) copy-start(bf16[640,1024]{1,0:T(8,128)(2,1)S(1)} %multiply_convert_fusion.5.refs_10_) | copy-start | bytes 3932164
  424.4 14.4 %copy-start.17 = (f32[640,1024]{1,0:T(8,128)S(1)}, f32[640,1024]{1,0:T(8,128)}, u32[]{:S(2)}) copy-start(f32[640,1024]{1,0:T(8,128)} %copy-done.16) | copy-start | bytes 7864324
  455.7 13.6 %copy-start.10 = (f32[640,1024]{1,0:T(8,128)S(1)}, f32[640,1024]{1,0:T(8,128)}, u32[]{:S(2)}) copy-start(f32[640,1024]{1,0:T(8,128)} %copy-done.9) | copy-start | bytes 7864324
  479.8 38.2 %slice-start = ((s8[6291456]{0:T(1024)(128)(4,1)}), s8[2097152]{0:T(1024)(128)(4,1)S(1)}, s32[]{:S(2)}) async-start(s8[6291456]{0:T(1024)(128)(4,1)} %bitcast.206), calls=%async_computation.4 | async-start | bytes 4194304
  480.0 9.5 collective-permute-start.3
  489.5 28.4 %slice-start.1 = ((s8[6291456]{0:T(1024)(128)(4,1)}), s8[4194304]{0:T(1024)(128)(4,1)S(1)}, s32[]{:S(2)}) async-start(s8[6291456]{0:T(1024)(128)(4,1)} %bitcast.206), calls=%async_computation.5 | async-start | bytes 8388608
  524.6 17.2 %collective-permute-start.4 = (f32[10,32,1024]{2,1,0:T(8,128)S(1)}, f32[10,32,1024]{2,1,0:T(8,128)S(1)}, u32[]{:S(2)}, u32[]{:S(2)}) collective-permute-start(f32[10,32,1024]{2,1,0:T(8,128)S(1)} %get-tuple-element.111), channel_id=1, source_target_pairs={{0,1},{1,2},{2,3},{3,0},{4,5},{5,6},{6,7},{7,4},{8,9},{9,10},{10,1... | collective-permute-start | bytes 3932168 | tf_op jit(solution)/shard_map/ppermute | solution.py:43
  547.4 14.4 %copy-start.27 = (bf16[640,1024]{1,0:T(8,128)(2,1)}, bf16[640,1024]{1,0:T(8,128)(2,1)S(1)}, u32[]{:S(2)}) copy-start(bf16[640,1024]{1,0:T(8,128)(2,1)S(1)} %multiply_convert_fusion.3.refs_16_) | copy-start | bytes 3932164
  547.5 14.3 %copy-start.15 = (f32[640,1024]{1,0:T(8,128)S(1)}, f32[640,1024]{1,0:T(8,128)}, u32[]{:S(2)}) copy-start(f32[640,1024]{1,0:T(8,128)} %copy-done.14) | copy-start | bytes 7864324
  547.5 14.3 %copy-start.52 = (f32[640]{0:T(1024)S(1)}, f32[640]{0:T(1024)}, u32[]{:S(2)}) copy-start(f32[640]{0:T(1024)} %copy-done.51) | copy-start | bytes 7684
  547.5 14.3 %copy-start.56 = (f32[1024]{0:T(1024)S(1)}, f32[1024]{0:T(1024)}, u32[]{:S(2)}) copy-start(f32[1024]{0:T(1024)} %copy-done.55) | copy-start | bytes 12292
  547.5 14.3 %copy-start.58 = (f32[640]{0:T(1024)S(1)}, f32[640]{0:T(1024)}, u32[]{:S(2)}) copy-start(f32[640]{0:T(1024)} %copy-done.57) | copy-start | bytes 7684
  561.8 10.3 copy-start.66
  617.3 9.1 collective-permute-start.5
  1017.6 19.5 %copy-start.37 = (f32[19,1024]{1,0:T(8,128)S(1)}, f32[19,1024]{1,0:T(8,128)}, u32[]{:S(2)}) copy-start(f32[19,1024]{1,0:T(8,128)} %param.27) | copy-start | bytes 233476
  1017.6 19.5 %copy-start.47 = (f32[19,1024]{1,0:T(8,128)S(1)}, f32[19,1024]{1,0:T(8,128)}, u32[]{:S(2)}) copy-start(f32[19,1024]{1,0:T(8,128)} %param.28) | copy-start | bytes 233476
  1017.6 19.5 %copy-start.48 = (f32[19,1024]{1,0:T(8,128)S(1)}, f32[19,1024]{1,0:T(8,128)}, u32[]{:S(2)}) copy-start(f32[19,1024]{1,0:T(8,128)} %param.29) | copy-start | bytes 233476
  (44 other events, 127.4 us)
Sparse Core Ops, SparseCore 0:
  10.9 91.3 all-gather.4
  105.2 87.7 all-gather.6
  195.8 90.6 all-gather.8
  289.2 78.6 all-gather.10

commit v7 on v6

--- a/solution.py
+++ b/solution.py
@@ -121,13 +121,12 @@
         done += many
 
 
-def softmax_rows(queries, keys, text_len):
-    scores = matmul_nt(queries, keys)
+def softmax_of(scores, axis, text_len):
     if text_len:
-        place = lax.broadcasted_iota(jnp.int32, scores.shape, 1)
+        place = lax.broadcasted_iota(jnp.int32, scores.shape, axis)
         scores = jnp.where(place < text_len, scores, -1e30)
-    weight = jnp.exp(scores - jnp.max(scores, -1, keepdims=True))
-    return weight / jnp.sum(weight, -1, keepdims=True)
+    weight = jnp.exp(scores - jnp.max(scores, axis, keepdims=True))
+    return weight * (1.0 / jnp.sum(weight, axis, keepdims=True))
 
 
 def lanes_of(head, shape):
@@ -153,7 +152,7 @@
         keys, values = key_sets(k_refs, runs, text_len), key_sets(v_refs, runs, text_len)
         outs = []
         for head in range(2):
-            probs = softmax_rows(only(head, queries), keys, text_len)
+            probs = softmax_of(matmul_nt(only(head, queries), keys), 1, text_len)
             outs.append(matmul(probs.astype(jnp.bfloat16), values))
         put(out_ref, slice(None), runs, jnp.where(lanes_of(0, outs[0].shape), *outs))
 
@@ -173,13 +172,13 @@
         grad_out = take(grad_ref, runs)
         dq, dk, dv = [], [], []
         for head in range(2):
-            probs = softmax_rows(only(head, queries), keys, text_len)
-            dprobs = matmul_nt(only(head, grad_out), values)
-            dv.append(matmul_tn(probs.astype(jnp.bfloat16), grad_out))
-            inner = jnp.sum(probs * dprobs, -1, keepdims=True)
+            probs = softmax_of(matmul_nt(keys, only(head, queries)), 0, text_len)
+            dprobs = matmul_nt(values, only(head, grad_out))
+            dv.append(matmul(probs.astype(jnp.bfloat16), grad_out))
+            inner = jnp.sum(probs * dprobs, 0, keepdims=True)
             dscores = (probs * (dprobs - inner)).astype(jnp.bfloat16)
-            dq.append(matmul(dscores, keys))
-            dk.append(matmul_tn(dscores, queries))
+            dk.append(matmul(dscores, queries))
+            dq.append(matmul_tn(dscores, keys))
         dq, dk, dv = (jnp.where(lanes_of(0, x[0].shape), *x) for x in (dq, dk, dv))
         put(dq_ref, cols[0], runs, dq * HEAD_DIM ** (-0.5))
         if merged:
@@ -559,7 +558,9 @@
 def unit_parts(kind, first):
     if kind == 0:
         return ((0, 4, lambda u: u, lambda u: 0), (4, 4, lambda u: 4, lambda u: u - 3))
-    return ((first, 3 - first, lambda u: u, lambda u: u), (3, 3, lambda u: 3, lambda u: u))
+    if first:
+        return ((2, 2, lambda u: u, lambda u: u), (4, 2, lambda u: 3, lambda u: u))
+    return ((0, 3, lambda u: u, lambda u: u), (3, 3, lambda u: 3, lambda u: u))
 
 
 def reduce_kernel(count, tokens, phases, *refs):
@@ -590,6 +591,12 @@
         out_sem,
         out_send,
         out_recv,
+        last_put,
+        last_put_scale,
+        last_got,
+        last_got_scale,
+        push_send,
+        push_recv,
         vec_got,
         kv_got,
         vec_sum,
@@ -731,16 +738,34 @@
             )
         ]
 
-    def plane_copy(at, part):
+    def plane_copies(at, part):
         kind = phases[at]["kind"]
-        start, many = unit_parts(kind, phases[at]["first"])[part][:2]
-        units = pl.ds(start, many)
+        units = pl.ds(*unit_parts(kind, phases[at]["first"])[part][:2])
+        pairs = ((plane_put[kind], plane_got[at]),)
+        if at + 1 == len(phases):
+            pairs = ((last_put, last_got), (last_put_scale, last_got_scale))
+        return [
+            pltpu.make_async_remote_copy(
+                here.at[units],
+                there.at[units],
+                plane_send.at[at, part, i],
+                plane_recv.at[at, part, i],
+                mirror,
+                MESH,
+            )
+            for i, (here, there) in enumerate(pairs)
+        ]
+
+    def push_right(block):
+        operand, which = [entry[1:] for entry in right_blocks(0) if entry[0] == block][0]
+        half = rights[operand].shape[1] // 2
+        begin = pl.multiple_of((1 - core) * half + which * UNIT[1], 128)
         return pltpu.make_async_remote_copy(
-            plane_put[kind].at[units],
-            plane_got[at].at[units],
-            plane_send.at[at, part],
-            plane_recv.at[at, part],
-            mirror,
+            rights[operand].at[:, pl.ds(begin, UNIT[1])],
+            right_buf[phases[0]["kind"]].at[block, pl.ds(tokens, tokens), :],
+            push_send.at[block],
+            push_recv.at[block],
+            partner,
             MESH,
         )
 
@@ -791,18 +816,29 @@
         before = (step + 1) % 2
         for far in range(2):
             finish(load_left(at, step, slot, far))
-        if not last:
+
+        def load_next():
             for copy in pair_left(at, step + 1):
                 copy.wait_recv()
             for far in range(2):
                 start(load_left(at, step + 1, before, far))
+
+        opening = first and at == 0
+        if not (last or opening):
+            load_next()
         parts = unit_parts(kind, phase["first"])
+
         def encode(term):
             largest = jnp.maximum(jnp.max(jnp.abs(term), axis=0, keepdims=True), WIRE_LEAST)
             low = jnp.round(term * (WIRE_MAX / largest)).astype(jnp.int16)
             return low, largest * (1.0 / WIRE_MAX)
 
         for part, (low, many, left_of, right_of) in enumerate(parts):
+            if opening:
+                blocks = range(1) if part == 0 else range(1, 5)
+                finish(load_right(0, 0)[blocks.start : blocks.stop])
+                for block in blocks:
+                    push_right(block).wait_recv()
             if not first:
                 for copy in ring_copies(at, part, before):
                     copy.wait_recv()
@@ -818,7 +854,9 @@
                 if not first:
                     came = got_low[kind][before, position].astype(jnp.float32)
                     term = term + came * got_scale[kind][before, position]
-                if last:
+                if last and at + 1 == len(phases):
+                    last_put[unit], last_put_scale[unit] = encode(term)
+                elif last:
                     plane_put[kind][unit] = term
                 else:
                     low_part, scale_part = encode(term)
@@ -830,7 +868,7 @@
                 settle(unit, unit, product(kind, slot, left_of(unit), right_of(unit)))
 
             if last:
-                plane_copy(at, part).start()
+                start(plane_copies(at, part))
             else:
                 start(ring_copies(at, part, slot))
             if not (first or last):
@@ -841,6 +879,9 @@
                         credit.at[kind, part], inc=1, device_id=preceding, device_id_type=MESH
                     )
 
+        if opening:
+            load_next()
+
     def close(at):
         kind = phases[at]["kind"]
 
@@ -848,11 +889,15 @@
             square_buf[...] += jnp.sum((total * total).reshape(UNIT[0] // 8, 8, UNIT[1]), axis=0)
 
         for part, (low, many, _, _) in enumerate(unit_parts(kind, phases[at]["first"])):
-            plane_copy(at, part).wait()
+            finish(plane_copies(at, part))
 
             @pl.loop(low, low + many)
             def _(unit):
-                total = plane_put[kind][unit] + plane_got[at][unit]
+                if at + 1 == len(phases):
+                    total = last_put[unit].astype(jnp.float32) * last_put_scale[unit]
+                    total += last_got[unit].astype(jnp.float32) * last_got_scale[unit]
+                else:
+                    total = plane_put[kind][unit] + plane_got[at][unit]
                 plane_got[at][unit] = total
                 add_square(total)
 
@@ -959,58 +1004,60 @@
     square_buf[...] = jnp.zeros_like(square_buf)
     start(side_local + side_remote)
     start(load_right(0, 0))
-    start(pair_right(0))
-
-    @pl.loop(0, count)
+    start(load_left(0, 0, 0, 0))
+    push_right(0).start()
+    start(pair_left(0, 0))
+    for block in range(1, 5):
+        push_right(block).start()
+
+    @pl.loop(1, count)
     def _(step):
         start(pair_left(0, step))
 
-    start(load_left(0, 0, 0, 0))
+    for copy in pair_left(0, 0):
+        copy.wait_recv()
+    start(load_left(0, 0, 0, 1))
+    take_step(0, 0, True, False)
     for at in range(len(phases)):
-        if at == 0:
-            for copy in pair_right(0):
-                copy.wait_recv()
-            start(load_right(0, 1))
-            for copy in pair_left(0, 0):
-                copy.wait_recv()
-            start(load_left(0, 0, 0, 1))
-        for far in range(2):
-            finish(load_right(at, far))
         more = at + 1 < len(phases)
         if more:
             start(pair_right(at + 1))
             start(load_right(at + 1, 0))
-        take_step(at, 0, True, False)
-        if at == 0:
+            start(pair_left(at + 1, 0))
+        if at == 1:
             sum_bands()
-        if more:
-            start(pair_left(at + 1, 0))
 
         @pl.loop(1, count - 1)
         def _(step, at=at, more=more):
             take_step(at, step, False, False)
-            if at == 0:
+            if at == 1:
                 pass_sums(step)
             if more:
                 start(pair_left(at + 1, step))
 
+                @pl.when(step == count // 2)
+                def _():
+                    for copy in pair_right(at + 1):
+                        copy.wait_recv()
+                    start(load_right(at + 1, 1))
+                    for copy in pair_left(at + 1, 0):
+                        copy.wait_recv()
+                    for far in range(2):
+                        start(load_left(at + 1, 0, 0, far))
+
         if more:
             start(pair_left(at + 1, count - 1))
-            for copy in pair_right(at + 1):
-                copy.wait_recv()
-            start(load_right(at + 1, 1))
-            for copy in pair_left(at + 1, 0):
-                copy.wait_recv()
             for far in range(2):
-                start(load_left(at + 1, 0, 0, far))
+                finish(load_right(at + 1, far))
+            take_step(at + 1, 0, True, False)
         take_step(at, count - 1, False, True)
-        if at == 0:
+        if at == 1:
             multiply_text()
         for part in range(2):
             for slot in range(2):
                 for copy in ring_copies(at, part, slot):
                     copy.wait_send()
-        if at == 1:
+        if at == 2:
             kv_copy(1).wait_recv()
             kv_passed().start()
         if at:
@@ -1030,7 +1077,7 @@
 
     square_out[...] = square_buf[...]
     for at, phase in enumerate(phases):
-        for copy in pair_right(at):
+        for copy in pair_right(at) if at else [push_right(block) for block in range(5)]:
             copy.wait_send()
 
         @pl.loop(0, count)
@@ -1069,13 +1116,17 @@
         dma((2, 2, 2, 2)),
         dma((2, 2, 2, 2)),
         pltpu.SemaphoreType.REGULAR((2, 2)),
-        dma((len(phases), 2)),
-        dma((len(phases), 2)),
+        dma((len(phases), 2, 2)),
+        dma((len(phases), 2, 2)),
         dma((len(phases), 8)),
         dma((len(phases), 8)),
         dma((len(phases), 8)),
     ]
+    for _ in range(2):
+        scratch += [pltpu.VMEM((6,) + UNIT, jnp.int16), pltpu.VMEM((6, 1, UNIT[1]), jnp.float32)]
     scratch += [
+        dma((5,)),
+        dma((5,)),
         pltpu.VMEM((band_count,) + vectors.shape, jnp.float32),
         pltpu.VMEM(keyvals.shape, jnp.float32),
         pltpu.VMEM(vectors.shape, jnp.float32),
@@ -1209,24 +1260,19 @@
         w_deep, (0, D + band_at * kv_cols), (deep_rows, kv_cols)
     ).astype(jnp.bfloat16)
     part_kv = matmul(all_text.reshape(clip_count * TEXT_PAD, deep_rows), kv_weight)
-    qkv_b_w = gather_quarters(w_wide[:, 15 * D : 18 * D])
-    small_b_w = gather_quarters(w_wide[:, 19 * D : 22 * D])
     up_b_w = gather_quarters(w_wide[:, 22 * D + FF :])
-    down_b_w = gather_quarters(w_deep[:, 3 * D :])
-    out_b_w, query_w, cross_out_w = (small_b_w[:, i * D : (i + 1) * D] for i in range(3))
-    shards = (
-        w_wide[:, 12 * D : 15 * D].astype(jnp.bfloat16),
-        w_wide[:, 18 * D : 19 * D].astype(jnp.bfloat16),
-        w_wide[:, 22 * D : 22 * D + FF].astype(jnp.bfloat16),
-        w_deep[:, :D].astype(jnp.bfloat16),
-    )
+    edges = (12 * D, 15 * D, 18 * D, 19 * D, 20 * D, 21 * D, 22 * D, 22 * D + FF)
+    shards = [w_wide[:, low:high].astype(jnp.bfloat16) for low, high in zip(edges, edges[1:])]
+    shards += [w_deep[:, :D].astype(jnp.bfloat16)]
     gathered, all_modul, all_kv = gather_weights(
         shards,
-        (0, 0, 1, 2),
+        (0, 0, 1, 2, 1, 2, 1, 2),
         part_modul.reshape(clip_count, 12 * D // 128, 128),
         part_kv.reshape(clip_count, TEXT_PAD, kv_cols),
     )
-    qkv_a_w, out_a_w, up_a_w, down_a_w = gathered
+    qkv_a_w, qkv_b_w, out_a_w, out_b_w, query_w, cross_out_w, up_a_w, down_a_w = gathered
+    late_down_b, all_modul = lax.optimization_barrier((w_deep[:, 3 * D :], all_modul))
+    down_b_w = gather_quarters(late_down_b)
     keyval = lax.all_gather(jnp.sum(all_kv, 0).astype(jnp.bfloat16), "band", axis=1, tiled=True)
     small_low = w_small.astype(jnp.bfloat16)
     small_val = small_low.astype(jnp.float32)

time: 1110 us -> 1040 us (0.937)
  Pallas kernels: 709 us -> 650 us
    pallas_call x1, Pallas kernels: 360 us -> 326 us  [reduce_gradients(): pl.pallas_call(partial(reduce_kernel, count, tokens, phases), out_shape=(...]
    pallas_call x3, Pallas kernels: 82.6 us -> 63.1 us  [attend_back(): pl.pallas_call(partial(attend_back_kernel, windows, text_len, sets), grid...]
    pallas_call x1, Pallas kernels: 198 us -> 185 us  [gather_weights(): pl.pallas_call(partial(gather_kernel, count, [shard.shape for shard in sh...]
    unnamed x167 -> x183, local copies, waits for them, and re-layouts: 20.5 us -> 22.9 us
  transfers between devices with their start and end apart: 10 -> 8, of which waited for: 5 -> 5; matrix products, arithmetic and copies ran while one was open for 10% -> 10% of each run, Pallas kernels for 23% -> 24%
where the time goes in v7:
time: 1040 us; the launch traced here: 1030 us
  Pallas kernels  650 us (62%)
  matrix products  149 us (14%)
  other arithmetic  104 us (10%)
  local copies, waits for them, and re-layouts  52 us (5%)
  waiting for transfers between devices  41.7 us (4%)
  between operations  24.2 us (2%)
    pallas_call x1, Pallas kernels, reduce_gradients(): pl.pallas_call(partial(reduce_kernel, count, tokens, phases), out_shape=(...  326 us
    pallas_call x1, Pallas kernels, gather_weights(): pl.pallas_call(partial(gather_kernel, count, [shard.shape for shard in sh...  185 us
    dot_general x11, matrix products, matmul_nt(): lax.dot_general(left_op, right_op, (((1,), (1,)), ((), ())), preferred_el...  74.1 us
    dot_general x14, matrix products, matmul(): return jnp.dot(left_op, right_op, preferred_element_type=jnp.float32)  68.2 us
    pallas_call x3, Pallas kernels, attend_back(): pl.pallas_call(partial(attend_back_kernel, windows, text_len, sets), grid...  63.1 us
    sub x3, other arithmetic, adam_update(): weight - learn_rate * (first_hat / (jnp.sqrt(second_hat) + ADAM_EPS) + DE...  57 us
    pallas_call x3, Pallas kernels, attend(): pl.pallas_call(partial(attend_kernel, windows, text_len, len(key_values))...  36.9 us
    ppermute x4, waiting for transfers between devices, shifted(): lax.ppermute(value, axis, [(i, (i + by) % length) for i in range(length)])  32 us
  transfers between devices with their start and end apart: 8, of which 5 were waited for; matrix products, arithmetic and copies ran while one was open for 10% of the time, Pallas kernels for 24%

profile of v7, /device:TPU:0, one launch (start us, length us, event | category | flops | bytes accessed | tf_op | source)
XLA Modules:
  0.0 1033.2 jit_solution(13766399183569335100)
XLA Ops:
  10.6 9.6 convert.17
  20.2 2.3 slice.229.refs_6_
  22.6 2.3 fusion.67
  24.8 2.7 fusion.68
  32.6 27.6 %shard_map.230 = (s32[8,8,128]{2,1,0:T(8,128)}, bf16[8,80,512]{2,1,0:T(8,128)(2,1)}) custom-call(s32[8,128]{1,0:T(8,128)} %pad.12.facts_ref, bf16[8,80,512]{2,1,0:T(8,128)(2,1)} %pad.13.text_ref), custom_call_target="tpu_custom_call" | custom-call | tf_op jit(solution)/shard_map/pallas_call | solution.py:333
  61.1 3.9 fusion.66
  65.7 2.4 fusion.17
  68.9 2.8 fusion.21.refs_9_
  71.7 184.8 %shard_map.231 = (bf16[1024,3072]{1,0:T(8,128)(2,1)}, bf16[1024,3072]{1,0:T(8,128)(2,1)}, bf16[1024,1024]{1,0:T(8,128)(2,1)}, bf16[1024,1024]{1,0:T(8,128)(2,1)}...) custom-call(bf16[128,3072]{1,0:T(8,128)(2,1)} %get-tuple-element.120, ...), custom_call_target="tpu_custom_call" | custom-call | flops 199999995904 | bytes 600000000 | tf_op jit(solution)/shard_map/pallas_call | solution.py:532
  259.9 2.5 copy-done.83
  262.5 4.5 convolution_convert_fusion.1.refs_0_.refs_1_.refs_3_
  271.5 3.3 collective-permute-done.refs_2_.refs_4_
  274.8 2.1 copy-done.1
  276.9 11.9 %shard_map.232.refs_8_ = bf16[640,1024]{1,0:T(8,128)(2,1)S(1)} custom-call(bf16[640,3072]{1,0:T(8,128)(2,1)S(1)} %copy-done.1, bf16[640,3072]{1,0:T(8,128)(2,1)S(1)} %copy-done.1, bf16[640,2048]{1,0:T(8,128)(2,1)S(1)} %collective-permute-done.refs_2_.refs_4_, bf16[640,3072]{1,0:T(8,128)(2,1)S(1)} %copy-done.1, ...), custom_call_target="tpu_custom_call" | custom-call | flops 1677721600 | bytes 10485760 | tf_op jit(solution)/shard_map/pallas_call | solution.py:218
  288.9 3.2 fusion.65
  293.2 8.2 multiply_convert_fusion.1
  301.5 11.3 %fusion.64 = (f32[640]{0:T(1024)S(1)}, f32[640,1024]{1,0:T(8,128)S(1)}, f32[640,1024]{1,0:T(8,128)}) fusion(f32[640,1024]{1,0:T(8,128)S(1)} %get-tuple-element.112, f32[1024]{0:T(1024)S(1)} %get-tuple-element.147, bf16[640,4096]{1,0:T(8,128)(2,1)S(1)} %get-tuple-element.156.refs_6_, bf16[4096,1024]{1,0:T(8,128)(2,1)} %get-tuple-element.43), kind=kOutput, calls=%fused_computation.207 | convolution fusion | flops 5370674688 | bytes 21502464 | tf_op jit(solution)/shard_map/dot_general | solution.py:47
  314.2 8.1 collective-permute-done.1
  323.6 4.5 convolution_convert_fusion.refs_0_.refs_1_.refs_2_
  328.1 16.4 %shard_map.233 = bf16[640,1024]{1,0:T(8,128)(2,1)S(1)} custom-call(bf16[640,3072]{1,0:T(8,128)(2,1)S(1)} %convolution_convert_fusion.refs_0_.refs_1_.refs_2_, bf16[640,3072]{1,0:T(8,128)(2,1)S(1)} %convolution_convert_fusion.refs_0_.refs_1_.refs_2_, bf16[640,3072]{1,0:T(8,128)(2,1)S(1)} %convolution_convert_fusion.refs_0_.refs_1_.refs_2_), custom_call_target="tpu_custom_call" | custom-call | flops 1677721600 | bytes 10485760 | tf_op jit(solution)/shard_map/pallas_call | solution.py:218
  351.8 6.8 all_gather.9.refs_1_.refs_2_
  360.1 3.0 fusion.63
  367.6 8.6 shard_map.234.refs_2_
  379.9 12.0 %multiply_convert_fusion = (bf16[640,4096]{1,0:T(8,128)(2,1)}, f32[640,4096]{1,0:T(8,128)}) fusion(bf16[640,1024]{1,0:T(8,128)(2,1)S(1)} %add_convert_fusion.1.refs_1_, bf16[1024,4096]{1,0:T(8,128)(2,1)} %all-gather.3.cloned.1.call-done), kind=kOutput, calls=%fused_computation.20 | convolution fusion | flops 5381816320 | bytes 25427968 | tf_op jit(solution)/shard_map/dot_general | solution.py:47
  391.9 11.1 %fusion.62 = (f32[640]{0:T(1024)S(1)}, f32[640,1024]{1,0:T(8,128)S(1)}, f32[640,1024]{1,0:T(8,128)}) fusion(f32[640,1024]{1,0:T(8,128)} %copy-done.16, f32[1024]{0:T(1024)S(1)} %get-tuple-element.139, bf16[640,4096]{1,0:T(8,128)(2,1)} %get-tuple-element.162.refs_0_, bf16[4096,1024]{1,0:T(8,128)(2,1)} %all-gather.5.cloned.1.call-done), kind=kOutput, calls=%fused_computation.205 | convolution fusion | flops 5370674688 | bytes 21502464 | tf_op jit(solution)/shard_map/dot_general | solution.py:47
  407.5 12.7 %fusion.6.refs_11_ = bf16[640,4096]{1,0:T(8,128)(2,1)S(1)} fusion(f32[640,4096]{1,0:T(8,128)} %get-tuple-element.163, bf16[640,1024]{1,0:T(8,128)(2,1)S(1)} %multiply_convert_fusion.5.refs_10_, bf16[4096,1024]{1,0:T(8,128)(2,1)} %all-gather.5.cloned.1.call-done), kind=kOutput, calls=%fused_computation.13 | convolution fusion | flops 5394923520 | bytes 25427968 | tf_op jit(solution)/shard_map/dot_general | solution.py:61
  420.2 10.6 %multiply_reduce_fusion.5 = (f32[1024]{0:T(1024)S(1)}, f32[640]{0:T(1024)S(1)}, f32[1024]{0:T(1024)S(1)}, f32[640,1024]{1,0:T(8,128)S(1)}) fusion(f32[640,1024]{1,0:T(8,128)S(1)} %copy-done.17, f32[640]{0:T(1024)S(1)} %fusion.45, f32[640]{0:T(1024)S(1)} %broadcast_multiply_fusion.3, f32[1024]{0:T(1024)S(1)} %get-tuple-element.141, ...), kind=kOutput, calls=%fused_computation.50 | convolution fusion | flops 5373949440 | bytes 18894336 | tf_op jit(solution)/shard_map/dot_general | solution.py:61
  434.3 2.7 convolution_convert_fusion.4.refs_3_
  436.9 8.7 shard_map.235
  445.6 4.0 multiply_reduce_fusion.2
  456.4 8.1 collective-permute-done.3
  464.6 22.9 %shard_map.236.refs_15_ = bf16[640,3072]{1,0:T(8,128)(2,1)} custom-call(bf16[640,3072]{1,0:T(8,128)(2,1)} %copy-done.2, bf16[640,3072]{1,0:T(8,128)(2,1)} %copy-done.2, bf16[640,3072]{1,0:T(8,128)(2,1)} %copy-done.2, bf16[640,1024]{1,0:T(8,128)(2,1)S(1)} %bitcast.163), custom_call_target="tpu_custom_call" | custom-call | flops 4194304000 | bytes 10485760 | tf_op jit(solution)/shard_map/pallas_call | solution.py:239
  487.5 7.6 fusion.75
  496.9 15.8 %collective-permute-done.4 = f32[10,32,1024]{2,1,0:T(8,128)S(1)} collective-permute-done((f32[10,32,1024]{2,1,0:T(8,128)S(1)}, f32[10,32,1024]{2,1,0:T(8,128)S(1)}, u32[]{:S(2)}, u32[]{:S(2)}) %collective-permute-start.4) | collective-permute-done | bytes 1310752 | tf_op jit(solution)/shard_map/ppermute | solution.py:43
  518.4 14.6 %fusion.12.refs_17_ = bf16[640,4096]{1,0:T(8,128)(2,1)} fusion(f32[640,4096]{1,0:T(8,128)} %get-tuple-element.157, bf16[640,1024]{1,0:T(8,128)(2,1)S(1)} %multiply_convert_fusion.3.refs_16_, bf16[4096,1024]{1,0:T(8,128)(2,1)} %get-tuple-element.43), kind=kOutput, calls=%fused_computation.19 | convolution fusion | flops 5394923520 | bytes 25427968 | tf_op jit(solution)/shard_map/dot_general | solution.py:61
  533.0 10.3 multiply_reduce_fusion.8
  544.3 1.9 multiply_convert_fusion.2
  547.9 31.5 %shard_map.237 = (bf16[640,1024]{1,0:T(8,128)(2,1)S(1)}, f32[640,2048]{1,0:T(8,128)}, f32[640,2048]{1,0:T(8,128)}) custom-call(bf16[640,3072]{1,0:T(8,128)(2,1)} %copy-done, bf16[640,3072]{1,0:T(8,128)(2,1)} %copy-done, bf16[640,2048]{1,0:T(8,128)(2,1)} %copy-done.3, bf16[640,3072]{1,0:T(8,128)(2,1)} %copy-done, bf16[640,2048]{1,0:T(8,128)(2,1)} %copy-done.3, ...), custom_call_target="tpu_custom_call" | custom-call | flops 4194304000 | bytes 10485760 | tf_op jit(solution)/shard_map/pallas_call | solution.py:239
  582.1 6.3 collective-permute-done.5
  588.5 5.0 add_convert_fusion
  593.5 7.6 multiply_reduce_fusion.10
  601.1 2.3 pad_maximum_fusion.refs_19_
  608.9 325.6 %shard_map.238 = (f32[128,18432]{1,0:T(8,128)}, f32[512,2048]{1,0:T(8,128)}, f32[8,512]{1,0:T(8,128)}, f32[8,256,128]{2,1,0:T(8,128)}, f32[512,2048]{1,0:T(8,128...) custom-call(bf16[640,4096]{1,0:T(8,128)(2,1)} %get-tuple-element.162, ...), custom_call_target="tpu_custom_call" | custom-call | flops 299999985664 | bytes 800000000 | tf_op jit(solution)/shard_map/pallas_call | solution.py:1147
  937.3 5.6 multiply_reduce_fusion
  945.3 4.0 fusion.69
  951.9 12.2 %shard_map.239 = f32[8,128]{1,0:T(8,128)} custom-call(f32[8,128]{1,0:T(8,128)} %broadcast_in_dim.87.part_ref), custom_call_target="tpu_custom_call" | custom-call | tf_op jit(solution)/shard_map/pallas_call | solution.py:1200
  967.6 36.8 %multiply_subtract_fusion = (f32[128,30720]{1,0:T(8,128)}, f32[128,30720]{1,0:T(8,128)}, f32[128,30720]{1,0:T(8,128)}) fusion(f32[128,30720]{1,0:T(8,128)} %param.21, f32[]{:T(128)S(6)} %div.227, f32[128,18432]{1,0:T(8,128)} %get-tuple-element.58, f32[128,12288]{1,0:T(8,128)} %get-tuple-element.173, f32[128,30720]{1,0:T(8,128)} %param.22, f32[128,30720]{1,0:T(8,128)} %param.23), kind=kLoop, calls=%fused_computation.3 | loop fusion | flops 66846720 | bytes 110100480 | tf_op jit(solution)/shard_map/sub | solution.py:277
  1004.3 19.5 %multiply_subtract_fusion.1 = (f32[512,4096]{1,0:T(8,128)}, f32[512,4096]{1,0:T(8,128)}, f32[512,4096]{1,0:T(8,128)}) fusion(f32[512,4096]{1,0:T(8,128)} %param.24, f32[]{:T(128)S(6)} %div.227, f32[512,1024]{1,0:T(8,128)} %get-tuple-element.122, f32[512,2048]{1,0:T(8,128)} %get-tuple-element.60, f32[512,1024]{1,0:T(8,128)S(1)} %get-tuple-element.121, ...), kind=kLoop, calls=%fused_computation.26 | loop fusion | flops 37748736 | bytes 58720260 | tf_op jit(solution)/shard_map/sub | solution.py:277
  (312 shorter events, 77.0 us)
Async XLA Ops:
  7.2 372.7 %all-gather.3.cloned.1.call-start = ((), (), s32[]{:S(2)}) async-start(), calls=%async_computation | async-start | bytes 8650752 | tf_op jit(solution)/shard_map/all_gather | solution.py:518
  9.7 382.1 %all-gather.5.cloned.1.call-start = ((), (), s32[]{:S(2)}) async-start(), calls=%async_computation.1 | async-start | bytes 8650752 | tf_op jit(solution)/shard_map/all_gather | solution.py:518
  22.6 6.9 copy-start.43
  22.6 6.9 copy-start.44
  71.7 185.8 %copy-start.42 = (bf16[19,1024]{1,0:T(8,128)(2,1)S(1)}, bf16[19,1024]{1,0:T(8,128)(2,1)}, u32[]{:S(2)}) copy-start(bf16[19,1024]{1,0:T(8,128)(2,1)} %convert_element_type.141) | copy-start | bytes 116740
  71.7 185.9 %copy-start.53 = (bf16[640,8]{0,1:T(8,128)(2,1)S(1)}, bf16[640,8]{0,1:T(8,128)(2,1)}, u32[]{:S(2)}) copy-start(bf16[640,8]{0,1:T(8,128)(2,1)} %convert_element_type.140) | copy-start | bytes 30724
  257.6 31.2 %copy-start.49 = (f32[1,1024]{1,0:T(1,128)}, f32[1,1024]{1,0:T(1,128)S(1)}, u32[]{:S(2)}) copy-start(f32[1,1024]{1,0:T(1,128)S(1)} %get-tuple-element.138) | copy-start | bytes 12292
  259.3 7.6 copy-start.65
  259.3 7.6 copy-start.63
  259.4 29.5 %copy-start.71 = (f32[1024]{0:T(1024)}, f32[1024]{0:T(1024)S(1)}, u32[]{:S(2)}) copy-start(f32[1024]{0:T(1024)S(1)} %get-tuple-element.150) | copy-start | bytes 12292
  259.4 33.1 %copy-start.59 = (f32[1024]{0:T(1024)}, f32[1024]{0:T(1024)S(1)}, u32[]{:S(2)}) copy-start(f32[1024]{0:T(1024)S(1)} %get-tuple-element.146) | copy-start | bytes 12292
  259.9 7.0 copy-start.28
  269.6 5.1 collective-permute-start
  276.9 11.9 %copy-start.3 = (bf16[640,2048]{1,0:T(8,128)(2,1)}, bf16[640,2048]{1,0:T(8,128)(2,1)S(1)}, u32[]{:S(2)}) copy-start(bf16[640,2048]{1,0:T(8,128)(2,1)S(1)} %collective-permute-done.refs_2_.refs_4_) | copy-start | bytes 7864324
  276.9 11.9 %copy-start.12 = (f32[640,1024]{1,0:T(8,128)S(1)}, f32[640,1024]{1,0:T(8,128)}, u32[]{:S(2)}) copy-start(f32[640,1024]{1,0:T(8,128)} %copy-done.11) | copy-start | bytes 7864324
  276.9 12.0 %copy-start.78 = (bf16[1024,1024]{1,0:T(8,128)(2,1)S(1)}, bf16[1024,1024]{1,0:T(8,128)(2,1)}, u32[]{:S(2)}) copy-start(bf16[1024,1024]{1,0:T(8,128)(2,1)} %get-tuple-element.41) | copy-start | bytes 6291460
  276.9 16.4 %slice-start = ((s8[8388608]{0:T(1024)(128)(4,1)}), s8[4194304]{0:T(1024)(128)(4,1)S(1)}, s32[]{:S(2)}) async-start(s8[8388608]{0:T(1024)(128)(4,1)} %bitcast.213), calls=%async_computation.2 | async-start | bytes 8388608
  292.0 9.4 copy-start.14
  292.4 9.0 copy-start.69
  292.5 9.0 copy-start.61
  293.2 8.2 copy-start.33
  301.5 11.3 %copy-start.84 = (bf16[640,4096]{1,0:T(8,128)(2,1)}, bf16[640,4096]{1,0:T(8,128)(2,1)S(1)}, u32[]{:S(2)}) copy-start(bf16[640,4096]{1,0:T(8,128)(2,1)S(1)} %get-tuple-element.156.refs_6_) | copy-start | bytes 15728644
  312.8 47.2 %copy-start.7 = (f32[640,1024]{1,0:T(8,128)}, f32[640,1024]{1,0:T(8,128)S(1)}, u32[]{:S(2)}) copy-start(f32[640,1024]{1,0:T(8,128)S(1)} %get-tuple-element.110) | copy-start | bytes 7864324
  312.8 10.7 %slice-start.2 = ((s8[6291456]{0:T(1024)(128)(4,1)}), s8[4194304]{0:T(1024)(128)(4,1)S(1)}, s32[]{:S(2)}) async-start(s8[6291456]{0:T(1024)(128)(4,1)} %bitcast.215), calls=%async_computation.4 | async-start | bytes 8388608
  313.3 10.3 slice-start.3
  313.9 8.4 collective-permute-start.1
  328.0 16.4 %copy-start.2 = (bf16[640,3072]{1,0:T(8,128)(2,1)}, bf16[640,3072]{1,0:T(8,128)(2,1)S(1)}, u32[]{:S(2)}) copy-start(bf16[640,3072]{1,0:T(8,128)(2,1)S(1)} %convolution_convert_fusion.refs_0_.refs_1_.refs_2_) | copy-start | bytes 11796484
  345.7 13.0 %collective-permute-start.2 = (bf16[10,32,1024]{2,1,0:T(8,128)(2,1)}, bf16[10,32,1024]{2,1,0:T(8,128)(2,1)}, u32[]{:S(2)}, u32[]{:S(2)}) collective-permute-start(bf16[10,32,1024]{2,1,0:T(8,128)(2,1)} %get-tuple-element.130), channel_id=1, source_target_pairs={{0,1},{1,2},{2,3},{3,0},{4,5},{5,6},{6,7},{7,4},{8,9},{9,10},{10,1... | collective-permute-start | bytes 1966088 | tf_op jit(solution)/shard_map/ppermute | solution.py:43
  351.8 8.2 copy-start.25
  363.1 13.1 %copy-start.9 = (f32[640,1024]{1,0:T(8,128)}, f32[640,1024]{1,0:T(8,128)S(1)}, u32[]{:S(2)}) copy-start(f32[640,1024]{1,0:T(8,128)S(1)} %get-tuple-element.108) | copy-start | bytes 7864324
  367.6 8.6 copy-start.80
  379.8 12.0 %copy-start.34 = (bf16[640,1024]{1,0:T(8,128)(2,1)}, bf16[640,1024]{1,0:T(8,128)(2,1)S(1)}, u32[]{:S(2)}) copy-start(bf16[640,1024]{1,0:T(8,128)(2,1)S(1)} %add_convert_fusion.1.refs_1_) | copy-start | bytes 3932164
  407.4 12.7 %copy-start.35 = (bf16[640,1024]{1,0:T(8,128)(2,1)}, bf16[640,1024]{1,0:T(8,128)(2,1)S(1)}, u32[]{:S(2)}) copy-start(bf16[640,1024]{1,0:T(8,128)(2,1)S(1)} %multiply_convert_fusion.5.refs_10_) | copy-start | bytes 3932164
  407.4 12.7 %copy-start.17 = (f32[640,1024]{1,0:T(8,128)S(1)}, f32[640,1024]{1,0:T(8,128)}, u32[]{:S(2)}) copy-start(f32[640,1024]{1,0:T(8,128)} %copy-done.16) | copy-start | bytes 7864324
  420.2 10.6 %copy-start.85 = (bf16[640,4096]{1,0:T(8,128)(2,1)}, bf16[640,4096]{1,0:T(8,128)(2,1)S(1)}, u32[]{:S(2)}) copy-start(bf16[640,4096]{1,0:T(8,128)(2,1)S(1)} %fusion.6.refs_11_) | copy-start | bytes 15728644
  436.9 8.7 copy-start.10
  455.4 9.1 collective-permute-start.3
  495.5 17.2 %collective-permute-start.4 = (f32[10,32,1024]{2,1,0:T(8,128)S(1)}, f32[10,32,1024]{2,1,0:T(8,128)S(1)}, u32[]{:S(2)}, u32[]{:S(2)}) collective-permute-start(f32[10,32,1024]{2,1,0:T(8,128)S(1)} %get-tuple-element.127), channel_id=1, source_target_pairs={{0,1},{1,2},{2,3},{3,0},{4,5},{5,6},{6,7},{7,4},{8,9},{9,10},{10,1... | collective-permute-start | bytes 3932168 | tf_op jit(solution)/shard_map/ppermute | solution.py:43
  518.3 14.7 %copy-start.32 = (bf16[640,1024]{1,0:T(8,128)(2,1)}, bf16[640,1024]{1,0:T(8,128)(2,1)S(1)}, u32[]{:S(2)}) copy-start(bf16[640,1024]{1,0:T(8,128)(2,1)S(1)} %multiply_convert_fusion.3.refs_16_) | copy-start | bytes 3932164
  518.3 14.7 %copy-start.15 = (f32[640,1024]{1,0:T(8,128)S(1)}, f32[640,1024]{1,0:T(8,128)}, u32[]{:S(2)}) copy-start(f32[640,1024]{1,0:T(8,128)} %copy-done.14) | copy-start | bytes 7864324
  518.3 14.7 %copy-start.56 = (f32[640]{0:T(1024)S(1)}, f32[640]{0:T(1024)}, u32[]{:S(2)}) copy-start(f32[640]{0:T(1024)} %copy-done.55) | copy-start | bytes 7684
  518.3 14.7 %copy-start.60 = (f32[1024]{0:T(1024)S(1)}, f32[1024]{0:T(1024)}, u32[]{:S(2)}) copy-start(f32[1024]{0:T(1024)} %copy-done.59) | copy-start | bytes 12292
  518.3 14.7 %copy-start.62 = (f32[640]{0:T(1024)S(1)}, f32[640]{0:T(1024)}, u32[]{:S(2)}) copy-start(f32[640]{0:T(1024)} %copy-done.61) | copy-start | bytes 7684
  533.0 10.3 copy-start.70
  579.4 9.1 collective-permute-start.5
  945.3 21.4 %copy-start.41 = (f32[19,1024]{1,0:T(8,128)S(1)}, f32[19,1024]{1,0:T(8,128)}, u32[]{:S(2)}) copy-start(f32[19,1024]{1,0:T(8,128)} %param.27) | copy-start | bytes 233476
  945.3 21.5 %copy-start.51 = (f32[19,1024]{1,0:T(8,128)S(1)}, f32[19,1024]{1,0:T(8,128)}, u32[]{:S(2)}) copy-start(f32[19,1024]{1,0:T(8,128)} %param.28) | copy-start | bytes 233476
  945.3 21.5 %copy-start.52 = (f32[19,1024]{1,0:T(8,128)S(1)}, f32[19,1024]{1,0:T(8,128)}, u32[]{:S(2)}) copy-start(f32[19,1024]{1,0:T(8,128)} %param.29) | copy-start | bytes 233476
  (50 other events, 138.6 us)
Sparse Core Ops, SparseCore 0:
  10.9 105.6 all-gather.2
  271.6 87.3 all-gather.4

commit v8 on v7

--- a/solution.py
+++ b/solution.py
@@ -301,60 +301,52 @@
     pl.semaphore_wait(barrier, len(peers))
 
 
-def exchange_kernel(count, facts_ref, text_ref, facts_out, text_out, send, recv, local):
+def exchange_kernel(count, facts_ref, facts_out, send, recv):
     me = lax.axis_index("clip")
     band = lax.axis_index("band")
     peers = [((me + step) % count, band) for step in range(1, count)]
     greet(peers)
-    own = [
-        pltpu.make_async_copy(facts_ref, facts_out.at[me], local.at[0]),
-        pltpu.make_async_copy(text_ref.at[me], text_out.at[me], local.at[1]),
+    sent = [
+        pltpu.make_async_remote_copy(
+            facts_ref, facts_out.at[me], send.at[step], recv.at[step], peer, MESH
+        )
+        for step, peer in enumerate(peers)
     ]
-    for copy in own:
-        copy.start()
-    sent = []
-    for step, peer in enumerate(peers):
-        sent += [
-            pltpu.make_async_remote_copy(
-                facts_ref, facts_out.at[me], send.at[0, step], recv.at[0, step], peer, MESH
-            ),
-            pltpu.make_async_remote_copy(
-                text_ref.at[peer[0]], text_out.at[me], send.at[1, step], recv.at[1, step], peer, MESH
-            ),
-        ]
     for copy in sent:
         copy.start()
-    for copy in own + sent:
+    facts_out[me] = facts_ref[...]
+    for copy in sent:
         copy.wait()
 
 
-def exchange_facts(facts, text):
+def exchange_facts(facts):
     count = lax.axis_size("clip")
     return pl.pallas_call(
         partial(exchange_kernel, count),
-        out_shape=(
-            jax.ShapeDtypeStruct((count,) + facts.shape, facts.dtype),
-            jax.ShapeDtypeStruct(text.shape, text.dtype),
-        ),
-        in_specs=[ANY] * 2,
-        out_specs=(ANY,) * 2,
-        scratch_shapes=[
-            pltpu.SemaphoreType.DMA((2, count - 1)),
-            pltpu.SemaphoreType.DMA((2, count - 1)),
-            pltpu.SemaphoreType.DMA((2,)),
-        ],
+        out_shape=jax.ShapeDtypeStruct((count,) + facts.shape, facts.dtype),
+        in_specs=[IN_VMEM],
+        out_specs=IN_VMEM,
+        scratch_shapes=[pltpu.SemaphoreType.DMA((count - 1,))] * 2,
         compiler_params=pltpu.CompilerParams(collective_id=0, has_side_effects=True),
-    )(facts, text)
-
-
-def gather_kernel(count, shapes, sides, *refs):
-    num = len(shapes)
-    shards, (vec_ref, text_ref) = refs[:num], refs[num : num + 2]
-    full, (vec_out, text_out) = refs[num + 2 : 2 * num + 2], refs[2 * num + 2 : 2 * num + 4]
-    ring_send, ring_recv, pair_send, pair_recv, cross_send, cross_recv = refs[
-        2 * num + 4 : 2 * num + 10
+    )(facts)
+
+
+def gather_kernel(count, picks, sides, *refs):
+    num = len(picks)
+    packs, vec_ref, text_ref = refs[:2], refs[2], refs[3]
+    full, (vec_out, text_out), refs = refs[4 : 4 + num], refs[4 + num : 6 + num], refs[6 + num :]
+    wide, shards = refs[:num], refs[num : 2 * num]
+    ring_send, ring_recv, pair_send, pair_recv, cross_send, cross_recv = refs[2 * num : 2 * num + 6]
+    load_sem, own_sem, part_send, part_recv, part_own = refs[2 * num + 6 :]
+    shapes = [(packs[pack].shape[0], cols) for pack, _, cols in picks]
+    loads = [
+        pltpu.make_async_copy(
+            packs[pack].at[:, pl.ds(start, cols)], wide[group], load_sem.at[group]
+        )
+        for group, (pack, start, cols) in enumerate(picks)
     ]
-    own_sem, part_send, part_recv, part_own = refs[2 * num + 10 :]
+    for copy in loads:
+        copy.start()
     me = lax.axis_index("clip")
     band = lax.axis_index("band")
     core = band % 2
@@ -448,8 +440,12 @@
         pltpu.make_async_copy(src.at[me], dst.at[me], part_own.at[which])
         for which, (src, dst) in enumerate(((vec_ref, vec_out), (text_ref, text_out)))
     ]
+    for copy in parts_own + parts[::2]:
+        copy.start()
     for group in range(num):
         rows, cols = shapes[group]
+        loads[group].wait()
+        shards[group][...] = wide[group][...].astype(jnp.bfloat16)
         own_copy(group).start()
 
         @in_ring(group)
@@ -463,7 +459,7 @@
                 MESH,
             ).start()
 
-    for copy in parts_own + parts:
+    for copy in parts[1::2]:
         copy.start()
 
     @pl.loop(1, count - 1)
@@ -525,28 +521,34 @@
     return lax.all_gather(part, "band", axis=0, tiled=True)
 
 
-def gather_weights(shards, sides, vectors, texts):
+def gather_weights(packs, picks, sides, vectors, texts):
     count = lax.axis_size("clip")
-    num = len(shards)
+    num = len(picks)
     steps = pltpu.SemaphoreType.DMA((count - 1, num))
+    shapes = [(packs[pack].shape[0], cols) for pack, _, cols in picks]
     out = pl.pallas_call(
-        partial(gather_kernel, count, [shard.shape for shard in shards], sides),
+        partial(gather_kernel, count, picks, sides),
         out_shape=tuple(
-            jax.ShapeDtypeStruct((count * s.shape[0], s.shape[1]), s.dtype) for s in shards
+            jax.ShapeDtypeStruct((count * rows, cols), jnp.bfloat16) for rows, cols in shapes
         )
         + tuple(jax.ShapeDtypeStruct(v.shape, v.dtype) for v in (vectors, texts)),
-        in_specs=[ANY] * (num + 2),
+        in_specs=[ANY] * 4,
         out_specs=(ANY,) * (num + 2),
-        scratch_shapes=[
-            *[steps] * 6,
+        scratch_shapes=[pltpu.VMEM(shape, jnp.float32) for shape in shapes]
+        + [pltpu.VMEM(shape, jnp.bfloat16) for shape in shapes]
+        + [steps] * 6
+        + [
+            pltpu.SemaphoreType.DMA((num,)),
             pltpu.SemaphoreType.DMA((num,)),
             pltpu.SemaphoreType.DMA((2, count - 1)),
             pltpu.SemaphoreType.DMA((2, count - 1)),
             pltpu.SemaphoreType.DMA((2,)),
         ],
-        compiler_params=pltpu.CompilerParams(collective_id=1, has_side_effects=True),
+        compiler_params=pltpu.CompilerParams(
+            collective_id=1, has_side_effects=True, vmem_limit_bytes=32 << 20
+        ),
         cost_estimate=pl.CostEstimate(flops=2 * 10**11, bytes_accessed=6 * 10**8, transcendentals=0),
-    )(*shards, vectors, texts)
+    )(*packs, vectors, texts)
     return out[:num], out[num], out[num + 1]
 
 
@@ -1248,7 +1250,7 @@
         kept_text.reshape(text_len, clip_count, deep_rows).transpose(1, 0, 2),
         ((0, 0), (0, TEXT_PAD - text_len), (0, 0)),
     )
-    all_facts, all_text = exchange_facts(facts, text_cols)
+    all_facts = exchange_facts(facts)
     all_times = all_facts[:, 0, 0].astype(jnp.float32)
     all_time_low = jax.nn.silu(time_features(all_times)).astype(jnp.bfloat16)
     time_rows = lax.dynamic_slice(
@@ -1259,21 +1261,29 @@
     kv_weight = lax.dynamic_slice(
         w_deep, (0, D + band_at * kv_cols), (deep_rows, kv_cols)
     ).astype(jnp.bfloat16)
+    up_b_w = gather_quarters(w_wide[:, 22 * D + FF :])
+    gathered, all_modul, all_text = gather_weights(
+        (w_wide, w_deep),
+        (
+            (0, 22 * D, FF),
+            (1, 0, D),
+            (0, 18 * D, D),
+            (0, 19 * D, D),
+            (0, 20 * D, D),
+            (0, 21 * D, D),
+            (0, 12 * D, 3 * D),
+            (0, 15 * D, 3 * D),
+        ),
+        (1, 2, 1, 2, 1, 2, 0, 0),
+        part_modul.reshape(clip_count, 12 * D // 128, 128),
+        text_cols,
+    )
+    up_a_w, down_a_w, out_a_w, out_b_w, query_w, cross_out_w, qkv_a_w, qkv_b_w = gathered
     part_kv = matmul(all_text.reshape(clip_count * TEXT_PAD, deep_rows), kv_weight)
-    up_b_w = gather_quarters(w_wide[:, 22 * D + FF :])
-    edges = (12 * D, 15 * D, 18 * D, 19 * D, 20 * D, 21 * D, 22 * D, 22 * D + FF)
-    shards = [w_wide[:, low:high].astype(jnp.bfloat16) for low, high in zip(edges, edges[1:])]
-    shards += [w_deep[:, :D].astype(jnp.bfloat16)]
-    gathered, all_modul, all_kv = gather_weights(
-        shards,
-        (0, 0, 1, 2, 1, 2, 1, 2),
-        part_modul.reshape(clip_count, 12 * D // 128, 128),
-        part_kv.reshape(clip_count, TEXT_PAD, kv_cols),
-    )
-    qkv_a_w, qkv_b_w, out_a_w, out_b_w, query_w, cross_out_w, up_a_w, down_a_w = gathered
+    keyval = lax.psum_scatter(part_kv, "clip", scatter_dimension=0, tiled=True)
     late_down_b, all_modul = lax.optimization_barrier((w_deep[:, 3 * D :], all_modul))
     down_b_w = gather_quarters(late_down_b)
-    keyval = lax.all_gather(jnp.sum(all_kv, 0).astype(jnp.bfloat16), "band", axis=1, tiled=True)
+    keyval = lax.all_gather(keyval.astype(jnp.bfloat16), "band", axis=1, tiled=True)
     small_low = w_small.astype(jnp.bfloat16)
     small_val = small_low.astype(jnp.float32)
     num_frames, num_rows, num_cols = (latents.shape[1], latents.shape[2], latents.shape[3])

time: 1040 us -> 984 us (0.946)
  Pallas kernels: 650 us -> 576 us
  waiting for transfers between devices: 41.7 us -> 75.8 us
  other arithmetic: 104 us -> 92.2 us
    pallas_call x2, Pallas kernels: 212 us -> 156 us  [the longest x1 147 us: gather_weights(): pl.pallas_call(partial(gather_kernel, count, picks, sides), out_shape=tup...]
    all_gather x2, waiting for transfers between devices: 0.02 us -> 21.2 us  [gather_quarters(): lax.all_gather(own.astype(jnp.bfloat16), ('clip', 'band'), axis=0, tiled=...]
    pallas_call x1, Pallas kernels: 326 us -> 310 us  [reduce_gradients(): pl.pallas_call(partial(reduce_kernel, count, tokens, phases), out_shape=(...]
    ppermute x4, waiting for transfers between devices: 32 us -> 43.6 us  [shifted(): lax.ppermute(value, axis, [(i, (i + by) % length) for i in range(length)])]
    unnamed x183 -> x203, local copies, waits for them, and re-layouts: 22.9 us -> 29.6 us
  transfers between devices with their start and end apart: 8 -> 9, of which waited for: 5 -> 6; matrix products, arithmetic and copies ran while one was open for 10% -> 7% of each run, Pallas kernels for 24% -> 4%
where the time goes in v8:
time: 984 us; the launch traced here: 978 us
  Pallas kernels  576 us (59%)
  matrix products  144 us (15%)
  other arithmetic  92.2 us (9%)
  waiting for transfers between devices  75.8 us (8%)
  local copies, waits for them, and re-layouts  48.7 us (5%)
  between operations  25.6 us (3%)
    pallas_call x1, Pallas kernels, reduce_gradients(): pl.pallas_call(partial(reduce_kernel, count, tokens, phases), out_shape=(...  310 us
    pallas_call x1, Pallas kernels, gather_weights(): pl.pallas_call(partial(gather_kernel, count, picks, sides), out_shape=tup...  147 us
    dot_general x11, matrix products, matmul_nt(): lax.dot_general(left_op, right_op, (((1,), (1,)), ((), ())), preferred_el...  71.4 us
    dot_general x14, matrix products, matmul(): return jnp.dot(left_op, right_op, preferred_element_type=jnp.float32)  65.8 us
    pallas_call x3, Pallas kernels, attend_back(): pl.pallas_call(partial(attend_back_kernel, windows, text_len, sets), grid...  63.3 us
    sub x3, other arithmetic, adam_update(): weight - learn_rate * (first_hat / (jnp.sqrt(second_hat) + ADAM_EPS) + DE...  56.9 us
    ppermute x4, waiting for transfers between devices, shifted(): lax.ppermute(value, axis, [(i, (i + by) % length) for i in range(length)])  43.6 us
    pallas_call x3, Pallas kernels, attend(): pl.pallas_call(partial(attend_kernel, windows, text_len, len(key_values))...  36.6 us
  transfers between devices with their start and end apart: 9, of which 6 were waited for; matrix products, arithmetic and copies ran while one was open for 7% of the time, Pallas kernels for 4%

profile of v8, /device:TPU:0, one launch (start us, length us, event | category | flops | bytes accessed | tf_op | source)
XLA Modules:
  0.0 977.8 jit_solution(11548497888246395683)
XLA Ops:
  10.7 9.7 shard_map.230
  21.5 3.4 fusion.16
  25.6 146.6 %shard_map.231 = (bf16[1024,4096]{1,0:T(8,128)(2,1)}, bf16[4096,1024]{1,0:T(8,128)(2,1)}, bf16[1024,1024]{1,0:T(8,128)(2,1)S(1)}, bf16[1024,1024]{1,0:T(8,128)(2...) custom-call(f32[128,30720]{1,0:T(8,128)} %refs_0_.1, ...), custom_call_target="tpu_custom_call" | custom-call | flops 199999995904 | bytes 600000000 | tf_op jit(solution)/shard_map/pallas_call | solution.py:529
  177.6 2.7 copy-done.21
  181.2 2.9 fusion.17
  187.0 2.8 slice.146
  193.5 4.8 convolution_convert_fusion.1.refs_0_.refs_1_.refs_3_
  198.3 1.9 slice.187
  202.9 3.3 collective-permute-done.refs_2_.refs_4_
  206.2 2.2 copy-done.1
  208.3 11.9 %shard_map.232.refs_8_ = bf16[640,1024]{1,0:T(8,128)(2,1)S(1)} custom-call(bf16[640,3072]{1,0:T(8,128)(2,1)S(1)} %copy-done.1, bf16[640,3072]{1,0:T(8,128)(2,1)S(1)} %copy-done.1, bf16[640,2048]{1,0:T(8,128)(2,1)S(1)} %collective-permute-done.refs_2_.refs_4_, bf16[640,3072]{1,0:T(8,128)(2,1)S(1)} %copy-done.1, ...), custom_call_target="tpu_custom_call" | custom-call | flops 1677721600 | bytes 10485760 | tf_op jit(solution)/shard_map/pallas_call | solution.py:218
  220.3 3.1 fusion.60
  224.7 8.2 multiply_convert_fusion.1
  232.9 7.1 fusion.59
  242.8 19.1 %collective-permute-done.1 = bf16[10,32,1024]{2,1,0:T(8,128)(2,1)S(1)} collective-permute-done((bf16[10,32,1024]{2,1,0:T(8,128)(2,1)S(1)}, bf16[10,32,1024]{2,1,0:T(8,128)(2,1)S(1)}, u32[]{:S(2)}, u32[]{:S(2)}) %collective-permute-start.1) | collective-permute-done | bytes 655392 | tf_op jit(solution)/shard_map/ppermute | solution.py:43
  263.2 5.0 convolution_convert_fusion.refs_0_.refs_1_.refs_2_
  268.2 16.4 %shard_map.233 = bf16[640,1024]{1,0:T(8,128)(2,1)S(1)} custom-call(bf16[640,3072]{1,0:T(8,128)(2,1)S(1)} %convolution_convert_fusion.refs_0_.refs_1_.refs_2_, bf16[640,3072]{1,0:T(8,128)(2,1)S(1)} %convolution_convert_fusion.refs_0_.refs_1_.refs_2_, bf16[640,3072]{1,0:T(8,128)(2,1)S(1)} %convolution_convert_fusion.refs_0_.refs_1_.refs_2_), custom_call_target="tpu_custom_call" | custom-call | flops 1677721600 | bytes 10485760 | tf_op jit(solution)/shard_map/pallas_call | solution.py:218
  285.6 2.4 collective-permute-start.2
  292.0 8.6 all_gather.9.refs_1_.refs_2_
  301.9 3.0 fusion.58
  309.4 8.3 shard_map.234.refs_2_
  322.5 11.9 %multiply_convert_fusion = (bf16[640,4096]{1,0:T(8,128)(2,1)}, f32[640,4096]{1,0:T(8,128)}) fusion(bf16[640,1024]{1,0:T(8,128)(2,1)} %add_convert_fusion.1.refs_1_, bf16[1024,4096]{1,0:T(8,128)(2,1)} %all-gather.3.cloned.1.call-done), kind=kOutput, calls=%fused_computation.20 | convolution fusion | flops 5381816320 | bytes 25427968 | tf_op jit(solution)/shard_map/dot_general | solution.py:47
  334.5 21.2 %all-gather.5.cloned.1.call-done = bf16[4096,1024]{1,0:T(8,128)(2,1)} async-done(((bf16[128,1024]{1,0:T(8,128)(2,1)}), bf16[4096,1024]{1,0:T(8,128)(2,1)}) %all-gather.5.cloned.1.call-update) | async-done | bytes 8388624 | tf_op jit(solution)/shard_map/all_gather | solution.py:514
  355.6 11.1 %fusion.57 = (f32[640]{0:T(1024)S(1)}, f32[640,1024]{1,0:T(8,128)S(1)}, f32[640,1024]{1,0:T(8,128)}) fusion(f32[640,1024]{1,0:T(8,128)} %copy-done.32, f32[1024]{0:T(1024)S(1)} %get-tuple-element.127, bf16[640,4096]{1,0:T(8,128)(2,1)} %get-tuple-element.150.refs_0_, bf16[4096,1024]{1,0:T(8,128)(2,1)} %all-gather.5.cloned.1.call-done), kind=kOutput, calls=%fused_computation.203 | convolution fusion | flops 5370674688 | bytes 21502464 | tf_op jit(solution)/shard_map/dot_general | solution.py:47
  371.2 12.7 %fusion.6.refs_11_ = bf16[640,4096]{1,0:T(8,128)(2,1)S(1)} fusion(f32[640,4096]{1,0:T(8,128)} %get-tuple-element.151, bf16[640,1024]{1,0:T(8,128)(2,1)S(1)} %multiply_convert_fusion.5.refs_10_, bf16[4096,1024]{1,0:T(8,128)(2,1)} %all-gather.5.cloned.1.call-done), kind=kOutput, calls=%fused_computation.13 | convolution fusion | flops 5394923520 | bytes 25427968 | tf_op jit(solution)/shard_map/dot_general | solution.py:61
  384.0 10.6 %multiply_reduce_fusion.5 = (f32[1024]{0:T(1024)S(1)}, f32[640]{0:T(1024)S(1)}, f32[1024]{0:T(1024)S(1)}, f32[640,1024]{1,0:T(8,128)S(1)}) fusion(f32[640,1024]{1,0:T(8,128)S(1)} %copy-done.33, f32[640]{0:T(1024)S(1)} %fusion.40, f32[640]{0:T(1024)S(1)} %broadcast_multiply_fusion.3, f32[1024]{0:T(1024)S(1)} %get-tuple-element.129, ...), kind=kOutput, calls=%fused_computation.50 | convolution fusion | flops 5373949440 | bytes 18894336 | tf_op jit(solution)/shard_map/dot_general | solution.py:61
  398.1 2.7 convolution_convert_fusion.4.refs_3_
  400.8 8.9 shard_map.235
  409.7 2.0 multiply_reduce_fusion.2
  418.4 8.1 collective-permute-done.3
  426.7 22.9 %shard_map.236.refs_15_ = bf16[640,3072]{1,0:T(8,128)(2,1)} custom-call(bf16[640,3072]{1,0:T(8,128)(2,1)} %copy-done.2, bf16[640,3072]{1,0:T(8,128)(2,1)} %copy-done.2, bf16[640,3072]{1,0:T(8,128)(2,1)} %copy-done.2, bf16[640,1024]{1,0:T(8,128)(2,1)S(1)} %bitcast.160), custom_call_target="tpu_custom_call" | custom-call | flops 4194304000 | bytes 10485760 | tf_op jit(solution)/shard_map/pallas_call | solution.py:239
  449.6 7.6 fusion.67
  458.3 16.4 %collective-permute-done.4 = f32[10,32,1024]{2,1,0:T(8,128)S(1)} collective-permute-done((f32[10,32,1024]{2,1,0:T(8,128)S(1)}, f32[10,32,1024]{2,1,0:T(8,128)S(1)}, u32[]{:S(2)}, u32[]{:S(2)}) %collective-permute-start.4) | collective-permute-done | bytes 1310752 | tf_op jit(solution)/shard_map/ppermute | solution.py:43
  480.9 13.9 %fusion.12.refs_17_ = bf16[640,4096]{1,0:T(8,128)(2,1)} fusion(f32[640,4096]{1,0:T(8,128)} %get-tuple-element.145, bf16[640,1024]{1,0:T(8,128)(2,1)S(1)} %multiply_convert_fusion.3.refs_16_, bf16[4096,1024]{1,0:T(8,128)(2,1)} %get-tuple-element.39), kind=kOutput, calls=%fused_computation.19 | convolution fusion | flops 5394923520 | bytes 25427968 | tf_op jit(solution)/shard_map/dot_general | solution.py:61
  494.8 10.3 %multiply_reduce_fusion.8 = (f32[1024]{0:T(1024)S(1)}, f32[640]{0:T(1024)S(1)}, f32[1024]{0:T(1024)S(1)}, f32[640,1024]{1,0:T(8,128)S(1)}) fusion(f32[640,1024]{1,0:T(8,128)S(1)} %copy-done.31, f32[640]{0:T(1024)S(1)} %copy-done.75, f32[640]{0:T(1024)S(1)} %copy-done.69, f32[1024]{0:T(1024)S(1)} %copy-done.73, bf16[640,4096]{1,0:T(8,128)(2,1)} %fusion.12.refs_17_, ...), kind=kOutput, calls=%fused_computation.53 | convolution fusion | flops 5373949440 | bytes 18894336 | tf_op jit(solution)/shard_map/dot_general | solution.py:61
  506.0 1.9 multiply_convert_fusion.2
  509.7 31.5 %shard_map.237 = (bf16[640,1024]{1,0:T(8,128)(2,1)S(1)}, f32[640,2048]{1,0:T(8,128)}, f32[640,2048]{1,0:T(8,128)}) custom-call(bf16[640,3072]{1,0:T(8,128)(2,1)} %copy-done, bf16[640,3072]{1,0:T(8,128)(2,1)} %copy-done, bf16[640,2048]{1,0:T(8,128)(2,1)} %copy-done.3, bf16[640,3072]{1,0:T(8,128)(2,1)} %copy-done, bf16[640,2048]{1,0:T(8,128)(2,1)} %copy-done.3, ...), custom_call_target="tpu_custom_call" | custom-call | flops 4194304000 | bytes 10485760 | tf_op jit(solution)/shard_map/pallas_call | solution.py:239
  542.6 7.7 collective-permute-done.5
  550.3 5.0 add_convert_fusion
  555.4 7.6 multiply_reduce_fusion.10
  563.0 2.3 pad_maximum_fusion.refs_19_
  570.8 309.9 %shard_map.238 = (f32[128,18432]{1,0:T(8,128)}, f32[512,2048]{1,0:T(8,128)}, f32[8,512]{1,0:T(8,128)}, f32[8,256,128]{2,1,0:T(8,128)}, f32[512,2048]{1,0:T(8,128...) custom-call(bf16[640,4096]{1,0:T(8,128)(2,1)} %get-tuple-element.150, ...), custom_call_target="tpu_custom_call" | custom-call | flops 299999985664 | bytes 800000000 | tf_op jit(solution)/shard_map/pallas_call | solution.py:1149
  880.8 1.8 copy.41
  883.4 5.6 multiply_reduce_fusion
  891.5 4.0 fusion.61
  898.1 10.3 %shard_map.239 = f32[8,128]{1,0:T(8,128)} custom-call(f32[8,128]{1,0:T(8,128)} %broadcast_in_dim.87.part_ref), custom_call_target="tpu_custom_call" | custom-call | tf_op jit(solution)/shard_map/pallas_call | solution.py:1202
  911.8 36.7 %multiply_subtract_fusion = (f32[128,30720]{1,0:T(8,128)}, f32[128,30720]{1,0:T(8,128)}, f32[128,30720]{1,0:T(8,128)}) fusion(f32[128,30720]{1,0:T(8,128)} %refs_0_.1, f32[]{:T(128)S(6)} %div.227, f32[128,18432]{1,0:T(8,128)} %get-tuple-element.54, f32[128,12288]{1,0:T(8,128)} %get-tuple-element.161, f32[128,30720]{1,0:T(8,128)} %param.22, f32[128,30720]{1,0:T(8,128)} %param.23), kind=kLoop, calls=%fused_computation.3 | loop fusion | flops 66846720 | bytes 110100480 | tf_op jit(solution)/shard_map/sub | solution.py:277
  948.4 19.5 %multiply_subtract_fusion.1 = (f32[512,4096]{1,0:T(8,128)}, f32[512,4096]{1,0:T(8,128)}, f32[512,4096]{1,0:T(8,128)}) fusion(f32[512,4096]{1,0:T(8,128)} %refs_1_.1, f32[]{:T(128)S(6)} %div.227, f32[512,1024]{1,0:T(8,128)} %get-tuple-element.110, f32[512,2048]{1,0:T(8,128)} %get-tuple-element.56, f32[512,1024]{1,0:T(8,128)S(1)} %get-tuple-element.109, ...), kind=kLoop, calls=%fused_computation.26 | loop fusion | flops 37748736 | bytes 58720260 | tf_op jit(solution)/shard_map/sub | solution.py:277
  (333 shorter events, 74.8 us)
Async XLA Ops:
  8.0 282.9 %reduce-scatter.2.cloned.1.call-start = ((), (), s32[]{:S(2)}) async-start(), calls=%async_computation.1 | async-start | bytes 1474560 | tf_op jit(solution)/shard_map/reduce_scatter | solution.py:1283
  184.1 138.4 %all-gather.3.cloned.1.call-start = ((), (), s32[]{:S(2)}) async-start(), calls=%async_computation.2 | async-start | bytes 8650752 | tf_op jit(solution)/shard_map/all_gather | solution.py:514
  186.8 168.9 %all-gather.5.cloned.1.call-start = ((), (), s32[]{:S(2)}) async-start(), calls=%async_computation.3 | async-start | bytes 8650752 | tf_op jit(solution)/shard_map/all_gather | solution.py:514
  190.3 30.0 %copy-start.62 = (f32[1,1024]{1,0:T(1,128)}, f32[1,1024]{1,0:T(1,128)S(1)}, u32[]{:S(2)}) copy-start(f32[1,1024]{1,0:T(1,128)S(1)} %get-tuple-element.126) | copy-start | bytes 12292
  192.0 6.2 copy-start.78
  192.1 6.2 copy-start.76
  192.1 28.2 %copy-start.84 = (f32[1024]{0:T(1024)}, f32[1024]{0:T(1024)S(1)}, u32[]{:S(2)}) copy-start(f32[1024]{0:T(1024)S(1)} %get-tuple-element.138) | copy-start | bytes 12292
  192.1 31.8 %copy-start.72 = (f32[1024]{0:T(1024)}, f32[1024]{0:T(1024)S(1)}, u32[]{:S(2)}) copy-start(f32[1024]{0:T(1024)S(1)} %get-tuple-element.134) | copy-start | bytes 12292
  201.0 5.1 collective-permute-start
  208.3 11.9 %copy-start.3 = (bf16[640,2048]{1,0:T(8,128)(2,1)}, bf16[640,2048]{1,0:T(8,128)(2,1)S(1)}, u32[]{:S(2)}) copy-start(bf16[640,2048]{1,0:T(8,128)(2,1)S(1)} %collective-permute-done.refs_2_.refs_4_) | copy-start | bytes 7864324
  208.3 11.9 %copy-start.9 = (bf16[1024,1024]{1,0:T(8,128)(2,1)S(1)}, bf16[1024,1024]{1,0:T(8,128)(2,1)}, u32[]{:S(2)}) copy-start(bf16[1024,1024]{1,0:T(8,128)(2,1)} %copy-done.8) | copy-start | bytes 6291460
  208.3 12.0 %copy-start.28 = (f32[640,1024]{1,0:T(8,128)S(1)}, f32[640,1024]{1,0:T(8,128)}, u32[]{:S(2)}) copy-start(f32[640,1024]{1,0:T(8,128)} %copy-done.27) | copy-start | bytes 7864324
  208.3 16.3 %slice-start.2 = ((s8[8388608]{0:T(1024)(128)(4,1)}), s8[4194304]{0:T(1024)(128)(4,1)S(1)}, s32[]{:S(2)}) async-start(s8[8388608]{0:T(1024)(128)(4,1)} %bitcast.213), calls=%async_computation.6 | async-start | bytes 8388608
  223.5 9.5 copy-start.30
  223.9 9.0 copy-start.82
  223.9 9.0 copy-start.74
  223.9 9.0 slice-start.6
  224.7 8.2 copy-start.50
  224.7 8.3 slice-start.7
  232.9 7.2 copy-start.90
  240.1 23.1 %slice-start.4 = ((s8[6291456]{0:T(1024)(128)(4,1)}), s8[4194304]{0:T(1024)(128)(4,1)S(1)}, s32[]{:S(2)}) async-start(s8[6291456]{0:T(1024)(128)(4,1)} %bitcast.215), calls=%async_computation.8 | async-start | bytes 8388608
  240.5 22.7 %slice-start.5 = ((s8[6291456]{0:T(1024)(128)(4,1)}), s8[2097152]{0:T(1024)(128)(4,1)S(1)}, s32[]{:S(2)}) async-start(s8[6291456]{0:T(1024)(128)(4,1)} %bitcast.215), calls=%async_computation.9 | async-start | bytes 4194304
  241.7 20.2 %collective-permute-start.1 = (bf16[10,32,1024]{2,1,0:T(8,128)(2,1)S(1)}, bf16[10,32,1024]{2,1,0:T(8,128)(2,1)S(1)}, u32[]{:S(2)}, u32[]{:S(2)}) collective-permute-start(bf16[10,32,1024]{2,1,0:T(8,128)(2,1)S(1)} %get-tuple-element.120), channel_id=1, source_target_pairs={{0,3},{1,0},{2,1},{3,2},{4,7},{5,4},{6,5},{7,6},{8,11},{9,8},{10,9... | collective-permute-start | bytes 1966088 | tf_op jit(solution)/shard_map/ppermute | solution.py:43
  268.2 16.4 %copy-start.2 = (bf16[640,3072]{1,0:T(8,128)(2,1)}, bf16[640,3072]{1,0:T(8,128)(2,1)S(1)}, u32[]{:S(2)}) copy-start(bf16[640,3072]{1,0:T(8,128)(2,1)S(1)} %convolution_convert_fusion.refs_0_.refs_1_.refs_2_) | copy-start | bytes 11796484
  285.6 16.3 %copy-start.5 = (bf16[1024,1024]{1,0:T(8,128)(2,1)S(1)}, bf16[1024,1024]{1,0:T(8,128)(2,1)}, u32[]{:S(2)}) copy-start(bf16[1024,1024]{1,0:T(8,128)(2,1)} %copy-done.4) | copy-start | bytes 6291460
  285.6 15.0 %collective-permute-start.2 = (bf16[10,32,1024]{2,1,0:T(8,128)(2,1)}, bf16[10,32,1024]{2,1,0:T(8,128)(2,1)}, u32[]{:S(2)}, u32[]{:S(2)}) collective-permute-start(bf16[10,32,1024]{2,1,0:T(8,128)(2,1)} %get-tuple-element.118), channel_id=1, source_target_pairs={{0,1},{1,2},{2,3},{3,0},{4,5},{5,6},{6,7},{7,4},{8,9},{9,10},{10,1... | collective-permute-start | bytes 1966088 | tf_op jit(solution)/shard_map/ppermute | solution.py:43
  290.9 10.9 %copy-start.23 = (f32[640,1024]{1,0:T(8,128)S(1)}, f32[640,1024]{1,0:T(8,128)}, u32[]{:S(2)}) copy-start(f32[640,1024]{1,0:T(8,128)} %copy-done.22) | copy-start | bytes 7864324
  304.9 12.9 %copy-start.25 = (f32[640,1024]{1,0:T(8,128)}, f32[640,1024]{1,0:T(8,128)S(1)}, u32[]{:S(2)}) copy-start(f32[640,1024]{1,0:T(8,128)S(1)} %get-tuple-element.104) | copy-start | bytes 7864324
  309.4 8.4 copy-start.15
  309.4 8.4 copy-start.12
  371.2 12.8 %copy-start.51 = (bf16[640,1024]{1,0:T(8,128)(2,1)}, bf16[640,1024]{1,0:T(8,128)(2,1)S(1)}, u32[]{:S(2)}) copy-start(bf16[640,1024]{1,0:T(8,128)(2,1)S(1)} %multiply_convert_fusion.5.refs_10_) | copy-start | bytes 3932164
  371.2 12.8 %copy-start.33 = (f32[640,1024]{1,0:T(8,128)S(1)}, f32[640,1024]{1,0:T(8,128)}, u32[]{:S(2)}) copy-start(f32[640,1024]{1,0:T(8,128)} %copy-done.32) | copy-start | bytes 7864324
  384.0 10.6 %copy-start.91 = (bf16[640,4096]{1,0:T(8,128)(2,1)}, bf16[640,4096]{1,0:T(8,128)(2,1)S(1)}, u32[]{:S(2)}) copy-start(bf16[640,4096]{1,0:T(8,128)(2,1)S(1)} %fusion.6.refs_11_) | copy-start | bytes 15728644
  400.8 8.9 copy-start.19
  400.8 8.9 copy-start.26
  417.1 9.5 collective-permute-start.3
  457.4 17.2 %collective-permute-start.4 = (f32[10,32,1024]{2,1,0:T(8,128)S(1)}, f32[10,32,1024]{2,1,0:T(8,128)S(1)}, u32[]{:S(2)}, u32[]{:S(2)}) collective-permute-start(f32[10,32,1024]{2,1,0:T(8,128)S(1)} %get-tuple-element.115), channel_id=1, source_target_pairs={{0,1},{1,2},{2,3},{3,0},{4,5},{5,6},{6,7},{7,4},{8,9},{9,10},{10,1... | collective-permute-start | bytes 3932168 | tf_op jit(solution)/shard_map/ppermute | solution.py:43
  480.9 13.9 %copy-start.31 = (f32[640,1024]{1,0:T(8,128)S(1)}, f32[640,1024]{1,0:T(8,128)}, u32[]{:S(2)}) copy-start(f32[640,1024]{1,0:T(8,128)} %copy-done.30) | copy-start | bytes 7864324
  480.9 13.9 %copy-start.69 = (f32[640]{0:T(1024)S(1)}, f32[640]{0:T(1024)}, u32[]{:S(2)}) copy-start(f32[640]{0:T(1024)} %copy-done.68) | copy-start | bytes 7684
  480.9 13.9 %copy-start.73 = (f32[1024]{0:T(1024)S(1)}, f32[1024]{0:T(1024)}, u32[]{:S(2)}) copy-start(f32[1024]{0:T(1024)} %copy-done.72) | copy-start | bytes 12292
  480.9 13.9 %copy-start.75 = (f32[640]{0:T(1024)S(1)}, f32[640]{0:T(1024)}, u32[]{:S(2)}) copy-start(f32[640]{0:T(1024)} %copy-done.74) | copy-start | bytes 7684
  494.8 10.3 %copy-start.83 = (f32[640]{0:T(1024)S(1)}, f32[640]{0:T(1024)}, u32[]{:S(2)}) copy-start(f32[640]{0:T(1024)} %copy-done.82) | copy-start | bytes 7684
  509.7 32.5 %copy-start.39 = (bf16[640,1024]{1,0:T(8,128)(2,1)S(1)}, bf16[640,1024]{1,0:T(8,128)(2,1)}, u32[]{:S(2)}) copy-start(bf16[640,1024]{1,0:T(8,128)(2,1)} %copy-done.38) | copy-start | bytes 3932164
  541.2 9.1 collective-permute-start.5
  883.4 6.2 copy-start.87
  891.5 19.5 %copy-start.55 = (f32[19,1024]{1,0:T(8,128)S(1)}, f32[19,1024]{1,0:T(8,128)}, u32[]{:S(2)}) copy-start(f32[19,1024]{1,0:T(8,128)} %param.27) | copy-start | bytes 233476
  891.5 19.5 %copy-start.64 = (f32[19,1024]{1,0:T(8,128)S(1)}, f32[19,1024]{1,0:T(8,128)}, u32[]{:S(2)}) copy-start(f32[19,1024]{1,0:T(8,128)} %param.28) | copy-start | bytes 233476
  891.5 19.5 %copy-start.65 = (f32[19,1024]{1,0:T(8,128)S(1)}, f32[19,1024]{1,0:T(8,128)}, u32[]{:S(2)}) copy-start(f32[19,1024]{1,0:T(8,128)} %param.29) | copy-start | bytes 233476
  (61 other events, 158.6 us)
Sparse Core Ops, SparseCore 0:
  184.2 88.7 reduce-scatter.1
Sparse Core Ops, SparseCore 1:
  187.5 87.1 all-gather.2
  277.4 78.2 all-gather.4

commit v9 on v8

--- a/solution.py
+++ b/solution.py
@@ -28,16 +28,6 @@
 DECAY = 0.1
 
 
-def from_partner(block, axis, distance):
-    count = lax.axis_size(axis)
-    route = []
-    for low in range(count):
-        high = low | 1 << distance
-        if high != low and high < count:
-            route += [(low, high), (high, low)]
-    return lax.ppermute(block, axis, route)
-
-
 def shifted(value, axis, by):
     length = lax.axis_size(axis)
     return lax.ppermute(value, axis, [(i, (i + by) % length) for i in range(length)])
@@ -136,6 +126,20 @@
 
 def only(head, value):
     return jnp.where(lanes_of(head, value.shape), value, jnp.zeros_like(value))
+
+
+def attention_gradients(queries, keys, values, grad_out, text_len):
+    dq, dk, dv = [], [], []
+    for head in range(2):
+        probs = softmax_of(matmul_nt(keys, only(head, queries)), 0, text_len)
+        dprobs = matmul_nt(values, only(head, grad_out))
+        dv.append(matmul(probs.astype(jnp.bfloat16), grad_out))
+        inner = jnp.sum(probs * dprobs, 0, keepdims=True)
+        dscores = (probs * (dprobs - inner)).astype(jnp.bfloat16)
+        dk.append(matmul(dscores, queries))
+        dq.append(matmul_tn(dscores, keys))
+    dq, dk, dv = (jnp.where(lanes_of(0, x[0].shape), *x) for x in (dq, dk, dv))
+    return dq * HEAD_DIM ** (-0.5), dk, dv
 
 
 def key_sets(key_refs, runs, text_len):
@@ -161,8 +165,7 @@
     q_ref, k_refs, v_refs = refs[0], refs[1 : 1 + sets], refs[1 + sets : 1 + 2 * sets]
     grad_ref = refs[1 + 2 * sets]
     dq_ref = refs[2 + 2 * sets]
-    own_ref = refs[3 + 2 * sets] if len(refs) > 3 + 2 * sets else None
-    far_ref = refs[4 + 2 * sets] if sets == 2 else None
+    own_ref = refs[3 + 2 * sets] if text_len else None
     pair = pl.program_id(0)
     cols = [pl.ds(pl.multiple_of(i * D + pair * 2 * HEAD_DIM, 128), 2 * HEAD_DIM) for i in range(3)]
     merged = dq_ref.shape[1] == 3 * D
@@ -170,29 +173,171 @@
         queries = take(q_ref, runs) * HEAD_DIM ** (-0.5)
         keys, values = key_sets(k_refs, runs, text_len), key_sets(v_refs, runs, text_len)
         grad_out = take(grad_ref, runs)
-        dq, dk, dv = [], [], []
-        for head in range(2):
-            probs = softmax_of(matmul_nt(keys, only(head, queries)), 0, text_len)
-            dprobs = matmul_nt(values, only(head, grad_out))
-            dv.append(matmul(probs.astype(jnp.bfloat16), grad_out))
-            inner = jnp.sum(probs * dprobs, 0, keepdims=True)
-            dscores = (probs * (dprobs - inner)).astype(jnp.bfloat16)
-            dk.append(matmul(dscores, queries))
-            dq.append(matmul_tn(dscores, keys))
-        dq, dk, dv = (jnp.where(lanes_of(0, x[0].shape), *x) for x in (dq, dk, dv))
-        put(dq_ref, cols[0], runs, dq * HEAD_DIM ** (-0.5))
+        dq, dk, dv = attention_gradients(queries, keys, values, grad_out, text_len)
+        put(dq_ref, cols[0], runs, dq)
         if merged:
             put(dq_ref, cols[1], runs, dk)
             put(dq_ref, cols[2], runs, dv)
-        elif text_len:
+        else:
             own_ref[:, cols[0]] = dk
             own_ref[:, cols[1]] = dv
-        else:
-            half = dk.shape[0] // 2
-            put(own_ref, cols[0], runs, dk[:half])
-            put(own_ref, cols[1], runs, dv[:half])
-            put(far_ref, cols[0], runs, dk[half:])
-            put(far_ref, cols[1], runs, dv[half:])
+
+
+def pair_cols(which, pair):
+    return pl.ds(pl.multiple_of(which * D + pair * 2 * HEAD_DIM, 128), 2 * HEAD_DIM)
+
+
+def take_cols(ref, cols, runs):
+    return jnp.concatenate([ref[low : low + many, cols] for low, many in runs], 0)
+
+
+def attend_frames_kernel(windows, qkv_ref, out_ref, far_ref, send, recv):
+    band = lax.axis_index("band")
+    partner = (lax.axis_index("clip"), band + 1 - 2 * (band % 2))
+    greet([partner])
+
+    def copies(pair):
+        return [
+            pltpu.make_async_remote_copy(
+                qkv_ref.at[:, pair_cols(1 + i, pair)],
+                far_ref.at[:, pair_cols(i, pair)],
+                send.at[pair, i],
+                recv.at[pair, i],
+                partner,
+                MESH,
+            )
+            for i in range(2)
+        ]
+
+    @pl.loop(0, HEADS // 2)
+    def _(pair):
+        for copy in copies(pair):
+            copy.start()
+
+    @pl.loop(0, HEADS // 2)
+    def _(pair):
+        for copy in copies(pair):
+            copy.wait_recv()
+        for runs in windows:
+            queries = take_cols(qkv_ref, pair_cols(0, pair), runs) * HEAD_DIM ** (-0.5)
+            keys, values = (
+                jnp.concatenate(
+                    [
+                        take_cols(qkv_ref, pair_cols(1 + i, pair), runs),
+                        take_cols(far_ref, pair_cols(i, pair), runs),
+                    ],
+                    0,
+                )
+                for i in range(2)
+            )
+            outs = []
+            for head in range(2):
+                probs = softmax_of(matmul_nt(only(head, queries), keys), 1, 0)
+                outs.append(matmul(probs.astype(jnp.bfloat16), values))
+            put(out_ref, pair_cols(0, pair), runs, jnp.where(lanes_of(0, outs[0].shape), *outs))
+
+    @pl.loop(0, HEADS // 2)
+    def _(pair):
+        for copy in copies(pair):
+            copy.wait_send()
+
+
+def attend_frames_back_kernel(
+    windows, qkv_ref, far_ref, grad_ref, out_ref, own_buf, far_put, far_got, send, recv
+):
+    band = lax.axis_index("band")
+    partner = (lax.axis_index("clip"), band + 1 - 2 * (band % 2))
+    greet([partner])
+
+    def copies(pair):
+        return [
+            pltpu.make_async_remote_copy(
+                far_put.at[:, pair_cols(i, pair)],
+                far_got.at[:, pair_cols(i, pair)],
+                send.at[pair, i],
+                recv.at[pair, i],
+                partner,
+                MESH,
+            )
+            for i in range(2)
+        ]
+
+    def merge(pair):
+        for i, copy in enumerate(copies(pair)):
+            copy.wait_recv()
+            cols = pair_cols(i, pair)
+            total = own_buf[:, cols] + far_got[:, cols]
+            out_ref[:, pair_cols(1 + i, pair)] = total.astype(jnp.bfloat16)
+
+    @pl.loop(0, HEADS // 2)
+    def _(pair):
+        for runs in windows:
+            queries = take_cols(qkv_ref, pair_cols(0, pair), runs) * HEAD_DIM ** (-0.5)
+            keys, values = (
+                jnp.concatenate(
+                    [
+                        take_cols(qkv_ref, pair_cols(1 + i, pair), runs),
+                        take_cols(far_ref, pair_cols(i, pair), runs),
+                    ],
+                    0,
+                )
+                for i in range(2)
+            )
+            grad_out = take_cols(grad_ref, pair_cols(0, pair), runs)
+            dq, *dkv = attention_gradients(queries, keys, values, grad_out, 0)
+            put(out_ref, pair_cols(0, pair), runs, dq)
+            half = keys.shape[0] // 2
+            for i, value in enumerate(dkv):
+                put(own_buf, pair_cols(i, pair), runs, value[:half])
+                put(far_put, pair_cols(i, pair), runs, value[half:])
+        for copy in copies(pair):
+            copy.start()
+
+        @pl.when(pair >= 1)
+        def _():
+            merge(pair - 1)
+
+    merge(HEADS // 2 - 1)
+
+    @pl.loop(0, HEADS // 2)
+    def _(pair):
+        for copy in copies(pair):
+            copy.wait_send()
+
+
+def attend_frames(qkv, windows):
+    tokens = qkv.shape[0]
+    dma = pltpu.SemaphoreType.DMA((HEADS // 2, 2))
+    return pl.pallas_call(
+        partial(attend_frames_kernel, windows),
+        out_shape=(
+            jax.ShapeDtypeStruct((tokens, D), jnp.bfloat16),
+            jax.ShapeDtypeStruct((tokens, 2 * D), jnp.bfloat16),
+        ),
+        in_specs=[IN_VMEM],
+        out_specs=(IN_VMEM,) * 2,
+        scratch_shapes=[dma, dma],
+        compiler_params=pltpu.CompilerParams(
+            collective_id=4, has_side_effects=True, vmem_limit_bytes=40 << 20
+        ),
+        cost_estimate=attention_cost(tokens, 256, 2),
+    )(qkv)
+
+
+def attend_frames_back(qkv, far_kv, grad_out, windows):
+    tokens = qkv.shape[0]
+    dma = pltpu.SemaphoreType.DMA((HEADS // 2, 2))
+    return pl.pallas_call(
+        partial(attend_frames_back_kernel, windows),
+        out_shape=jax.ShapeDtypeStruct(qkv.shape, jnp.bfloat16),
+        in_specs=[IN_VMEM] * 3,
+        out_specs=IN_VMEM,
+        scratch_shapes=[pltpu.VMEM((tokens, 2 * D), jnp.float32)] * 3 + [dma, dma],
+        compiler_params=pltpu.CompilerParams(
+            collective_id=5, has_side_effects=True, vmem_limit_bytes=50 << 20
+        ),
+        cost_estimate=attention_cost(tokens, 256, 5),
+    )(qkv, far_kv, grad_out)
 
 
 def head_cols(array, first):
@@ -334,10 +479,14 @@
 def gather_kernel(count, picks, sides, *refs):
     num = len(picks)
     packs, vec_ref, text_ref = refs[:2], refs[2], refs[3]
-    full, (vec_out, text_out), refs = refs[4 : 4 + num], refs[4 + num : 6 + num], refs[6 + num :]
+    full, (vec_out, text_out, kv_out) = refs[4 : 4 + num], refs[4 + num : 7 + num]
+    refs = refs[7 + num :]
     wide, shards = refs[:num], refs[num : 2 * num]
     ring_send, ring_recv, pair_send, pair_recv, cross_send, cross_recv = refs[2 * num : 2 * num + 6]
-    load_sem, own_sem, part_send, part_recv, part_own = refs[2 * num + 6 :]
+    load_sem, own_sem, part_send, part_recv, part_own = refs[2 * num + 6 : 2 * num + 11]
+    kv_wide, kv_part, kv_put, kv_got, kv_sum, kv_load, kv_send, kv_recv, band_send, band_recv = refs[
+        2 * num + 11 :
+    ]
     shapes = [(packs[pack].shape[0], cols) for pack, _, cols in picks]
     loads = [
         pltpu.make_async_copy(
@@ -345,7 +494,12 @@
         )
         for group, (pack, start, cols) in enumerate(picks)
     ]
-    for copy in loads:
+    kv_width = kv_wide.shape[1]
+    kv_first = D + lax.axis_index("band") * kv_width
+    kv_weight = pltpu.make_async_copy(
+        packs[1].at[:, pl.ds(pl.multiple_of(kv_first, 128), kv_width)], kv_wide, kv_load
+    )
+    for copy in loads + [kv_weight]:
         copy.start()
     me = lax.axis_index("clip")
     band = lax.axis_index("band")
@@ -357,7 +511,9 @@
     partner = (me, band + 1 - 2 * core)
     mirror = (me, band + 2 - 4 * plane)
     peers = [((me + step) % count, band) for step in range(1, count)]
-    greet(peers + [partner, mirror])
+    band_count = 2 * D // kv_width
+    band_peers = [(me, (band + step) % band_count) for step in range(1, band_count)]
+    greet(peers + band_peers)
 
     def block(ref, group, owner):
         rows, cols = shapes[group]
@@ -462,6 +618,36 @@
     for copy in parts[1::2]:
         copy.start()
 
+    def kv_copy(hop):
+        return pltpu.make_async_remote_copy(
+            kv_put.at[hop], kv_got.at[hop], kv_send.at[hop], kv_recv.at[hop], following, MESH
+        )
+
+    def kv_hop(hop):
+        owner = ring_clip((place - onward * (hop + 1) + 2 * count) % count, count)
+        total = kv_part[owner]
+        if not isinstance(hop, int) or hop > 0:
+            kv_copy(hop - 1).wait_recv()
+            total = total + kv_got[hop - 1]
+        kv_put[hop] = total
+        kv_copy(hop).start()
+
+    def band_copies():
+        return [
+            pltpu.make_async_remote_copy(
+                kv_sum, kv_out.at[band], band_send.at[step], band_recv.at[step], peer, MESH
+            )
+            for step, peer in enumerate(band_peers)
+        ]
+
+    for copy in parts_own + parts:
+        copy.wait()
+    kv_weight.wait()
+    weight = kv_wide[...].astype(jnp.bfloat16)
+    for owner in range(count):
+        kv_part[owner] = matmul(text_out[owner], weight)
+    kv_hop(0)
+
     @pl.loop(1, count - 1)
     def _(step):
         for group in range(num):
@@ -470,6 +656,7 @@
             def _(group=group):
                 ring_arrival(group, step - 1, True)
 
+        kv_hop(step)
         for group in range(num):
 
             @off_ring(group, step >= 2)
@@ -489,8 +676,11 @@
             def _(group=group, late=late):
                 cross_arrival(group, late)
 
-    for copy in parts_own + parts:
-        copy.wait()
+    kv_copy(count - 2).wait_recv()
+    kv_sum[...] = (kv_part[me] + kv_got[count - 2]).astype(jnp.bfloat16)
+    kv_out[band] = kv_sum[...]
+    for copy in band_copies():
+        copy.start()
     for group in range(num):
         own_copy(group).wait()
 
@@ -505,6 +695,10 @@
                     cross_copy(group, step).wait_send()
 
             pair_copy(group, step).wait()
+        kv_copy(step).wait_send()
+
+    for copy in band_copies():
+        copy.wait()
 
 
 def gather_quarters(shard):
@@ -522,34 +716,44 @@
 
 
 def gather_weights(packs, picks, sides, vectors, texts):
-    count = lax.axis_size("clip")
+    count, band_count = lax.axis_size("clip"), lax.axis_size("band")
     num = len(picks)
-    steps = pltpu.SemaphoreType.DMA((count - 1, num))
+    dma = pltpu.SemaphoreType.DMA
     shapes = [(packs[pack].shape[0], cols) for pack, _, cols in picks]
+    kv_shape = (texts.shape[1], 2 * D // band_count)
+    kv_all = pltpu.VMEM((count,) + kv_shape, jnp.float32)
+    kv_hops = pltpu.VMEM((count - 1,) + kv_shape, jnp.float32)
     out = pl.pallas_call(
         partial(gather_kernel, count, picks, sides),
         out_shape=tuple(
             jax.ShapeDtypeStruct((count * rows, cols), jnp.bfloat16) for rows, cols in shapes
         )
-        + tuple(jax.ShapeDtypeStruct(v.shape, v.dtype) for v in (vectors, texts)),
+        + tuple(jax.ShapeDtypeStruct(v.shape, v.dtype) for v in (vectors, texts))
+        + (jax.ShapeDtypeStruct((band_count,) + kv_shape, jnp.bfloat16),),
         in_specs=[ANY] * 4,
-        out_specs=(ANY,) * (num + 2),
+        out_specs=(ANY,) * (num + 1) + (IN_VMEM,) * 2,
         scratch_shapes=[pltpu.VMEM(shape, jnp.float32) for shape in shapes]
         + [pltpu.VMEM(shape, jnp.bfloat16) for shape in shapes]
-        + [steps] * 6
+        + [dma((count - 1, num))] * 6
+        + [dma((num,)), dma((num,)), dma((2, count - 1)), dma((2, count - 1)), dma((2,))]
         + [
-            pltpu.SemaphoreType.DMA((num,)),
-            pltpu.SemaphoreType.DMA((num,)),
-            pltpu.SemaphoreType.DMA((2, count - 1)),
-            pltpu.SemaphoreType.DMA((2, count - 1)),
-            pltpu.SemaphoreType.DMA((2,)),
+            pltpu.VMEM((packs[1].shape[0], kv_shape[1]), jnp.float32),
+            kv_all,
+            kv_hops,
+            kv_hops,
+            pltpu.VMEM(kv_shape, jnp.bfloat16),
+            dma,
+            dma((count - 1,)),
+            dma((count - 1,)),
+            dma((band_count - 1,)),
+            dma((band_count - 1,)),
         ],
         compiler_params=pltpu.CompilerParams(
-            collective_id=1, has_side_effects=True, vmem_limit_bytes=32 << 20
+            collective_id=1, has_side_effects=True, vmem_limit_bytes=50 << 20
         ),
         cost_estimate=pl.CostEstimate(flops=2 * 10**11, bytes_accessed=6 * 10**8, transcendentals=0),
     )(*packs, vectors, texts)
-    return out[:num], out[num], out[num + 1]
+    return out[:num], out[num], out[num + 1], out[num + 2]
 
 
 WIRE_MAX = 32767.0
@@ -1258,11 +1462,8 @@
     )
     part_modul = matmul(time_rows, w_wide[:, : 12 * D].astype(jnp.bfloat16))
     kv_cols = 2 * D // band_count
-    kv_weight = lax.dynamic_slice(
-        w_deep, (0, D + band_at * kv_cols), (deep_rows, kv_cols)
-    ).astype(jnp.bfloat16)
     up_b_w = gather_quarters(w_wide[:, 22 * D + FF :])
-    gathered, all_modul, all_text = gather_weights(
+    gathered, all_modul, all_text, keyval = gather_weights(
         (w_wide, w_deep),
         (
             (0, 22 * D, FF),
@@ -1279,11 +1480,9 @@
         text_cols,
     )
     up_a_w, down_a_w, out_a_w, out_b_w, query_w, cross_out_w, qkv_a_w, qkv_b_w = gathered
-    part_kv = matmul(all_text.reshape(clip_count * TEXT_PAD, deep_rows), kv_weight)
-    keyval = lax.psum_scatter(part_kv, "clip", scatter_dimension=0, tiled=True)
+    keyval = keyval.transpose(1, 0, 2).reshape(TEXT_PAD, 2 * D)
     late_down_b, all_modul = lax.optimization_barrier((w_deep[:, 3 * D :], all_modul))
     down_b_w = gather_quarters(late_down_b)
-    keyval = lax.all_gather(keyval.astype(jnp.bfloat16), "band", axis=1, tiled=True)
     small_low = w_small.astype(jnp.bfloat16)
     small_val = small_low.astype(jnp.float32)
     num_frames, num_rows, num_cols = (latents.shape[1], latents.shape[2], latents.shape[3])
@@ -1308,9 +1507,7 @@
     normed_a, back_a = jax.vjp(norm_modulated, stream_zero, mod_a[0], mod_a[1])
     in_a = normed_a.astype(jnp.bfloat16)
     qkv_a = matmul(in_a, qkv_a_w).astype(jnp.bfloat16)
-    far_kv = from_partner(qkv_a[:, D:], "band", 0)
-    space_kv = [(qkv_a, HEADS // 2, HEADS), (far_kv, 0, HEADS // 2)]
-    att_a = attend(qkv_a, space_kv, frame_windows)
+    att_a, far_kv = attend_frames(qkv_a, frame_windows)
     proj_a = matmul(att_a, out_a_w)
     stream_one = stream_zero + mod_a[2] * proj_a
     stream_two, saved_a = mlp_forward(stream_one, mod_a, up_a_w, down_a_w)
@@ -1370,9 +1567,7 @@
     grad_gate_a = jnp.sum(grad_stream * proj_a, 0)
     factors_oa = (att_a, grad_proj)
     grad_att = matmul_nt(grad_proj, out_a_w).astype(jnp.bfloat16)
-    grad_q, grad_own, grad_far = attend_back(qkv_a, space_kv, grad_att, frame_windows)
-    grad_kv = grad_own + from_partner(grad_far, "band", 0)
-    grad_qkv = jnp.concatenate([grad_q, grad_kv.astype(jnp.bfloat16)], 1)
+    grad_qkv = attend_frames_back(qkv_a, far_kv, grad_att, frame_windows)
     factors_qkva = (in_a, grad_qkv)
     grad_part, grad_shift_a, grad_scale_a = back_a(matmul_nt(grad_qkv, qkv_a_w))
     grad_stream = grad_stream + grad_part

time: 984 us -> 998 us (1.014)
  Pallas kernels: 576 us -> 640 us
  waiting for transfers between devices: 75.8 us -> 43.2 us
    pallas_call x1, Pallas kernels: 147 us -> 207 us  [gather_weights(): pl.pallas_call(partial(gather_kernel, count, picks, sides), out_shape=tup...]
    pallas_call x0 -> x2, Pallas kernels: none -> 45.3 us  [the longest x1 33.4 us: attend_frames_back(): pl.pallas_call(partial(attend_frames_back_kernel, windows), out_shape=jax...]
    pallas_call x3 -> x2, Pallas kernels: 63.3 us -> 31.5 us  [attend_back(): pl.pallas_call(partial(attend_back_kernel, windows, text_len, sets), grid...]
    all_gather x2, waiting for transfers between devices: 21.2 us -> 0.01 us  [gather_quarters(): lax.all_gather(own.astype(jnp.bfloat16), ('clip', 'band'), axis=0, tiled=...]
    pallas_call x3 -> x2, Pallas kernels: 36.6 us -> 25 us  [attend(): pl.pallas_call(partial(attend_kernel, windows, text_len, len(key_values))...]
    ppermute x2 -> x0, waiting for transfers between devices: 11 us -> none  [from_partner(): return lax.ppermute(block, axis, route)]
    unnamed x203 -> x215, local copies, waits for them, and re-layouts: 29.6 us -> 22.2 us
    dot_general x14 -> x13, matrix products: 65.8 us -> 67.4 us  [matmul(): return jnp.dot(left_op, right_op, preferred_element_type=jnp.float32)]
  transfers between devices with their start and end apart: 9 -> 6, of which waited for: 6 -> 4; matrix products, arithmetic and copies ran while one was open for 7% -> 8% of each run, Pallas kernels for 4% -> 26%
where the time goes in v9:
time: 998 us; the launch traced here: 987 us
  Pallas kernels  640 us (64%)
  matrix products  147 us (15%)
  other arithmetic  84.1 us (8%)
  waiting for transfers between devices  43.2 us (4%)
  local copies, waits for them, and re-layouts  42.3 us (4%)
  between operations  24.5 us (2%)
    pallas_call x1, Pallas kernels, reduce_gradients(): pl.pallas_call(partial(reduce_kernel, count, tokens, phases), out_shape=(...  311 us
    pallas_call x1, Pallas kernels, gather_weights(): pl.pallas_call(partial(gather_kernel, count, picks, sides), out_shape=tup...  207 us
    dot_general x11, matrix products, matmul_nt(): lax.dot_general(left_op, right_op, (((1,), (1,)), ((), ())), preferred_el...  72.8 us
    dot_general x13, matrix products, matmul(): return jnp.dot(left_op, right_op, preferred_element_type=jnp.float32)  67.4 us
    sub x3, other arithmetic, adam_update(): weight - learn_rate * (first_hat / (jnp.sqrt(second_hat) + ADAM_EPS) + DE...  56.7 us
    ppermute x4, waiting for transfers between devices, shifted(): lax.ppermute(value, axis, [(i, (i + by) % length) for i in range(length)])  43.1 us
    pallas_call x1, Pallas kernels, attend_frames_back(): pl.pallas_call(partial(attend_frames_back_kernel, windows), out_shape=jax...  33.4 us
    pallas_call x2, Pallas kernels, attend_back(): pl.pallas_call(partial(attend_back_kernel, windows, text_len, sets), grid...  31.5 us
  transfers between devices with their start and end apart: 6, of which 4 were waited for; matrix products, arithmetic and copies ran while one was open for 8% of the time, Pallas kernels for 26%

profile of v9, /device:TPU:0, one launch (start us, length us, event | category | flops | bytes accessed | tf_op | source)
XLA Modules:
  0.0 987.3 jit_solution(255783995376513296)
XLA Ops:
  7.2 1.7 slice.162
  11.8 9.7 shard_map.230
  22.6 3.4 fusion.16
  26.6 2.7 slice.143
  29.5 207.0 %shard_map.231 = (bf16[1024,4096]{1,0:T(8,128)(2,1)}, bf16[4096,1024]{1,0:T(8,128)(2,1)}, bf16[1024,1024]{1,0:T(8,128)(2,1)}, bf16[1024,1024]{1,0:T(8,128)(2,1)}...) custom-call(f32[128,30720]{1,0:T(8,128)} %refs_0_.1, ...), custom_call_target="tpu_custom_call" | custom-call | flops 199999995904 | bytes 600000000 | tf_op jit(solution)/shard_map/pallas_call | solution.py:726
  237.3 1.7 dynamic-slice_convert_fusion
  247.3 4.5 convolution_convert_fusion.1.qkv_ref
  251.9 12.0 %shard_map.232 = (bf16[640,1024]{1,0:T(8,128)(2,1)S(1)}, bf16[640,2048]{1,0:T(8,128)(2,1)S(1)}) custom-call(bf16[640,3072]{1,0:T(8,128)(2,1)S(1)} %convolution_convert_fusion.1.qkv_ref), custom_call_target="tpu_custom_call" | custom-call | flops 1342177280 | bytes 10485760 | tf_op jit(solution)/shard_map/pallas_call | solution.py:311
  263.9 3.2 fusion.57
  268.3 8.2 multiply_convert_fusion.1
  276.6 11.1 %fusion.56 = (f32[640]{0:T(1024)S(1)}, f32[640,1024]{1,0:T(8,128)S(1)}, f32[640,1024]{1,0:T(8,128)}) fusion(f32[640,1024]{1,0:T(8,128)S(1)} %get-tuple-element.108, f32[1024]{0:T(1024)S(1)} %get-tuple-element.135, bf16[640,4096]{1,0:T(8,128)(2,1)S(1)} %get-tuple-element.144.refs_6_, bf16[4096,1024]{1,0:T(8,128)(2,1)} %get-tuple-element.40), kind=kOutput, calls=%fused_computation.199 | convolution fusion | flops 5370674688 | bytes 21502464 | tf_op jit(solution)/shard_map/dot_general | solution.py:37
  289.2 1.9 collective-permute-start
  291.2 17.2 %collective-permute-done = bf16[10,32,1024]{2,1,0:T(8,128)(2,1)S(1)} collective-permute-done((bf16[10,32,1024]{2,1,0:T(8,128)(2,1)S(1)}, bf16[10,32,1024]{2,1,0:T(8,128)(2,1)S(1)}, u32[]{:S(2)}, u32[]{:S(2)}) %collective-permute-start) | collective-permute-done | bytes 655392 | tf_op jit(solution)/shard_map/ppermute | solution.py:33
  309.6 4.5 convolution_convert_fusion.refs_0_.refs_1_.refs_2_
  314.1 16.4 %shard_map.233 = bf16[640,1024]{1,0:T(8,128)(2,1)S(1)} custom-call(bf16[640,3072]{1,0:T(8,128)(2,1)S(1)} %convolution_convert_fusion.refs_0_.refs_1_.refs_2_, bf16[640,3072]{1,0:T(8,128)(2,1)S(1)} %convolution_convert_fusion.refs_0_.refs_1_.refs_2_, bf16[640,3072]{1,0:T(8,128)(2,1)S(1)} %convolution_convert_fusion.refs_0_.refs_1_.refs_2_), custom_call_target="tpu_custom_call" | custom-call | flops 1677721600 | bytes 10485760 | tf_op jit(solution)/shard_map/pallas_call | solution.py:363
  331.7 2.0 collective-permute-start.1
  338.4 3.8 collective-permute-done.1
  343.6 5.1 fusion.55
  349.8 1.9 copy-done.97
  351.7 1.5 convolution_convert_fusion.5.refs_0_
  353.3 8.6 shard_map.234.refs_2_
  361.9 1.6 fusion.63
  365.0 1.6 add_convert_fusion.refs_1_
  366.6 11.9 %multiply_convert_fusion = (bf16[640,4096]{1,0:T(8,128)(2,1)}, f32[640,4096]{1,0:T(8,128)}) fusion(bf16[640,1024]{1,0:T(8,128)(2,1)} %add_convert_fusion.refs_1_, bf16[1024,4096]{1,0:T(8,128)(2,1)} %all-gather.3.cloned.1.call-done), kind=kOutput, calls=%fused_computation.20 | convolution fusion | flops 5381816320 | bytes 25427968 | tf_op jit(solution)/shard_map/dot_general | solution.py:37
  378.6 10.1 %fusion.54 = (f32[640]{0:T(1024)S(1)}, f32[640,1024]{1,0:T(8,128)S(1)}, f32[640,1024]{1,0:T(8,128)S(1)}) fusion(f32[640,1024]{1,0:T(8,128)} %copy-done.18, f32[1024]{0:T(1024)S(1)} %get-tuple-element.127, bf16[640,4096]{1,0:T(8,128)(2,1)} %get-tuple-element.150.refs_0_, bf16[4096,1024]{1,0:T(8,128)(2,1)} %all-gather.5.cloned.1.call-done), kind=kOutput, calls=%fused_computation.197 | convolution fusion | flops 5370674688 | bytes 21502464 | tf_op jit(solution)/shard_map/dot_general | solution.py:37
  393.0 14.4 %fusion.6.refs_11_ = bf16[640,4096]{1,0:T(8,128)(2,1)} fusion(f32[640,4096]{1,0:T(8,128)} %get-tuple-element.151, bf16[640,1024]{1,0:T(8,128)(2,1)S(1)} %multiply_convert_fusion.5.refs_10_, bf16[4096,1024]{1,0:T(8,128)(2,1)} %all-gather.5.cloned.1.call-done), kind=kOutput, calls=%fused_computation.13 | convolution fusion | flops 5394923520 | bytes 25427968 | tf_op jit(solution)/shard_map/dot_general | solution.py:51
  407.4 10.3 %multiply_reduce_fusion.5 = (f32[1024]{0:T(1024)S(1)}, f32[640]{0:T(1024)S(1)}, f32[1024]{0:T(1024)S(1)}, f32[640,1024]{1,0:T(8,128)S(1)}) fusion(f32[640,1024]{1,0:T(8,128)S(1)} %copy-done.19, f32[640]{0:T(1024)S(1)} %fusion.39, f32[640]{0:T(1024)S(1)} %broadcast_multiply_fusion.3, f32[1024]{0:T(1024)S(1)} %get-tuple-element.129, ...), kind=kOutput, calls=%fused_computation.48 | convolution fusion | flops 5373949440 | bytes 18894336 | tf_op jit(solution)/shard_map/dot_general | solution.py:51
  421.3 2.7 convolution_convert_fusion.4.refs_3_
  424.0 8.7 shard_map.235
  432.8 2.0 multiply_reduce_fusion.2
  439.6 1.6 convolution_convert_fusion.3
  441.4 8.1 collective-permute-done.2
  449.6 22.8 %shard_map.236.refs_15_ = bf16[640,3072]{1,0:T(8,128)(2,1)} custom-call(bf16[640,3072]{1,0:T(8,128)(2,1)} %copy-done, bf16[640,3072]{1,0:T(8,128)(2,1)} %copy-done, bf16[640,3072]{1,0:T(8,128)(2,1)} %copy-done, bf16[640,1024]{1,0:T(8,128)(2,1)S(1)} %bitcast.163), custom_call_target="tpu_custom_call" | custom-call | flops 4194304000 | bytes 10485760 | tf_op jit(solution)/shard_map/pallas_call | solution.py:384
  472.4 7.6 fusion.64
  480.3 2.0 collective-permute-start.3
  483.6 14.0 %collective-permute-done.3 = f32[10,32,1024]{2,1,0:T(8,128)S(1)} collective-permute-done((f32[10,32,1024]{2,1,0:T(8,128)S(1)}, f32[10,32,1024]{2,1,0:T(8,128)S(1)}, u32[]{:S(2)}, u32[]{:S(2)}) %collective-permute-start.3) | collective-permute-done | bytes 1310752 | tf_op jit(solution)/shard_map/ppermute | solution.py:33
  504.5 12.7 %fusion.12.refs_17_ = bf16[640,4096]{1,0:T(8,128)(2,1)S(1)} fusion(f32[640,4096]{1,0:T(8,128)} %get-tuple-element.145, bf16[640,1024]{1,0:T(8,128)(2,1)S(1)} %multiply_convert_fusion.3.refs_16_, bf16[4096,1024]{1,0:T(8,128)(2,1)} %get-tuple-element.40), kind=kOutput, calls=%fused_computation.19 | convolution fusion | flops 5394923520 | bytes 25427968 | tf_op jit(solution)/shard_map/dot_general | solution.py:51
  517.3 10.6 %multiply_reduce_fusion.8 = (f32[1024]{0:T(1024)S(1)}, f32[640]{0:T(1024)S(1)}, f32[1024]{0:T(1024)S(1)}, f32[640,1024]{1,0:T(8,128)S(1)}) fusion(f32[640,1024]{1,0:T(8,128)S(1)} %copy-done.17, f32[640]{0:T(1024)S(1)} %copy-done.74, f32[640]{0:T(1024)S(1)} %copy-done.59, f32[1024]{0:T(1024)S(1)} %copy-done.72, bf16[640,4096]{1,0:T(8,128)(2,1)S(1)} %fusion.12.refs_17_, ...), kind=kOutput, calls=%fused_computation.51 | convolution fusion | flops 5373949440 | bytes 18894336 | tf_op jit(solution)/shard_map/dot_general | solution.py:51
  530.7 1.6 convolution_convert_fusion.2.grad_ref
  532.3 33.4 %shard_map.237.refs_19_ = bf16[640,3072]{1,0:T(8,128)(2,1)} custom-call(bf16[640,3072]{1,0:T(8,128)(2,1)} %copy-done.2, bf16[640,2048]{1,0:T(8,128)(2,1)S(1)} %get-tuple-element.48.far_ref, bf16[640,1024]{1,0:T(8,128)(2,1)S(1)} %convolution_convert_fusion.2.grad_ref), custom_call_target="tpu_custom_call" | custom-call | flops 3355443200 | bytes 10485760 | tf_op jit(solution)/shard_map/pallas_call | solution.py:330
  565.8 8.4 multiply_reduce_fusion.10
  579.8 311.0 %shard_map.238 = (f32[128,18432]{1,0:T(8,128)}, f32[512,2048]{1,0:T(8,128)}, f32[8,512]{1,0:T(8,128)}, f32[8,256,128]{2,1,0:T(8,128)}, f32[512,2048]{1,0:T(8,128...) custom-call(bf16[640,4096]{1,0:T(8,128)(2,1)} %get-tuple-element.150, ...), custom_call_target="tpu_custom_call" | custom-call | flops 299999985664 | bytes 800000000 | tf_op jit(solution)/shard_map/pallas_call | solution.py:1353
  890.8 1.8 copy.44
  893.5 5.6 multiply_reduce_fusion
  901.6 4.0 fusion.58
  908.1 10.3 %shard_map.239 = f32[8,128]{1,0:T(8,128)} custom-call(f32[8,128]{1,0:T(8,128)} %broadcast_in_dim.87.part_ref), custom_call_target="tpu_custom_call" | custom-call | tf_op jit(solution)/shard_map/pallas_call | solution.py:1406
  921.9 36.5 %multiply_subtract_fusion = (f32[128,30720]{1,0:T(8,128)}, f32[128,30720]{1,0:T(8,128)}, f32[128,30720]{1,0:T(8,128)}) fusion(f32[128,30720]{1,0:T(8,128)} %refs_0_.1, f32[]{:T(128)S(6)} %div.227, f32[128,18432]{1,0:T(8,128)} %get-tuple-element.54, f32[128,12288]{1,0:T(8,128)} %get-tuple-element.161, f32[128,30720]{1,0:T(8,128)} %param.22, f32[128,30720]{1,0:T(8,128)} %param.23), kind=kLoop, calls=%fused_computation.3 | loop fusion | flops 66846720 | bytes 110100480 | tf_op jit(solution)/shard_map/sub | solution.py:422
  958.4 19.5 %multiply_subtract_fusion.1 = (f32[512,4096]{1,0:T(8,128)}, f32[512,4096]{1,0:T(8,128)}, f32[512,4096]{1,0:T(8,128)}) fusion(f32[512,4096]{1,0:T(8,128)} %refs_1_.1, f32[]{:T(128)S(6)} %div.227, f32[512,1024]{1,0:T(8,128)} %get-tuple-element.110, f32[512,2048]{1,0:T(8,128)} %get-tuple-element.56, f32[512,1024]{1,0:T(8,128)S(1)} %get-tuple-element.109, ...), kind=kLoop, calls=%fused_computation.26 | loop fusion | flops 37748736 | bytes 58720260 | tf_op jit(solution)/shard_map/sub | solution.py:422
  (331 shorter events, 60.0 us)
Async XLA Ops:
  7.2 359.4 %all-gather.3.cloned.1.call-start = ((), (), s32[]{:S(2)}) async-start(), calls=%async_computation | async-start | bytes 8650752 | tf_op jit(solution)/shard_map/all_gather | solution.py:708
  9.7 368.8 %all-gather.5.cloned.1.call-start = ((), (), s32[]{:S(2)}) async-start(), calls=%async_computation.1 | async-start | bytes 8650752 | tf_op jit(solution)/shard_map/all_gather | solution.py:708
  29.4 209.7 %copy-start.41 = (f32[19,1024]{1,0:T(8,128)S(1)}, f32[19,1024]{1,0:T(8,128)}, u32[]{:S(2)}) copy-start(f32[19,1024]{1,0:T(8,128)} %param.27) | copy-start | bytes 233476
  29.4 210.3 %copy-start.44 = (f32[1,5,8,16,8]{3,4,2,1,0:T(8,128)S(1)}, f32[1,5,8,16,8]{3,4,2,1,0:T(8,128)}, u32[]{:S(2)}) copy-start(f32[1,5,8,16,8]{3,4,2,1,0:T(8,128)} %param.15) | copy-start | bytes 61444
  29.5 210.3 %copy-start.45 = (f32[1,5,8,16,8]{3,4,2,1,0:T(8,128)S(1)}, f32[1,5,8,16,8]{3,4,2,1,0:T(8,128)}, u32[]{:S(2)}) copy-start(f32[1,5,8,16,8]{3,4,2,1,0:T(8,128)} %param.16) | copy-start | bytes 61444
  245.5 18.3 %copy-start.85 = (f32[1024]{0:T(1024)}, f32[1024]{0:T(1024)S(1)}, u32[]{:S(2)}) copy-start(f32[1024]{0:T(1024)S(1)} %get-tuple-element.138) | copy-start | bytes 12292
  245.5 22.0 %copy-start.71 = (f32[1024]{0:T(1024)}, f32[1024]{0:T(1024)S(1)}, u32[]{:S(2)}) copy-start(f32[1024]{0:T(1024)S(1)} %get-tuple-element.134) | copy-start | bytes 12292
  245.5 31.0 %copy-start.87 = (f32[1024]{0:T(1024)}, f32[1024]{0:T(1024)S(1)}, u32[]{:S(2)}) copy-start(f32[1024]{0:T(1024)S(1)} %get-tuple-element.135) | copy-start | bytes 12292
  245.5 42.5 %copy-start.60 = (f32[1024]{0:T(1024)}, f32[1024]{0:T(1024)S(1)}, u32[]{:S(2)}) copy-start(f32[1024]{0:T(1024)S(1)} %get-tuple-element.131) | copy-start | bytes 12292
  245.6 98.0 %copy-start.62 = (f32[1024]{0:T(1024)}, f32[1024]{0:T(1024)S(1)}, u32[]{:S(2)}) copy-start(f32[1024]{0:T(1024)S(1)} %get-tuple-element.132) | copy-start | bytes 12292
  251.8 15.2 %copy-start.2 = (bf16[640,3072]{1,0:T(8,128)(2,1)}, bf16[640,3072]{1,0:T(8,128)(2,1)S(1)}, u32[]{:S(2)}) copy-start(bf16[640,3072]{1,0:T(8,128)(2,1)S(1)} %convolution_convert_fusion.1.qkv_ref) | copy-start | bytes 11796484
  251.8 12.0 %copy-start.14 = (f32[640,1024]{1,0:T(8,128)S(1)}, f32[640,1024]{1,0:T(8,128)}, u32[]{:S(2)}) copy-start(f32[640,1024]{1,0:T(8,128)} %copy-done.13) | copy-start | bytes 7864324
  251.8 12.0 %copy-start.93 = (bf16[1024,1024]{1,0:T(8,128)(2,1)S(1)}, bf16[1024,1024]{1,0:T(8,128)(2,1)}, u32[]{:S(2)}) copy-start(bf16[1024,1024]{1,0:T(8,128)(2,1)} %get-tuple-element.38) | copy-start | bytes 6291460
  251.8 16.4 %slice-start = ((s8[8388608]{0:T(1024)(128)(4,1)}), s8[4194304]{0:T(1024)(128)(4,1)S(1)}, s32[]{:S(2)}) async-start(s8[8388608]{0:T(1024)(128)(4,1)} %bitcast.218), calls=%async_computation.2 | async-start | bytes 8388608
  267.1 9.5 copy-start.16
  267.5 9.0 copy-start.81
  267.5 9.0 copy-start.73
  276.5 11.1 %copy-start.100 = (bf16[640,4096]{1,0:T(8,128)(2,1)}, bf16[640,4096]{1,0:T(8,128)(2,1)S(1)}, u32[]{:S(2)}) copy-start(bf16[640,4096]{1,0:T(8,128)(2,1)S(1)} %get-tuple-element.144.refs_6_) | copy-start | bytes 15728644
  287.6 22.0 %slice-start.2 = ((s8[6291456]{0:T(1024)(128)(4,1)}), s8[4194304]{0:T(1024)(128)(4,1)S(1)}, s32[]{:S(2)}) async-start(s8[6291456]{0:T(1024)(128)(4,1)} %bitcast.220), calls=%async_computation.4 | async-start | bytes 8388608
  288.1 21.5 %slice-start.3 = ((s8[6291456]{0:T(1024)(128)(4,1)}), s8[2097152]{0:T(1024)(128)(4,1)S(1)}, s32[]{:S(2)}) async-start(s8[6291456]{0:T(1024)(128)(4,1)} %bitcast.220), calls=%async_computation.5 | async-start | bytes 4194304
  289.2 19.1 %collective-permute-start = (bf16[10,32,1024]{2,1,0:T(8,128)(2,1)S(1)}, bf16[10,32,1024]{2,1,0:T(8,128)(2,1)S(1)}, u32[]{:S(2)}, u32[]{:S(2)}) collective-permute-start(bf16[10,32,1024]{2,1,0:T(8,128)(2,1)S(1)} %get-tuple-element.120), channel_id=1, source_target_pairs={{0,3},{1,0},{2,1},{3,2},{4,7},{5,4},{6,5},{7,6},{8,11},{9,8},{10,9... | collective-permute-start | bytes 1966088 | tf_op jit(solution)/shard_map/ppermute | solution.py:33
  314.1 16.4 %copy-start = (bf16[640,3072]{1,0:T(8,128)(2,1)}, bf16[640,3072]{1,0:T(8,128)(2,1)S(1)}, u32[]{:S(2)}) copy-start(bf16[640,3072]{1,0:T(8,128)(2,1)S(1)} %convolution_convert_fusion.refs_0_.refs_1_.refs_2_) | copy-start | bytes 11796484
  331.7 10.5 %collective-permute-start.1 = (bf16[10,32,1024]{2,1,0:T(8,128)(2,1)}, bf16[10,32,1024]{2,1,0:T(8,128)(2,1)}, u32[]{:S(2)}, u32[]{:S(2)}) collective-permute-start(bf16[10,32,1024]{2,1,0:T(8,128)(2,1)} %get-tuple-element.118), channel_id=1, source_target_pairs={{0,1},{1,2},{2,3},{3,0},{4,5},{5,6},{6,7},{7,4},{8,9},{9,10},{10,1... | collective-permute-start | bytes 1966088 | tf_op jit(solution)/shard_map/ppermute | solution.py:33
  333.9 56.9 %copy-start.64 = (f32[640]{0:T(1024)}, f32[640]{0:T(1024)S(1)}, u32[]{:S(2)}) copy-start(f32[640]{0:T(1024)S(1)} %mul.714) | copy-start | bytes 7684
  348.7 13.2 %copy-start.11 = (f32[640,1024]{1,0:T(8,128)}, f32[640,1024]{1,0:T(8,128)S(1)}, u32[]{:S(2)}) copy-start(f32[640,1024]{1,0:T(8,128)S(1)} %get-tuple-element.104) | copy-start | bytes 7864324
  353.3 8.6 copy-start.5
  353.3 8.6 copy-start.95
  393.0 14.4 %copy-start.38 = (bf16[640,1024]{1,0:T(8,128)(2,1)}, bf16[640,1024]{1,0:T(8,128)(2,1)S(1)}, u32[]{:S(2)}) copy-start(bf16[640,1024]{1,0:T(8,128)(2,1)S(1)} %multiply_convert_fusion.5.refs_10_) | copy-start | bytes 3932164
  393.0 14.4 %copy-start.19 = (f32[640,1024]{1,0:T(8,128)S(1)}, f32[640,1024]{1,0:T(8,128)}, u32[]{:S(2)}) copy-start(f32[640,1024]{1,0:T(8,128)} %copy-done.18) | copy-start | bytes 7864324
  424.0 8.7 copy-start.12
  424.0 8.7 copy-start.98
  441.3 8.2 collective-permute-start.2
  480.3 17.3 %collective-permute-start.3 = (f32[10,32,1024]{2,1,0:T(8,128)S(1)}, f32[10,32,1024]{2,1,0:T(8,128)S(1)}, u32[]{:S(2)}, u32[]{:S(2)}) collective-permute-start(f32[10,32,1024]{2,1,0:T(8,128)S(1)} %get-tuple-element.115), channel_id=1, source_target_pairs={{0,1},{1,2},{2,3},{3,0},{4,5},{5,6},{6,7},{7,4},{8,9},{9,10},{10,1... | collective-permute-start | bytes 3932168 | tf_op jit(solution)/shard_map/ppermute | solution.py:33
  504.5 12.7 %copy-start.17 = (f32[640,1024]{1,0:T(8,128)S(1)}, f32[640,1024]{1,0:T(8,128)}, u32[]{:S(2)}) copy-start(f32[640,1024]{1,0:T(8,128)} %copy-done.16) | copy-start | bytes 7864324
  504.5 12.7 %copy-start.59 = (f32[640]{0:T(1024)S(1)}, f32[640]{0:T(1024)}, u32[]{:S(2)}) copy-start(f32[640]{0:T(1024)} %copy-done.58) | copy-start | bytes 7684
  504.5 12.7 %copy-start.72 = (f32[1024]{0:T(1024)S(1)}, f32[1024]{0:T(1024)}, u32[]{:S(2)}) copy-start(f32[1024]{0:T(1024)} %copy-done.71) | copy-start | bytes 12292
  504.5 12.7 %copy-start.74 = (f32[640]{0:T(1024)S(1)}, f32[640]{0:T(1024)}, u32[]{:S(2)}) copy-start(f32[640]{0:T(1024)} %copy-done.73) | copy-start | bytes 7684
  517.2 10.7 %copy-start.101 = (bf16[640,4096]{1,0:T(8,128)(2,1)}, bf16[640,4096]{1,0:T(8,128)(2,1)S(1)}, u32[]{:S(2)}) copy-start(bf16[640,4096]{1,0:T(8,128)(2,1)S(1)} %fusion.12.refs_17_) | copy-start | bytes 15728644
  517.2 10.7 %copy-start.82 = (f32[640]{0:T(1024)S(1)}, f32[640]{0:T(1024)}, u32[]{:S(2)}) copy-start(f32[640]{0:T(1024)} %copy-done.81) | copy-start | bytes 7684
  532.3 33.4 %copy-start.15 = (f32[640,1024]{1,0:T(8,128)S(1)}, f32[640,1024]{1,0:T(8,128)}, u32[]{:S(2)}) copy-start(f32[640,1024]{1,0:T(8,128)} %copy-done.13) | copy-start | bytes 7864324
  532.3 33.4 %copy-start.53 = (f32[1,1024]{1,0:T(1,128)S(1)}, f32[1,1024]{1,0:T(1,128)}, u32[]{:S(2)}) copy-start(f32[1,1024]{1,0:T(1,128)} %get-tuple-element.126) | copy-start | bytes 12292
  532.3 33.4 %copy-start.67 = (f32[640]{0:T(1024)S(1)}, f32[640]{0:T(1024)}, u32[]{:S(2)}) copy-start(f32[640]{0:T(1024)} %broadcast_multiply_fusion.7) | copy-start | bytes 7684
  532.3 33.4 %copy-start.76 = (f32[1024]{0:T(1024)S(1)}, f32[1024]{0:T(1024)}, u32[]{:S(2)}) copy-start(f32[1024]{0:T(1024)} %copy-done.75) | copy-start | bytes 12292
  532.3 33.4 %copy-start.78 = (f32[640]{0:T(1024)S(1)}, f32[640]{0:T(1024)}, u32[]{:S(2)}) copy-start(f32[640]{0:T(1024)} %copy-done.77) | copy-start | bytes 7684
  565.8 8.4 copy-start.80
  901.6 19.5 %copy-start.42 = (f32[19,1024]{1,0:T(8,128)S(1)}, f32[19,1024]{1,0:T(8,128)}, u32[]{:S(2)}) copy-start(f32[19,1024]{1,0:T(8,128)} %param.27) | copy-start | bytes 233476
  901.6 19.5 %copy-start.54 = (f32[19,1024]{1,0:T(8,128)S(1)}, f32[19,1024]{1,0:T(8,128)}, u32[]{:S(2)}) copy-start(f32[19,1024]{1,0:T(8,128)} %param.28) | copy-start | bytes 233476
  901.6 19.5 %copy-start.55 = (f32[19,1024]{1,0:T(8,128)S(1)}, f32[19,1024]{1,0:T(8,128)}, u32[]{:S(2)}) copy-start(f32[19,1024]{1,0:T(8,128)} %param.29) | copy-start | bytes 233476
  (64 other events, 158.6 us)
Sparse Core Ops, SparseCore 0:
  10.9 96.0 all-gather.2
  239.1 82.4 all-gather.4

commit v10 on v9

--- a/solution.py
+++ b/solution.py
@@ -129,17 +129,28 @@
 
 
 def attention_gradients(queries, keys, values, grad_out, text_len):
-    dq, dk, dv = [], [], []
-    for head in range(2):
-        probs = softmax_of(matmul_nt(keys, only(head, queries)), 0, text_len)
-        dprobs = matmul_nt(values, only(head, grad_out))
-        dv.append(matmul(probs.astype(jnp.bfloat16), grad_out))
-        inner = jnp.sum(probs * dprobs, 0, keepdims=True)
-        dscores = (probs * (dprobs - inner)).astype(jnp.bfloat16)
-        dk.append(matmul(dscores, queries))
-        dq.append(matmul_tn(dscores, keys))
-    dq, dk, dv = (jnp.where(lanes_of(0, x[0].shape), *x) for x in (dq, dk, dv))
-    return dq * HEAD_DIM ** (-0.5), dk, dv
+    queries, grad_out = stacked(queries), stacked(grad_out)
+    probs = softmax_of(matmul_nt(keys, queries), 0, text_len)
+    dprobs = matmul_nt(values, grad_out)
+    dv = matmul(probs.astype(jnp.bfloat16), grad_out)
+    inner = jnp.sum(probs * dprobs, 0, keepdims=True)
+    dscores = (probs * (dprobs - inner)).astype(jnp.bfloat16)
+    dk = matmul(dscores, queries)
+    return unstacked(matmul_tn(dscores, keys)) * HEAD_DIM ** (-0.5), dk, dv
+
+
+def attention_values(queries, keys, values, text_len):
+    probs = softmax_of(matmul_nt(stacked(queries), keys), 1, text_len)
+    return unstacked(matmul(probs.astype(jnp.bfloat16), values))
+
+
+def stacked(rows):
+    return jnp.concatenate([only(head, rows) for head in range(2)], 0)
+
+
+def unstacked(rows):
+    half = rows.shape[0] // 2
+    return jnp.where(lanes_of(0, (half, rows.shape[1])), rows[:half], rows[half:])
 
 
 def key_sets(key_refs, runs, text_len):
@@ -154,11 +165,7 @@
     for runs in windows:
         queries = take(q_ref, runs) * HEAD_DIM ** (-0.5)
         keys, values = key_sets(k_refs, runs, text_len), key_sets(v_refs, runs, text_len)
-        outs = []
-        for head in range(2):
-            probs = softmax_of(matmul_nt(only(head, queries), keys), 1, text_len)
-            outs.append(matmul(probs.astype(jnp.bfloat16), values))
-        put(out_ref, slice(None), runs, jnp.where(lanes_of(0, outs[0].shape), *outs))
+        put(out_ref, slice(None), runs, attention_values(queries, keys, values, text_len))
 
 
 def attend_back_kernel(windows, text_len, sets, *refs):
@@ -230,11 +237,9 @@
                 )
                 for i in range(2)
             )
-            outs = []
-            for head in range(2):
-                probs = softmax_of(matmul_nt(only(head, queries), keys), 1, 0)
-                outs.append(matmul(probs.astype(jnp.bfloat16), values))
-            put(out_ref, pair_cols(0, pair), runs, jnp.where(lanes_of(0, outs[0].shape), *outs))
+            put(
+                out_ref, pair_cols(0, pair), runs, attention_values(queries, keys, values, 0)
+            )
 
     @pl.loop(0, HEADS // 2)
     def _(pair):
@@ -485,8 +490,9 @@
     ring_send, ring_recv, pair_send, pair_recv, cross_send, cross_recv = refs[2 * num : 2 * num + 6]
     load_sem, own_sem, part_send, part_recv, part_own = refs[2 * num + 6 : 2 * num + 11]
     kv_wide, kv_part, kv_put, kv_got, kv_sum, kv_load, kv_send, kv_recv, band_send, band_recv = refs[
-        2 * num + 11 :
+        2 * num + 11 : 2 * num + 21
     ]
+    share_send, share_recv = refs[2 * num + 21 :]
     shapes = [(packs[pack].shape[0], cols) for pack, _, cols in picks]
     loads = [
         pltpu.make_async_copy(
@@ -584,8 +590,8 @@
         for which, (src, dst) in enumerate(((vec_ref, vec_out), (text_ref, text_out))):
             parts.append(
                 pltpu.make_async_remote_copy(
-                    src.at[peer[0]],
-                    dst.at[me],
+                    src.at[peer[0], band],
+                    dst.at[me, band],
                     part_send.at[which, step],
                     part_recv.at[which, step],
                     peer,
@@ -593,10 +599,10 @@
                 )
             )
     parts_own = [
-        pltpu.make_async_copy(src.at[me], dst.at[me], part_own.at[which])
+        pltpu.make_async_copy(src.at[me, band], dst.at[me, band], part_own.at[which])
         for which, (src, dst) in enumerate(((vec_ref, vec_out), (text_ref, text_out)))
     ]
-    for copy in parts_own + parts[::2]:
+    for copy in parts_own + parts:
         copy.start()
     for group in range(num):
         rows, cols = shapes[group]
@@ -615,9 +621,6 @@
                 MESH,
             ).start()
 
-    for copy in parts[1::2]:
-        copy.start()
-
     def kv_copy(hop):
         return pltpu.make_async_remote_copy(
             kv_put.at[hop], kv_got.at[hop], kv_send.at[hop], kv_recv.at[hop], following, MESH
@@ -642,10 +645,30 @@
 
     for copy in parts_own + parts:
         copy.wait()
+    shares = [
+        pltpu.make_async_remote_copy(
+            out.at[:, band],
+            out.at[:, band],
+            share_send.at[which, step],
+            share_recv.at[which, step],
+            peer,
+            MESH,
+        )
+        for step, peer in enumerate(band_peers)
+        for which, out in enumerate((vec_out, text_out))
+    ]
+    for copy in shares:
+        copy.start()
     kv_weight.wait()
     weight = kv_wide[...].astype(jnp.bfloat16)
+    depth = weight.shape[0] // band_count
+    for copy in shares:
+        copy.wait()
     for owner in range(count):
-        kv_part[owner] = matmul(text_out[owner], weight)
+        kv_part[owner] = sum(
+            matmul(text_out[owner, part], weight[part * depth : (part + 1) * depth])
+            for part in range(band_count)
+        )
     kv_hop(0)
 
     @pl.loop(1, count - 1)
@@ -720,7 +743,7 @@
     num = len(picks)
     dma = pltpu.SemaphoreType.DMA
     shapes = [(packs[pack].shape[0], cols) for pack, _, cols in picks]
-    kv_shape = (texts.shape[1], 2 * D // band_count)
+    kv_shape = (texts.shape[2], 2 * D // band_count)
     kv_all = pltpu.VMEM((count,) + kv_shape, jnp.float32)
     kv_hops = pltpu.VMEM((count - 1,) + kv_shape, jnp.float32)
     out = pl.pallas_call(
@@ -731,7 +754,7 @@
         + tuple(jax.ShapeDtypeStruct(v.shape, v.dtype) for v in (vectors, texts))
         + (jax.ShapeDtypeStruct((band_count,) + kv_shape, jnp.bfloat16),),
         in_specs=[ANY] * 4,
-        out_specs=(ANY,) * (num + 1) + (IN_VMEM,) * 2,
+        out_specs=(ANY,) * num + (IN_VMEM,) * 3,
         scratch_shapes=[pltpu.VMEM(shape, jnp.float32) for shape in shapes]
         + [pltpu.VMEM(shape, jnp.bfloat16) for shape in shapes]
         + [dma((count - 1, num))] * 6
@@ -747,6 +770,8 @@
             dma((count - 1,)),
             dma((band_count - 1,)),
             dma((band_count - 1,)),
+            dma((2, band_count - 1)),
+            dma((2, band_count - 1)),
         ],
         compiler_params=pltpu.CompilerParams(
             collective_id=1, has_side_effects=True, vmem_limit_bytes=50 << 20
@@ -1451,8 +1476,8 @@
     )
     kept_text = context[0] * (1 - null_flags[0]).astype(jnp.bfloat16)
     text_cols = jnp.pad(
-        kept_text.reshape(text_len, clip_count, deep_rows).transpose(1, 0, 2),
-        ((0, 0), (0, TEXT_PAD - text_len), (0, 0)),
+        kept_text.reshape(text_len, clip_count, band_count, -1).transpose(1, 2, 0, 3),
+        ((0, 0), (0, 0), (0, TEXT_PAD - text_len), (0, 0)),
     )
     all_facts = exchange_facts(facts)
     all_times = all_facts[:, 0, 0].astype(jnp.float32)
@@ -1476,10 +1501,11 @@
             (0, 15 * D, 3 * D),
         ),
         (1, 2, 1, 2, 1, 2, 0, 0),
-        part_modul.reshape(clip_count, 12 * D // 128, 128),
+        part_modul.reshape(clip_count, band_count, -1, 128),
         text_cols,
     )
     up_a_w, down_a_w, out_a_w, out_b_w, query_w, cross_out_w, qkv_a_w, qkv_b_w = gathered
+    all_text = all_text.transpose(0, 2, 1, 3)
     keyval = keyval.transpose(1, 0, 2).reshape(TEXT_PAD, 2 * D)
     late_down_b, all_modul = lax.optimization_barrier((w_deep[:, 3 * D :], all_modul))
     down_b_w = gather_quarters(late_down_b)

time: 998 us -> 950 us (0.952)
  Pallas kernels: 640 us -> 595 us
    pallas_call x1, Pallas kernels: 207 us -> 181 us  [gather_weights(): pl.pallas_call(partial(gather_kernel, count, picks, sides), out_shape=tup...]
    unnamed x215 -> x165, local copies, waits for them, and re-layouts: 22.2 us -> 19.2 us
  transfers between devices with their start and end apart: 6 -> 6, of which waited for: 4 -> 4; matrix products, arithmetic and copies ran while one was open for 8% -> 9% of each run, Pallas kernels for 26% -> 23%
where the time goes in v10:
time: 950 us; the launch traced here: 946 us
  Pallas kernels  595 us (63%)
  matrix products  154 us (16%)
  other arithmetic  83.4 us (9%)
  waiting for transfers between devices  49.9 us (5%)
  local copies, waits for them, and re-layouts  35.9 us (4%)
  between operations  24.2 us (3%)
    pallas_call x1, Pallas kernels, reduce_gradients(): pl.pallas_call(partial(reduce_kernel, count, tokens, phases), out_shape=(...  313 us
    pallas_call x1, Pallas kernels, gather_weights(): pl.pallas_call(partial(gather_kernel, count, picks, sides), out_shape=tup...  181 us
    dot_general x11, matrix products, matmul_nt(): lax.dot_general(left_op, right_op, (((1,), (1,)), ((), ())), preferred_el...  75 us
    dot_general x13, matrix products, matmul(): return jnp.dot(left_op, right_op, preferred_element_type=jnp.float32)  71.9 us
    sub x3, other arithmetic, adam_update(): weight - learn_rate * (first_hat / (jnp.sqrt(second_hat) + ADAM_EPS) + DE...  56.7 us
    ppermute x4, waiting for transfers between devices, shifted(): lax.ppermute(value, axis, [(i, (i + by) % length) for i in range(length)])  49.8 us
    pallas_call x2, Pallas kernels, attend_back(): pl.pallas_call(partial(attend_back_kernel, windows, text_len, sets), grid...  26.1 us
    pallas_call x1, Pallas kernels, attend_frames_back(): pl.pallas_call(partial(attend_frames_back_kernel, windows), out_shape=jax...  25 us
  transfers between devices with their start and end apart: 6, of which 4 were waited for; matrix products, arithmetic and copies ran while one was open for 9% of the time, Pallas kernels for 23%

profile of v10, /device:TPU:0, one launch (start us, length us, event | category | flops | bytes accessed | tf_op | source)
XLA Modules:
  0.0 946.0 jit_solution(12720932568769262263)
XLA Ops:
  7.2 1.7 slice.150
  11.8 9.7 %shard_map.230 = s32[8,8,128]{2,1,0:T(8,128)} custom-call(s32[8,128]{1,0:T(8,128)} %pad.12.facts_ref), custom_call_target="tpu_custom_call" | custom-call | tf_op jit(solution)/shard_map/pallas_call | solution.py:474
  22.6 3.5 fusion.16
  26.8 2.7 slice.127
  29.6 180.5 %shard_map.231 = (bf16[1024,4096]{1,0:T(8,128)(2,1)}, bf16[4096,1024]{1,0:T(8,128)(2,1)}, bf16[1024,1024]{1,0:T(8,128)(2,1)}, bf16[1024,1024]{1,0:T(8,128)(2,1)}...) custom-call(f32[128,30720]{1,0:T(8,128)} %refs_0_.1, ...), custom_call_target="tpu_custom_call" | custom-call | flops 199999995904 | bytes 600000000 | tf_op jit(solution)/shard_map/pallas_call | solution.py:749
  210.2 1.7 dynamic-slice_convert_fusion
  212.6 2.0 add_reduce_fusion
  214.7 2.3 multiply_reduce_fusion.21
  218.8 7.3 convolution_convert_fusion.1.qkv_ref
  226.1 12.1 %shard_map.232 = (bf16[640,1024]{1,0:T(8,128)(2,1)S(1)}, bf16[640,2048]{1,0:T(8,128)(2,1)S(1)}) custom-call(bf16[640,3072]{1,0:T(8,128)(2,1)S(1)} %convolution_convert_fusion.1.qkv_ref), custom_call_target="tpu_custom_call" | custom-call | flops 1342177280 | bytes 10485760 | tf_op jit(solution)/shard_map/pallas_call | solution.py:316
  238.3 3.2 fusion.53
  243.6 8.2 multiply_convert_fusion.1
  251.8 11.1 %fusion.52 = (f32[640]{0:T(1024)S(1)}, f32[640,1024]{1,0:T(8,128)S(1)}, f32[640,1024]{1,0:T(8,128)}) fusion(f32[640,1024]{1,0:T(8,128)S(1)} %get-tuple-element.108, f32[1024]{0:T(1024)S(1)} %bitcast.208, bf16[640,4096]{1,0:T(8,128)(2,1)S(1)} %get-tuple-element.146.refs_6_, bf16[4096,1024]{1,0:T(8,128)(2,1)} %get-tuple-element.40), kind=kOutput, calls=%fused_computation.187 | convolution fusion | flops 5370674688 | bytes 21502464 | tf_op jit(solution)/shard_map/dot_general | solution.py:37
  265.3 21.6 %collective-permute-done = bf16[10,32,1024]{2,1,0:T(8,128)(2,1)S(1)} collective-permute-done((bf16[10,32,1024]{2,1,0:T(8,128)(2,1)S(1)}, bf16[10,32,1024]{2,1,0:T(8,128)(2,1)S(1)}, u32[]{:S(2)}, u32[]{:S(2)}) %collective-permute-start) | collective-permute-done | bytes 655392 | tf_op jit(solution)/shard_map/ppermute | solution.py:33
  288.2 4.5 convolution_convert_fusion.refs_0_.refs_1_.refs_2_
  292.7 12.4 %shard_map.233 = bf16[640,1024]{1,0:T(8,128)(2,1)S(1)} custom-call(bf16[640,3072]{1,0:T(8,128)(2,1)S(1)} %convolution_convert_fusion.refs_0_.refs_1_.refs_2_, bf16[640,3072]{1,0:T(8,128)(2,1)S(1)} %convolution_convert_fusion.refs_0_.refs_1_.refs_2_, bf16[640,3072]{1,0:T(8,128)(2,1)S(1)} %convolution_convert_fusion.refs_0_.refs_1_.refs_2_), custom_call_target="tpu_custom_call" | custom-call | flops 1677721600 | bytes 10485760 | tf_op jit(solution)/shard_map/pallas_call | solution.py:368
  309.6 6.3 collective-permute-done.1
  317.2 5.1 fusion.51
  323.1 2.2 copy-done.74
  326.8 6.7 shard_map.234.refs_2_
  333.5 1.6 fusion.62
  336.6 1.6 add_convert_fusion.refs_1_
  338.2 11.9 %multiply_convert_fusion = (bf16[640,4096]{1,0:T(8,128)(2,1)}, f32[640,4096]{1,0:T(8,128)}) fusion(bf16[640,1024]{1,0:T(8,128)(2,1)} %add_convert_fusion.refs_1_, bf16[1024,4096]{1,0:T(8,128)(2,1)} %all-gather.3.cloned.1.call-done), kind=kOutput, calls=%fused_computation.20 | convolution fusion | flops 5381816320 | bytes 25427968 | tf_op jit(solution)/shard_map/dot_general | solution.py:37
  350.2 11.1 %fusion.50 = (f32[640]{0:T(1024)S(1)}, f32[640,1024]{1,0:T(8,128)S(1)}, f32[640,1024]{1,0:T(8,128)}) fusion(f32[640,1024]{1,0:T(8,128)} %copy-done.16, f32[1024]{0:T(1024)S(1)} %bitcast.216, bf16[640,4096]{1,0:T(8,128)(2,1)} %get-tuple-element.152.refs_0_, bf16[4096,1024]{1,0:T(8,128)(2,1)} %all-gather.5.cloned.1.call-done), kind=kOutput, calls=%fused_computation.185 | convolution fusion | flops 5370674688 | bytes 21502464 | tf_op jit(solution)/shard_map/dot_general | solution.py:37
  365.2 12.7 %fusion.6.refs_11_ = bf16[640,4096]{1,0:T(8,128)(2,1)S(1)} fusion(f32[640,4096]{1,0:T(8,128)} %get-tuple-element.153, bf16[640,1024]{1,0:T(8,128)(2,1)S(1)} %multiply_convert_fusion.5.refs_10_, bf16[4096,1024]{1,0:T(8,128)(2,1)} %all-gather.5.cloned.1.call-done), kind=kOutput, calls=%fused_computation.13 | convolution fusion | flops 5394923520 | bytes 25427968 | tf_op jit(solution)/shard_map/dot_general | solution.py:51
  377.9 10.6 %multiply_reduce_fusion.5 = (f32[1024]{0:T(1024)S(1)}, f32[640]{0:T(1024)S(1)}, f32[1024]{0:T(1024)S(1)}, f32[640,1024]{1,0:T(8,128)S(1)}) fusion(f32[640,1024]{1,0:T(8,128)S(1)} %copy-done.17, f32[640]{0:T(1024)S(1)} %fusion.35, f32[640]{0:T(1024)S(1)} %broadcast_multiply_fusion.3, f32[1024]{0:T(1024)S(1)} %bitcast.199, ...), kind=kOutput, calls=%fused_computation.48 | convolution fusion | flops 5373949440 | bytes 18894336 | tf_op jit(solution)/shard_map/dot_general | solution.py:51
  392.0 2.7 convolution_convert_fusion.4.refs_3_
  394.7 7.8 shard_map.235
  402.5 4.0 multiply_reduce_fusion.2
  410.6 1.6 convolution_convert_fusion.3
  412.4 8.1 collective-permute-done.2
  420.6 18.3 %shard_map.236.refs_15_ = bf16[640,3072]{1,0:T(8,128)(2,1)} custom-call(bf16[640,3072]{1,0:T(8,128)(2,1)} %copy-done, bf16[640,3072]{1,0:T(8,128)(2,1)} %copy-done, bf16[640,3072]{1,0:T(8,128)(2,1)} %copy-done, bf16[640,1024]{1,0:T(8,128)(2,1)S(1)} %bitcast.151), custom_call_target="tpu_custom_call" | custom-call | flops 4194304000 | bytes 10485760 | tf_op jit(solution)/shard_map/pallas_call | solution.py:389
  439.0 7.6 fusion.63
  450.3 13.8 %collective-permute-done.3 = f32[10,32,1024]{2,1,0:T(8,128)S(1)} collective-permute-done((f32[10,32,1024]{2,1,0:T(8,128)S(1)}, f32[10,32,1024]{2,1,0:T(8,128)S(1)}, u32[]{:S(2)}, u32[]{:S(2)}) %collective-permute-start.3) | collective-permute-done | bytes 1310752 | tf_op jit(solution)/shard_map/ppermute | solution.py:33
  464.3 1.6 copy-done.9
  469.3 14.7 %fusion.12.refs_17_ = bf16[640,4096]{1,0:T(8,128)(2,1)} fusion(f32[640,4096]{1,0:T(8,128)} %get-tuple-element.147, bf16[640,1024]{1,0:T(8,128)(2,1)S(1)} %multiply_convert_fusion.3.refs_16_, bf16[4096,1024]{1,0:T(8,128)(2,1)} %get-tuple-element.40), kind=kOutput, calls=%fused_computation.19 | convolution fusion | flops 5394923520 | bytes 25427968 | tf_op jit(solution)/shard_map/dot_general | solution.py:51
  484.0 10.3 %multiply_reduce_fusion.8 = (f32[1024]{0:T(1024)S(1)}, f32[640]{0:T(1024)S(1)}, f32[1024]{0:T(1024)S(1)}, f32[640,1024]{1,0:T(8,128)S(1)}) fusion(f32[640,1024]{1,0:T(8,128)S(1)} %copy-done.15, f32[640]{0:T(1024)S(1)} %copy-done.55, f32[640]{0:T(1024)S(1)} %copy-done.49, f32[1024]{0:T(1024)S(1)} %bitcast.196, bf16[640,4096]{1,0:T(8,128)(2,1)} %fusion.12.refs_17_, ...), kind=kOutput, calls=%fused_computation.51 | convolution fusion | flops 5373949440 | bytes 18894336 | tf_op jit(solution)/shard_map/dot_general | solution.py:51
  495.7 1.6 copy-done.71
  497.2 1.6 convolution_convert_fusion.2.grad_ref
  499.0 25.0 %shard_map.237.refs_19_ = bf16[640,3072]{1,0:T(8,128)(2,1)} custom-call(bf16[640,3072]{1,0:T(8,128)(2,1)} %copy-done.1, bf16[640,2048]{1,0:T(8,128)(2,1)S(1)} %copy-done.3, bf16[640,1024]{1,0:T(8,128)(2,1)S(1)} %convolution_convert_fusion.2.grad_ref), custom_call_target="tpu_custom_call" | custom-call | flops 3355443200 | bytes 10485760 | tf_op jit(solution)/shard_map/pallas_call | solution.py:335
  524.1 8.4 multiply_reduce_fusion.10
  537.2 312.6 %shard_map.238 = (f32[128,18432]{1,0:T(8,128)}, f32[512,2048]{1,0:T(8,128)}, f32[8,512]{1,0:T(8,128)}, f32[8,256,128]{2,1,0:T(8,128)}, f32[512,2048]{1,0:T(8,128...) custom-call(bf16[640,4096]{1,0:T(8,128)(2,1)} %get-tuple-element.152, ...), custom_call_target="tpu_custom_call" | custom-call | flops 299999985664 | bytes 800000000 | tf_op jit(solution)/shard_map/pallas_call | solution.py:1378
  849.8 1.8 copy.46
  852.5 5.6 multiply_reduce_fusion
  860.6 4.0 fusion.54
  867.2 10.2 %shard_map.239 = f32[8,128]{1,0:T(8,128)} custom-call(f32[8,128]{1,0:T(8,128)} %broadcast_in_dim.87.part_ref), custom_call_target="tpu_custom_call" | custom-call | tf_op jit(solution)/shard_map/pallas_call | solution.py:1431
  880.7 36.5 %multiply_subtract_fusion = (f32[128,30720]{1,0:T(8,128)}, f32[128,30720]{1,0:T(8,128)}, f32[128,30720]{1,0:T(8,128)}) fusion(f32[128,30720]{1,0:T(8,128)} %refs_0_.1, f32[]{:T(128)S(6)} %div.227, f32[128,18432]{1,0:T(8,128)} %get-tuple-element.54, f32[128,12288]{1,0:T(8,128)} %get-tuple-element.163, f32[128,30720]{1,0:T(8,128)} %param.22, f32[128,30720]{1,0:T(8,128)} %param.23), kind=kLoop, calls=%fused_computation.3 | loop fusion | flops 66846720 | bytes 110100480 | tf_op jit(solution)/shard_map/sub | solution.py:427
  917.2 19.5 %multiply_subtract_fusion.1 = (f32[512,4096]{1,0:T(8,128)}, f32[512,4096]{1,0:T(8,128)}, f32[512,4096]{1,0:T(8,128)}) fusion(f32[512,4096]{1,0:T(8,128)} %refs_1_.1, f32[]{:T(128)S(6)} %div.227, f32[512,1024]{1,0:T(8,128)} %get-tuple-element.110, f32[512,2048]{1,0:T(8,128)} %get-tuple-element.56, f32[512,1024]{1,0:T(8,128)S(1)} %get-tuple-element.109, ...), kind=kLoop, calls=%fused_computation.26 | loop fusion | flops 37748736 | bytes 58720260 | tf_op jit(solution)/shard_map/sub | solution.py:427
  (286 shorter events, 50.5 us)
Async XLA Ops:
  7.2 331.0 %all-gather.3.cloned.1.call-start = ((), (), s32[]{:S(2)}) async-start(), calls=%async_computation | async-start | bytes 8650752 | tf_op jit(solution)/shard_map/all_gather | solution.py:731
  9.7 340.4 %all-gather.5.cloned.1.call-start = ((), (), s32[]{:S(2)}) async-start(), calls=%async_computation.1 | async-start | bytes 8650752 | tf_op jit(solution)/shard_map/all_gather | solution.py:731
  29.6 182.5 %copy-start.34 = (f32[19,1024]{1,0:T(8,128)S(1)}, f32[19,1024]{1,0:T(8,128)}, u32[]{:S(2)}) copy-start(f32[19,1024]{1,0:T(8,128)} %param.27) | copy-start | bytes 233476
  29.6 182.5 %copy-start.36 = (f32[1,5,8,16,8]{3,4,2,1,0:T(8,128)S(1)}, f32[1,5,8,16,8]{3,4,2,1,0:T(8,128)}, u32[]{:S(2)}) copy-start(f32[1,5,8,16,8]{3,4,2,1,0:T(8,128)} %param.15) | copy-start | bytes 61444
  29.6 182.5 %copy-start.37 = (f32[1,5,8,16,8]{3,4,2,1,0:T(8,128)S(1)}, f32[1,5,8,16,8]{3,4,2,1,0:T(8,128)}, u32[]{:S(2)}) copy-start(f32[1,5,8,16,8]{3,4,2,1,0:T(8,128)} %param.16) | copy-start | bytes 61444
  212.1 26.1 %copy-start.42 = (f32[1,1024]{1,0:T(1,128)}, f32[1,1024]{1,0:T(1,128)S(1)}, u32[]{:S(2)}) copy-start(f32[1,1024]{1,0:T(1,128)S(1)} %get-tuple-element.126) | copy-start | bytes 12292
  217.0 9.0 copy-start.60
  217.0 9.0 copy-start.58
  217.1 9.0 copy-start.56
  217.1 21.2 %copy-start.64 = (f32[1,1024]{1,0:T(1,128)}, f32[1,1024]{1,0:T(1,128)S(1)}, u32[]{:S(2)}) copy-start(f32[1,1024]{1,0:T(1,128)S(1)} %get-tuple-element.140) | copy-start | bytes 12292
  217.1 24.9 %copy-start.52 = (f32[1,1024]{1,0:T(1,128)}, f32[1,1024]{1,0:T(1,128)S(1)}, u32[]{:S(2)}) copy-start(f32[1,1024]{1,0:T(1,128)S(1)} %get-tuple-element.137) | copy-start | bytes 12292
  226.1 15.4 %copy-start.1 = (bf16[640,3072]{1,0:T(8,128)(2,1)}, bf16[640,3072]{1,0:T(8,128)(2,1)S(1)}, u32[]{:S(2)}) copy-start(bf16[640,3072]{1,0:T(8,128)(2,1)S(1)} %convolution_convert_fusion.1.qkv_ref) | copy-start | bytes 11796484
  226.1 12.2 %copy-start.70 = (bf16[1024,1024]{1,0:T(8,128)(2,1)S(1)}, bf16[1024,1024]{1,0:T(8,128)(2,1)}, u32[]{:S(2)}) copy-start(bf16[1024,1024]{1,0:T(8,128)(2,1)} %get-tuple-element.38) | copy-start | bytes 6291460
  226.1 16.4 %slice-start = ((s8[8388608]{0:T(1024)(128)(4,1)}), s8[4194304]{0:T(1024)(128)(4,1)S(1)}, s32[]{:S(2)}) async-start(s8[8388608]{0:T(1024)(128)(4,1)} %bitcast.230), calls=%async_computation.2 | async-start | bytes 8388608
  241.5 10.3 %copy-start.14 = (f32[640,1024]{1,0:T(8,128)}, f32[640,1024]{1,0:T(8,128)S(1)}, u32[]{:S(2)}) copy-start(f32[640,1024]{1,0:T(8,128)S(1)} %get-tuple-element.108) | copy-start | bytes 7864324
  241.9 9.8 %copy-start.62 = (f32[640]{0:T(1024)}, f32[640]{0:T(1024)S(1)}, u32[]{:S(2)}) copy-start(f32[640]{0:T(1024)S(1)} %multiply_reduce_fusion.20) | copy-start | bytes 7684
  242.0 9.8 %copy-start.54 = (f32[640]{0:T(1024)}, f32[640]{0:T(1024)S(1)}, u32[]{:S(2)}) copy-start(f32[640]{0:T(1024)S(1)} %fusion.32) | copy-start | bytes 7684
  242.6 9.2 copy-start.30
  251.8 11.1 %copy-start.75 = (bf16[640,4096]{1,0:T(8,128)(2,1)}, bf16[640,4096]{1,0:T(8,128)(2,1)S(1)}, u32[]{:S(2)}) copy-start(bf16[640,4096]{1,0:T(8,128)(2,1)S(1)} %get-tuple-element.146.refs_6_) | copy-start | bytes 15728644
  262.9 25.3 %slice-start.2 = ((s8[6291456]{0:T(1024)(128)(4,1)}), s8[4194304]{0:T(1024)(128)(4,1)S(1)}, s32[]{:S(2)}) async-start(s8[6291456]{0:T(1024)(128)(4,1)} %bitcast.232), calls=%async_computation.4 | async-start | bytes 8388608
  263.3 24.8 %slice-start.3 = ((s8[6291456]{0:T(1024)(128)(4,1)}), s8[2097152]{0:T(1024)(128)(4,1)S(1)}, s32[]{:S(2)}) async-start(s8[6291456]{0:T(1024)(128)(4,1)} %bitcast.232), calls=%async_computation.5 | async-start | bytes 4194304
  264.6 22.4 %collective-permute-start = (bf16[10,32,1024]{2,1,0:T(8,128)(2,1)S(1)}, bf16[10,32,1024]{2,1,0:T(8,128)(2,1)S(1)}, u32[]{:S(2)}, u32[]{:S(2)}) collective-permute-start(bf16[10,32,1024]{2,1,0:T(8,128)(2,1)S(1)} %get-tuple-element.120), channel_id=1, source_target_pairs={{0,3},{1,0},{2,1},{3,2},{4,7},{5,4},{6,5},{7,6},{8,11},{9,8},{10,9... | collective-permute-start | bytes 1966088 | tf_op jit(solution)/shard_map/ppermute | solution.py:33
  292.7 12.4 %copy-start = (bf16[640,3072]{1,0:T(8,128)(2,1)}, bf16[640,3072]{1,0:T(8,128)(2,1)S(1)}, u32[]{:S(2)}) copy-start(bf16[640,3072]{1,0:T(8,128)(2,1)S(1)} %convolution_convert_fusion.refs_0_.refs_1_.refs_2_) | copy-start | bytes 11796484
  305.2 10.7 %collective-permute-start.1 = (bf16[10,32,1024]{2,1,0:T(8,128)(2,1)S(1)}, bf16[10,32,1024]{2,1,0:T(8,128)(2,1)}, u32[]{:S(2)}, u32[]{:S(2)}) collective-permute-start(bf16[10,32,1024]{2,1,0:T(8,128)(2,1)S(1)} %get-tuple-element.118), channel_id=1, source_target_pairs={{0,1},{1,2},{2,3},{3,0},{4,5},{5,6},{6,7},{7,4},{8,9},{9,10},{10,1... | collective-permute-start | bytes 1966088 | tf_op jit(solution)/shard_map/ppermute | solution.py:33
  309.6 7.6 copy-start.8
  322.3 11.2 %copy-start.10 = (f32[640,1024]{1,0:T(8,128)}, f32[640,1024]{1,0:T(8,128)S(1)}, u32[]{:S(2)}) copy-start(f32[640,1024]{1,0:T(8,128)S(1)} %get-tuple-element.104) | copy-start | bytes 7864324
  326.8 6.7 copy-start.72
  365.2 12.7 %copy-start.31 = (bf16[640,1024]{1,0:T(8,128)(2,1)}, bf16[640,1024]{1,0:T(8,128)(2,1)S(1)}, u32[]{:S(2)}) copy-start(bf16[640,1024]{1,0:T(8,128)(2,1)S(1)} %multiply_convert_fusion.5.refs_10_) | copy-start | bytes 3932164
  365.2 12.7 %copy-start.17 = (f32[640,1024]{1,0:T(8,128)S(1)}, f32[640,1024]{1,0:T(8,128)}, u32[]{:S(2)}) copy-start(f32[640,1024]{1,0:T(8,128)} %copy-done.16) | copy-start | bytes 7864324
  377.9 10.7 %copy-start.76 = (bf16[640,4096]{1,0:T(8,128)(2,1)}, bf16[640,4096]{1,0:T(8,128)(2,1)S(1)}, u32[]{:S(2)}) copy-start(bf16[640,4096]{1,0:T(8,128)(2,1)S(1)} %fusion.6.refs_11_) | copy-start | bytes 15728644
  394.7 7.8 copy-start.11
  412.4 8.2 collective-permute-start.2
  446.9 17.2 %collective-permute-start.3 = (f32[10,32,1024]{2,1,0:T(8,128)S(1)}, f32[10,32,1024]{2,1,0:T(8,128)S(1)}, u32[]{:S(2)}, u32[]{:S(2)}) collective-permute-start(f32[10,32,1024]{2,1,0:T(8,128)S(1)} %get-tuple-element.115), channel_id=1, source_target_pairs={{0,1},{1,2},{2,3},{3,0},{4,5},{5,6},{6,7},{7,4},{8,9},{9,10},{10,1... | collective-permute-start | bytes 3932168 | tf_op jit(solution)/shard_map/ppermute | solution.py:33
  469.3 14.7 %copy-start.29 = (bf16[640,1024]{1,0:T(8,128)(2,1)}, bf16[640,1024]{1,0:T(8,128)(2,1)S(1)}, u32[]{:S(2)}) copy-start(bf16[640,1024]{1,0:T(8,128)(2,1)S(1)} %multiply_convert_fusion.3.refs_16_) | copy-start | bytes 3932164
  469.3 14.7 %copy-start.15 = (f32[640,1024]{1,0:T(8,128)S(1)}, f32[640,1024]{1,0:T(8,128)}, u32[]{:S(2)}) copy-start(f32[640,1024]{1,0:T(8,128)} %copy-done.14) | copy-start | bytes 7864324
  469.3 14.7 %copy-start.49 = (f32[640]{0:T(1024)S(1)}, f32[640]{0:T(1024)}, u32[]{:S(2)}) copy-start(f32[640]{0:T(1024)} %copy-done.48) | copy-start | bytes 7684
  469.3 14.7 %copy-start.53 = (f32[1,1024]{1,0:T(1,128)S(1)}, f32[1,1024]{1,0:T(1,128)}, u32[]{:S(2)}) copy-start(f32[1,1024]{1,0:T(1,128)} %copy-done.52) | copy-start | bytes 12292
  469.3 14.7 %copy-start.55 = (f32[640]{0:T(1024)S(1)}, f32[640]{0:T(1024)}, u32[]{:S(2)}) copy-start(f32[640]{0:T(1024)} %copy-done.54) | copy-start | bytes 7684
  484.0 10.3 %copy-start.63 = (f32[640]{0:T(1024)S(1)}, f32[640]{0:T(1024)}, u32[]{:S(2)}) copy-start(f32[640]{0:T(1024)} %copy-done.62) | copy-start | bytes 7684
  499.0 25.0 %copy-start.13 = (f32[640,1024]{1,0:T(8,128)S(1)}, f32[640,1024]{1,0:T(8,128)}, u32[]{:S(2)}) copy-start(f32[640,1024]{1,0:T(8,128)} %get-tuple-element.144) | copy-start | bytes 7864324
  499.0 25.0 %copy-start.43 = (f32[1,1024]{1,0:T(1,128)S(1)}, f32[1,1024]{1,0:T(1,128)}, u32[]{:S(2)}) copy-start(f32[1,1024]{1,0:T(1,128)} %copy-done.42) | copy-start | bytes 12292
  499.0 25.0 %copy-start.51 = (f32[640]{0:T(1024)S(1)}, f32[640]{0:T(1024)}, u32[]{:S(2)}) copy-start(f32[640]{0:T(1024)} %copy-done.50) | copy-start | bytes 7684
  499.0 25.1 %copy-start.57 = (f32[1,1024]{1,0:T(1,128)S(1)}, f32[1,1024]{1,0:T(1,128)}, u32[]{:S(2)}) copy-start(f32[1,1024]{1,0:T(1,128)} %copy-done.56) | copy-start | bytes 12292
  499.0 25.1 %copy-start.59 = (f32[640]{0:T(1024)S(1)}, f32[640]{0:T(1024)}, u32[]{:S(2)}) copy-start(f32[640]{0:T(1024)} %copy-done.58) | copy-start | bytes 7684
  524.1 8.4 copy-start.61
  860.6 19.4 %copy-start.35 = (f32[19,1024]{1,0:T(8,128)S(1)}, f32[19,1024]{1,0:T(8,128)}, u32[]{:S(2)}) copy-start(f32[19,1024]{1,0:T(8,128)} %param.27) | copy-start | bytes 233476
  860.6 19.4 %copy-start.44 = (f32[19,1024]{1,0:T(8,128)S(1)}, f32[19,1024]{1,0:T(8,128)}, u32[]{:S(2)}) copy-start(f32[19,1024]{1,0:T(8,128)} %param.28) | copy-start | bytes 233476
  860.6 19.4 %copy-start.45 = (f32[19,1024]{1,0:T(8,128)S(1)}, f32[19,1024]{1,0:T(8,128)}, u32[]{:S(2)}) copy-start(f32[19,1024]{1,0:T(8,128)} %param.29) | copy-start | bytes 233476
  (39 other events, 99.4 us)
Sparse Core Ops, SparseCore 0:
  11.5 97.3 all-gather.2
  212.0 88.0 all-gather.4

commit v11 on v10

--- a/solution.py
+++ b/solution.py
@@ -786,7 +786,12 @@
 UNIT = (128, 512)
 
 
-def unit_parts(kind, first):
+SPLIT = 2
+
+
+def unit_parts(at, kind, first):
+    if at == 0:
+        return ((0, 4, lambda u: u, lambda u: 0), (4, SPLIT, lambda u: 4, lambda u: u - 3))
     if kind == 0:
         return ((0, 4, lambda u: u, lambda u: 0), (4, 4, lambda u: 4, lambda u: u - 3))
     if first:
@@ -828,10 +833,18 @@
         last_got_scale,
         push_send,
         push_recv,
+        cross_put,
+        cross_put_scale,
+        cross_got,
+        cross_got_scale,
+        cross_send,
+        cross_recv,
+        cross_credit,
         vec_got,
         kv_got,
         vec_sum,
         all_kv,
+        all_kv_scale,
         text_buf,
         kv_grad,
         side_own,
@@ -954,7 +967,7 @@
 
     def ring_copies(at, part, slot):
         kind = phases[at]["kind"]
-        units = pl.ds(*unit_parts(kind, phases[at]["first"])[part][:2])
+        units = pl.ds(*unit_parts(at, kind, phases[at]["first"])[part][:2])
         return [
             pltpu.make_async_remote_copy(
                 put.at[slot, units],
@@ -971,7 +984,7 @@
 
     def plane_copies(at, part):
         kind = phases[at]["kind"]
-        units = pl.ds(*unit_parts(kind, phases[at]["first"])[part][:2])
+        units = pl.ds(*unit_parts(at, kind, phases[at]["first"])[part][:2])
         pairs = ((plane_put[kind], plane_got[at]),)
         if at + 1 == len(phases):
             pairs = ((last_put, last_got), (last_put_scale, last_got_scale))
@@ -985,6 +998,30 @@
                 MESH,
             )
             for i, (here, there) in enumerate(pairs)
+        ]
+
+    def split_unit(pair, of_plane):
+        return 4 + 2 * pair + of_plane
+
+    def split_copy(pair, of_plane):
+        unit = split_unit(pair, of_plane)
+        return pltpu.make_async_remote_copy(
+            plane_put[0].at[unit],
+            plane_got[0].at[unit],
+            plane_send.at[0, 1, pair],
+            plane_recv.at[0, 1, pair],
+            mirror,
+            MESH,
+        )
+
+    def cross_copies(slot):
+        return [
+            pltpu.make_async_remote_copy(
+                here.at[slot], there.at[slot], cross_send.at[slot, i], cross_recv.at[slot, i], mirror, MESH
+            )
+            for i, (here, there) in enumerate(
+                ((cross_put, cross_got), (cross_put_scale, cross_got_scale))
+            )
         ]
 
     def push_right(block):
@@ -1040,6 +1077,11 @@
         for copy in copies:
             copy.wait()
 
+    def encode(term):
+        largest = jnp.maximum(jnp.max(jnp.abs(term), axis=0, keepdims=True), WIRE_LEAST)
+        low = jnp.round(term * (WIRE_MAX / largest)).astype(jnp.int16)
+        return low, largest * (1.0 / WIRE_MAX)
+
     def take_step(at, step, first, last):
         phase = phases[at]
         kind = phase["kind"]
@@ -1057,19 +1099,34 @@
         opening = first and at == 0
         if not (last or opening):
             load_next()
-        parts = unit_parts(kind, phase["first"])
-
-        def encode(term):
-            largest = jnp.maximum(jnp.max(jnp.abs(term), axis=0, keepdims=True), WIRE_LEAST)
-            low = jnp.round(term * (WIRE_MAX / largest)).astype(jnp.int16)
-            return low, largest * (1.0 / WIRE_MAX)
-
+        parts = unit_parts(at, kind, phase["first"])
+
+        def send_theirs():
+            def spend():
+                for copy in cross_copies(slot):
+                    copy.wait_send()
+                pl.semaphore_wait(cross_credit, 1)
+
+            if last:
+                spend()
+            elif not first:
+                pl.when(step >= 2)(spend)
+            for pair in range(SPLIT):
+                unit = split_unit(pair, 1 - plane)
+                term = product(kind, slot, parts[1][2](unit), parts[1][3](unit))
+                cross_put[slot, pair], cross_put_scale[slot, pair] = encode(term)
+            start(cross_copies(slot))
+
+        if at == 0 and not opening:
+            send_theirs()
         for part, (low, many, left_of, right_of) in enumerate(parts):
             if opening:
                 blocks = range(1) if part == 0 else range(1, 5)
                 finish(load_right(0, 0)[blocks.start : blocks.stop])
                 for block in blocks:
                     push_right(block).wait_recv()
+                if part:
+                    send_theirs()
             if not first:
                 for copy in ring_copies(at, part, before):
                     copy.wait_recv()
@@ -1094,11 +1151,35 @@
                     put_low[kind][slot, position] = low_part
                     put_scale[kind][slot, position] = scale_part
 
+            split = at == 0 and part == 1
+            if split:
+                for copy in cross_copies(slot):
+                    copy.wait_recv()
+
             @pl.loop(low, low + many)
-            def _(unit, left_of=left_of, right_of=right_of):
-                settle(unit, unit, product(kind, slot, left_of(unit), right_of(unit)))
-
-            if last:
+            def _(position, left_of=left_of, right_of=right_of):
+                unit = split_unit(position - 4, plane) if split else position
+                term = product(kind, slot, left_of(unit), right_of(unit))
+                if split:
+                    came = cross_got[slot, position - 4].astype(jnp.float32)
+                    term = term + came * cross_got_scale[slot, position - 4]
+                settle(position, unit, term)
+
+            if split and not last:
+
+                def credit_cross():
+                    pl.semaphore_signal(
+                        cross_credit, inc=1, device_id=mirror, device_id_type=MESH
+                    )
+
+                if first:
+                    credit_cross()
+                else:
+                    pl.when(step < count - 2)(credit_cross)
+
+            if last and split:
+                start([split_copy(pair, plane) for pair in range(SPLIT)])
+            elif last:
                 start(plane_copies(at, part))
             else:
                 start(ring_copies(at, part, slot))
@@ -1119,7 +1200,17 @@
         def add_square(total):
             square_buf[...] += jnp.sum((total * total).reshape(UNIT[0] // 8, 8, UNIT[1]), axis=0)
 
-        for part, (low, many, _, _) in enumerate(unit_parts(kind, phases[at]["first"])):
+        for part, (low, many, _, _) in enumerate(unit_parts(at, kind, phases[at]["first"])):
+            if at == 0 and part == 1:
+                for pair in range(SPLIT):
+                    split_copy(pair, plane).wait_send()
+                    split_copy(pair, 1 - plane).wait_recv()
+                    ours = split_unit(pair, plane)
+                    plane_got[0][ours] = plane_put[0][ours]
+                for unit in range(4, 8):
+                    add_square(plane_got[0][unit])
+                    start(out_copies(0, unit))
+                continue
             finish(plane_copies(at, part))
 
             @pl.loop(low, low + many)
@@ -1158,6 +1249,9 @@
         ]
     vec_own = pltpu.make_async_copy(vec_sum, all_vec.at[me], side_own.at[3])
 
+    def kv_parts(owner):
+        return [(ref.at[owner], ref.at[owner]) for ref in (all_kv, all_kv_scale)]
+
     def vec_copies(step):
         owner = ring_clip((place - onward * step + 2 * count) % count, count)
         vec = all_vec.at[owner, half_rows]
@@ -1165,7 +1259,7 @@
             pltpu.make_async_remote_copy(
                 here, there, vec_send.at[step, i], vec_recv.at[step, i], following, MESH
             )
-            for i, (here, there) in enumerate(((vec, vec), (all_kv.at[owner], all_kv.at[owner])))
+            for i, (here, there) in enumerate([(vec, vec)] + kv_parts(owner))
         ]
 
     def vec_first():
@@ -1174,9 +1268,7 @@
             pltpu.make_async_remote_copy(
                 here, there, vec_send.at[0, i], vec_recv.at[0, i], following, MESH
             )
-            for i, (here, there) in enumerate(
-                ((vec_sum.at[half_rows], vec), (all_kv.at[me], all_kv.at[me]))
-            )
+            for i, (here, there) in enumerate([(vec_sum.at[half_rows], vec)] + kv_parts(me))
         ]
 
     def vec_pair(step):
@@ -1208,7 +1300,7 @@
     def sum_bands():
         finish(side_local + side_remote)
         vec_sum[...] = jnp.sum(vec_got[...], 0)
-        all_kv[me] = jnp.sum(kv_got[...], 0)
+        all_kv[me], all_kv_scale[me] = encode(jnp.sum(kv_got[...], 0))
         vec_own.start()
         start(vec_first())
 
@@ -1222,7 +1314,8 @@
         for copy in vec_copies(count - 2):
             copy.wait_recv()
         vec_pair(count - 2).start()
-        grads = all_kv[...].reshape(text_buf.shape[0], -1)
+        grads = all_kv[...].astype(jnp.float32) * all_kv_scale[...]
+        grads = grads.reshape(text_buf.shape[0], -1)
         total = jnp.zeros_like(kv_grad)
         for _ in range(3):
             part = grads.astype(jnp.bfloat16)
@@ -1284,9 +1377,12 @@
         take_step(at, count - 1, False, True)
         if at == 1:
             multiply_text()
-        for part in range(2):
-            for slot in range(2):
+        for slot in range(2):
+            for part in range(2):
                 for copy in ring_copies(at, part, slot):
+                    copy.wait_send()
+            if at == 0:
+                for copy in cross_copies(slot):
                     copy.wait_send()
         if at == 2:
             kv_copy(1).wait_recv()
@@ -1358,17 +1454,26 @@
     scratch += [
         dma((5,)),
         dma((5,)),
+        *[
+            pltpu.VMEM((2, SPLIT) + tile, kind)
+            for _ in range(2)
+            for tile, kind in ((UNIT, jnp.int16), ((1, UNIT[1]), jnp.float32))
+        ],
+        dma((2, 2)),
+        dma((2, 2)),
+        pltpu.SemaphoreType.REGULAR,
         pltpu.VMEM((band_count,) + vectors.shape, jnp.float32),
         pltpu.VMEM(keyvals.shape, jnp.float32),
         pltpu.VMEM(vectors.shape, jnp.float32),
-        pltpu.VMEM((count,) + keyvals.shape[1:], jnp.float32),
+        pltpu.VMEM((count,) + keyvals.shape[1:], jnp.int16),
+        pltpu.VMEM((count, 1, kv_cols), jnp.float32),
         pltpu.VMEM(text.shape, jnp.bfloat16),
         pltpu.VMEM((text.shape[1], kv_cols), jnp.float32),
         dma((4,)),
         dma((2, band_count - 1)),
         dma((2, band_count - 1)),
-        dma((count - 1, 2)),
-        dma((count - 1, 2)),
+        dma((count - 1, 3)),
+        dma((count - 1, 3)),
         dma((count - 1,)),
         dma((count - 1,)),
         dma,
@@ -1493,18 +1598,18 @@
         (
             (0, 22 * D, FF),
             (1, 0, D),
+            (0, 20 * D, D),
+            (0, 21 * D, D),
             (0, 18 * D, D),
             (0, 19 * D, D),
-            (0, 20 * D, D),
-            (0, 21 * D, D),
             (0, 12 * D, 3 * D),
             (0, 15 * D, 3 * D),
         ),
-        (1, 2, 1, 2, 1, 2, 0, 0),
+        (1, 2, 1, 2, 0, 0, 0, 0),
         part_modul.reshape(clip_count, band_count, -1, 128),
         text_cols,
     )
-    up_a_w, down_a_w, out_a_w, out_b_w, query_w, cross_out_w, qkv_a_w, qkv_b_w = gathered
+    up_a_w, down_a_w, query_w, cross_out_w, out_a_w, out_b_w, qkv_a_w, qkv_b_w = gathered
     all_text = all_text.transpose(0, 2, 1, 3)
     keyval = keyval.transpose(1, 0, 2).reshape(TEXT_PAD, 2 * D)
     late_down_b, all_modul = lax.optimization_barrier((w_deep[:, 3 * D :], all_modul))

time: 950 us -> 943 us (level)
    pallas_call x1, Pallas kernels: 313 us -> 299 us  [reduce_gradients(): pl.pallas_call(partial(reduce_kernel, count, tokens, phases), out_shape=(...]
    pallas_call x1, Pallas kernels: 181 us -> 190 us  [gather_weights(): pl.pallas_call(partial(gather_kernel, count, picks, sides), out_shape=tup...]
  transfers between devices with their start and end apart: 6 -> 6, of which waited for: 4 -> 4; matrix products, arithmetic and copies ran while one was open for 9% -> 9% of each run, Pallas kernels for 23% -> 25%
where the time goes in v11:
time: 943 us; the launch traced here: 940 us
  Pallas kernels  592 us (63%)
  matrix products  154 us (16%)
  other arithmetic  83.4 us (9%)
  waiting for transfers between devices  45.8 us (5%)
  local copies, waits for them, and re-layouts  36 us (4%)
  between operations  24.2 us (3%)
    pallas_call x1, Pallas kernels, reduce_gradients(): pl.pallas_call(partial(reduce_kernel, count, tokens, phases), out_shape=(...  299 us
    pallas_call x1, Pallas kernels, gather_weights(): pl.pallas_call(partial(gather_kernel, count, picks, sides), out_shape=tup...  190 us
    dot_general x11, matrix products, matmul_nt(): lax.dot_general(left_op, right_op, (((1,), (1,)), ((), ())), preferred_el...  75 us
    dot_general x13, matrix products, matmul(): return jnp.dot(left_op, right_op, preferred_element_type=jnp.float32)  71.9 us
    sub x3, other arithmetic, adam_update(): weight - learn_rate * (first_hat / (jnp.sqrt(second_hat) + ADAM_EPS) + DE...  56.7 us
    ppermute x4, waiting for transfers between devices, shifted(): lax.ppermute(value, axis, [(i, (i + by) % length) for i in range(length)])  45.8 us
    pallas_call x2, Pallas kernels, attend_back(): pl.pallas_call(partial(attend_back_kernel, windows, text_len, sets), grid...  26.1 us
    pallas_call x1, Pallas kernels, attend_frames_back(): pl.pallas_call(partial(attend_frames_back_kernel, windows), out_shape=jax...  25 us
  transfers between devices with their start and end apart: 6, of which 4 were waited for; matrix products, arithmetic and copies ran while one was open for 9% of the time, Pallas kernels for 25%

profile of v11, /device:TPU:0, one launch (start us, length us, event | category | flops | bytes accessed | tf_op | source)
XLA Modules:
  0.0 939.8 jit_solution(9487640566414926921)
XLA Ops:
  7.2 1.7 slice.150
  11.8 9.7 %shard_map.230 = s32[8,8,128]{2,1,0:T(8,128)} custom-call(s32[8,128]{1,0:T(8,128)} %pad.12.facts_ref), custom_call_target="tpu_custom_call" | custom-call | tf_op jit(solution)/shard_map/pallas_call | solution.py:474
  22.6 3.5 fusion.16
  26.8 2.7 slice.127
  29.6 190.4 %shard_map.231 = (bf16[1024,4096]{1,0:T(8,128)(2,1)}, bf16[4096,1024]{1,0:T(8,128)(2,1)}, bf16[1024,1024]{1,0:T(8,128)(2,1)}, bf16[1024,1024]{1,0:T(8,128)(2,1)}...) custom-call(f32[128,30720]{1,0:T(8,128)} %refs_0_.1, ...), custom_call_target="tpu_custom_call" | custom-call | flops 199999995904 | bytes 600000000 | tf_op jit(solution)/shard_map/pallas_call | solution.py:749
  220.0 1.7 dynamic-slice_convert_fusion
  222.4 2.0 add_reduce_fusion
  224.5 2.3 multiply_reduce_fusion.21
  228.6 7.3 convolution_convert_fusion.1.qkv_ref
  235.9 12.1 %shard_map.232 = (bf16[640,1024]{1,0:T(8,128)(2,1)S(1)}, bf16[640,2048]{1,0:T(8,128)(2,1)S(1)}) custom-call(bf16[640,3072]{1,0:T(8,128)(2,1)S(1)} %convolution_convert_fusion.1.qkv_ref), custom_call_target="tpu_custom_call" | custom-call | flops 1342177280 | bytes 10485760 | tf_op jit(solution)/shard_map/pallas_call | solution.py:316
  248.1 3.2 fusion.53
  253.4 8.2 multiply_convert_fusion.1
  261.7 11.1 %fusion.52 = (f32[640]{0:T(1024)S(1)}, f32[640,1024]{1,0:T(8,128)S(1)}, f32[640,1024]{1,0:T(8,128)}) fusion(f32[640,1024]{1,0:T(8,128)S(1)} %get-tuple-element.108, f32[1024]{0:T(1024)S(1)} %bitcast.208, bf16[640,4096]{1,0:T(8,128)(2,1)S(1)} %get-tuple-element.146.refs_6_, bf16[4096,1024]{1,0:T(8,128)(2,1)} %get-tuple-element.40), kind=kOutput, calls=%fused_computation.187 | convolution fusion | flops 5370674688 | bytes 21502464 | tf_op jit(solution)/shard_map/dot_general | solution.py:37
  275.1 19.5 %collective-permute-done = bf16[10,32,1024]{2,1,0:T(8,128)(2,1)S(1)} collective-permute-done((bf16[10,32,1024]{2,1,0:T(8,128)(2,1)S(1)}, bf16[10,32,1024]{2,1,0:T(8,128)(2,1)S(1)}, u32[]{:S(2)}, u32[]{:S(2)}) %collective-permute-start) | collective-permute-done | bytes 655392 | tf_op jit(solution)/shard_map/ppermute | solution.py:33
  295.8 4.5 convolution_convert_fusion.refs_0_.refs_1_.refs_2_
  300.4 12.4 %shard_map.233 = bf16[640,1024]{1,0:T(8,128)(2,1)S(1)} custom-call(bf16[640,3072]{1,0:T(8,128)(2,1)S(1)} %convolution_convert_fusion.refs_0_.refs_1_.refs_2_, bf16[640,3072]{1,0:T(8,128)(2,1)S(1)} %convolution_convert_fusion.refs_0_.refs_1_.refs_2_, bf16[640,3072]{1,0:T(8,128)(2,1)S(1)} %convolution_convert_fusion.refs_0_.refs_1_.refs_2_), custom_call_target="tpu_custom_call" | custom-call | flops 1677721600 | bytes 10485760 | tf_op jit(solution)/shard_map/pallas_call | solution.py:368
  312.9 2.0 collective-permute-start.1
  317.9 5.3 collective-permute-done.1
  324.5 5.1 fusion.51
  330.4 2.2 copy-done.74
  334.1 6.7 shard_map.234.refs_2_
  340.8 1.6 fusion.62
  343.9 1.6 add_convert_fusion.refs_1_
  345.5 11.9 %multiply_convert_fusion = (bf16[640,4096]{1,0:T(8,128)(2,1)}, f32[640,4096]{1,0:T(8,128)}) fusion(bf16[640,1024]{1,0:T(8,128)(2,1)} %add_convert_fusion.refs_1_, bf16[1024,4096]{1,0:T(8,128)(2,1)} %all-gather.3.cloned.1.call-done), kind=kOutput, calls=%fused_computation.20 | convolution fusion | flops 5381816320 | bytes 25427968 | tf_op jit(solution)/shard_map/dot_general | solution.py:37
  357.4 11.1 %fusion.50 = (f32[640]{0:T(1024)S(1)}, f32[640,1024]{1,0:T(8,128)S(1)}, f32[640,1024]{1,0:T(8,128)}) fusion(f32[640,1024]{1,0:T(8,128)} %copy-done.16, f32[1024]{0:T(1024)S(1)} %bitcast.216, bf16[640,4096]{1,0:T(8,128)(2,1)} %get-tuple-element.152.refs_0_, bf16[4096,1024]{1,0:T(8,128)(2,1)} %all-gather.5.cloned.1.call-done), kind=kOutput, calls=%fused_computation.185 | convolution fusion | flops 5370674688 | bytes 21502464 | tf_op jit(solution)/shard_map/dot_general | solution.py:37
  372.5 12.7 %fusion.6.refs_11_ = bf16[640,4096]{1,0:T(8,128)(2,1)S(1)} fusion(f32[640,4096]{1,0:T(8,128)} %get-tuple-element.153, bf16[640,1024]{1,0:T(8,128)(2,1)S(1)} %multiply_convert_fusion.5.refs_10_, bf16[4096,1024]{1,0:T(8,128)(2,1)} %all-gather.5.cloned.1.call-done), kind=kOutput, calls=%fused_computation.13 | convolution fusion | flops 5394923520 | bytes 25427968 | tf_op jit(solution)/shard_map/dot_general | solution.py:51
  385.2 10.6 %multiply_reduce_fusion.5 = (f32[1024]{0:T(1024)S(1)}, f32[640]{0:T(1024)S(1)}, f32[1024]{0:T(1024)S(1)}, f32[640,1024]{1,0:T(8,128)S(1)}) fusion(f32[640,1024]{1,0:T(8,128)S(1)} %copy-done.17, f32[640]{0:T(1024)S(1)} %fusion.35, f32[640]{0:T(1024)S(1)} %broadcast_multiply_fusion.3, f32[1024]{0:T(1024)S(1)} %bitcast.199, ...), kind=kOutput, calls=%fused_computation.48 | convolution fusion | flops 5373949440 | bytes 18894336 | tf_op jit(solution)/shard_map/dot_general | solution.py:51
  399.3 2.7 convolution_convert_fusion.4.refs_3_
  402.0 7.8 shard_map.235
  409.8 4.0 multiply_reduce_fusion.2
  419.7 8.1 collective-permute-done.2
  427.9 18.3 %shard_map.236.refs_15_ = bf16[640,3072]{1,0:T(8,128)(2,1)} custom-call(bf16[640,3072]{1,0:T(8,128)(2,1)} %copy-done, bf16[640,3072]{1,0:T(8,128)(2,1)} %copy-done, bf16[640,3072]{1,0:T(8,128)(2,1)} %copy-done, bf16[640,1024]{1,0:T(8,128)(2,1)S(1)} %bitcast.151), custom_call_target="tpu_custom_call" | custom-call | flops 4194304000 | bytes 10485760 | tf_op jit(solution)/shard_map/pallas_call | solution.py:389
  446.2 7.6 fusion.63
  454.2 2.0 collective-permute-start.3
  458.6 12.8 %collective-permute-done.3 = f32[10,32,1024]{2,1,0:T(8,128)S(1)} collective-permute-done((f32[10,32,1024]{2,1,0:T(8,128)S(1)}, f32[10,32,1024]{2,1,0:T(8,128)S(1)}, u32[]{:S(2)}, u32[]{:S(2)}) %collective-permute-start.3) | collective-permute-done | bytes 1310752 | tf_op jit(solution)/shard_map/ppermute | solution.py:33
  471.6 1.6 copy-done.9
  476.6 14.7 %fusion.12.refs_17_ = bf16[640,4096]{1,0:T(8,128)(2,1)} fusion(f32[640,4096]{1,0:T(8,128)} %get-tuple-element.147, bf16[640,1024]{1,0:T(8,128)(2,1)S(1)} %multiply_convert_fusion.3.refs_16_, bf16[4096,1024]{1,0:T(8,128)(2,1)} %get-tuple-element.40), kind=kOutput, calls=%fused_computation.19 | convolution fusion | flops 5394923520 | bytes 25427968 | tf_op jit(solution)/shard_map/dot_general | solution.py:51
  491.3 10.3 %multiply_reduce_fusion.8 = (f32[1024]{0:T(1024)S(1)}, f32[640]{0:T(1024)S(1)}, f32[1024]{0:T(1024)S(1)}, f32[640,1024]{1,0:T(8,128)S(1)}) fusion(f32[640,1024]{1,0:T(8,128)S(1)} %copy-done.15, f32[640]{0:T(1024)S(1)} %copy-done.55, f32[640]{0:T(1024)S(1)} %copy-done.49, f32[1024]{0:T(1024)S(1)} %bitcast.196, bf16[640,4096]{1,0:T(8,128)(2,1)} %fusion.12.refs_17_, ...), kind=kOutput, calls=%fused_computation.51 | convolution fusion | flops 5373949440 | bytes 18894336 | tf_op jit(solution)/shard_map/dot_general | solution.py:51
  502.9 1.6 copy-done.71
  506.3 25.0 %shard_map.237.refs_19_ = bf16[640,3072]{1,0:T(8,128)(2,1)} custom-call(bf16[640,3072]{1,0:T(8,128)(2,1)} %copy-done.1, bf16[640,2048]{1,0:T(8,128)(2,1)S(1)} %copy-done.3, bf16[640,1024]{1,0:T(8,128)(2,1)S(1)} %convolution_convert_fusion.2.grad_ref), custom_call_target="tpu_custom_call" | custom-call | flops 3355443200 | bytes 10485760 | tf_op jit(solution)/shard_map/pallas_call | solution.py:335
  531.3 8.4 multiply_reduce_fusion.10
  544.5 299.2 %shard_map.238 = (f32[128,18432]{1,0:T(8,128)}, f32[512,2048]{1,0:T(8,128)}, f32[8,512]{1,0:T(8,128)}, f32[8,256,128]{2,1,0:T(8,128)}, f32[512,2048]{1,0:T(8,128...) custom-call(bf16[640,4096]{1,0:T(8,128)(2,1)} %get-tuple-element.152, ...), custom_call_target="tpu_custom_call" | custom-call | flops 299999985664 | bytes 800000000 | tf_op jit(solution)/shard_map/pallas_call | solution.py:1483
  843.7 1.8 copy.46
  846.4 5.6 multiply_reduce_fusion
  854.5 4.0 fusion.54
  861.0 10.1 %shard_map.239 = f32[8,128]{1,0:T(8,128)} custom-call(f32[8,128]{1,0:T(8,128)} %broadcast_in_dim.87.part_ref), custom_call_target="tpu_custom_call" | custom-call | tf_op jit(solution)/shard_map/pallas_call | solution.py:1536
  874.5 36.5 %multiply_subtract_fusion = (f32[128,30720]{1,0:T(8,128)}, f32[128,30720]{1,0:T(8,128)}, f32[128,30720]{1,0:T(8,128)}) fusion(f32[128,30720]{1,0:T(8,128)} %refs_0_.1, f32[]{:T(128)S(6)} %div.227, f32[128,18432]{1,0:T(8,128)} %get-tuple-element.54, f32[128,12288]{1,0:T(8,128)} %get-tuple-element.163, f32[128,30720]{1,0:T(8,128)} %param.22, f32[128,30720]{1,0:T(8,128)} %param.23), kind=kLoop, calls=%fused_computation.3 | loop fusion | flops 66846720 | bytes 110100480 | tf_op jit(solution)/shard_map/sub | solution.py:427
  911.0 19.5 %multiply_subtract_fusion.1 = (f32[512,4096]{1,0:T(8,128)}, f32[512,4096]{1,0:T(8,128)}, f32[512,4096]{1,0:T(8,128)}) fusion(f32[512,4096]{1,0:T(8,128)} %refs_1_.1, f32[]{:T(128)S(6)} %div.227, f32[512,1024]{1,0:T(8,128)} %get-tuple-element.110, f32[512,2048]{1,0:T(8,128)} %get-tuple-element.56, f32[512,1024]{1,0:T(8,128)S(1)} %get-tuple-element.109, ...), kind=kLoop, calls=%fused_computation.26 | loop fusion | flops 37748736 | bytes 58720260 | tf_op jit(solution)/shard_map/sub | solution.py:427
  (286 shorter events, 51.0 us)
Async XLA Ops:
  7.2 338.3 %all-gather.3.cloned.1.call-start = ((), (), s32[]{:S(2)}) async-start(), calls=%async_computation | async-start | bytes 8650752 | tf_op jit(solution)/shard_map/all_gather | solution.py:731
  9.7 347.7 %all-gather.5.cloned.1.call-start = ((), (), s32[]{:S(2)}) async-start(), calls=%async_computation.1 | async-start | bytes 8650752 | tf_op jit(solution)/shard_map/all_gather | solution.py:731
  29.6 192.3 %copy-start.34 = (f32[19,1024]{1,0:T(8,128)S(1)}, f32[19,1024]{1,0:T(8,128)}, u32[]{:S(2)}) copy-start(f32[19,1024]{1,0:T(8,128)} %param.27) | copy-start | bytes 233476
  29.6 192.3 %copy-start.36 = (f32[1,5,8,16,8]{3,4,2,1,0:T(8,128)S(1)}, f32[1,5,8,16,8]{3,4,2,1,0:T(8,128)}, u32[]{:S(2)}) copy-start(f32[1,5,8,16,8]{3,4,2,1,0:T(8,128)} %param.15) | copy-start | bytes 61444
  29.6 192.3 %copy-start.37 = (f32[1,5,8,16,8]{3,4,2,1,0:T(8,128)S(1)}, f32[1,5,8,16,8]{3,4,2,1,0:T(8,128)}, u32[]{:S(2)}) copy-start(f32[1,5,8,16,8]{3,4,2,1,0:T(8,128)} %param.16) | copy-start | bytes 61444
  221.9 26.1 %copy-start.42 = (f32[1,1024]{1,0:T(1,128)}, f32[1,1024]{1,0:T(1,128)S(1)}, u32[]{:S(2)}) copy-start(f32[1,1024]{1,0:T(1,128)S(1)} %get-tuple-element.126) | copy-start | bytes 12292
  226.8 9.0 copy-start.60
  226.9 9.0 copy-start.58
  226.9 9.0 copy-start.56
  226.9 21.2 %copy-start.64 = (f32[1,1024]{1,0:T(1,128)}, f32[1,1024]{1,0:T(1,128)S(1)}, u32[]{:S(2)}) copy-start(f32[1,1024]{1,0:T(1,128)S(1)} %get-tuple-element.140) | copy-start | bytes 12292
  226.9 24.9 %copy-start.52 = (f32[1,1024]{1,0:T(1,128)}, f32[1,1024]{1,0:T(1,128)S(1)}, u32[]{:S(2)}) copy-start(f32[1,1024]{1,0:T(1,128)S(1)} %get-tuple-element.137) | copy-start | bytes 12292
  235.9 15.4 %copy-start.1 = (bf16[640,3072]{1,0:T(8,128)(2,1)}, bf16[640,3072]{1,0:T(8,128)(2,1)S(1)}, u32[]{:S(2)}) copy-start(bf16[640,3072]{1,0:T(8,128)(2,1)S(1)} %convolution_convert_fusion.1.qkv_ref) | copy-start | bytes 11796484
  235.9 12.2 %copy-start.70 = (bf16[1024,1024]{1,0:T(8,128)(2,1)S(1)}, bf16[1024,1024]{1,0:T(8,128)(2,1)}, u32[]{:S(2)}) copy-start(bf16[1024,1024]{1,0:T(8,128)(2,1)} %get-tuple-element.38) | copy-start | bytes 6291460
  235.9 16.5 %slice-start = ((s8[8388608]{0:T(1024)(128)(4,1)}), s8[4194304]{0:T(1024)(128)(4,1)S(1)}, s32[]{:S(2)}) async-start(s8[8388608]{0:T(1024)(128)(4,1)} %bitcast.230), calls=%async_computation.2 | async-start | bytes 8388608
  251.4 10.3 %copy-start.14 = (f32[640,1024]{1,0:T(8,128)}, f32[640,1024]{1,0:T(8,128)S(1)}, u32[]{:S(2)}) copy-start(f32[640,1024]{1,0:T(8,128)S(1)} %get-tuple-element.108) | copy-start | bytes 7864324
  251.8 9.8 %copy-start.62 = (f32[640]{0:T(1024)}, f32[640]{0:T(1024)S(1)}, u32[]{:S(2)}) copy-start(f32[640]{0:T(1024)S(1)} %multiply_reduce_fusion.20) | copy-start | bytes 7684
  251.8 9.8 %copy-start.54 = (f32[640]{0:T(1024)}, f32[640]{0:T(1024)S(1)}, u32[]{:S(2)}) copy-start(f32[640]{0:T(1024)S(1)} %fusion.32) | copy-start | bytes 7684
  252.4 9.2 copy-start.30
  261.6 11.2 %copy-start.75 = (bf16[640,4096]{1,0:T(8,128)(2,1)}, bf16[640,4096]{1,0:T(8,128)(2,1)S(1)}, u32[]{:S(2)}) copy-start(bf16[640,4096]{1,0:T(8,128)(2,1)S(1)} %get-tuple-element.146.refs_6_) | copy-start | bytes 15728644
  272.8 23.1 %slice-start.2 = ((s8[6291456]{0:T(1024)(128)(4,1)}), s8[4194304]{0:T(1024)(128)(4,1)S(1)}, s32[]{:S(2)}) async-start(s8[6291456]{0:T(1024)(128)(4,1)} %bitcast.232), calls=%async_computation.4 | async-start | bytes 8388608
  273.2 22.6 %slice-start.3 = ((s8[6291456]{0:T(1024)(128)(4,1)}), s8[2097152]{0:T(1024)(128)(4,1)S(1)}, s32[]{:S(2)}) async-start(s8[6291456]{0:T(1024)(128)(4,1)} %bitcast.232), calls=%async_computation.5 | async-start | bytes 4194304
  274.5 20.1 %collective-permute-start = (bf16[10,32,1024]{2,1,0:T(8,128)(2,1)S(1)}, bf16[10,32,1024]{2,1,0:T(8,128)(2,1)S(1)}, u32[]{:S(2)}, u32[]{:S(2)}) collective-permute-start(bf16[10,32,1024]{2,1,0:T(8,128)(2,1)S(1)} %get-tuple-element.120), channel_id=1, source_target_pairs={{0,3},{1,0},{2,1},{3,2},{4,7},{5,4},{6,5},{7,6},{8,11},{9,8},{10,9... | collective-permute-start | bytes 1966088 | tf_op jit(solution)/shard_map/ppermute | solution.py:33
  300.3 12.4 %copy-start = (bf16[640,3072]{1,0:T(8,128)(2,1)}, bf16[640,3072]{1,0:T(8,128)(2,1)S(1)}, u32[]{:S(2)}) copy-start(bf16[640,3072]{1,0:T(8,128)(2,1)S(1)} %convolution_convert_fusion.refs_0_.refs_1_.refs_2_) | copy-start | bytes 11796484
  312.9 10.3 %collective-permute-start.1 = (bf16[10,32,1024]{2,1,0:T(8,128)(2,1)S(1)}, bf16[10,32,1024]{2,1,0:T(8,128)(2,1)}, u32[]{:S(2)}, u32[]{:S(2)}) collective-permute-start(bf16[10,32,1024]{2,1,0:T(8,128)(2,1)S(1)} %get-tuple-element.118), channel_id=1, source_target_pairs={{0,1},{1,2},{2,3},{3,0},{4,5},{5,6},{6,7},{7,4},{8,9},{9,10},{10,1... | collective-permute-start | bytes 1966088 | tf_op jit(solution)/shard_map/ppermute | solution.py:33
  317.9 6.6 copy-start.8
  329.6 11.2 %copy-start.10 = (f32[640,1024]{1,0:T(8,128)}, f32[640,1024]{1,0:T(8,128)S(1)}, u32[]{:S(2)}) copy-start(f32[640,1024]{1,0:T(8,128)S(1)} %get-tuple-element.104) | copy-start | bytes 7864324
  334.1 6.7 copy-start.72
  372.5 12.7 %copy-start.31 = (bf16[640,1024]{1,0:T(8,128)(2,1)}, bf16[640,1024]{1,0:T(8,128)(2,1)S(1)}, u32[]{:S(2)}) copy-start(bf16[640,1024]{1,0:T(8,128)(2,1)S(1)} %multiply_convert_fusion.5.refs_10_) | copy-start | bytes 3932164
  372.5 12.7 %copy-start.17 = (f32[640,1024]{1,0:T(8,128)S(1)}, f32[640,1024]{1,0:T(8,128)}, u32[]{:S(2)}) copy-start(f32[640,1024]{1,0:T(8,128)} %copy-done.16) | copy-start | bytes 7864324
  385.2 10.7 %copy-start.76 = (bf16[640,4096]{1,0:T(8,128)(2,1)}, bf16[640,4096]{1,0:T(8,128)(2,1)S(1)}, u32[]{:S(2)}) copy-start(bf16[640,4096]{1,0:T(8,128)(2,1)S(1)} %fusion.6.refs_11_) | copy-start | bytes 15728644
  402.0 7.8 copy-start.11
  419.6 8.2 collective-permute-start.2
  454.2 17.2 %collective-permute-start.3 = (f32[10,32,1024]{2,1,0:T(8,128)S(1)}, f32[10,32,1024]{2,1,0:T(8,128)S(1)}, u32[]{:S(2)}, u32[]{:S(2)}) collective-permute-start(f32[10,32,1024]{2,1,0:T(8,128)S(1)} %get-tuple-element.115), channel_id=1, source_target_pairs={{0,1},{1,2},{2,3},{3,0},{4,5},{5,6},{6,7},{7,4},{8,9},{9,10},{10,1... | collective-permute-start | bytes 3932168 | tf_op jit(solution)/shard_map/ppermute | solution.py:33
  476.6 14.7 %copy-start.29 = (bf16[640,1024]{1,0:T(8,128)(2,1)}, bf16[640,1024]{1,0:T(8,128)(2,1)S(1)}, u32[]{:S(2)}) copy-start(bf16[640,1024]{1,0:T(8,128)(2,1)S(1)} %multiply_convert_fusion.3.refs_16_) | copy-start | bytes 3932164
  476.6 14.7 %copy-start.15 = (f32[640,1024]{1,0:T(8,128)S(1)}, f32[640,1024]{1,0:T(8,128)}, u32[]{:S(2)}) copy-start(f32[640,1024]{1,0:T(8,128)} %copy-done.14) | copy-start | bytes 7864324
  476.6 14.7 %copy-start.49 = (f32[640]{0:T(1024)S(1)}, f32[640]{0:T(1024)}, u32[]{:S(2)}) copy-start(f32[640]{0:T(1024)} %copy-done.48) | copy-start | bytes 7684
  476.6 14.7 %copy-start.53 = (f32[1,1024]{1,0:T(1,128)S(1)}, f32[1,1024]{1,0:T(1,128)}, u32[]{:S(2)}) copy-start(f32[1,1024]{1,0:T(1,128)} %copy-done.52) | copy-start | bytes 12292
  476.6 14.7 %copy-start.55 = (f32[640]{0:T(1024)S(1)}, f32[640]{0:T(1024)}, u32[]{:S(2)}) copy-start(f32[640]{0:T(1024)} %copy-done.54) | copy-start | bytes 7684
  491.3 10.3 %copy-start.63 = (f32[640]{0:T(1024)S(1)}, f32[640]{0:T(1024)}, u32[]{:S(2)}) copy-start(f32[640]{0:T(1024)} %copy-done.62) | copy-start | bytes 7684
  506.3 25.0 %copy-start.13 = (f32[640,1024]{1,0:T(8,128)S(1)}, f32[640,1024]{1,0:T(8,128)}, u32[]{:S(2)}) copy-start(f32[640,1024]{1,0:T(8,128)} %get-tuple-element.144) | copy-start | bytes 7864324
  506.3 25.0 %copy-start.43 = (f32[1,1024]{1,0:T(1,128)S(1)}, f32[1,1024]{1,0:T(1,128)}, u32[]{:S(2)}) copy-start(f32[1,1024]{1,0:T(1,128)} %copy-done.42) | copy-start | bytes 12292
  506.3 25.0 %copy-start.51 = (f32[640]{0:T(1024)S(1)}, f32[640]{0:T(1024)}, u32[]{:S(2)}) copy-start(f32[640]{0:T(1024)} %copy-done.50) | copy-start | bytes 7684
  506.3 25.1 %copy-start.57 = (f32[1,1024]{1,0:T(1,128)S(1)}, f32[1,1024]{1,0:T(1,128)}, u32[]{:S(2)}) copy-start(f32[1,1024]{1,0:T(1,128)} %copy-done.56) | copy-start | bytes 12292
  506.3 25.1 %copy-start.59 = (f32[640]{0:T(1024)S(1)}, f32[640]{0:T(1024)}, u32[]{:S(2)}) copy-start(f32[640]{0:T(1024)} %copy-done.58) | copy-start | bytes 7684
  531.3 8.4 copy-start.61
  854.4 19.3 %copy-start.35 = (f32[19,1024]{1,0:T(8,128)S(1)}, f32[19,1024]{1,0:T(8,128)}, u32[]{:S(2)}) copy-start(f32[19,1024]{1,0:T(8,128)} %param.27) | copy-start | bytes 233476
  854.4 19.3 %copy-start.44 = (f32[19,1024]{1,0:T(8,128)S(1)}, f32[19,1024]{1,0:T(8,128)}, u32[]{:S(2)}) copy-start(f32[19,1024]{1,0:T(8,128)} %param.28) | copy-start | bytes 233476
  854.4 19.3 %copy-start.45 = (f32[19,1024]{1,0:T(8,128)S(1)}, f32[19,1024]{1,0:T(8,128)}, u32[]{:S(2)}) copy-start(f32[19,1024]{1,0:T(8,128)} %param.29) | copy-start | bytes 233476
  (39 other events, 100.0 us)
Sparse Core Ops, SparseCore 0:
  11.5 94.2 all-gather.2
  221.9 84.6 all-gather.4

commit v12 on v11

--- a/solution.py
+++ b/solution.py
@@ -643,8 +643,6 @@
             for step, peer in enumerate(band_peers)
         ]
 
-    for copy in parts_own + parts:
-        copy.wait()
     shares = [
         pltpu.make_async_remote_copy(
             out.at[:, band],
@@ -657,19 +655,25 @@
         for step, peer in enumerate(band_peers)
         for which, out in enumerate((vec_out, text_out))
     ]
-    for copy in shares:
-        copy.start()
-    kv_weight.wait()
-    weight = kv_wide[...].astype(jnp.bfloat16)
-    depth = weight.shape[0] // band_count
-    for copy in shares:
-        copy.wait()
-    for owner in range(count):
-        kv_part[owner] = sum(
-            matmul(text_out[owner, part], weight[part * depth : (part + 1) * depth])
-            for part in range(band_count)
-        )
-    kv_hop(0)
+
+    def share():
+        for copy in parts_own + parts:
+            copy.wait()
+        for copy in shares:
+            copy.start()
+
+    def multiply():
+        for copy in shares:
+            copy.wait()
+        kv_weight.wait()
+        weight = kv_wide[...].astype(jnp.bfloat16)
+        depth = weight.shape[0] // band_count
+        for owner in range(count):
+            kv_part[owner] = sum(
+                matmul(text_out[owner, part], weight[part * depth : (part + 1) * depth])
+                for part in range(band_count)
+            )
+        kv_hop(0)
 
     @pl.loop(1, count - 1)
     def _(step):
@@ -679,7 +683,12 @@
             def _(group=group):
                 ring_arrival(group, step - 1, True)
 
-        kv_hop(step)
+        pl.when(step == 1)(share)
+        pl.when(step == 2)(multiply)
+
+        @pl.when(step >= 3)
+        def _():
+            kv_hop(step - 2)
         for group in range(num):
 
             @off_ring(group, step >= 2)
@@ -692,6 +701,7 @@
         def _(group=group):
             ring_arrival(group, count - 2, False)
 
+    kv_hop(count - 3)
     for late in (count - 3, count - 2):
         for group in range(num):
 
@@ -699,6 +709,8 @@
             def _(group=group, late=late):
                 cross_arrival(group, late)
 
+        if late == count - 3:
+            kv_hop(count - 2)
     kv_copy(count - 2).wait_recv()
     kv_sum[...] = (kv_part[me] + kv_got[count - 2]).astype(jnp.bfloat16)
     kv_out[band] = kv_sum[...]
@@ -804,9 +816,9 @@
     lefts, rights = refs[:num], refs[num : 2 * num]
     vec_ref, kv_ref, text_ref = refs[2 * num : 2 * num + 3]
     refs = refs[2 * num + 3 :]
-    wide_out, deep_out, square_out, all_vec, kv_out, kv_square = refs[:6]
-    left_far, right_far = refs[6 : 6 + num], refs[6 + num : 6 + 2 * num]
-    scratch = refs[6 + 2 * num :]
+    wide_out, deep_out, square_out, all_vec, kv_square = refs[:5]
+    left_far, right_far = refs[5 : 5 + num], refs[5 + num : 5 + 2 * num]
+    scratch = refs[5 + 2 * num :]
     left_buf, right_buf, got_low, got_scale, put_low, put_scale, plane_put = (
         scratch[2 * i : 2 * i + 2] for i in range(7)
     )
@@ -1281,7 +1293,7 @@
     kv_width = kv_grad.shape[1]
 
     def kv_place(owner):
-        return kv_out.at[:, pl.ds(pl.multiple_of(owner * kv_width, 128), kv_width)]
+        return deep_out.at[:, pl.ds(pl.multiple_of(D + owner * kv_width, 128), kv_width)]
 
     def kv_copy(i):
         if i == 2:
@@ -1487,20 +1499,19 @@
             jax.ShapeDtypeStruct((deep_rows, deep_cols), jnp.float32),
             jax.ShapeDtypeStruct((8, UNIT[1]), jnp.float32),
             jax.ShapeDtypeStruct((count,) + vectors.shape, jnp.float32),
-            jax.ShapeDtypeStruct((deep_rows, band_count * kv_cols), jnp.float32),
             jax.ShapeDtypeStruct((8, kv_cols), jnp.float32),
         )
         + tuple(jax.ShapeDtypeStruct(x.shape, x.dtype) for x in lefts)
         + tuple(jax.ShapeDtypeStruct((tokens, x.shape[1] // 2), x.dtype) for x in rights),
         in_specs=[ANY] * (2 * num + 3),
-        out_specs=(ANY, ANY, IN_VMEM, ANY, ANY, IN_VMEM) + (ANY,) * (2 * num),
+        out_specs=(ANY, ANY, IN_VMEM, ANY, IN_VMEM) + (ANY,) * (2 * num),
         scratch_shapes=scratch,
         compiler_params=pltpu.CompilerParams(
             collective_id=2, has_side_effects=True, vmem_limit_bytes=58 << 20
         ),
         cost_estimate=pl.CostEstimate(flops=3 * 10**11, bytes_accessed=8 * 10**8, transcendentals=0),
     )(*lefts, *rights, vectors, keyvals, text)
-    return out[:6]
+    return out[:5]
 
 
 def total_kernel(count, part_ref, out_ref, mid, band_got, clip_got, *sems):
@@ -1605,7 +1616,7 @@
             (0, 12 * D, 3 * D),
             (0, 15 * D, 3 * D),
         ),
-        (1, 2, 1, 2, 0, 0, 0, 0),
+        (1, 2, 1, 2, 1, 2, 0, 0),
         part_modul.reshape(clip_count, band_count, -1, 128),
         text_cols,
     )
@@ -1732,7 +1743,7 @@
     factors += mlp_factors_a + (factors_oa, factors_qkva)
     if wide_rows == 128 and deep_rows == 512:
         phases = (
-            {"kind": 0, "first": 0, "lefts": (0, 1), "cols": (D, 10 * D + FF)},
+            {"kind": 0, "first": 0, "lefts": (0, 1), "cols": (3 * D, 10 * D + FF)},
             {"kind": 1, "first": 0, "lefts": (2, 3, 4, 5), "cols": (9 * D, 8 * D, 7 * D, 3 * D)},
             {"kind": 0, "first": 0, "lefts": (6, 7), "cols": (0, 10 * D)},
             {"kind": 1, "first": 2, "lefts": (8, 9), "cols": (6 * D, 0)},
@@ -1743,7 +1754,7 @@
         )
         vectors = jnp.pad(vectors, (0, 256 * 128 - vectors.shape[0])).reshape(256, 128)
         keyvals = grad_keyval.reshape(TEXT_PAD, band_count, kv_cols).transpose(1, 0, 2)
-        wide_rest, deep_rest, squares, all_vectors, grad_w_ckv, kv_squares = reduce_gradients(
+        wide_rest, deep_sum, squares, all_vectors, kv_squares = reduce_gradients(
             phases,
             [f[0] for f in factors],
             [f[1] for f in factors],
@@ -1751,7 +1762,7 @@
             keyvals,
             all_text.reshape(clip_count * TEXT_PAD, deep_rows),
             10 * D + 2 * FF,
-            2 * D,
+            4 * D,
         )
         all_vectors = all_vectors.reshape(clip_count, -1)
         all_grad_modul = all_vectors[:, : 12 * D]
@@ -1761,7 +1772,6 @@
     else:
         summed = [sum_rows(*pair) for pair in factors]
         wide_rest = jnp.concatenate([summed[i] for i in (9, 5, 8, 4, 3, 2, 7, 1)], 1)
-        deep_rest = jnp.concatenate([summed[6], summed[0]], 1)
         grad_keyval = lax.psum_scatter(grad_keyval, "band", scatter_dimension=1, tiled=True)
         grad_keyval = lax.all_gather(grad_keyval, "clip", axis=0, tiled=True)
         grad_w_ckv = matmul_tn(
@@ -1772,10 +1782,10 @@
         grad_w_ckv = lax.all_gather(grad_w_ckv, "band", axis=1, tiled=True)
         all_grad_modul = lax.all_gather(lax.psum(grad_modul, "band"), "clip", axis=0, tiled=True)
         loss_sum, small_sum = lax.psum((loss_part, grad_small), ("clip", "band"))
-        square_part = sum(jnp.sum(x * x) for x in (wide_rest, deep_rest, grad_w_ckv)) / band_count
+        deep_sum = jnp.concatenate([summed[6], grad_w_ckv, summed[0]], 1)
+        square_part = sum(jnp.sum(x * x) for x in (wide_rest, deep_sum)) / band_count
     grad_w_ada = matmul_tn(time_rows.astype(jnp.float32), all_grad_modul, lax.Precision.HIGHEST)
     wide_sum = jnp.concatenate([grad_w_ada, wide_rest], 1)
-    deep_sum = jnp.concatenate([deep_rest[:, :D], grad_w_ckv, deep_rest[:, D:]], 1)
     square_part += jnp.sum(grad_w_ada * grad_w_ada) / band_count
     square_sum = total_over_devices(square_part)
     grad_norm = jnp.sqrt(square_sum + jnp.sum(small_sum * small_sum))

time: 943 us -> 935 us (level)
  no operation moved by 1% of the time
where the time goes in v12:
time: 935 us; the launch traced here: 932 us
  Pallas kernels  589 us (63%)
  matrix products  154 us (16%)
  other arithmetic  86.3 us (9%)
  waiting for transfers between devices  40.4 us (4%)
  local copies, waits for them, and re-layouts  32 us (3%)
  between operations  24.2 us (3%)
    pallas_call x1, Pallas kernels, reduce_gradients(): pl.pallas_call(partial(reduce_kernel, count, tokens, phases), out_shape=(...  299 us
    pallas_call x1, Pallas kernels, gather_weights(): pl.pallas_call(partial(gather_kernel, count, picks, sides), out_shape=tup...  188 us
    dot_general x11, matrix products, matmul_nt(): lax.dot_general(left_op, right_op, (((1,), (1,)), ((), ())), preferred_el...  75 us
    dot_general x13, matrix products, matmul(): return jnp.dot(left_op, right_op, preferred_element_type=jnp.float32)  71.9 us
    sub x3, other arithmetic, adam_update(): weight - learn_rate * (first_hat / (jnp.sqrt(second_hat) + ADAM_EPS) + DE...  59.7 us
    ppermute x4, waiting for transfers between devices, shifted(): lax.ppermute(value, axis, [(i, (i + by) % length) for i in range(length)])  40.4 us
    pallas_call x2, Pallas kernels, attend_back(): pl.pallas_call(partial(attend_back_kernel, windows, text_len, sets), grid...  26.1 us
    pallas_call x1, Pallas kernels, attend_frames_back(): pl.pallas_call(partial(attend_frames_back_kernel, windows), out_shape=jax...  25 us
  transfers between devices with their start and end apart: 6, of which 4 were waited for; matrix products, arithmetic and copies ran while one was open for 9% of the time, Pallas kernels for 25%

profile of v12, /device:TPU:0, one launch (start us, length us, event | category | flops | bytes accessed | tf_op | source)
XLA Modules:
  0.0 931.6 jit_solution(15763807240356694587)
XLA Ops:
  7.2 1.7 slice.144
  11.8 9.7 %shard_map.230 = s32[8,8,128]{2,1,0:T(8,128)} custom-call(s32[8,128]{1,0:T(8,128)} %pad.12.facts_ref), custom_call_target="tpu_custom_call" | custom-call | tf_op jit(solution)/shard_map/pallas_call | solution.py:474
  22.6 3.5 fusion.16
  26.8 2.7 slice.121
  29.7 187.6 %shard_map.231 = (bf16[1024,4096]{1,0:T(8,128)(2,1)}, bf16[4096,1024]{1,0:T(8,128)(2,1)}, bf16[1024,1024]{1,0:T(8,128)(2,1)}, bf16[1024,1024]{1,0:T(8,128)(2,1)}...) custom-call(f32[128,30720]{1,0:T(8,128)} %refs_0_.1, ...), custom_call_target="tpu_custom_call" | custom-call | flops 199999995904 | bytes 600000000 | tf_op jit(solution)/shard_map/pallas_call | solution.py:761
  217.2 1.7 dynamic-slice_convert_fusion
  219.6 2.0 add_reduce_fusion
  221.7 2.3 multiply_reduce_fusion.21
  225.8 7.4 convolution_convert_fusion.1.qkv_ref
  233.3 12.1 %shard_map.232 = (bf16[640,1024]{1,0:T(8,128)(2,1)S(1)}, bf16[640,2048]{1,0:T(8,128)(2,1)S(1)}) custom-call(bf16[640,3072]{1,0:T(8,128)(2,1)S(1)} %convolution_convert_fusion.1.qkv_ref), custom_call_target="tpu_custom_call" | custom-call | flops 1342177280 | bytes 10485760 | tf_op jit(solution)/shard_map/pallas_call | solution.py:316
  245.4 3.1 fusion.53
  250.7 8.2 multiply_convert_fusion.1
  258.9 11.1 %fusion.52 = (f32[640]{0:T(1024)S(1)}, f32[640,1024]{1,0:T(8,128)S(1)}, f32[640,1024]{1,0:T(8,128)}) fusion(f32[640,1024]{1,0:T(8,128)S(1)} %get-tuple-element.106, f32[1024]{0:T(1024)S(1)} %bitcast.208, bf16[640,4096]{1,0:T(8,128)(2,1)S(1)} %get-tuple-element.142.refs_6_, bf16[4096,1024]{1,0:T(8,128)(2,1)} %get-tuple-element.39), kind=kOutput, calls=%fused_computation.186 | convolution fusion | flops 5370674688 | bytes 21502464 | tf_op jit(solution)/shard_map/dot_general | solution.py:37
  273.2 14.2 %collective-permute-done = bf16[10,32,1024]{2,1,0:T(8,128)(2,1)S(1)} collective-permute-done((bf16[10,32,1024]{2,1,0:T(8,128)(2,1)S(1)}, bf16[10,32,1024]{2,1,0:T(8,128)(2,1)S(1)}, u32[]{:S(2)}, u32[]{:S(2)}) %collective-permute-start) | collective-permute-done | bytes 655392 | tf_op jit(solution)/shard_map/ppermute | solution.py:33
  288.6 4.5 convolution_convert_fusion.refs_0_.refs_1_.refs_2_
  293.1 12.4 %shard_map.233 = bf16[640,1024]{1,0:T(8,128)(2,1)S(1)} custom-call(bf16[640,3072]{1,0:T(8,128)(2,1)S(1)} %convolution_convert_fusion.refs_0_.refs_1_.refs_2_, bf16[640,3072]{1,0:T(8,128)(2,1)S(1)} %convolution_convert_fusion.refs_0_.refs_1_.refs_2_, bf16[640,3072]{1,0:T(8,128)(2,1)S(1)} %convolution_convert_fusion.refs_0_.refs_1_.refs_2_), custom_call_target="tpu_custom_call" | custom-call | flops 1677721600 | bytes 10485760 | tf_op jit(solution)/shard_map/pallas_call | solution.py:368
  305.6 2.0 collective-permute-start.1
  310.6 5.3 collective-permute-done.1
  317.2 5.1 fusion.51
  323.1 2.2 copy-done.74
  326.8 6.7 shard_map.234.refs_2_
  333.5 1.6 fusion.61
  338.2 11.9 %multiply_convert_fusion = (bf16[640,4096]{1,0:T(8,128)(2,1)}, f32[640,4096]{1,0:T(8,128)}) fusion(bf16[640,1024]{1,0:T(8,128)(2,1)} %add_convert_fusion.refs_1_, bf16[1024,4096]{1,0:T(8,128)(2,1)} %all-gather.3.cloned.1.call-done), kind=kOutput, calls=%fused_computation.20 | convolution fusion | flops 5381816320 | bytes 25427968 | tf_op jit(solution)/shard_map/dot_general | solution.py:37
  350.1 11.1 %fusion.50 = (f32[640]{0:T(1024)S(1)}, f32[640,1024]{1,0:T(8,128)S(1)}, f32[640,1024]{1,0:T(8,128)}) fusion(f32[640,1024]{1,0:T(8,128)} %copy-done.16, f32[1024]{0:T(1024)S(1)} %bitcast.216, bf16[640,4096]{1,0:T(8,128)(2,1)} %get-tuple-element.148.refs_0_, bf16[4096,1024]{1,0:T(8,128)(2,1)} %all-gather.5.cloned.1.call-done), kind=kOutput, calls=%fused_computation.184 | convolution fusion | flops 5370674688 | bytes 21502464 | tf_op jit(solution)/shard_map/dot_general | solution.py:37
  365.2 12.7 %fusion.6.refs_11_ = bf16[640,4096]{1,0:T(8,128)(2,1)S(1)} fusion(f32[640,4096]{1,0:T(8,128)} %get-tuple-element.149, bf16[640,1024]{1,0:T(8,128)(2,1)S(1)} %multiply_convert_fusion.5.refs_10_, bf16[4096,1024]{1,0:T(8,128)(2,1)} %all-gather.5.cloned.1.call-done), kind=kOutput, calls=%fused_computation.13 | convolution fusion | flops 5394923520 | bytes 25427968 | tf_op jit(solution)/shard_map/dot_general | solution.py:51
  377.9 10.6 %multiply_reduce_fusion.5 = (f32[1024]{0:T(1024)S(1)}, f32[640]{0:T(1024)S(1)}, f32[1024]{0:T(1024)S(1)}, f32[640,1024]{1,0:T(8,128)S(1)}) fusion(f32[640,1024]{1,0:T(8,128)S(1)} %copy-done.17, f32[640]{0:T(1024)S(1)} %fusion.35, f32[640]{0:T(1024)S(1)} %broadcast_multiply_fusion.3, f32[1024]{0:T(1024)S(1)} %bitcast.199, ...), kind=kOutput, calls=%fused_computation.47 | convolution fusion | flops 5373949440 | bytes 18894336 | tf_op jit(solution)/shard_map/dot_general | solution.py:51
  392.0 2.7 convolution_convert_fusion.4.refs_3_
  394.6 7.8 shard_map.235
  402.5 4.0 multiply_reduce_fusion.2
  410.6 1.5 convolution_convert_fusion.3
  412.4 8.1 collective-permute-done.2
  420.6 18.3 %shard_map.236.refs_15_ = bf16[640,3072]{1,0:T(8,128)(2,1)} custom-call(bf16[640,3072]{1,0:T(8,128)(2,1)} %copy-done, bf16[640,3072]{1,0:T(8,128)(2,1)} %copy-done, bf16[640,3072]{1,0:T(8,128)(2,1)} %copy-done, bf16[640,1024]{1,0:T(8,128)(2,1)S(1)} %bitcast.151), custom_call_target="tpu_custom_call" | custom-call | flops 4194304000 | bytes 10485760 | tf_op jit(solution)/shard_map/pallas_call | solution.py:389
  438.8 7.6 fusion.62
  446.8 2.0 collective-permute-start.3
  451.2 12.8 %collective-permute-done.3 = f32[10,32,1024]{2,1,0:T(8,128)S(1)} collective-permute-done((f32[10,32,1024]{2,1,0:T(8,128)S(1)}, f32[10,32,1024]{2,1,0:T(8,128)S(1)}, u32[]{:S(2)}, u32[]{:S(2)}) %collective-permute-start.3) | collective-permute-done | bytes 1310752 | tf_op jit(solution)/shard_map/ppermute | solution.py:33
  464.2 1.6 copy-done.9
  469.2 14.6 %fusion.12.refs_17_ = bf16[640,4096]{1,0:T(8,128)(2,1)} fusion(f32[640,4096]{1,0:T(8,128)} %get-tuple-element.143, bf16[640,1024]{1,0:T(8,128)(2,1)S(1)} %multiply_convert_fusion.3.refs_16_, bf16[4096,1024]{1,0:T(8,128)(2,1)} %get-tuple-element.39), kind=kOutput, calls=%fused_computation.19 | convolution fusion | flops 5394923520 | bytes 25427968 | tf_op jit(solution)/shard_map/dot_general | solution.py:51
  483.9 10.3 %multiply_reduce_fusion.8 = (f32[1024]{0:T(1024)S(1)}, f32[640]{0:T(1024)S(1)}, f32[1024]{0:T(1024)S(1)}, f32[640,1024]{1,0:T(8,128)S(1)}) fusion(f32[640,1024]{1,0:T(8,128)S(1)} %copy-done.15, f32[640]{0:T(1024)S(1)} %copy-done.55, f32[640]{0:T(1024)S(1)} %copy-done.49, f32[1024]{0:T(1024)S(1)} %bitcast.196, bf16[640,4096]{1,0:T(8,128)(2,1)} %fusion.12.refs_17_, ...), kind=kOutput, calls=%fused_computation.50 | convolution fusion | flops 5373949440 | bytes 18894336 | tf_op jit(solution)/shard_map/dot_general | solution.py:51
  495.5 1.6 copy-done.71
  497.1 1.6 convolution_convert_fusion.2.grad_ref
  498.9 25.0 %shard_map.237.refs_19_ = bf16[640,3072]{1,0:T(8,128)(2,1)} custom-call(bf16[640,3072]{1,0:T(8,128)(2,1)} %copy-done.1, bf16[640,2048]{1,0:T(8,128)(2,1)S(1)} %copy-done.3, bf16[640,1024]{1,0:T(8,128)(2,1)S(1)} %convolution_convert_fusion.2.grad_ref), custom_call_target="tpu_custom_call" | custom-call | flops 3355443200 | bytes 10485760 | tf_op jit(solution)/shard_map/pallas_call | solution.py:335
  523.9 8.4 multiply_reduce_fusion.10
  537.1 298.9 %shard_map.238 = (f32[128,18432]{1,0:T(8,128)}, f32[512,4096]{1,0:T(8,128)}, f32[8,512]{1,0:T(8,128)}, f32[8,256,128]{2,1,0:T(8,128)}, f32[8,512]{1,0:T(8,128)},...) custom-call(bf16[640,4096]{1,0:T(8,128)(2,1)} %get-tuple-element.148, ...), custom_call_target="tpu_custom_call" | custom-call | flops 299999985664 | bytes 800000000 | tf_op jit(solution)/shard_map/pallas_call | solution.py:1495
  836.0 1.8 copy.46
  838.7 5.6 multiply_reduce_fusion
  849.4 10.5 %shard_map.239 = f32[8,128]{1,0:T(8,128)} custom-call(f32[8,128]{1,0:T(8,128)} %broadcast_in_dim.87.part_ref), custom_call_target="tpu_custom_call" | custom-call | tf_op jit(solution)/shard_map/pallas_call | solution.py:1547
  863.3 22.5 %multiply_subtract_fusion.1 = (f32[512,4096]{1,0:T(8,128)}, f32[512,4096]{1,0:T(8,128)}, f32[512,4096]{1,0:T(8,128)}) fusion(f32[512,4096]{1,0:T(8,128)} %refs_1_.1, f32[512,4096]{1,0:T(8,128)} %get-tuple-element.54, f32[]{:T(128)S(6)} %div.227, f32[512,4096]{1,0:T(8,128)} %param.25, f32[512,4096]{1,0:T(8,128)} %param.26), kind=kLoop, calls=%fused_computation.25 | loop fusion | flops 33554432 | bytes 58720260 | tf_op jit(solution)/shard_map/sub | solution.py:427
  885.8 36.5 %multiply_subtract_fusion = (f32[128,30720]{1,0:T(8,128)}, f32[128,30720]{1,0:T(8,128)}, f32[128,30720]{1,0:T(8,128)}) fusion(f32[128,30720]{1,0:T(8,128)} %refs_0_.1, f32[]{:T(128)S(6)} %div.227, f32[128,18432]{1,0:T(8,128)} %get-tuple-element.53, f32[128,12288]{1,0:T(8,128)} %get-tuple-element.159, f32[128,30720]{1,0:T(8,128)} %param.22, f32[128,30720]{1,0:T(8,128)} %param.23), kind=kLoop, calls=%fused_computation.3 | loop fusion | flops 66846720 | bytes 110100480 | tf_op jit(solution)/shard_map/sub | solution.py:427
  (285 shorter events, 50.4 us)
Async XLA Ops:
  7.2 331.0 %all-gather.3.cloned.1.call-start = ((), (), s32[]{:S(2)}) async-start(), calls=%async_computation | async-start | bytes 8650752 | tf_op jit(solution)/shard_map/all_gather | solution.py:743
  9.7 340.4 %all-gather.5.cloned.1.call-start = ((), (), s32[]{:S(2)}) async-start(), calls=%async_computation.1 | async-start | bytes 8650752 | tf_op jit(solution)/shard_map/all_gather | solution.py:743
  29.6 189.5 %copy-start.34 = (f32[19,1024]{1,0:T(8,128)S(1)}, f32[19,1024]{1,0:T(8,128)}, u32[]{:S(2)}) copy-start(f32[19,1024]{1,0:T(8,128)} %param.27) | copy-start | bytes 233476
  29.6 189.5 %copy-start.36 = (f32[1,5,8,16,8]{3,4,2,1,0:T(8,128)S(1)}, f32[1,5,8,16,8]{3,4,2,1,0:T(8,128)}, u32[]{:S(2)}) copy-start(f32[1,5,8,16,8]{3,4,2,1,0:T(8,128)} %param.15) | copy-start | bytes 61444
  29.6 189.5 %copy-start.37 = (f32[1,5,8,16,8]{3,4,2,1,0:T(8,128)S(1)}, f32[1,5,8,16,8]{3,4,2,1,0:T(8,128)}, u32[]{:S(2)}) copy-start(f32[1,5,8,16,8]{3,4,2,1,0:T(8,128)} %param.16) | copy-start | bytes 61444
  219.2 26.2 %copy-start.42 = (f32[1,1024]{1,0:T(1,128)}, f32[1,1024]{1,0:T(1,128)S(1)}, u32[]{:S(2)}) copy-start(f32[1,1024]{1,0:T(1,128)S(1)} %get-tuple-element.122) | copy-start | bytes 12292
  224.1 9.2 copy-start.60
  224.1 9.1 copy-start.58
  224.1 9.1 copy-start.56
  224.1 21.3 %copy-start.64 = (f32[1,1024]{1,0:T(1,128)}, f32[1,1024]{1,0:T(1,128)S(1)}, u32[]{:S(2)}) copy-start(f32[1,1024]{1,0:T(1,128)S(1)} %get-tuple-element.136) | copy-start | bytes 12292
  224.1 25.0 %copy-start.52 = (f32[1,1024]{1,0:T(1,128)}, f32[1,1024]{1,0:T(1,128)S(1)}, u32[]{:S(2)}) copy-start(f32[1,1024]{1,0:T(1,128)S(1)} %get-tuple-element.133) | copy-start | bytes 12292
  233.2 15.3 %copy-start.1 = (bf16[640,3072]{1,0:T(8,128)(2,1)}, bf16[640,3072]{1,0:T(8,128)(2,1)S(1)}, u32[]{:S(2)}) copy-start(bf16[640,3072]{1,0:T(8,128)(2,1)S(1)} %convolution_convert_fusion.1.qkv_ref) | copy-start | bytes 11796484
  233.2 12.1 %copy-start.70 = (bf16[1024,1024]{1,0:T(8,128)(2,1)S(1)}, bf16[1024,1024]{1,0:T(8,128)(2,1)}, u32[]{:S(2)}) copy-start(bf16[1024,1024]{1,0:T(8,128)(2,1)} %get-tuple-element.37) | copy-start | bytes 6291460
  233.3 16.4 %slice-start = ((s8[8388608]{0:T(1024)(128)(4,1)}), s8[4194304]{0:T(1024)(128)(4,1)S(1)}, s32[]{:S(2)}) async-start(s8[8388608]{0:T(1024)(128)(4,1)} %bitcast.230), calls=%async_computation.2 | async-start | bytes 8388608
  248.7 10.3 %copy-start.14 = (f32[640,1024]{1,0:T(8,128)}, f32[640,1024]{1,0:T(8,128)S(1)}, u32[]{:S(2)}) copy-start(f32[640,1024]{1,0:T(8,128)S(1)} %get-tuple-element.106) | copy-start | bytes 7864324
  249.1 9.8 %copy-start.62 = (f32[640]{0:T(1024)}, f32[640]{0:T(1024)S(1)}, u32[]{:S(2)}) copy-start(f32[640]{0:T(1024)S(1)} %multiply_reduce_fusion.20) | copy-start | bytes 7684
  249.1 9.8 %copy-start.54 = (f32[640]{0:T(1024)}, f32[640]{0:T(1024)S(1)}, u32[]{:S(2)}) copy-start(f32[640]{0:T(1024)S(1)} %fusion.32) | copy-start | bytes 7684
  249.7 9.2 copy-start.30
  258.9 11.1 %copy-start.75 = (bf16[640,4096]{1,0:T(8,128)(2,1)}, bf16[640,4096]{1,0:T(8,128)(2,1)S(1)}, u32[]{:S(2)}) copy-start(bf16[640,4096]{1,0:T(8,128)(2,1)S(1)} %get-tuple-element.142.refs_6_) | copy-start | bytes 15728644
  270.0 18.6 %slice-start.2 = ((s8[6291456]{0:T(1024)(128)(4,1)}), s8[4194304]{0:T(1024)(128)(4,1)S(1)}, s32[]{:S(2)}) async-start(s8[6291456]{0:T(1024)(128)(4,1)} %bitcast.232), calls=%async_computation.4 | async-start | bytes 8388608
  270.4 18.1 %slice-start.3 = ((s8[6291456]{0:T(1024)(128)(4,1)}), s8[2097152]{0:T(1024)(128)(4,1)S(1)}, s32[]{:S(2)}) async-start(s8[6291456]{0:T(1024)(128)(4,1)} %bitcast.232), calls=%async_computation.5 | async-start | bytes 4194304
  271.7 15.6 %collective-permute-start = (bf16[10,32,1024]{2,1,0:T(8,128)(2,1)S(1)}, bf16[10,32,1024]{2,1,0:T(8,128)(2,1)S(1)}, u32[]{:S(2)}, u32[]{:S(2)}) collective-permute-start(bf16[10,32,1024]{2,1,0:T(8,128)(2,1)S(1)} %get-tuple-element.116), channel_id=1, source_target_pairs={{0,3},{1,0},{2,1},{3,2},{4,7},{5,4},{6,5},{7,6},{8,11},{9,8},{10,9... | collective-permute-start | bytes 1966088 | tf_op jit(solution)/shard_map/ppermute | solution.py:33
  293.1 12.4 %copy-start = (bf16[640,3072]{1,0:T(8,128)(2,1)}, bf16[640,3072]{1,0:T(8,128)(2,1)S(1)}, u32[]{:S(2)}) copy-start(bf16[640,3072]{1,0:T(8,128)(2,1)S(1)} %convolution_convert_fusion.refs_0_.refs_1_.refs_2_) | copy-start | bytes 11796484
  305.6 10.3 %collective-permute-start.1 = (bf16[10,32,1024]{2,1,0:T(8,128)(2,1)S(1)}, bf16[10,32,1024]{2,1,0:T(8,128)(2,1)}, u32[]{:S(2)}, u32[]{:S(2)}) collective-permute-start(bf16[10,32,1024]{2,1,0:T(8,128)(2,1)S(1)} %get-tuple-element.114), channel_id=1, source_target_pairs={{0,1},{1,2},{2,3},{3,0},{4,5},{5,6},{6,7},{7,4},{8,9},{9,10},{10,1... | collective-permute-start | bytes 1966088 | tf_op jit(solution)/shard_map/ppermute | solution.py:33
  310.6 6.6 copy-start.8
  322.3 11.2 %copy-start.10 = (f32[640,1024]{1,0:T(8,128)}, f32[640,1024]{1,0:T(8,128)S(1)}, u32[]{:S(2)}) copy-start(f32[640,1024]{1,0:T(8,128)S(1)} %get-tuple-element.102) | copy-start | bytes 7864324
  326.8 6.7 copy-start.72
  365.2 12.7 %copy-start.31 = (bf16[640,1024]{1,0:T(8,128)(2,1)}, bf16[640,1024]{1,0:T(8,128)(2,1)S(1)}, u32[]{:S(2)}) copy-start(bf16[640,1024]{1,0:T(8,128)(2,1)S(1)} %multiply_convert_fusion.5.refs_10_) | copy-start | bytes 3932164
  365.2 12.7 %copy-start.17 = (f32[640,1024]{1,0:T(8,128)S(1)}, f32[640,1024]{1,0:T(8,128)}, u32[]{:S(2)}) copy-start(f32[640,1024]{1,0:T(8,128)} %copy-done.16) | copy-start | bytes 7864324
  377.9 10.7 %copy-start.76 = (bf16[640,4096]{1,0:T(8,128)(2,1)}, bf16[640,4096]{1,0:T(8,128)(2,1)S(1)}, u32[]{:S(2)}) copy-start(bf16[640,4096]{1,0:T(8,128)(2,1)S(1)} %fusion.6.refs_11_) | copy-start | bytes 15728644
  394.6 7.8 copy-start.11
  412.3 8.2 collective-permute-start.2
  446.8 17.2 %collective-permute-start.3 = (f32[10,32,1024]{2,1,0:T(8,128)S(1)}, f32[10,32,1024]{2,1,0:T(8,128)S(1)}, u32[]{:S(2)}, u32[]{:S(2)}) collective-permute-start(f32[10,32,1024]{2,1,0:T(8,128)S(1)} %get-tuple-element.111), channel_id=1, source_target_pairs={{0,1},{1,2},{2,3},{3,0},{4,5},{5,6},{6,7},{7,4},{8,9},{9,10},{10,1... | collective-permute-start | bytes 3932168 | tf_op jit(solution)/shard_map/ppermute | solution.py:33
  469.2 14.7 %copy-start.29 = (bf16[640,1024]{1,0:T(8,128)(2,1)}, bf16[640,1024]{1,0:T(8,128)(2,1)S(1)}, u32[]{:S(2)}) copy-start(bf16[640,1024]{1,0:T(8,128)(2,1)S(1)} %multiply_convert_fusion.3.refs_16_) | copy-start | bytes 3932164
  469.2 14.7 %copy-start.15 = (f32[640,1024]{1,0:T(8,128)S(1)}, f32[640,1024]{1,0:T(8,128)}, u32[]{:S(2)}) copy-start(f32[640,1024]{1,0:T(8,128)} %copy-done.14) | copy-start | bytes 7864324
  469.2 14.7 %copy-start.49 = (f32[640]{0:T(1024)S(1)}, f32[640]{0:T(1024)}, u32[]{:S(2)}) copy-start(f32[640]{0:T(1024)} %copy-done.48) | copy-start | bytes 7684
  469.2 14.7 %copy-start.53 = (f32[1,1024]{1,0:T(1,128)S(1)}, f32[1,1024]{1,0:T(1,128)}, u32[]{:S(2)}) copy-start(f32[1,1024]{1,0:T(1,128)} %copy-done.52) | copy-start | bytes 12292
  469.2 14.7 %copy-start.55 = (f32[640]{0:T(1024)S(1)}, f32[640]{0:T(1024)}, u32[]{:S(2)}) copy-start(f32[640]{0:T(1024)} %copy-done.54) | copy-start | bytes 7684
  483.9 10.3 %copy-start.63 = (f32[640]{0:T(1024)S(1)}, f32[640]{0:T(1024)}, u32[]{:S(2)}) copy-start(f32[640]{0:T(1024)} %copy-done.62) | copy-start | bytes 7684
  498.8 25.0 %copy-start.13 = (f32[640,1024]{1,0:T(8,128)S(1)}, f32[640,1024]{1,0:T(8,128)}, u32[]{:S(2)}) copy-start(f32[640,1024]{1,0:T(8,128)} %get-tuple-element.140) | copy-start | bytes 7864324
  498.8 25.0 %copy-start.43 = (f32[1,1024]{1,0:T(1,128)S(1)}, f32[1,1024]{1,0:T(1,128)}, u32[]{:S(2)}) copy-start(f32[1,1024]{1,0:T(1,128)} %copy-done.42) | copy-start | bytes 12292
  498.8 25.0 %copy-start.51 = (f32[640]{0:T(1024)S(1)}, f32[640]{0:T(1024)}, u32[]{:S(2)}) copy-start(f32[640]{0:T(1024)} %copy-done.50) | copy-start | bytes 7684
  498.8 25.0 %copy-start.57 = (f32[1,1024]{1,0:T(1,128)S(1)}, f32[1,1024]{1,0:T(1,128)}, u32[]{:S(2)}) copy-start(f32[1,1024]{1,0:T(1,128)} %copy-done.56) | copy-start | bytes 12292
  498.8 25.0 %copy-start.59 = (f32[640]{0:T(1024)S(1)}, f32[640]{0:T(1024)}, u32[]{:S(2)}) copy-start(f32[640]{0:T(1024)} %copy-done.58) | copy-start | bytes 7684
  523.9 8.4 copy-start.61
  838.7 23.9 %copy-start.35 = (f32[19,1024]{1,0:T(8,128)S(1)}, f32[19,1024]{1,0:T(8,128)}, u32[]{:S(2)}) copy-start(f32[19,1024]{1,0:T(8,128)} %param.27) | copy-start | bytes 233476
  838.7 23.9 %copy-start.44 = (f32[19,1024]{1,0:T(8,128)S(1)}, f32[19,1024]{1,0:T(8,128)}, u32[]{:S(2)}) copy-start(f32[19,1024]{1,0:T(8,128)} %param.28) | copy-start | bytes 233476
  838.7 23.9 %copy-start.45 = (f32[19,1024]{1,0:T(8,128)S(1)}, f32[19,1024]{1,0:T(8,128)}, u32[]{:S(2)}) copy-start(f32[19,1024]{1,0:T(8,128)} %param.29) | copy-start | bytes 233476
  (39 other events, 100.1 us)
Sparse Core Ops, SparseCore 0:
  11.5 104.2 all-gather.2
  219.1 81.6 all-gather.4

commit v13 on v12

--- a/solution.py
+++ b/solution.py
@@ -736,11 +736,10 @@
         copy.wait()
 
 
-def gather_quarters(shard):
-    band_count = lax.axis_size("band")
-    rows = shard.shape[0] // band_count
+def own_quarter(shard):
+    rows = shard.shape[0] // lax.axis_size("band")
     own = lax.dynamic_slice_in_dim(shard, lax.axis_index("band") * rows, rows, 0)
-    return lax.all_gather(own.astype(jnp.bfloat16), ("clip", "band"), axis=0, tiled=True)
+    return own.astype(jnp.bfloat16)
 
 
 def sum_rows(left, right):
@@ -843,6 +842,10 @@
         last_put_scale,
         last_got,
         last_got_scale,
+        late_put,
+        late_put_scale,
+        late_got,
+        late_got_scale,
         push_send,
         push_recv,
         cross_put,
@@ -998,8 +1001,8 @@
         kind = phases[at]["kind"]
         units = pl.ds(*unit_parts(at, kind, phases[at]["first"])[part][:2])
         pairs = ((plane_put[kind], plane_got[at]),)
-        if at + 1 == len(phases):
-            pairs = ((last_put, last_got), (last_put_scale, last_got_scale))
+        if at in coded:
+            pairs = (coded[at][::2], coded[at][1::2])
         return [
             pltpu.make_async_remote_copy(
                 here.at[units],
@@ -1011,6 +1014,11 @@
             )
             for i, (here, there) in enumerate(pairs)
         ]
+
+    coded = {
+        len(phases) - 2: (late_put, late_put_scale, late_got, late_got_scale),
+        len(phases) - 1: (last_put, last_put_scale, last_got, last_got_scale),
+    }
 
     def split_unit(pair, of_plane):
         return 4 + 2 * pair + of_plane
@@ -1154,8 +1162,8 @@
                 if not first:
                     came = got_low[kind][before, position].astype(jnp.float32)
                     term = term + came * got_scale[kind][before, position]
-                if last and at + 1 == len(phases):
-                    last_put[unit], last_put_scale[unit] = encode(term)
+                if last and at in coded:
+                    coded[at][0][unit], coded[at][1][unit] = encode(term)
                 elif last:
                     plane_put[kind][unit] = term
                 else:
@@ -1227,9 +1235,10 @@
 
             @pl.loop(low, low + many)
             def _(unit):
-                if at + 1 == len(phases):
-                    total = last_put[unit].astype(jnp.float32) * last_put_scale[unit]
-                    total += last_got[unit].astype(jnp.float32) * last_got_scale[unit]
+                if at in coded:
+                    here, here_scale, there, there_scale = coded[at]
+                    total = here[unit].astype(jnp.float32) * here_scale[unit]
+                    total += there[unit].astype(jnp.float32) * there_scale[unit]
                 else:
                     total = plane_put[kind][unit] + plane_got[at][unit]
                 plane_got[at][unit] = total
@@ -1461,8 +1470,9 @@
         dma((len(phases), 8)),
         dma((len(phases), 8)),
     ]
-    for _ in range(2):
-        scratch += [pltpu.VMEM((6,) + UNIT, jnp.int16), pltpu.VMEM((6, 1, UNIT[1]), jnp.float32)]
+    for many in (6, 6, 8, 8):
+        scratch += [pltpu.VMEM((many,) + UNIT, jnp.int16)]
+        scratch += [pltpu.VMEM((many, 1, UNIT[1]), jnp.float32)]
     scratch += [
         dma((5,)),
         dma((5,)),
@@ -1603,7 +1613,6 @@
     )
     part_modul = matmul(time_rows, w_wide[:, : 12 * D].astype(jnp.bfloat16))
     kv_cols = 2 * D // band_count
-    up_b_w = gather_quarters(w_wide[:, 22 * D + FF :])
     gathered, all_modul, all_text, keyval = gather_weights(
         (w_wide, w_deep),
         (
@@ -1623,8 +1632,11 @@
     up_a_w, down_a_w, query_w, cross_out_w, out_a_w, out_b_w, qkv_a_w, qkv_b_w = gathered
     all_text = all_text.transpose(0, 2, 1, 3)
     keyval = keyval.transpose(1, 0, 2).reshape(TEXT_PAD, 2 * D)
-    late_down_b, all_modul = lax.optimization_barrier((w_deep[:, 3 * D :], all_modul))
-    down_b_w = gather_quarters(late_down_b)
+    late_up_b, late_down_b, all_modul = lax.optimization_barrier(
+        (own_quarter(w_wide[:, 22 * D + FF :]), own_quarter(w_deep[:, 3 * D :]), all_modul)
+    )
+    up_b_w = lax.all_gather(late_up_b, ("clip", "band"), axis=0, tiled=True)
+    down_b_w = lax.all_gather(late_down_b, ("clip", "band"), axis=0, tiled=True)
     small_low = w_small.astype(jnp.bfloat16)
     small_val = small_low.astype(jnp.float32)
     num_frames, num_rows, num_cols = (latents.shape[1], latents.shape[2], latents.shape[3])

time: 935 us -> 933 us (level)
  Pallas kernels: 589 us -> 552 us
  waiting for transfers between devices: 40.4 us -> 70.2 us
    pallas_call x1, Pallas kernels: 188 us -> 154 us  [gather_weights(): pl.pallas_call(partial(gather_kernel, count, picks, sides), out_shape=tup...]
    all_gather x2, waiting for transfers between devices: 0.01 us -> 26.6 us  [the longest x1 26.5 us: per_device(): down_b_w = lax.all_gather(late_down_b, ('clip', 'band'), axis=0, tiled=True)]
    unnamed x165 -> x163, local copies, waits for them, and re-layouts: 19.2 us -> 19.7 us
  transfers between devices with their start and end apart: 6 -> 6, of which waited for: 4 -> 5; matrix products, arithmetic and copies ran while one was open for 9% -> 8% of each run, Pallas kernels for 25% -> 3%
where the time goes in v13:
time: 933 us; the launch traced here: 927 us
  Pallas kernels  552 us (59%)
  matrix products  154 us (17%)
  other arithmetic  87.2 us (9%)
  waiting for transfers between devices  70.2 us (8%)
  local copies, waits for them, and re-layouts  32.5 us (3%)
  between operations  24.2 us (3%)
    pallas_call x1, Pallas kernels, reduce_gradients(): pl.pallas_call(partial(reduce_kernel, count, tokens, phases), out_shape=(...  296 us
    pallas_call x1, Pallas kernels, gather_weights(): pl.pallas_call(partial(gather_kernel, count, picks, sides), out_shape=tup...  154 us
    dot_general x11, matrix products, matmul_nt(): lax.dot_general(left_op, right_op, (((1,), (1,)), ((), ())), preferred_el...  75 us
    dot_general x13, matrix products, matmul(): return jnp.dot(left_op, right_op, preferred_element_type=jnp.float32)  71.9 us
    sub x3, other arithmetic, adam_update(): weight - learn_rate * (first_hat / (jnp.sqrt(second_hat) + ADAM_EPS) + DE...  60 us
    ppermute x4, waiting for transfers between devices, shifted(): lax.ppermute(value, axis, [(i, (i + by) % length) for i in range(length)])  43.1 us
    all_gather x1, waiting for transfers between devices, per_device(): down_b_w = lax.all_gather(late_down_b, ('clip', 'band'), axis=0, tiled=True)  26.5 us
    pallas_call x2, Pallas kernels, attend_back(): pl.pallas_call(partial(attend_back_kernel, windows, text_len, sets), grid...  26.1 us
  transfers between devices with their start and end apart: 6, of which 5 were waited for; matrix products, arithmetic and copies ran while one was open for 8% of the time, Pallas kernels for 3%

profile of v13, /device:TPU:0, one launch (start us, length us, event | category | flops | bytes accessed | tf_op | source)
XLA Modules:
  0.0 927.4 jit_solution(9975590822904478690)
XLA Ops:
  9.9 9.7 %shard_map.230 = s32[8,8,128]{2,1,0:T(8,128)} custom-call(s32[8,128]{1,0:T(8,128)} %pad.12.facts_ref), custom_call_target="tpu_custom_call" | custom-call | tf_op jit(solution)/shard_map/pallas_call | solution.py:474
  20.5 1.7 slice.121
  22.4 3.4 fusion.16
  26.6 2.7 slice.122
  29.3 1.7 dynamic-slice_convert_fusion
  31.8 153.8 %shard_map.231 = (bf16[1024,4096]{1,0:T(8,128)(2,1)}, bf16[4096,1024]{1,0:T(8,128)(2,1)}, bf16[1024,1024]{1,0:T(8,128)(2,1)}, bf16[1024,1024]{1,0:T(8,128)(2,1)}...) custom-call(f32[128,30720]{1,0:T(8,128)} %refs_0_.1, ...), custom_call_target="tpu_custom_call" | custom-call | flops 199999995904 | bytes 600000000 | tf_op jit(solution)/shard_map/pallas_call | solution.py:760
  187.0 2.0 add_reduce_fusion
  189.1 2.3 multiply_reduce_fusion.21
  193.7 7.4 convolution_convert_fusion.1.qkv_ref
  201.2 11.9 %shard_map.232 = (bf16[640,1024]{1,0:T(8,128)(2,1)S(1)}, bf16[640,2048]{1,0:T(8,128)(2,1)S(1)}) custom-call(bf16[640,3072]{1,0:T(8,128)(2,1)S(1)} %convolution_convert_fusion.1.qkv_ref), custom_call_target="tpu_custom_call" | custom-call | flops 1342177280 | bytes 10485760 | tf_op jit(solution)/shard_map/pallas_call | solution.py:316
  213.2 3.1 fusion.53
  218.5 8.2 multiply_convert_fusion.1
  226.7 11.1 %fusion.52 = (f32[640]{0:T(1024)S(1)}, f32[640,1024]{1,0:T(8,128)S(1)}, f32[640,1024]{1,0:T(8,128)}) fusion(f32[640,1024]{1,0:T(8,128)S(1)} %get-tuple-element.108, f32[1024]{0:T(1024)S(1)} %bitcast.208, bf16[640,4096]{1,0:T(8,128)(2,1)S(1)} %get-tuple-element.144.refs_6_, bf16[4096,1024]{1,0:T(8,128)(2,1)} %get-tuple-element.40), kind=kOutput, calls=%fused_computation.186 | convolution fusion | flops 5370674688 | bytes 21502464 | tf_op jit(solution)/shard_map/dot_general | solution.py:37
  239.5 2.1 collective-permute-start
  241.6 13.8 %collective-permute-done = bf16[10,32,1024]{2,1,0:T(8,128)(2,1)S(1)} collective-permute-done((bf16[10,32,1024]{2,1,0:T(8,128)(2,1)S(1)}, bf16[10,32,1024]{2,1,0:T(8,128)(2,1)S(1)}, u32[]{:S(2)}, u32[]{:S(2)}) %collective-permute-start) | collective-permute-done | bytes 655392 | tf_op jit(solution)/shard_map/ppermute | solution.py:33
  256.6 4.5 convolution_convert_fusion.refs_0_.refs_1_.refs_2_
  261.2 12.4 %shard_map.233 = bf16[640,1024]{1,0:T(8,128)(2,1)S(1)} custom-call(bf16[640,3072]{1,0:T(8,128)(2,1)S(1)} %convolution_convert_fusion.refs_0_.refs_1_.refs_2_, bf16[640,3072]{1,0:T(8,128)(2,1)S(1)} %convolution_convert_fusion.refs_0_.refs_1_.refs_2_, bf16[640,3072]{1,0:T(8,128)(2,1)S(1)} %convolution_convert_fusion.refs_0_.refs_1_.refs_2_), custom_call_target="tpu_custom_call" | custom-call | flops 1677721600 | bytes 10485760 | tf_op jit(solution)/shard_map/pallas_call | solution.py:368
  273.7 2.4 collective-permute-start.1
  279.1 7.2 collective-permute-done.1
  287.5 5.1 fusion.51
  293.5 2.2 copy-done.73
  297.2 6.7 shard_map.234.refs_2_
  303.9 1.6 fusion.61
  308.5 11.9 %multiply_convert_fusion = (bf16[640,4096]{1,0:T(8,128)(2,1)}, f32[640,4096]{1,0:T(8,128)}) fusion(bf16[640,1024]{1,0:T(8,128)(2,1)} %add_convert_fusion.refs_1_, bf16[1024,4096]{1,0:T(8,128)(2,1)} %all-gather.3.cloned.1.call-done), kind=kOutput, calls=%fused_computation.20 | convolution fusion | flops 5381816320 | bytes 25427968 | tf_op jit(solution)/shard_map/dot_general | solution.py:37
  320.5 26.5 %all-gather.5.cloned.1.call-done = bf16[4096,1024]{1,0:T(8,128)(2,1)} async-done(((bf16[128,1024]{1,0:T(8,128)(2,1)}), bf16[4096,1024]{1,0:T(8,128)(2,1)}) %all-gather.5.cloned.1.call-update) | async-done | bytes 8388624 | tf_op jit(solution)/shard_map/all_gather | solution.py:1639
  347.0 11.1 %fusion.50 = (f32[640]{0:T(1024)S(1)}, f32[640,1024]{1,0:T(8,128)S(1)}, f32[640,1024]{1,0:T(8,128)}) fusion(f32[640,1024]{1,0:T(8,128)} %copy-done.16, f32[1024]{0:T(1024)S(1)} %bitcast.216, bf16[640,4096]{1,0:T(8,128)(2,1)} %get-tuple-element.150.refs_0_, bf16[4096,1024]{1,0:T(8,128)(2,1)} %all-gather.5.cloned.1.call-done), kind=kOutput, calls=%fused_computation.184 | convolution fusion | flops 5370674688 | bytes 21502464 | tf_op jit(solution)/shard_map/dot_general | solution.py:37
  362.1 12.7 %fusion.6.refs_11_ = bf16[640,4096]{1,0:T(8,128)(2,1)S(1)} fusion(f32[640,4096]{1,0:T(8,128)} %get-tuple-element.151, bf16[640,1024]{1,0:T(8,128)(2,1)S(1)} %multiply_convert_fusion.5.refs_10_, bf16[4096,1024]{1,0:T(8,128)(2,1)} %all-gather.5.cloned.1.call-done), kind=kOutput, calls=%fused_computation.13 | convolution fusion | flops 5394923520 | bytes 25427968 | tf_op jit(solution)/shard_map/dot_general | solution.py:51
  374.8 10.6 %multiply_reduce_fusion.5 = (f32[1024]{0:T(1024)S(1)}, f32[640]{0:T(1024)S(1)}, f32[1024]{0:T(1024)S(1)}, f32[640,1024]{1,0:T(8,128)S(1)}) fusion(f32[640,1024]{1,0:T(8,128)S(1)} %copy-done.17, f32[640]{0:T(1024)S(1)} %fusion.35, f32[640]{0:T(1024)S(1)} %broadcast_multiply_fusion.3, f32[1024]{0:T(1024)S(1)} %bitcast.199, ...), kind=kOutput, calls=%fused_computation.47 | convolution fusion | flops 5373949440 | bytes 18894336 | tf_op jit(solution)/shard_map/dot_general | solution.py:51
  388.9 2.7 convolution_convert_fusion.4.refs_3_
  391.6 7.8 shard_map.235
  399.4 4.0 multiply_reduce_fusion.2
  410.6 8.1 collective-permute-done.2
  418.8 18.3 %shard_map.236.refs_15_ = bf16[640,3072]{1,0:T(8,128)(2,1)} custom-call(bf16[640,3072]{1,0:T(8,128)(2,1)} %copy-done, bf16[640,3072]{1,0:T(8,128)(2,1)} %copy-done, bf16[640,3072]{1,0:T(8,128)(2,1)} %copy-done, bf16[640,1024]{1,0:T(8,128)(2,1)S(1)} %bitcast.151), custom_call_target="tpu_custom_call" | custom-call | flops 4194304000 | bytes 10485760 | tf_op jit(solution)/shard_map/pallas_call | solution.py:389
  437.1 7.6 fusion.62
  448.3 14.0 %collective-permute-done.3 = f32[10,32,1024]{2,1,0:T(8,128)S(1)} collective-permute-done((f32[10,32,1024]{2,1,0:T(8,128)S(1)}, f32[10,32,1024]{2,1,0:T(8,128)S(1)}, u32[]{:S(2)}, u32[]{:S(2)}) %collective-permute-start.3) | collective-permute-done | bytes 1310752 | tf_op jit(solution)/shard_map/ppermute | solution.py:33
  462.4 1.6 copy-done.9
  467.4 14.6 %fusion.12.refs_17_ = bf16[640,4096]{1,0:T(8,128)(2,1)} fusion(f32[640,4096]{1,0:T(8,128)} %get-tuple-element.145, bf16[640,1024]{1,0:T(8,128)(2,1)S(1)} %multiply_convert_fusion.3.refs_16_, bf16[4096,1024]{1,0:T(8,128)(2,1)} %get-tuple-element.40), kind=kOutput, calls=%fused_computation.19 | convolution fusion | flops 5394923520 | bytes 25427968 | tf_op jit(solution)/shard_map/dot_general | solution.py:51
  482.1 10.3 %multiply_reduce_fusion.8 = (f32[1024]{0:T(1024)S(1)}, f32[640]{0:T(1024)S(1)}, f32[1024]{0:T(1024)S(1)}, f32[640,1024]{1,0:T(8,128)S(1)}) fusion(f32[640,1024]{1,0:T(8,128)S(1)} %copy-done.15, f32[640]{0:T(1024)S(1)} %copy-done.55, f32[640]{0:T(1024)S(1)} %copy-done.49, f32[1024]{0:T(1024)S(1)} %bitcast.196, bf16[640,4096]{1,0:T(8,128)(2,1)} %fusion.12.refs_17_, ...), kind=kOutput, calls=%fused_computation.50 | convolution fusion | flops 5373949440 | bytes 18894336 | tf_op jit(solution)/shard_map/dot_general | solution.py:51
  493.8 1.6 copy-done.70
  495.3 1.6 convolution_convert_fusion.2.grad_ref
  497.1 25.0 %shard_map.237.refs_19_ = bf16[640,3072]{1,0:T(8,128)(2,1)} custom-call(bf16[640,3072]{1,0:T(8,128)(2,1)} %copy-done.1, bf16[640,2048]{1,0:T(8,128)(2,1)S(1)} %copy-done.3, bf16[640,1024]{1,0:T(8,128)(2,1)S(1)} %convolution_convert_fusion.2.grad_ref), custom_call_target="tpu_custom_call" | custom-call | flops 3355443200 | bytes 10485760 | tf_op jit(solution)/shard_map/pallas_call | solution.py:335
  522.1 8.4 multiply_reduce_fusion.10
  535.3 296.3 %shard_map.238 = (f32[128,18432]{1,0:T(8,128)}, f32[512,4096]{1,0:T(8,128)}, f32[8,512]{1,0:T(8,128)}, f32[8,256,128]{2,1,0:T(8,128)}, f32[8,512]{1,0:T(8,128)},...) custom-call(bf16[640,4096]{1,0:T(8,128)(2,1)} %get-tuple-element.150, ...), custom_call_target="tpu_custom_call" | custom-call | flops 299999985664 | bytes 800000000 | tf_op jit(solution)/shard_map/pallas_call | solution.py:1505
  831.6 1.8 copy.46
  834.3 5.6 multiply_reduce_fusion
  845.0 10.4 %shard_map.239 = f32[8,128]{1,0:T(8,128)} custom-call(f32[8,128]{1,0:T(8,128)} %broadcast_in_dim.87.part_ref), custom_call_target="tpu_custom_call" | custom-call | tf_op jit(solution)/shard_map/pallas_call | solution.py:1557
  858.8 22.7 %multiply_subtract_fusion.1 = (f32[512,4096]{1,0:T(8,128)}, f32[512,4096]{1,0:T(8,128)}, f32[512,4096]{1,0:T(8,128)}) fusion(f32[512,4096]{1,0:T(8,128)} %refs_1_.1, f32[512,4096]{1,0:T(8,128)} %get-tuple-element.56, f32[]{:T(128)S(6)} %div.227, f32[512,4096]{1,0:T(8,128)} %param.25, f32[512,4096]{1,0:T(8,128)} %param.26), kind=kLoop, calls=%fused_computation.25 | loop fusion | flops 33554432 | bytes 58720260 | tf_op jit(solution)/shard_map/sub | solution.py:427
  881.5 36.5 %multiply_subtract_fusion = (f32[128,30720]{1,0:T(8,128)}, f32[128,30720]{1,0:T(8,128)}, f32[128,30720]{1,0:T(8,128)}) fusion(f32[128,30720]{1,0:T(8,128)} %refs_0_.1, f32[]{:T(128)S(6)} %div.227, f32[128,18432]{1,0:T(8,128)} %get-tuple-element.55, f32[128,12288]{1,0:T(8,128)} %get-tuple-element.161, f32[128,30720]{1,0:T(8,128)} %param.22, f32[128,30720]{1,0:T(8,128)} %param.23), kind=kLoop, calls=%fused_computation.3 | loop fusion | flops 66846720 | bytes 110100480 | tf_op jit(solution)/shard_map/sub | solution.py:427
  (283 shorter events, 54.5 us)
Async XLA Ops:
  7.2 301.4 %all-gather.3.cloned.1.call-start = ((), (), s32[]{:S(2)}) async-start(), calls=%async_computation | async-start | bytes 8650752 | tf_op jit(solution)/shard_map/all_gather | solution.py:1638
  31.7 154.8 %copy-start.34 = (f32[19,1024]{1,0:T(8,128)S(1)}, f32[19,1024]{1,0:T(8,128)}, u32[]{:S(2)}) copy-start(f32[19,1024]{1,0:T(8,128)} %param.27) | copy-start | bytes 233476
  31.8 154.8 %copy-start.36 = (f32[1,5,8,16,8]{3,4,2,1,0:T(8,128)S(1)}, f32[1,5,8,16,8]{3,4,2,1,0:T(8,128)}, u32[]{:S(2)}) copy-start(f32[1,5,8,16,8]{3,4,2,1,0:T(8,128)} %param.15) | copy-start | bytes 61444
  31.8 154.8 %copy-start.37 = (f32[1,5,8,16,8]{3,4,2,1,0:T(8,128)S(1)}, f32[1,5,8,16,8]{3,4,2,1,0:T(8,128)}, u32[]{:S(2)}) copy-start(f32[1,5,8,16,8]{3,4,2,1,0:T(8,128)} %param.16) | copy-start | bytes 61444
  185.6 161.4 %all-gather.5.cloned.1.call-start = ((), (), s32[]{:S(2)}) async-start(), calls=%async_computation.1 | async-start | bytes 8650752 | tf_op jit(solution)/shard_map/all_gather | solution.py:1639
  186.6 26.6 %copy-start.42 = (f32[1,1024]{1,0:T(1,128)}, f32[1,1024]{1,0:T(1,128)S(1)}, u32[]{:S(2)}) copy-start(f32[1,1024]{1,0:T(1,128)S(1)} %get-tuple-element.124) | copy-start | bytes 12292
  192.1 9.1 copy-start.58
  192.1 9.0 copy-start.56
  192.1 21.0 %copy-start.64 = (f32[1,1024]{1,0:T(1,128)}, f32[1,1024]{1,0:T(1,128)S(1)}, u32[]{:S(2)}) copy-start(f32[1,1024]{1,0:T(1,128)S(1)} %get-tuple-element.138) | copy-start | bytes 12292
  192.1 24.7 %copy-start.52 = (f32[1,1024]{1,0:T(1,128)}, f32[1,1024]{1,0:T(1,128)S(1)}, u32[]{:S(2)}) copy-start(f32[1,1024]{1,0:T(1,128)S(1)} %get-tuple-element.135) | copy-start | bytes 12292
  201.1 15.2 %copy-start.1 = (bf16[640,3072]{1,0:T(8,128)(2,1)}, bf16[640,3072]{1,0:T(8,128)(2,1)S(1)}, u32[]{:S(2)}) copy-start(bf16[640,3072]{1,0:T(8,128)(2,1)S(1)} %convolution_convert_fusion.1.qkv_ref) | copy-start | bytes 11796484
  201.2 12.0 %copy-start.69 = (bf16[1024,1024]{1,0:T(8,128)(2,1)S(1)}, bf16[1024,1024]{1,0:T(8,128)(2,1)}, u32[]{:S(2)}) copy-start(bf16[1024,1024]{1,0:T(8,128)(2,1)} %get-tuple-element.38) | copy-start | bytes 6291460
  201.2 16.3 %slice-start = ((s8[8388608]{0:T(1024)(128)(4,1)}), s8[4194304]{0:T(1024)(128)(4,1)S(1)}, s32[]{:S(2)}) async-start(s8[8388608]{0:T(1024)(128)(4,1)} %bitcast.230), calls=%async_computation.2 | async-start | bytes 8388608
  216.4 10.3 %copy-start.14 = (f32[640,1024]{1,0:T(8,128)}, f32[640,1024]{1,0:T(8,128)S(1)}, u32[]{:S(2)}) copy-start(f32[640,1024]{1,0:T(8,128)S(1)} %get-tuple-element.108) | copy-start | bytes 7864324
  216.8 9.8 %copy-start.62 = (f32[640]{0:T(1024)}, f32[640]{0:T(1024)S(1)}, u32[]{:S(2)}) copy-start(f32[640]{0:T(1024)S(1)} %multiply_reduce_fusion.20) | copy-start | bytes 7684
  216.8 9.8 %copy-start.54 = (f32[640]{0:T(1024)}, f32[640]{0:T(1024)S(1)}, u32[]{:S(2)}) copy-start(f32[640]{0:T(1024)S(1)} %fusion.32) | copy-start | bytes 7684
  217.4 9.2 copy-start.30
  226.7 11.1 %copy-start.74 = (bf16[640,4096]{1,0:T(8,128)(2,1)}, bf16[640,4096]{1,0:T(8,128)(2,1)S(1)}, u32[]{:S(2)}) copy-start(bf16[640,4096]{1,0:T(8,128)(2,1)S(1)} %get-tuple-element.144.refs_6_) | copy-start | bytes 15728644
  237.8 18.9 %slice-start.2 = ((s8[6291456]{0:T(1024)(128)(4,1)}), s8[4194304]{0:T(1024)(128)(4,1)S(1)}, s32[]{:S(2)}) async-start(s8[6291456]{0:T(1024)(128)(4,1)} %bitcast.232), calls=%async_computation.4 | async-start | bytes 8388608
  238.2 18.4 %slice-start.3 = ((s8[6291456]{0:T(1024)(128)(4,1)}), s8[2097152]{0:T(1024)(128)(4,1)S(1)}, s32[]{:S(2)}) async-start(s8[6291456]{0:T(1024)(128)(4,1)} %bitcast.232), calls=%async_computation.5 | async-start | bytes 4194304
  239.5 15.9 %collective-permute-start = (bf16[10,32,1024]{2,1,0:T(8,128)(2,1)S(1)}, bf16[10,32,1024]{2,1,0:T(8,128)(2,1)S(1)}, u32[]{:S(2)}, u32[]{:S(2)}) collective-permute-start(bf16[10,32,1024]{2,1,0:T(8,128)(2,1)S(1)} %get-tuple-element.118), channel_id=1, source_target_pairs={{0,3},{1,0},{2,1},{3,2},{4,7},{5,4},{6,5},{7,6},{8,11},{9,8},{10,9... | collective-permute-start | bytes 1966088 | tf_op jit(solution)/shard_map/ppermute | solution.py:33
  261.1 12.4 %copy-start = (bf16[640,3072]{1,0:T(8,128)(2,1)}, bf16[640,3072]{1,0:T(8,128)(2,1)S(1)}, u32[]{:S(2)}) copy-start(bf16[640,3072]{1,0:T(8,128)(2,1)S(1)} %convolution_convert_fusion.refs_0_.refs_1_.refs_2_) | copy-start | bytes 11796484
  273.7 12.6 %collective-permute-start.1 = (bf16[10,32,1024]{2,1,0:T(8,128)(2,1)S(1)}, bf16[10,32,1024]{2,1,0:T(8,128)(2,1)}, u32[]{:S(2)}, u32[]{:S(2)}) collective-permute-start(bf16[10,32,1024]{2,1,0:T(8,128)(2,1)S(1)} %get-tuple-element.116), channel_id=1, source_target_pairs={{0,1},{1,2},{2,3},{3,0},{4,5},{5,6},{6,7},{7,4},{8,9},{9,10},{10,1... | collective-permute-start | bytes 1966088 | tf_op jit(solution)/shard_map/ppermute | solution.py:33
  279.1 8.4 copy-start.8
  292.6 11.2 %copy-start.10 = (f32[640,1024]{1,0:T(8,128)}, f32[640,1024]{1,0:T(8,128)S(1)}, u32[]{:S(2)}) copy-start(f32[640,1024]{1,0:T(8,128)S(1)} %get-tuple-element.104) | copy-start | bytes 7864324
  297.2 6.7 copy-start.71
  362.1 12.7 %copy-start.31 = (bf16[640,1024]{1,0:T(8,128)(2,1)}, bf16[640,1024]{1,0:T(8,128)(2,1)S(1)}, u32[]{:S(2)}) copy-start(bf16[640,1024]{1,0:T(8,128)(2,1)S(1)} %multiply_convert_fusion.5.refs_10_) | copy-start | bytes 3932164
  362.1 12.7 %copy-start.17 = (f32[640,1024]{1,0:T(8,128)S(1)}, f32[640,1024]{1,0:T(8,128)}, u32[]{:S(2)}) copy-start(f32[640,1024]{1,0:T(8,128)} %copy-done.16) | copy-start | bytes 7864324
  374.8 10.7 %copy-start.75 = (bf16[640,4096]{1,0:T(8,128)(2,1)}, bf16[640,4096]{1,0:T(8,128)(2,1)S(1)}, u32[]{:S(2)}) copy-start(bf16[640,4096]{1,0:T(8,128)(2,1)S(1)} %fusion.6.refs_11_) | copy-start | bytes 15728644
  391.5 7.8 copy-start.11
  409.2 9.5 %collective-permute-start.2 = (bf16[10,32,1024]{2,1,0:T(8,128)(2,1)S(1)}, bf16[10,32,1024]{2,1,0:T(8,128)(2,1)S(1)}, u32[]{:S(2)}, u32[]{:S(2)}) collective-permute-start(bf16[10,32,1024]{2,1,0:T(8,128)(2,1)S(1)} %get-tuple-element.114), channel_id=1, source_target_pairs={{0,3},{1,0},{2,1},{3,2},{4,7},{5,4},{6,5},{7,6},{8,11},{9,8},{10,9... | collective-permute-start | bytes 1966088 | tf_op jit(solution)/shard_map/ppermute | solution.py:33
  445.0 17.2 %collective-permute-start.3 = (f32[10,32,1024]{2,1,0:T(8,128)S(1)}, f32[10,32,1024]{2,1,0:T(8,128)S(1)}, u32[]{:S(2)}, u32[]{:S(2)}) collective-permute-start(f32[10,32,1024]{2,1,0:T(8,128)S(1)} %get-tuple-element.113), channel_id=1, source_target_pairs={{0,1},{1,2},{2,3},{3,0},{4,5},{5,6},{6,7},{7,4},{8,9},{9,10},{10,1... | collective-permute-start | bytes 3932168 | tf_op jit(solution)/shard_map/ppermute | solution.py:33
  467.4 14.7 %copy-start.29 = (bf16[640,1024]{1,0:T(8,128)(2,1)}, bf16[640,1024]{1,0:T(8,128)(2,1)S(1)}, u32[]{:S(2)}) copy-start(bf16[640,1024]{1,0:T(8,128)(2,1)S(1)} %multiply_convert_fusion.3.refs_16_) | copy-start | bytes 3932164
  467.4 14.7 %copy-start.15 = (f32[640,1024]{1,0:T(8,128)S(1)}, f32[640,1024]{1,0:T(8,128)}, u32[]{:S(2)}) copy-start(f32[640,1024]{1,0:T(8,128)} %copy-done.14) | copy-start | bytes 7864324
  467.4 14.7 %copy-start.49 = (f32[640]{0:T(1024)S(1)}, f32[640]{0:T(1024)}, u32[]{:S(2)}) copy-start(f32[640]{0:T(1024)} %copy-done.48) | copy-start | bytes 7684
  467.4 14.7 %copy-start.53 = (f32[1,1024]{1,0:T(1,128)S(1)}, f32[1,1024]{1,0:T(1,128)}, u32[]{:S(2)}) copy-start(f32[1,1024]{1,0:T(1,128)} %copy-done.52) | copy-start | bytes 12292
  467.4 14.7 %copy-start.55 = (f32[640]{0:T(1024)S(1)}, f32[640]{0:T(1024)}, u32[]{:S(2)}) copy-start(f32[640]{0:T(1024)} %copy-done.54) | copy-start | bytes 7684
  482.1 10.3 %copy-start.63 = (f32[640]{0:T(1024)S(1)}, f32[640]{0:T(1024)}, u32[]{:S(2)}) copy-start(f32[640]{0:T(1024)} %copy-done.62) | copy-start | bytes 7684
  497.1 25.0 %copy-start.13 = (f32[640,1024]{1,0:T(8,128)S(1)}, f32[640,1024]{1,0:T(8,128)}, u32[]{:S(2)}) copy-start(f32[640,1024]{1,0:T(8,128)} %get-tuple-element.142) | copy-start | bytes 7864324
  497.1 25.0 %copy-start.43 = (f32[1,1024]{1,0:T(1,128)S(1)}, f32[1,1024]{1,0:T(1,128)}, u32[]{:S(2)}) copy-start(f32[1,1024]{1,0:T(1,128)} %copy-done.42) | copy-start | bytes 12292
  497.1 25.0 %copy-start.51 = (f32[640]{0:T(1024)S(1)}, f32[640]{0:T(1024)}, u32[]{:S(2)}) copy-start(f32[640]{0:T(1024)} %copy-done.50) | copy-start | bytes 7684
  497.1 25.0 %copy-start.57 = (f32[1,1024]{1,0:T(1,128)S(1)}, f32[1,1024]{1,0:T(1,128)}, u32[]{:S(2)}) copy-start(f32[1,1024]{1,0:T(1,128)} %copy-done.56) | copy-start | bytes 12292
  497.1 25.0 %copy-start.59 = (f32[640]{0:T(1024)S(1)}, f32[640]{0:T(1024)}, u32[]{:S(2)}) copy-start(f32[640]{0:T(1024)} %copy-done.58) | copy-start | bytes 7684
  522.1 8.4 copy-start.61
  834.3 6.3 copy-start.66
  834.3 23.8 %copy-start.35 = (f32[19,1024]{1,0:T(8,128)S(1)}, f32[19,1024]{1,0:T(8,128)}, u32[]{:S(2)}) copy-start(f32[19,1024]{1,0:T(8,128)} %param.27) | copy-start | bytes 233476
  834.3 23.8 %copy-start.44 = (f32[19,1024]{1,0:T(8,128)S(1)}, f32[19,1024]{1,0:T(8,128)}, u32[]{:S(2)}) copy-start(f32[19,1024]{1,0:T(8,128)} %param.28) | copy-start | bytes 233476
  834.3 23.8 %copy-start.45 = (f32[19,1024]{1,0:T(8,128)S(1)}, f32[19,1024]{1,0:T(8,128)}, u32[]{:S(2)}) copy-start(f32[19,1024]{1,0:T(8,128)} %param.29) | copy-start | bytes 233476
  (38 other events, 91.6 us)
Sparse Core Ops, SparseCore 0:
  185.7 80.2 all-gather.2
  268.9 78.0 all-gather.4

commit v14 on v13

--- a/solution.py
+++ b/solution.py
@@ -308,6 +308,121 @@
     def _(pair):
         for copy in copies(pair):
             copy.wait_send()
+
+
+def next_bands():
+    clip, band, count = lax.axis_index("clip"), lax.axis_index("band"), lax.axis_size("band")
+    return (clip, (band + 1) % count), (clip, (band + count - 1) % count)
+
+
+def half_window(qkv_ref, half, pair):
+    tokens = qkv_ref.shape[0] // 2
+    rows = pl.ds(half * tokens, tokens)
+    queries, keys, values = (qkv_ref[rows, pair_cols(i, pair)] for i in range(3))
+    return queries * HEAD_DIM ** (-0.5), keys, values
+
+
+def attend_halves_kernel(part, qkv_ref, out_ref, put_buf, send, recv):
+    following, preceding = next_bands()
+    greet([following, preceding])
+    runs, run = out_ref.shape[:2]
+
+    def copy(pair):
+        cols = pair_cols(0, pair)
+        return pltpu.make_async_remote_copy(
+            put_buf.at[:, :, cols],
+            out_ref.at[:, pl.ds(0, part), cols],
+            send.at[pair],
+            recv.at[pair],
+            following,
+            MESH,
+        )
+
+    @pl.loop(0, HEADS // 2)
+    def _(pair):
+        for half in range(2):
+            values = attention_values(*half_window(qkv_ref, half, pair), 0).astype(jnp.bfloat16)
+            values = values.reshape(runs // 2, run, 2 * HEAD_DIM)
+            low = half * (runs // 2)
+            put_buf[low : low + runs // 2, :, pair_cols(0, pair)] = values[:, :part]
+            out_ref[low : low + runs // 2, part:, pair_cols(0, pair)] = values[:, part:]
+        copy(pair).start()
+
+    @pl.loop(0, HEADS // 2)
+    def _(pair):
+        copy(pair).wait()
+
+
+def attend_halves_back_kernel(part, qkv_ref, grad_ref, out_ref, got_buf, send, recv):
+    following, preceding = next_bands()
+    greet([following, preceding])
+    runs, run = grad_ref.shape[:2]
+
+    def copy(pair):
+        cols = pair_cols(0, pair)
+        return pltpu.make_async_remote_copy(
+            grad_ref.at[:, pl.ds(0, part), cols],
+            got_buf.at[:, :, cols],
+            send.at[pair],
+            recv.at[pair],
+            preceding,
+            MESH,
+        )
+
+    @pl.loop(0, HEADS // 2)
+    def _(pair):
+        copy(pair).start()
+
+    @pl.loop(0, HEADS // 2)
+    def _(pair):
+        copy(pair).wait_recv()
+        for half in range(2):
+            low = half * (runs // 2)
+            pieces = (
+                got_buf[low : low + runs // 2, :, pair_cols(0, pair)],
+                grad_ref[low : low + runs // 2, part:, pair_cols(0, pair)],
+            )
+            grad_out = jnp.concatenate(pieces, 1).reshape(-1, 2 * HEAD_DIM)
+            parts = attention_gradients(*half_window(qkv_ref, half, pair), grad_out, 0)
+            rows = pl.ds(low * run, grad_out.shape[0])
+            for i, value in enumerate(parts):
+                out_ref[rows, pair_cols(i, pair)] = value.astype(jnp.bfloat16)
+
+    @pl.loop(0, HEADS // 2)
+    def _(pair):
+        copy(pair).wait_send()
+
+
+def attend_halves(qkv, run, part):
+    tokens = qkv.shape[0]
+    dma = pltpu.SemaphoreType.DMA((HEADS // 2,))
+    return pl.pallas_call(
+        partial(attend_halves_kernel, part),
+        out_shape=jax.ShapeDtypeStruct((tokens // run, run, D), jnp.bfloat16),
+        in_specs=[IN_VMEM],
+        out_specs=IN_VMEM,
+        scratch_shapes=[pltpu.VMEM((tokens // run, part, D), jnp.bfloat16), dma, dma],
+        compiler_params=pltpu.CompilerParams(
+            collective_id=6, has_side_effects=True, vmem_limit_bytes=40 << 20
+        ),
+        cost_estimate=attention_cost(tokens, 320, 2),
+    )(qkv).reshape(tokens, D)
+
+
+def attend_halves_back(qkv, grad_out, run, part):
+    tokens = qkv.shape[0]
+    dma = pltpu.SemaphoreType.DMA((HEADS // 2,))
+    return pl.pallas_call(
+        partial(attend_halves_back_kernel, part),
+        out_shape=jax.ShapeDtypeStruct(qkv.shape, jnp.bfloat16),
+        in_specs=[IN_VMEM] * 2,
+        out_specs=IN_VMEM,
+        scratch_shapes=[pltpu.VMEM((tokens // run, part, D), jnp.bfloat16), dma, dma],
+        compiler_params=pltpu.CompilerParams(
+            collective_id=7, has_side_effects=True, vmem_limit_bytes=50 << 20
+        ),
+        cost_estimate=attention_cost(tokens, 320, 5),
+    )(qkv, grad_out.reshape(tokens // run, run, D))
 
 
 def attend_frames(qkv, windows):
@@ -1651,7 +1766,6 @@
     run = num_rows * WIN
     part = SHIFT * WIN
     frame_windows = attend_pieces(tok_count, num_frames, "frame")
-    half_windows = attend_pieces(tok_count, num_frames, "half")
     text_windows = attend_pieces(tok_count, num_frames, "text")
     noisy_low = (signal * clean_tok + spread * noise_tok).astype(jnp.bfloat16)
     target = signal * noise_tok - spread * clean_tok
@@ -1669,9 +1783,7 @@
     low_b = normed_b.astype(jnp.bfloat16)
     rolled = with_rows(low_b, shifted(first_rows(low_b, run, part), "band", -1), run)
     qkv_b = matmul(rolled, qkv_b_w).astype(jnp.bfloat16)
-    win_kv = [(qkv_b, HEADS // 2, HEADS)]
-    win_out = attend(qkv_b, win_kv, half_windows)
-    att_b = with_rows(win_out, shifted(first_rows(win_out, run, part), "band", 1), run)
+    att_b = attend_halves(qkv_b, run, part)
     proj_b = matmul(att_b, out_b_w)
     stream_three = stream_two + mod_b[2] * proj_b
     cross_val, cross_back = jax.vjp(norm_gained, stream_three, small_val[2 * CH + 1])
@@ -1706,8 +1818,7 @@
     grad_gate_b = jnp.sum(grad_stream * proj_b, 0)
     factors_ob = (att_b, grad_proj)
     grad_att = matmul_nt(grad_proj, out_b_w).astype(jnp.bfloat16)
-    grad_win = with_rows(grad_att, shifted(first_rows(grad_att, run, part), "band", -1), run)
-    grad_qkv = attend_back(qkv_b, win_kv, grad_win, half_windows)[0]
+    grad_qkv = attend_halves_back(qkv_b, grad_att, run, part)
     factors_qkvb = (rolled, grad_qkv)
     grad_in_roll = matmul_nt(grad_qkv, qkv_b_w)
     sent_back = shifted(first_rows(grad_in_roll, run, part), "band", 1)

time: 933 us -> 927 us (level)
    pallas_call x0 -> x2, Pallas kernels: none -> 37.2 us  [the longest x1 21.7 us: attend_halves_back(): pl.pallas_call(partial(attend_halves_back_kernel, part), out_shape=jax.Sh...]
    pallas_call x2 -> x1, Pallas kernels: 26.1 us -> 7.6 us  [attend_back(): pl.pallas_call(partial(attend_back_kernel, windows, text_len, sets), grid...]
    ppermute x4 -> x2, waiting for transfers between devices: 43.1 us -> 29 us  [shifted(): lax.ppermute(value, axis, [(i, (i + by) % length) for i in range(length)])]
    pallas_call x2 -> x1, Pallas kernels: 19 us -> 6.27 us  [attend(): pl.pallas_call(partial(attend_kernel, windows, text_len, len(key_values))...]
    all_gather x1, waiting for transfers between devices: 26.5 us -> 38.2 us  [per_device(): down_b_w = lax.all_gather(late_down_b, ('clip', 'band'), axis=0, tiled=True)]
    unnamed x163 -> x169, local copies, waits for them, and re-layouts: 19.7 us -> 21.2 us
  transfers between devices with their start and end apart: 6 -> 4, of which waited for: 5 -> 3; matrix products, arithmetic and copies ran while one was open for 8% -> 7% of each run, Pallas kernels for 3% -> 4%
where the time goes in v14:
time: 927 us; the launch traced here: 922 us
  Pallas kernels  558 us (60%)
  matrix products  148 us (16%)
  other arithmetic  85.3 us (9%)
  waiting for transfers between devices  67.7 us (7%)
  local copies, waits for them, and re-layouts  33.6 us (4%)
  between operations  24.5 us (3%)
    pallas_call x1, Pallas kernels, reduce_gradients(): pl.pallas_call(partial(reduce_kernel, count, tokens, phases), out_shape=(...  296 us
    pallas_call x1, Pallas kernels, gather_weights(): pl.pallas_call(partial(gather_kernel, count, picks, sides), out_shape=tup...  154 us
    dot_general x11, matrix products, matmul_nt(): lax.dot_general(left_op, right_op, (((1,), (1,)), ((), ())), preferred_el...  73.5 us
    dot_general x13, matrix products, matmul(): return jnp.dot(left_op, right_op, preferred_element_type=jnp.float32)  67.4 us
    sub x3, other arithmetic, adam_update(): weight - learn_rate * (first_hat / (jnp.sqrt(second_hat) + ADAM_EPS) + DE...  60 us
    all_gather x1, waiting for transfers between devices, per_device(): down_b_w = lax.all_gather(late_down_b, ('clip', 'band'), axis=0, tiled=True)  38.2 us
    ppermute x2, waiting for transfers between devices, shifted(): lax.ppermute(value, axis, [(i, (i + by) % length) for i in range(length)])  29 us
    pallas_call x1, Pallas kernels, attend_frames_back(): pl.pallas_call(partial(attend_frames_back_kernel, windows), out_shape=jax...  25 us
  transfers between devices with their start and end apart: 4, of which 3 were waited for; matrix products, arithmetic and copies ran while one was open for 7% of the time, Pallas kernels for 4%

profile of v14, /device:TPU:0, one launch (start us, length us, event | category | flops | bytes accessed | tf_op | source)
XLA Modules:
  0.0 921.9 jit_solution(8488480570034614784)
XLA Ops:
  9.9 9.7 %shard_map.230 = s32[8,8,128]{2,1,0:T(8,128)} custom-call(s32[8,128]{1,0:T(8,128)} %pad.12.facts_ref), custom_call_target="tpu_custom_call" | custom-call | tf_op jit(solution)/shard_map/pallas_call | solution.py:589
  20.5 1.7 slice.109
  22.4 3.4 fusion.16
  26.6 2.7 slice.110
  29.3 1.7 dynamic-slice_convert_fusion
  31.8 153.8 %shard_map.231 = (bf16[1024,4096]{1,0:T(8,128)(2,1)}, bf16[4096,1024]{1,0:T(8,128)(2,1)}, bf16[1024,1024]{1,0:T(8,128)(2,1)}, bf16[1024,1024]{1,0:T(8,128)(2,1)}...) custom-call(f32[128,30720]{1,0:T(8,128)} %refs_0_.1, ...), custom_call_target="tpu_custom_call" | custom-call | flops 199999995904 | bytes 600000000 | tf_op jit(solution)/shard_map/pallas_call | solution.py:875
  189.9 2.0 copy-done.76
  191.9 4.5 convolution_convert_fusion.1.qkv_ref
  196.5 12.0 %shard_map.232 = (bf16[640,1024]{1,0:T(8,128)(2,1)S(1)}, bf16[640,2048]{1,0:T(8,128)(2,1)S(1)}) custom-call(bf16[640,3072]{1,0:T(8,128)(2,1)S(1)} %convolution_convert_fusion.1.qkv_ref), custom_call_target="tpu_custom_call" | custom-call | flops 1342177280 | bytes 10485760 | tf_op jit(solution)/shard_map/pallas_call | solution.py:431
  208.5 3.2 fusion.53
  213.8 8.2 multiply_convert_fusion.1
  222.0 11.1 %fusion.52 = (f32[640]{0:T(1024)S(1)}, f32[640,1024]{1,0:T(8,128)S(1)}, f32[640,1024]{1,0:T(8,128)}) fusion(f32[640,1024]{1,0:T(8,128)S(1)} %get-tuple-element.108, f32[1024]{0:T(1024)S(1)} %bitcast.204, bf16[640,4096]{1,0:T(8,128)(2,1)S(1)} %get-tuple-element.140.refs_6_, bf16[4096,1024]{1,0:T(8,128)(2,1)} %get-tuple-element.40), kind=kOutput, calls=%fused_computation.184 | convolution fusion | flops 5370674688 | bytes 21502464 | tf_op jit(solution)/shard_map/dot_general | solution.py:37
  234.8 2.3 collective-permute-start
  237.3 1.5 slice_reduce_fusion.2
  240.1 15.0 %collective-permute-done = bf16[10,32,1024]{2,1,0:T(8,128)(2,1)} collective-permute-done((bf16[10,32,1024]{2,1,0:T(8,128)(2,1)S(1)}, bf16[10,32,1024]{2,1,0:T(8,128)(2,1)}, u32[]{:S(2)}, u32[]{:S(2)}) %collective-permute-start) | collective-permute-done | bytes 655392 | tf_op jit(solution)/shard_map/ppermute | solution.py:33
  257.4 7.2 convolution_convert_fusion.qkv_ref
  264.6 15.6 %shard_map.233 = bf16[10,64,1024]{2,1,0:T(8,128)(2,1)S(1)} custom-call(bf16[640,3072]{1,0:T(8,128)(2,1)S(1)} %convolution_convert_fusion.qkv_ref), custom_call_target="tpu_custom_call" | custom-call | flops 1677721600 | bytes 10485760 | tf_op jit(solution)/shard_map/pallas_call | solution.py:399
  280.2 3.0 fusion.51
  284.1 2.2 copy-done.75
  286.3 1.5 convolution_convert_fusion.5.refs_0_
  287.8 6.3 shard_map.234.refs_2_
  294.1 1.6 fusion.59
  297.3 1.6 add_convert_fusion.refs_1_
  298.9 11.9 %multiply_convert_fusion = (bf16[640,4096]{1,0:T(8,128)(2,1)}, f32[640,4096]{1,0:T(8,128)}) fusion(bf16[640,1024]{1,0:T(8,128)(2,1)} %add_convert_fusion.refs_1_, bf16[1024,4096]{1,0:T(8,128)(2,1)} %all-gather.3.cloned.1.call-done), kind=kOutput, calls=%fused_computation.20 | convolution fusion | flops 5381816320 | bytes 25427968 | tf_op jit(solution)/shard_map/dot_general | solution.py:37
  310.8 38.2 %all-gather.5.cloned.1.call-done = bf16[4096,1024]{1,0:T(8,128)(2,1)} async-done(((bf16[128,1024]{1,0:T(8,128)(2,1)}), bf16[4096,1024]{1,0:T(8,128)(2,1)}) %all-gather.5.cloned.1.call-update) | async-done | bytes 8388624 | tf_op jit(solution)/shard_map/all_gather | solution.py:1754
  349.0 10.3 %fusion.50 = (f32[640]{0:T(1024)S(1)}, f32[640,1024]{1,0:T(8,128)S(1)}, f32[640,1024]{1,0:T(8,128)S(1)}) fusion(f32[640,1024]{1,0:T(8,128)} %copy-done.17, f32[1024]{0:T(1024)S(1)} %bitcast.212, bf16[640,4096]{1,0:T(8,128)(2,1)} %get-tuple-element.146.refs_0_, bf16[4096,1024]{1,0:T(8,128)(2,1)} %all-gather.5.cloned.1.call-done), kind=kOutput, calls=%fused_computation.182 | convolution fusion | flops 5370674688 | bytes 21502464 | tf_op jit(solution)/shard_map/dot_general | solution.py:37
  364.3 13.8 %fusion.6.refs_11_ = bf16[640,4096]{1,0:T(8,128)(2,1)} fusion(f32[640,4096]{1,0:T(8,128)} %get-tuple-element.147, bf16[640,1024]{1,0:T(8,128)(2,1)S(1)} %multiply_convert_fusion.5.refs_10_, bf16[4096,1024]{1,0:T(8,128)(2,1)} %all-gather.5.cloned.1.call-done), kind=kOutput, calls=%fused_computation.13 | convolution fusion | flops 5394923520 | bytes 25427968 | tf_op jit(solution)/shard_map/dot_general | solution.py:51
  378.0 10.5 %multiply_reduce_fusion.5 = (f32[1024]{0:T(1024)S(1)}, f32[640]{0:T(1024)S(1)}, f32[1024]{0:T(1024)S(1)}, f32[640,1024]{1,0:T(8,128)S(1)}) fusion(f32[640,1024]{1,0:T(8,128)S(1)} %copy-done.18, f32[640]{0:T(1024)S(1)} %fusion.35, f32[640]{0:T(1024)S(1)} %broadcast_multiply_fusion.3, f32[1024]{0:T(1024)S(1)} %bitcast.195, ...), kind=kOutput, calls=%fused_computation.47 | convolution fusion | flops 5373949440 | bytes 18894336 | tf_op jit(solution)/shard_map/dot_general | solution.py:51
  391.1 2.7 convolution_convert_fusion.4.refs_3_
  393.8 7.6 shard_map.235
  401.4 4.0 multiply_reduce_fusion.2
  409.6 1.6 convolution_convert_fusion.3
  411.2 21.7 %shard_map.236.refs_15_ = bf16[640,3072]{1,0:T(8,128)(2,1)} custom-call(bf16[640,3072]{1,0:T(8,128)(2,1)} %copy-done.4, bf16[10,64,1024]{2,1,0:T(8,128)(2,1)S(1)} %bitcast.159), custom_call_target="tpu_custom_call" | custom-call | flops 4194304000 | bytes 10485760 | tf_op jit(solution)/shard_map/pallas_call | solution.py:415
  432.9 6.4 fusion.60
  439.6 1.8 collective-permute-start.1
  443.8 14.0 %collective-permute-done.1 = f32[10,32,1024]{2,1,0:T(8,128)S(1)} collective-permute-done((f32[10,32,1024]{2,1,0:T(8,128)S(1)}, f32[10,32,1024]{2,1,0:T(8,128)S(1)}, u32[]{:S(2)}, u32[]{:S(2)}) %collective-permute-start.1) | collective-permute-done | bytes 1310752 | tf_op jit(solution)/shard_map/ppermute | solution.py:33
  458.0 1.5 copy-done.10
  462.9 12.7 %fusion.12.refs_17_ = bf16[640,4096]{1,0:T(8,128)(2,1)S(1)} fusion(f32[640,4096]{1,0:T(8,128)} %get-tuple-element.141, bf16[640,1024]{1,0:T(8,128)(2,1)S(1)} %multiply_convert_fusion.3.refs_16_, bf16[4096,1024]{1,0:T(8,128)(2,1)} %get-tuple-element.40), kind=kOutput, calls=%fused_computation.19 | convolution fusion | flops 5394923520 | bytes 25427968 | tf_op jit(solution)/shard_map/dot_general | solution.py:51
  475.7 11.0 %multiply_reduce_fusion.8 = (f32[1024]{0:T(1024)S(1)}, f32[640]{0:T(1024)S(1)}, f32[1024]{0:T(1024)S(1)}, f32[640,1024]{1,0:T(8,128)S(1)}) fusion(f32[640,1024]{1,0:T(8,128)S(1)} %copy-done.16, f32[640]{0:T(1024)S(1)} %copy-done.57, f32[640]{0:T(1024)S(1)} %copy-done.51, f32[1024]{0:T(1024)S(1)} %bitcast.192, bf16[640,4096]{1,0:T(8,128)(2,1)S(1)} %fusion.12.refs_17_, ...), kind=kOutput, calls=%fused_computation.50 | convolution fusion | flops 5373949440 | bytes 18894336 | tf_op jit(solution)/shard_map/dot_general | solution.py:51
  489.5 1.6 convolution_convert_fusion.2.grad_ref
  491.3 25.0 %shard_map.237.refs_19_ = bf16[640,3072]{1,0:T(8,128)(2,1)} custom-call(bf16[640,3072]{1,0:T(8,128)(2,1)} %copy-done.1, bf16[640,2048]{1,0:T(8,128)(2,1)S(1)} %copy-done.3, bf16[640,1024]{1,0:T(8,128)(2,1)S(1)} %convolution_convert_fusion.2.grad_ref), custom_call_target="tpu_custom_call" | custom-call | flops 3355443200 | bytes 10485760 | tf_op jit(solution)/shard_map/pallas_call | solution.py:450
  516.3 8.4 multiply_reduce_fusion.10
  529.5 296.3 %shard_map.238 = (f32[128,18432]{1,0:T(8,128)}, f32[512,4096]{1,0:T(8,128)}, f32[8,512]{1,0:T(8,128)}, f32[8,256,128]{2,1,0:T(8,128)}, f32[8,512]{1,0:T(8,128)},...) custom-call(bf16[640,4096]{1,0:T(8,128)(2,1)} %get-tuple-element.146, ...), custom_call_target="tpu_custom_call" | custom-call | flops 299999985664 | bytes 800000000 | tf_op jit(solution)/shard_map/pallas_call | solution.py:1620
  825.9 1.8 copy.46
  828.6 5.6 multiply_reduce_fusion
  839.2 10.4 %shard_map.239 = f32[8,128]{1,0:T(8,128)} custom-call(f32[8,128]{1,0:T(8,128)} %broadcast_in_dim.87.part_ref), custom_call_target="tpu_custom_call" | custom-call | tf_op jit(solution)/shard_map/pallas_call | solution.py:1672
  853.0 22.8 %multiply_subtract_fusion.1 = (f32[512,4096]{1,0:T(8,128)}, f32[512,4096]{1,0:T(8,128)}, f32[512,4096]{1,0:T(8,128)}) fusion(f32[512,4096]{1,0:T(8,128)} %refs_1_.1, f32[512,4096]{1,0:T(8,128)} %get-tuple-element.56, f32[]{:T(128)S(6)} %div.227, f32[512,4096]{1,0:T(8,128)} %param.25, f32[512,4096]{1,0:T(8,128)} %param.26), kind=kLoop, calls=%fused_computation.25 | loop fusion | flops 33554432 | bytes 58720260 | tf_op jit(solution)/shard_map/sub | solution.py:542
  875.8 36.5 %multiply_subtract_fusion = (f32[128,30720]{1,0:T(8,128)}, f32[128,30720]{1,0:T(8,128)}, f32[128,30720]{1,0:T(8,128)}) fusion(f32[128,30720]{1,0:T(8,128)} %refs_0_.1, f32[]{:T(128)S(6)} %div.227, f32[128,18432]{1,0:T(8,128)} %get-tuple-element.55, f32[128,12288]{1,0:T(8,128)} %get-tuple-element.157, f32[128,30720]{1,0:T(8,128)} %param.22, f32[128,30720]{1,0:T(8,128)} %param.23), kind=kLoop, calls=%fused_computation.3 | loop fusion | flops 66846720 | bytes 110100480 | tf_op jit(solution)/shard_map/sub | solution.py:542
  (281 shorter events, 47.8 us)
Async XLA Ops:
  7.2 291.7 %all-gather.3.cloned.1.call-start = ((), (), s32[]{:S(2)}) async-start(), calls=%async_computation | async-start | bytes 8650752 | tf_op jit(solution)/shard_map/all_gather | solution.py:1753
  31.7 154.8 %copy-start.38 = (f32[1,5,8,16,8]{3,4,2,1,0:T(8,128)S(1)}, f32[1,5,8,16,8]{3,4,2,1,0:T(8,128)}, u32[]{:S(2)}) copy-start(f32[1,5,8,16,8]{3,4,2,1,0:T(8,128)} %param.15) | copy-start | bytes 61444
  31.7 154.8 %copy-start.39 = (f32[1,5,8,16,8]{3,4,2,1,0:T(8,128)S(1)}, f32[1,5,8,16,8]{3,4,2,1,0:T(8,128)}, u32[]{:S(2)}) copy-start(f32[1,5,8,16,8]{3,4,2,1,0:T(8,128)} %param.16) | copy-start | bytes 61444
  31.7 154.9 %copy-start.36 = (f32[19,1024]{1,0:T(8,128)S(1)}, f32[19,1024]{1,0:T(8,128)}, u32[]{:S(2)}) copy-start(f32[19,1024]{1,0:T(8,128)} %param.27) | copy-start | bytes 233476
  185.6 163.4 %all-gather.5.cloned.1.call-start = ((), (), s32[]{:S(2)}) async-start(), calls=%async_computation.1 | async-start | bytes 8650752 | tf_op jit(solution)/shard_map/all_gather | solution.py:1754
  187.1 21.4 %copy-start.44 = (f32[1,1024]{1,0:T(1,128)}, f32[1,1024]{1,0:T(1,128)S(1)}, u32[]{:S(2)}) copy-start(f32[1,1024]{1,0:T(1,128)S(1)} %get-tuple-element.120) | copy-start | bytes 12292
  187.7 20.8 %copy-start.13 = (f32[640,1024]{1,0:T(8,128)}, f32[640,1024]{1,0:T(8,128)S(1)}, u32[]{:S(2)}) copy-start(f32[640,1024]{1,0:T(8,128)S(1)} %get-tuple-element.138) | copy-start | bytes 7864324
  188.2 8.2 copy-start.62
  188.2 8.2 copy-start.60
  188.3 8.2 copy-start.58
  188.3 20.2 %copy-start.66 = (f32[1,1024]{1,0:T(1,128)}, f32[1,1024]{1,0:T(1,128)S(1)}, u32[]{:S(2)}) copy-start(f32[1,1024]{1,0:T(1,128)S(1)} %get-tuple-element.134) | copy-start | bytes 12292
  188.3 23.9 %copy-start.54 = (f32[1,1024]{1,0:T(1,128)}, f32[1,1024]{1,0:T(1,128)S(1)}, u32[]{:S(2)}) copy-start(f32[1,1024]{1,0:T(1,128)S(1)} %get-tuple-element.131) | copy-start | bytes 12292
  196.4 15.2 %copy-start.1 = (bf16[640,3072]{1,0:T(8,128)(2,1)}, bf16[640,3072]{1,0:T(8,128)(2,1)S(1)}, u32[]{:S(2)}) copy-start(bf16[640,3072]{1,0:T(8,128)(2,1)S(1)} %convolution_convert_fusion.1.qkv_ref) | copy-start | bytes 11796484
  196.5 12.0 %copy-start.71 = (bf16[1024,1024]{1,0:T(8,128)(2,1)S(1)}, bf16[1024,1024]{1,0:T(8,128)(2,1)}, u32[]{:S(2)}) copy-start(bf16[1024,1024]{1,0:T(8,128)(2,1)} %get-tuple-element.38) | copy-start | bytes 6291460
  196.5 16.3 %slice-start = ((s8[8388608]{0:T(1024)(128)(4,1)}), s8[4194304]{0:T(1024)(128)(4,1)S(1)}, s32[]{:S(2)}) async-start(s8[8388608]{0:T(1024)(128)(4,1)} %bitcast.226), calls=%async_computation.2 | async-start | bytes 8388608
  211.8 10.3 %copy-start.15 = (f32[640,1024]{1,0:T(8,128)}, f32[640,1024]{1,0:T(8,128)S(1)}, u32[]{:S(2)}) copy-start(f32[640,1024]{1,0:T(8,128)S(1)} %get-tuple-element.108) | copy-start | bytes 7864324
  212.2 9.8 %copy-start.64 = (f32[640]{0:T(1024)}, f32[640]{0:T(1024)S(1)}, u32[]{:S(2)}) copy-start(f32[640]{0:T(1024)S(1)} %multiply_reduce_fusion.20) | copy-start | bytes 7684
  212.2 9.8 %copy-start.56 = (f32[640]{0:T(1024)}, f32[640]{0:T(1024)S(1)}, u32[]{:S(2)}) copy-start(f32[640]{0:T(1024)S(1)} %fusion.32) | copy-start | bytes 7684
  212.8 9.2 %copy-start.32 = (bf16[640,1024]{1,0:T(8,128)(2,1)}, bf16[640,1024]{1,0:T(8,128)(2,1)S(1)}, u32[]{:S(2)}) copy-start(bf16[640,1024]{1,0:T(8,128)(2,1)S(1)} %add_convert_fusion.2.refs_7_) | copy-start | bytes 3932164
  222.0 11.1 %copy-start.77 = (bf16[640,4096]{1,0:T(8,128)(2,1)}, bf16[640,4096]{1,0:T(8,128)(2,1)S(1)}, u32[]{:S(2)}) copy-start(bf16[640,4096]{1,0:T(8,128)(2,1)S(1)} %get-tuple-element.140.refs_6_) | copy-start | bytes 15728644
  234.8 20.3 %collective-permute-start = (bf16[10,32,1024]{2,1,0:T(8,128)(2,1)S(1)}, bf16[10,32,1024]{2,1,0:T(8,128)(2,1)}, u32[]{:S(2)}, u32[]{:S(2)}) collective-permute-start(bf16[10,32,1024]{2,1,0:T(8,128)(2,1)S(1)} %get-tuple-element.114), channel_id=1, source_target_pairs={{0,3},{1,0},{2,1},{3,2},{4,7},{5,4},{6,5},{7,6},{8,11},{9,8},{10,9... | collective-permute-start | bytes 1966088 | tf_op jit(solution)/shard_map/ppermute | solution.py:33
  264.6 15.6 %copy-start.4 = (bf16[640,3072]{1,0:T(8,128)(2,1)}, bf16[640,3072]{1,0:T(8,128)(2,1)S(1)}, u32[]{:S(2)}) copy-start(bf16[640,3072]{1,0:T(8,128)(2,1)S(1)} %convolution_convert_fusion.qkv_ref) | copy-start | bytes 11796484
  264.6 15.6 %copy-start.9 = (f32[640,1024]{1,0:T(8,128)S(1)}, f32[640,1024]{1,0:T(8,128)}, u32[]{:S(2)}) copy-start(f32[640,1024]{1,0:T(8,128)} %copy-done.8) | copy-start | bytes 7864324
  264.6 15.6 %copy-start.24 = (bf16[1024,1024]{1,0:T(8,128)(2,1)S(1)}, bf16[1024,1024]{1,0:T(8,128)(2,1)}, u32[]{:S(2)}) copy-start(bf16[1024,1024]{1,0:T(8,128)(2,1)} %get-tuple-element.42) | copy-start | bytes 6291460
  283.3 10.8 %copy-start.11 = (f32[640,1024]{1,0:T(8,128)}, f32[640,1024]{1,0:T(8,128)S(1)}, u32[]{:S(2)}) copy-start(f32[640,1024]{1,0:T(8,128)S(1)} %get-tuple-element.104) | copy-start | bytes 7864324
  287.8 6.3 copy-start.73
  364.3 13.8 %copy-start.18 = (f32[640,1024]{1,0:T(8,128)S(1)}, f32[640,1024]{1,0:T(8,128)}, u32[]{:S(2)}) copy-start(f32[640,1024]{1,0:T(8,128)} %copy-done.17) | copy-start | bytes 7864324
  393.8 7.6 copy-start.12
  409.6 23.3 %slice-start.2 = ((s8[6291456]{0:T(1024)(128)(4,1)}), s8[4194304]{0:T(1024)(128)(4,1)S(1)}, s32[]{:S(2)}) async-start(s8[6291456]{0:T(1024)(128)(4,1)} %bitcast.228), calls=%async_computation.4 | async-start | bytes 8388608
  411.1 21.7 %slice-start.3 = ((s8[6291456]{0:T(1024)(128)(4,1)}), s8[2097152]{0:T(1024)(128)(4,1)S(1)}, s32[]{:S(2)}) async-start(s8[6291456]{0:T(1024)(128)(4,1)} %bitcast.228), calls=%async_computation.5 | async-start | bytes 4194304
  439.6 18.2 %collective-permute-start.1 = (f32[10,32,1024]{2,1,0:T(8,128)S(1)}, f32[10,32,1024]{2,1,0:T(8,128)S(1)}, u32[]{:S(2)}, u32[]{:S(2)}) collective-permute-start(f32[10,32,1024]{2,1,0:T(8,128)S(1)} %get-tuple-element.113), channel_id=1, source_target_pairs={{0,1},{1,2},{2,3},{3,0},{4,5},{5,6},{6,7},{7,4},{8,9},{9,10},{10,1... | collective-permute-start | bytes 3932168 | tf_op jit(solution)/shard_map/ppermute | solution.py:33
  462.9 12.7 %copy-start.31 = (bf16[640,1024]{1,0:T(8,128)(2,1)}, bf16[640,1024]{1,0:T(8,128)(2,1)S(1)}, u32[]{:S(2)}) copy-start(bf16[640,1024]{1,0:T(8,128)(2,1)S(1)} %multiply_convert_fusion.3.refs_16_) | copy-start | bytes 3932164
  462.9 12.7 %copy-start.16 = (f32[640,1024]{1,0:T(8,128)S(1)}, f32[640,1024]{1,0:T(8,128)}, u32[]{:S(2)}) copy-start(f32[640,1024]{1,0:T(8,128)} %copy-done.15) | copy-start | bytes 7864324
  462.9 12.7 %copy-start.51 = (f32[640]{0:T(1024)S(1)}, f32[640]{0:T(1024)}, u32[]{:S(2)}) copy-start(f32[640]{0:T(1024)} %copy-done.50) | copy-start | bytes 7684
  462.9 12.7 %copy-start.55 = (f32[1,1024]{1,0:T(1,128)S(1)}, f32[1,1024]{1,0:T(1,128)}, u32[]{:S(2)}) copy-start(f32[1,1024]{1,0:T(1,128)} %copy-done.54) | copy-start | bytes 12292
  462.9 12.7 %copy-start.57 = (f32[640]{0:T(1024)S(1)}, f32[640]{0:T(1024)}, u32[]{:S(2)}) copy-start(f32[640]{0:T(1024)} %copy-done.56) | copy-start | bytes 7684
  475.7 11.0 %copy-start.78 = (bf16[640,4096]{1,0:T(8,128)(2,1)}, bf16[640,4096]{1,0:T(8,128)(2,1)S(1)}, u32[]{:S(2)}) copy-start(bf16[640,4096]{1,0:T(8,128)(2,1)S(1)} %fusion.12.refs_17_) | copy-start | bytes 15728644
  475.7 11.0 %copy-start.65 = (f32[640]{0:T(1024)S(1)}, f32[640]{0:T(1024)}, u32[]{:S(2)}) copy-start(f32[640]{0:T(1024)} %copy-done.64) | copy-start | bytes 7684
  491.2 25.0 %copy-start.14 = (f32[640,1024]{1,0:T(8,128)S(1)}, f32[640,1024]{1,0:T(8,128)}, u32[]{:S(2)}) copy-start(f32[640,1024]{1,0:T(8,128)} %copy-done.13) | copy-start | bytes 7864324
  491.2 25.0 %copy-start.45 = (f32[1,1024]{1,0:T(1,128)S(1)}, f32[1,1024]{1,0:T(1,128)}, u32[]{:S(2)}) copy-start(f32[1,1024]{1,0:T(1,128)} %copy-done.44) | copy-start | bytes 12292
  491.2 25.1 %copy-start.53 = (f32[640]{0:T(1024)S(1)}, f32[640]{0:T(1024)}, u32[]{:S(2)}) copy-start(f32[640]{0:T(1024)} %copy-done.52) | copy-start | bytes 7684
  491.2 25.1 %copy-start.59 = (f32[1,1024]{1,0:T(1,128)S(1)}, f32[1,1024]{1,0:T(1,128)}, u32[]{:S(2)}) copy-start(f32[1,1024]{1,0:T(1,128)} %copy-done.58) | copy-start | bytes 12292
  491.2 25.1 %copy-start.61 = (f32[640]{0:T(1024)S(1)}, f32[640]{0:T(1024)}, u32[]{:S(2)}) copy-start(f32[640]{0:T(1024)} %copy-done.60) | copy-start | bytes 7684
  516.3 8.4 copy-start.63
  828.5 6.3 copy-start.68
  828.5 23.7 %copy-start.37 = (f32[19,1024]{1,0:T(8,128)S(1)}, f32[19,1024]{1,0:T(8,128)}, u32[]{:S(2)}) copy-start(f32[19,1024]{1,0:T(8,128)} %param.27) | copy-start | bytes 233476
  828.5 23.7 %copy-start.46 = (f32[19,1024]{1,0:T(8,128)S(1)}, f32[19,1024]{1,0:T(8,128)}, u32[]{:S(2)}) copy-start(f32[19,1024]{1,0:T(8,128)} %param.28) | copy-start | bytes 233476
  828.5 23.7 %copy-start.47 = (f32[19,1024]{1,0:T(8,128)S(1)}, f32[19,1024]{1,0:T(8,128)}, u32[]{:S(2)}) copy-start(f32[19,1024]{1,0:T(8,128)} %param.29) | copy-start | bytes 233476
  (39 other events, 92.9 us)
Sparse Core Ops, SparseCore 0:
  185.7 82.0 all-gather.2
  271.2 77.7 all-gather.4

commit v15 on v14

--- a/solution.py
+++ b/solution.py
@@ -1732,25 +1732,25 @@
         (w_wide, w_deep),
         (
             (0, 22 * D, FF),
-            (1, 0, D),
-            (0, 20 * D, D),
-            (0, 21 * D, D),
+            (0, 12 * D, 3 * D),
+            (0, 15 * D, 3 * D),
             (0, 18 * D, D),
             (0, 19 * D, D),
-            (0, 12 * D, 3 * D),
-            (0, 15 * D, 3 * D),
+            (1, 0, D),
+            (0, 22 * D + FF, FF),
         ),
-        (1, 2, 1, 2, 1, 2, 0, 0),
+        (1, 2, 2, 1, 1, 0, 0),
         part_modul.reshape(clip_count, band_count, -1, 128),
         text_cols,
     )
-    up_a_w, down_a_w, query_w, cross_out_w, out_a_w, out_b_w, qkv_a_w, qkv_b_w = gathered
+    up_a_w, qkv_a_w, qkv_b_w, out_a_w, out_b_w, down_a_w, up_b_w = gathered
     all_text = all_text.transpose(0, 2, 1, 3)
     keyval = keyval.transpose(1, 0, 2).reshape(TEXT_PAD, 2 * D)
-    late_up_b, late_down_b, all_modul = lax.optimization_barrier(
-        (own_quarter(w_wide[:, 22 * D + FF :]), own_quarter(w_deep[:, 3 * D :]), all_modul)
-    )
-    up_b_w = lax.all_gather(late_up_b, ("clip", "band"), axis=0, tiled=True)
+    late_cross, late_down_b, all_modul = lax.optimization_barrier(
+        (own_quarter(w_wide[:, 20 * D : 22 * D]), own_quarter(w_deep[:, 3 * D :]), all_modul)
+    )
+    cross_w = lax.all_gather(late_cross, ("clip", "band"), axis=0, tiled=True)
+    query_w, cross_out_w = (cross_w[:, :D], cross_w[:, D:])
     down_b_w = lax.all_gather(late_down_b, ("clip", "band"), axis=0, tiled=True)
     small_low = w_small.astype(jnp.bfloat16)
     small_val = small_low.astype(jnp.float32)

time: 927 us -> 922 us (level)
  waiting for transfers between devices: 67.7 us -> 47.2 us
  Pallas kernels: 558 us -> 577 us
    pallas_call x1, Pallas kernels: 154 us -> 172 us  [gather_weights(): pl.pallas_call(partial(gather_kernel, count, picks, sides), out_shape=tup...]
    all_gather x1, waiting for transfers between devices: 38.2 us -> 27.9 us  [per_device(): down_b_w = lax.all_gather(late_down_b, ('clip', 'band'), axis=0, tiled=True)]
    ppermute x2, waiting for transfers between devices: 29 us -> 19.1 us  [shifted(): lax.ppermute(value, axis, [(i, (i + by) % length) for i in range(length)])]
    unnamed x169 -> x171, local copies, waits for them, and re-layouts: 21.2 us -> 20.5 us
where the time goes in v15:
time: 922 us; the launch traced here: 916 us
  Pallas kernels  577 us (63%)
  matrix products  148 us (16%)
  other arithmetic  85.3 us (9%)
  waiting for transfers between devices  47.2 us (5%)
  local copies, waits for them, and re-layouts  30.5 us (3%)
  between operations  24.2 us (3%)
    pallas_call x1, Pallas kernels, reduce_gradients(): pl.pallas_call(partial(reduce_kernel, count, tokens, phases), out_shape=(...  296 us
    pallas_call x1, Pallas kernels, gather_weights(): pl.pallas_call(partial(gather_kernel, count, picks, sides), out_shape=tup...  172 us
    dot_general x11, matrix products, matmul_nt(): lax.dot_general(left_op, right_op, (((1,), (1,)), ((), ())), preferred_el...  74.3 us
    dot_general x13, matrix products, matmul(): return jnp.dot(left_op, right_op, preferred_element_type=jnp.float32)  66.8 us
    sub x3, other arithmetic, adam_update(): weight - learn_rate * (first_hat / (jnp.sqrt(second_hat) + ADAM_EPS) + DE...  59.9 us
    all_gather x1, waiting for transfers between devices, per_device(): down_b_w = lax.all_gather(late_down_b, ('clip', 'band'), axis=0, tiled=True)  27.9 us
    pallas_call x1, Pallas kernels, attend_frames_back(): pl.pallas_call(partial(attend_frames_back_kernel, windows), out_shape=jax...  25.4 us
    pallas_call x1, Pallas kernels, attend_halves_back(): pl.pallas_call(partial(attend_halves_back_kernel, part), out_shape=jax.Sh...  21.5 us
  transfers between devices with their start and end apart: 4, of which 3 were waited for; matrix products, arithmetic and copies ran while one was open for 7% of the time, Pallas kernels for 4%

profile of v15, /device:TPU:0, one launch (start us, length us, event | category | flops | bytes accessed | tf_op | source)
XLA Modules:
  0.0 916.1 jit_solution(16885266791995507171)
XLA Ops:
  9.9 9.7 %shard_map.230 = s32[8,8,128]{2,1,0:T(8,128)} custom-call(s32[8,128]{1,0:T(8,128)} %pad.12.facts_ref), custom_call_target="tpu_custom_call" | custom-call | tf_op jit(solution)/shard_map/pallas_call | solution.py:589
  20.5 1.3 slice.115
  22.0 3.4 fusion.33
  26.1 1.8 slice.116
  29.4 171.9 %shard_map.231 = (bf16[1024,4096]{1,0:T(8,128)(2,1)}, bf16[1024,3072]{1,0:T(8,128)(2,1)}, bf16[1024,3072]{1,0:T(8,128)(2,1)}, bf16[1024,1024]{1,0:T(8,128)(2,1)}...) custom-call(f32[128,30720]{1,0:T(8,128)} %refs_0_.1, ...), custom_call_target="tpu_custom_call" | custom-call | flops 199999995904 | bytes 600000000 | tf_op jit(solution)/shard_map/pallas_call | solution.py:875
  206.2 1.5 copy-done.76
  207.6 4.5 convolution_convert_fusion.1.qkv_ref
  212.2 12.1 %shard_map.232 = (bf16[640,1024]{1,0:T(8,128)(2,1)S(1)}, bf16[640,2048]{1,0:T(8,128)(2,1)S(1)}) custom-call(bf16[640,3072]{1,0:T(8,128)(2,1)S(1)} %convolution_convert_fusion.1.qkv_ref), custom_call_target="tpu_custom_call" | custom-call | flops 1342177280 | bytes 10485760 | tf_op jit(solution)/shard_map/pallas_call | solution.py:431
  224.4 3.2 fusion.70
  229.7 8.2 multiply_convert_fusion.1
  237.9 11.1 %fusion.69 = (f32[640]{0:T(1024)S(1)}, f32[640,1024]{1,0:T(8,128)S(1)}, f32[640,1024]{1,0:T(8,128)}) fusion(f32[640,1024]{1,0:T(8,128)S(1)} %get-tuple-element.106, f32[1024]{0:T(1024)S(1)} %bitcast.200, bf16[640,4096]{1,0:T(8,128)(2,1)S(1)} %get-tuple-element.138.refs_6_, bf16[4096,1024]{1,0:T(8,128)(2,1)} %get-tuple-element.39), kind=kOutput, calls=%fused_computation.192 | convolution fusion | flops 5370674688 | bytes 21502464 | tf_op jit(solution)/shard_map/dot_general | solution.py:37
  250.6 1.7 collective-permute-start
  252.5 1.5 slice_reduce_fusion.2
  255.2 5.1 collective-permute-done
  262.7 7.4 convolution_convert_fusion.qkv_ref
  270.1 15.2 %shard_map.233 = bf16[10,64,1024]{2,1,0:T(8,128)(2,1)S(1)} custom-call(bf16[640,3072]{1,0:T(8,128)(2,1)S(1)} %convolution_convert_fusion.qkv_ref), custom_call_target="tpu_custom_call" | custom-call | flops 1677721600 | bytes 10485760 | tf_op jit(solution)/shard_map/pallas_call | solution.py:399
  285.4 3.1 fusion.68
  290.0 1.5 multiply_convert_fusion.7.refs_3_
  291.5 3.7 fusion.27.refs_0_
  295.1 6.3 shard_map.234.refs_2_
  301.5 1.6 fusion.76
  305.7 8.7 multiply_convert_fusion
  314.4 27.9 %all-gather.5.cloned.1.call-done = bf16[4096,1024]{1,0:T(8,128)(2,1)} async-done(((bf16[128,1024]{1,0:T(8,128)(2,1)}), bf16[4096,1024]{1,0:T(8,128)(2,1)}) %all-gather.5.cloned.1.call-update) | async-done | bytes 8388624 | tf_op jit(solution)/shard_map/all_gather | solution.py:1754
  342.3 10.5 %fusion.67 = (f32[640]{0:T(1024)S(1)}, f32[640,1024]{1,0:T(8,128)S(1)}, f32[640,1024]{1,0:T(8,128)S(1)}) fusion(f32[640,1024]{1,0:T(8,128)} %copy-done.18, f32[1024]{0:T(1024)S(1)} %bitcast.208, bf16[640,4096]{1,0:T(8,128)(2,1)} %get-tuple-element.144.refs_0_, bf16[4096,1024]{1,0:T(8,128)(2,1)} %all-gather.5.cloned.1.call-done), kind=kOutput, calls=%fused_computation.190 | convolution fusion | flops 5370674688 | bytes 21502464 | tf_op jit(solution)/shard_map/dot_general | solution.py:37
  356.8 14.0 %fusion.6.refs_11_ = bf16[640,4096]{1,0:T(8,128)(2,1)} fusion(f32[640,4096]{1,0:T(8,128)} %get-tuple-element.145, bf16[640,1024]{1,0:T(8,128)(2,1)S(1)} %multiply_convert_fusion.5.refs_10_, bf16[4096,1024]{1,0:T(8,128)(2,1)} %all-gather.5.cloned.1.call-done), kind=kOutput, calls=%fused_computation.13 | convolution fusion | flops 5394923520 | bytes 25427968 | tf_op jit(solution)/shard_map/dot_general | solution.py:51
  370.8 10.3 %multiply_reduce_fusion.5 = (f32[1024]{0:T(1024)S(1)}, f32[640]{0:T(1024)S(1)}, f32[1024]{0:T(1024)S(1)}, f32[640,1024]{1,0:T(8,128)S(1)}) fusion(f32[640,1024]{1,0:T(8,128)S(1)} %copy-done.19, f32[640]{0:T(1024)S(1)} %fusion.52, f32[640]{0:T(1024)S(1)} %broadcast_multiply_fusion.3, f32[1024]{0:T(1024)S(1)} %bitcast.191, ...), kind=kOutput, calls=%fused_computation.47 | convolution fusion | flops 5373949440 | bytes 18894336 | tf_op jit(solution)/shard_map/dot_general | solution.py:51
  384.7 2.7 fusion.30.refs_3_
  387.3 7.7 shard_map.235
  395.1 4.0 multiply_reduce_fusion.2
  403.3 1.6 convolution_convert_fusion.3
  404.8 21.5 %shard_map.236.refs_15_ = bf16[640,3072]{1,0:T(8,128)(2,1)} custom-call(bf16[640,3072]{1,0:T(8,128)(2,1)} %copy-done.4, bf16[10,64,1024]{2,1,0:T(8,128)(2,1)S(1)} %bitcast.155), custom_call_target="tpu_custom_call" | custom-call | flops 4194304000 | bytes 10485760 | tf_op jit(solution)/shard_map/pallas_call | solution.py:415
  426.3 7.6 fusion.77
  434.3 1.8 collective-permute-start.1
  438.5 14.0 %collective-permute-done.1 = f32[10,32,1024]{2,1,0:T(8,128)S(1)} collective-permute-done((f32[10,32,1024]{2,1,0:T(8,128)S(1)}, f32[10,32,1024]{2,1,0:T(8,128)S(1)}, u32[]{:S(2)}, u32[]{:S(2)}) %collective-permute-start.1) | collective-permute-done | bytes 1310752 | tf_op jit(solution)/shard_map/ppermute | solution.py:33
  452.8 1.5 copy-done.10
  457.7 14.7 %fusion.12.refs_17_ = bf16[640,4096]{1,0:T(8,128)(2,1)} fusion(f32[640,4096]{1,0:T(8,128)} %get-tuple-element.139, bf16[640,1024]{1,0:T(8,128)(2,1)S(1)} %multiply_convert_fusion.3.refs_16_, bf16[4096,1024]{1,0:T(8,128)(2,1)} %get-tuple-element.39), kind=kOutput, calls=%fused_computation.19 | convolution fusion | flops 5394923520 | bytes 25427968 | tf_op jit(solution)/shard_map/dot_general | solution.py:51
  472.5 8.6 multiply_reduce_fusion.8
  482.5 1.4 copy-done.75
  483.9 1.5 convolution_convert_fusion.2.grad_ref
  485.7 25.4 %shard_map.237.refs_19_ = bf16[640,3072]{1,0:T(8,128)(2,1)} custom-call(bf16[640,3072]{1,0:T(8,128)(2,1)} %copy-done.1, bf16[640,2048]{1,0:T(8,128)(2,1)S(1)} %copy-done.3, bf16[640,1024]{1,0:T(8,128)(2,1)S(1)} %convolution_convert_fusion.2.grad_ref), custom_call_target="tpu_custom_call" | custom-call | flops 3355443200 | bytes 10485760 | tf_op jit(solution)/shard_map/pallas_call | solution.py:450
  511.1 8.2 multiply_reduce_fusion.10
  522.8 1.3 fusion.38.refs_20_
  524.1 296.3 %shard_map.238 = (f32[128,18432]{1,0:T(8,128)}, f32[512,4096]{1,0:T(8,128)}, f32[8,512]{1,0:T(8,128)}, f32[8,256,128]{2,1,0:T(8,128)}, f32[8,512]{1,0:T(8,128)},...) custom-call(bf16[640,4096]{1,0:T(8,128)(2,1)} %get-tuple-element.144, ...), custom_call_target="tpu_custom_call" | custom-call | flops 299999985664 | bytes 800000000 | tf_op jit(solution)/shard_map/pallas_call | solution.py:1620
  820.4 1.8 copy.46
  823.1 5.6 multiply_reduce_fusion
  833.8 10.4 %shard_map.239 = f32[8,128]{1,0:T(8,128)} custom-call(f32[8,128]{1,0:T(8,128)} %broadcast_in_dim.87.part_ref), custom_call_target="tpu_custom_call" | custom-call | tf_op jit(solution)/shard_map/pallas_call | solution.py:1672
  847.6 22.7 %multiply_subtract_fusion.1 = (f32[512,4096]{1,0:T(8,128)}, f32[512,4096]{1,0:T(8,128)}, f32[512,4096]{1,0:T(8,128)}) fusion(f32[512,4096]{1,0:T(8,128)} %refs_1_.1, f32[512,4096]{1,0:T(8,128)} %get-tuple-element.54, f32[]{:T(128)S(6)} %div.227, f32[512,4096]{1,0:T(8,128)} %param.25, f32[512,4096]{1,0:T(8,128)} %param.26), kind=kLoop, calls=%fused_computation.25 | loop fusion | flops 33554432 | bytes 58720260 | tf_op jit(solution)/shard_map/sub | solution.py:542
  870.3 36.5 %multiply_subtract_fusion = (f32[128,30720]{1,0:T(8,128)}, f32[128,30720]{1,0:T(8,128)}, f32[128,30720]{1,0:T(8,128)}) fusion(f32[128,30720]{1,0:T(8,128)} %refs_0_.1, f32[]{:T(128)S(6)} %div.227, f32[128,18432]{1,0:T(8,128)} %get-tuple-element.53, f32[128,12288]{1,0:T(8,128)} %get-tuple-element.155, f32[128,30720]{1,0:T(8,128)} %param.22, f32[128,30720]{1,0:T(8,128)} %param.23), kind=kLoop, calls=%fused_computation.3 | loop fusion | flops 66846720 | bytes 110100480 | tf_op jit(solution)/shard_map/sub | solution.py:542
  (284 shorter events, 48.1 us)
Async XLA Ops:
  7.2 284.3 %all-gather.3.cloned.1.call-start = ((), (), s32[]{:S(2)}) async-start(), calls=%async_computation | async-start | bytes 4325376 | tf_op jit(solution)/shard_map/all_gather | solution.py:1752
  29.4 172.9 %copy-start.39 = (f32[1,5,8,16,8]{3,4,2,1,0:T(8,128)S(1)}, f32[1,5,8,16,8]{3,4,2,1,0:T(8,128)}, u32[]{:S(2)}) copy-start(f32[1,5,8,16,8]{3,4,2,1,0:T(8,128)} %param.15) | copy-start | bytes 61444
  29.4 172.9 %copy-start.40 = (f32[1,5,8,16,8]{3,4,2,1,0:T(8,128)S(1)}, f32[1,5,8,16,8]{3,4,2,1,0:T(8,128)}, u32[]{:S(2)}) copy-start(f32[1,5,8,16,8]{3,4,2,1,0:T(8,128)} %param.16) | copy-start | bytes 61444
  29.4 173.0 %copy-start.37 = (f32[19,1024]{1,0:T(8,128)S(1)}, f32[19,1024]{1,0:T(8,128)}, u32[]{:S(2)}) copy-start(f32[19,1024]{1,0:T(8,128)} %param.27) | copy-start | bytes 233476
  201.3 141.0 %all-gather.5.cloned.1.call-start = ((), (), s32[]{:S(2)}) async-start(), calls=%async_computation.1 | async-start | bytes 8650752 | tf_op jit(solution)/shard_map/all_gather | solution.py:1754
  202.8 21.5 %copy-start.45 = (f32[1,1024]{1,0:T(1,128)}, f32[1,1024]{1,0:T(1,128)S(1)}, u32[]{:S(2)}) copy-start(f32[1,1024]{1,0:T(1,128)S(1)} %get-tuple-element.118) | copy-start | bytes 12292
  203.4 20.9 %copy-start.14 = (f32[640,1024]{1,0:T(8,128)}, f32[640,1024]{1,0:T(8,128)S(1)}, u32[]{:S(2)}) copy-start(f32[640,1024]{1,0:T(8,128)S(1)} %get-tuple-element.136) | copy-start | bytes 7864324
  204.5 7.6 copy-start.61
  204.5 7.6 copy-start.59
  204.5 19.8 %copy-start.67 = (f32[1,1024]{1,0:T(1,128)}, f32[1,1024]{1,0:T(1,128)S(1)}, u32[]{:S(2)}) copy-start(f32[1,1024]{1,0:T(1,128)S(1)} %get-tuple-element.132) | copy-start | bytes 12292
  204.5 23.5 %copy-start.55 = (f32[1,1024]{1,0:T(1,128)}, f32[1,1024]{1,0:T(1,128)S(1)}, u32[]{:S(2)}) copy-start(f32[1,1024]{1,0:T(1,128)S(1)} %get-tuple-element.129) | copy-start | bytes 12292
  212.1 15.4 %copy-start.1 = (bf16[640,3072]{1,0:T(8,128)(2,1)}, bf16[640,3072]{1,0:T(8,128)(2,1)S(1)}, u32[]{:S(2)}) copy-start(bf16[640,3072]{1,0:T(8,128)(2,1)S(1)} %convolution_convert_fusion.1.qkv_ref) | copy-start | bytes 11796484
  212.2 12.2 %copy-start.74 = (bf16[1024,1024]{1,0:T(8,128)(2,1)S(1)}, bf16[1024,1024]{1,0:T(8,128)(2,1)}, u32[]{:S(2)}) copy-start(bf16[1024,1024]{1,0:T(8,128)(2,1)} %get-tuple-element.37) | copy-start | bytes 6291460
  212.2 16.5 %slice-start = ((s8[8388608]{0:T(1024)(128)(4,1)}), s8[4194304]{0:T(1024)(128)(4,1)S(1)}, s32[]{:S(2)}) async-start(s8[8388608]{0:T(1024)(128)(4,1)} %bitcast.222), calls=%async_computation.2 | async-start | bytes 8388608
  227.6 10.3 %copy-start.16 = (f32[640,1024]{1,0:T(8,128)}, f32[640,1024]{1,0:T(8,128)S(1)}, u32[]{:S(2)}) copy-start(f32[640,1024]{1,0:T(8,128)S(1)} %get-tuple-element.106) | copy-start | bytes 7864324
  228.0 9.8 %copy-start.65 = (f32[640]{0:T(1024)}, f32[640]{0:T(1024)S(1)}, u32[]{:S(2)}) copy-start(f32[640]{0:T(1024)S(1)} %multiply_reduce_fusion.20) | copy-start | bytes 7684
  228.0 9.8 %copy-start.57 = (f32[640]{0:T(1024)}, f32[640]{0:T(1024)S(1)}, u32[]{:S(2)}) copy-start(f32[640]{0:T(1024)S(1)} %fusion.49) | copy-start | bytes 7684
  228.6 9.2 %copy-start.32 = (bf16[640,1024]{1,0:T(8,128)(2,1)}, bf16[640,1024]{1,0:T(8,128)(2,1)S(1)}, u32[]{:S(2)}) copy-start(bf16[640,1024]{1,0:T(8,128)(2,1)S(1)} %add_convert_fusion.2.refs_7_) | copy-start | bytes 3932164
  237.9 11.1 %copy-start.77 = (bf16[640,4096]{1,0:T(8,128)(2,1)}, bf16[640,4096]{1,0:T(8,128)(2,1)S(1)}, u32[]{:S(2)}) copy-start(bf16[640,4096]{1,0:T(8,128)(2,1)S(1)} %get-tuple-element.138.refs_6_) | copy-start | bytes 15728644
  250.6 9.8 %collective-permute-start = (bf16[10,32,1024]{2,1,0:T(8,128)(2,1)S(1)}, bf16[10,32,1024]{2,1,0:T(8,128)(2,1)}, u32[]{:S(2)}, u32[]{:S(2)}) collective-permute-start(bf16[10,32,1024]{2,1,0:T(8,128)(2,1)S(1)} %get-tuple-element.112), channel_id=1, source_target_pairs={{0,3},{1,0},{2,1},{3,2},{4,7},{5,4},{6,5},{7,6},{8,11},{9,8},{10,9... | collective-permute-start | bytes 1966088 | tf_op jit(solution)/shard_map/ppermute | solution.py:33
  270.1 15.3 %copy-start.4 = (bf16[640,3072]{1,0:T(8,128)(2,1)}, bf16[640,3072]{1,0:T(8,128)(2,1)S(1)}, u32[]{:S(2)}) copy-start(bf16[640,3072]{1,0:T(8,128)(2,1)S(1)} %convolution_convert_fusion.qkv_ref) | copy-start | bytes 11796484
  270.1 15.3 %copy-start.9 = (f32[640,1024]{1,0:T(8,128)S(1)}, f32[640,1024]{1,0:T(8,128)}, u32[]{:S(2)}) copy-start(f32[640,1024]{1,0:T(8,128)} %copy-done.8) | copy-start | bytes 7864324
  270.1 15.3 %copy-start.25 = (bf16[1024,1024]{1,0:T(8,128)(2,1)S(1)}, bf16[1024,1024]{1,0:T(8,128)(2,1)}, u32[]{:S(2)}) copy-start(bf16[1024,1024]{1,0:T(8,128)(2,1)} %get-tuple-element.41) | copy-start | bytes 6291460
  291.5 10.0 %copy-start.71 = (bf16[1024,2048]{1,0:T(8,128)(2,1)S(1)}, bf16[1024,2048]{1,0:T(8,128)(2,1)}, u32[]{:S(2)}) copy-start(bf16[1024,2048]{1,0:T(8,128)(2,1)} %all-gather.3.cloned.1.call-done) | copy-start | bytes 12582916
  295.1 6.3 copy-start.12
  295.1 10.6 %slice-start.4 = ((s8[8388608]{0:T(1024)(128)(4,1)}), s8[4194304]{0:T(1024)(128)(4,1)S(1)}, s32[]{:S(2)}) async-start(s8[8388608]{0:T(1024)(128)(4,1)} %bitcast.226), calls=%async_computation.6 | async-start | bytes 8388608
  356.8 14.0 %copy-start.34 = (bf16[640,1024]{1,0:T(8,128)(2,1)}, bf16[640,1024]{1,0:T(8,128)(2,1)S(1)}, u32[]{:S(2)}) copy-start(bf16[640,1024]{1,0:T(8,128)(2,1)S(1)} %multiply_convert_fusion.5.refs_10_) | copy-start | bytes 3932164
  356.8 14.0 %copy-start.19 = (f32[640,1024]{1,0:T(8,128)S(1)}, f32[640,1024]{1,0:T(8,128)}, u32[]{:S(2)}) copy-start(f32[640,1024]{1,0:T(8,128)} %copy-done.18) | copy-start | bytes 7864324
  387.3 7.8 copy-start.13
  434.3 18.2 %collective-permute-start.1 = (f32[10,32,1024]{2,1,0:T(8,128)S(1)}, f32[10,32,1024]{2,1,0:T(8,128)S(1)}, u32[]{:S(2)}, u32[]{:S(2)}) collective-permute-start(f32[10,32,1024]{2,1,0:T(8,128)S(1)} %get-tuple-element.111), channel_id=1, source_target_pairs={{0,1},{1,2},{2,3},{3,0},{4,5},{5,6},{6,7},{7,4},{8,9},{9,10},{10,1... | collective-permute-start | bytes 3932168 | tf_op jit(solution)/shard_map/ppermute | solution.py:33
  456.8 15.6 %slice-start.2 = ((s8[8388608]{0:T(1024)(128)(4,1)}), s8[4194304]{0:T(1024)(128)(4,1)S(1)}, s32[]{:S(2)}) async-start(s8[8388608]{0:T(1024)(128)(4,1)} %bitcast.224), calls=%async_computation.4 | async-start | bytes 8388608
  457.6 14.8 %copy-start.31 = (bf16[640,1024]{1,0:T(8,128)(2,1)}, bf16[640,1024]{1,0:T(8,128)(2,1)S(1)}, u32[]{:S(2)}) copy-start(bf16[640,1024]{1,0:T(8,128)(2,1)S(1)} %multiply_convert_fusion.3.refs_16_) | copy-start | bytes 3932164
  457.6 14.8 %copy-start.17 = (f32[640,1024]{1,0:T(8,128)S(1)}, f32[640,1024]{1,0:T(8,128)}, u32[]{:S(2)}) copy-start(f32[640,1024]{1,0:T(8,128)} %copy-done.16) | copy-start | bytes 7864324
  457.7 14.8 %copy-start.52 = (f32[640]{0:T(1024)S(1)}, f32[640]{0:T(1024)}, u32[]{:S(2)}) copy-start(f32[640]{0:T(1024)} %copy-done.51) | copy-start | bytes 7684
  457.7 14.8 %copy-start.56 = (f32[1,1024]{1,0:T(1,128)S(1)}, f32[1,1024]{1,0:T(1,128)}, u32[]{:S(2)}) copy-start(f32[1,1024]{1,0:T(1,128)} %copy-done.55) | copy-start | bytes 12292
  457.7 14.8 %copy-start.58 = (f32[640]{0:T(1024)S(1)}, f32[640]{0:T(1024)}, u32[]{:S(2)}) copy-start(f32[640]{0:T(1024)} %copy-done.57) | copy-start | bytes 7684
  457.7 14.8 %slice-start.3 = ((s8[8388608]{0:T(1024)(128)(4,1)}), s8[4194304]{0:T(1024)(128)(4,1)S(1)}, s32[]{:S(2)}) async-start(s8[8388608]{0:T(1024)(128)(4,1)} %bitcast.224), calls=%async_computation.5 | async-start | bytes 8388608
  472.5 8.6 copy-start.66
  485.7 25.4 %copy-start.15 = (f32[640,1024]{1,0:T(8,128)S(1)}, f32[640,1024]{1,0:T(8,128)}, u32[]{:S(2)}) copy-start(f32[640,1024]{1,0:T(8,128)} %copy-done.14) | copy-start | bytes 7864324
  485.7 25.4 %copy-start.46 = (f32[1,1024]{1,0:T(1,128)S(1)}, f32[1,1024]{1,0:T(1,128)}, u32[]{:S(2)}) copy-start(f32[1,1024]{1,0:T(1,128)} %copy-done.45) | copy-start | bytes 12292
  485.7 25.4 %copy-start.54 = (f32[640]{0:T(1024)S(1)}, f32[640]{0:T(1024)}, u32[]{:S(2)}) copy-start(f32[640]{0:T(1024)} %copy-done.53) | copy-start | bytes 7684
  485.7 25.4 %copy-start.60 = (f32[1,1024]{1,0:T(1,128)S(1)}, f32[1,1024]{1,0:T(1,128)}, u32[]{:S(2)}) copy-start(f32[1,1024]{1,0:T(1,128)} %copy-done.59) | copy-start | bytes 12292
  485.7 25.4 %copy-start.62 = (f32[640]{0:T(1024)S(1)}, f32[640]{0:T(1024)}, u32[]{:S(2)}) copy-start(f32[640]{0:T(1024)} %copy-done.61) | copy-start | bytes 7684
  511.1 8.2 copy-start.64
  823.1 6.3 copy-start.69
  823.1 23.7 %copy-start.38 = (f32[19,1024]{1,0:T(8,128)S(1)}, f32[19,1024]{1,0:T(8,128)}, u32[]{:S(2)}) copy-start(f32[19,1024]{1,0:T(8,128)} %param.27) | copy-start | bytes 233476
  823.1 23.7 %copy-start.47 = (f32[19,1024]{1,0:T(8,128)S(1)}, f32[19,1024]{1,0:T(8,128)}, u32[]{:S(2)}) copy-start(f32[19,1024]{1,0:T(8,128)} %param.28) | copy-start | bytes 233476
  823.1 23.7 %copy-start.48 = (f32[19,1024]{1,0:T(8,128)S(1)}, f32[19,1024]{1,0:T(8,128)}, u32[]{:S(2)}) copy-start(f32[19,1024]{1,0:T(8,128)} %param.29) | copy-start | bytes 233476
  (40 other events, 93.8 us)
Sparse Core Ops, SparseCore 0:
  201.4 61.0 all-gather.2
  265.9 76.3 all-gather.4
